TPU v7x, 32 devices: a whole 2x2x4 slice. The times are simulated.
32 devices in a mesh: dp: 8 (over z, x), ctx: 4 (over y, core).
Axes of the slice: x: 2, y: 2, z: 4, core: 2. Of those that a mesh axis runs over, the one named last changes fastest.
Arguments:
- hidden_in: bfloat16 [8, 1024, 8192], P('dp', 'ctx'), may hold values from -6 to 6
- queries: bfloat16 [8, 1024, 4096], P('dp', 'ctx'), may hold values from -128 to 128
- key_projection_weight: bfloat16 [8192, 512], P('dp'), may hold values from -0.0625 to 0.0625
- value_projection_weight: bfloat16 [8192, 512], P('dp'), may hold values from -0.0625 to 0.0625
- key_projection_bias: float32 [512], replicated, may hold values from -2.5 to 2.5
- value_projection_bias: float32 [512], replicated, may hold values from -3 to 3
- block_segments: int32 [8, 8], P('dp'), may hold values from 0 to 4, never falling along the last dimension, each value on 1 to 3 neighbouring positions
Outputs:
- attended: bfloat16 [8, 1024, 4096], P('dp', 'ctx')
Inputs may be any that keep to these rules, and one draw needn't show every extreme that they name: `block_segments`: each row starts with segment 0 and never falls; every one of the 5 segments spans 1 to 3 blocks.
All inputs are finite; a program needn't handle non-finite values.
Results may differ from a plain program's by a relative error of at most 0.0079.
Values may be sent and summed in bfloat16 or wider, within the bound.
No kernel may reach another device: no remote copies, remote signals or barrier semaphores. Data moves between devices by JAX's collectives and lax.ppermute only.
A program may use at most 128 MiB of HBM per device.

v0:
```python
import functools
import math

import jax
import jax.numpy as jnp
from jax import lax
from jax.experimental import pallas as pl
from jax.experimental.pallas import tpu as pltpu
from jax.sharding import PartitionSpec as P


HEAD_SIZE = 128
KEY_VALUE_HEADS = 4
BLK = 128
MASKED = -1e30
CORES = 2

rope_base = 1000000.0


def ring_order(count):
    return list(range(0, count, 2)) + list(range(count - 1, 0, -2))


def rope_tables(token_positions):
    half_dim = HEAD_SIZE // 2
    frequency = rope_base ** (
        -(jnp.arange(half_dim, dtype=jnp.float32) * 2.0 / HEAD_SIZE)
    )
    angles = token_positions.astype(jnp.float32)[:, None] * frequency[None, :]
    cos_part, sine_part = jnp.cos(angles), jnp.sin(angles)
    return (
        jnp.concatenate([cos_part, cos_part], axis=1),
        jnp.concatenate([-sine_part, sine_part], axis=1),
    )


def project_kernel(plan, finish, columns, own_ref, sibling_ref, *refs):
    operands = 1 + max(part[0] for parts in plan for part in parts)
    piece_refs = refs[:operands]
    extra_refs = refs[operands:-6]
    out_ref, token_ref, weight_ref, acc_ref, token_sems, weight_sems = refs[-6:]
    number_of_rows, strip = own_ref.shape[0], weight_ref.shape[1]
    part_rows = strip // 2

    def token_copy(at, half):
        tokens_ref = (own_ref, sibling_ref)[half]
        return pltpu.make_async_copy(
            tokens_ref.at[:, pl.ds(pl.multiple_of(columns[at] * strip, strip), strip)],
            token_ref.at[at, pl.ds(half * number_of_rows, number_of_rows), :],
            token_sems.at[at, half],
        )

    def part_copy(operand, first_row, at, part):
        return pltpu.make_async_copy(
            piece_refs[operand].at[pl.ds(first_row, part_rows), :],
            weight_ref.at[at, pl.ds(part * part_rows, part_rows), :],
            weight_sems.at[at, part],
        )

    for at, parts in enumerate(plan):
        for part, (operand, first_row) in enumerate(parts):
            part_copy(operand, first_row, at, part).start()
        for half in range(2):
            token_copy(at, half).start()
    if finish == "add":
        acc_ref[...] = extra_refs[0][...]
    else:
        acc_ref[...] = jnp.zeros_like(acc_ref)

    @pl.loop(0, len(plan) // 2)
    def _(pair):
        for at in (2 * pair, 2 * pair + 1):
            for half in range(2):
                part_copy(0, 0, at, half).wait()
                token_copy(at, half).wait()
        acc_ref[...] += jnp.dot(
            token_ref[2 * pair], weight_ref[2 * pair], preferred_element_type=jnp.float32
        ) + jnp.dot(
            token_ref[2 * pair + 1], weight_ref[2 * pair + 1], preferred_element_type=jnp.float32
        )

    if finish == "key":
        bias_ref, cos_ref, sine_ref = extra_refs
        for first in range(0, acc_ref.shape[1], HEAD_SIZE):
            lanes = slice(first, first + HEAD_SIZE)
            head = acc_ref[:, lanes] + bias_ref[:, lanes]
            turned = head * cos_ref[...] + pltpu.roll(head, HEAD_SIZE // 2, 1) * sine_ref[...]
            out_ref[:, lanes] = turned.astype(out_ref.dtype)
    elif finish == "sum":
        out_ref[...] = acc_ref[...] + extra_refs[0][...]
    else:
        out_ref[...] = acc_ref[...].astype(out_ref.dtype)


def project(finish, strip, own_tokens, sibling_tokens, pieces, plan, columns, extras):
    number_of_rows = own_tokens.shape[0]
    width = pieces[0].shape[1]
    anywhere = pl.BlockSpec(memory_space=pl.ANY)
    chip_rows = CORES * number_of_rows
    out = jax.ShapeDtypeStruct(
        (chip_rows, width), jnp.float32 if finish == "sum" else jnp.bfloat16
    )
    return pl.pallas_call(
        functools.partial(project_kernel, plan, finish),
        out_shape=out,
        grid_spec=pltpu.PrefetchScalarGridSpec(
            num_scalar_prefetch=1,
            grid=(1,),
            in_specs=[anywhere] * (2 + len(pieces))
            + [pl.BlockSpec(x.shape, lambda p, b: (0, 0)) for x in extras],
            out_specs=pl.BlockSpec(out.shape, lambda p, b: (0, 0)),
            scratch_shapes=[
                pltpu.VMEM((len(plan), chip_rows, strip), jnp.bfloat16),
                pltpu.VMEM((len(plan), strip, width), jnp.bfloat16),
                pltpu.VMEM((chip_rows, width), jnp.float32),
                pltpu.SemaphoreType.DMA((len(plan), 2)),
                pltpu.SemaphoreType.DMA((len(plan), 2)),
            ],
        ),
        cost_estimate=pl.CostEstimate(
            flops=2 * len(plan) * strip * chip_rows * width,
            bytes_accessed=2 * len(plan) * strip * (chip_rows + width),
            transcendentals=0,
        ),
    )(columns, own_tokens, sibling_tokens, *pieces, *extras)


def attention_kernel(hops, row_blocks, group, facts, *refs):
    q_ref = refs[0]
    k_refs = refs[1 : 1 + hops]
    v_refs = refs[1 + hops : 1 + 2 * hops]
    out_ref, score_ref, peak_ref, total_ref, acc_ref = refs[-5:]
    chip_blocks = CORES * row_blocks
    row_block = pl.program_id(1)
    source_core, ctx_index = facts[1], facts[2]
    chip = ctx_index // CORES
    here = ctx_index * row_blocks + row_block
    segment = facts[3 + here]
    factor = math.log2(math.e) / math.sqrt(HEAD_SIZE)
    rows = group * BLK

    def place(local):
        core = local // row_blocks
        slot = jnp.where(core == source_core, 0, row_blocks) + local % row_blocks
        return pl.ds(pl.multiple_of(slot * BLK, BLK), BLK)

    def queries():
        return jnp.concatenate(
            [q_ref[:, h * HEAD_SIZE : (h + 1) * HEAD_SIZE] for h in range(group)], axis=0
        )

    def scores(k_ref, local):
        return lax.dot_general(
            queries(),
            k_ref[place(local), :],
            (((1,), (1,)), ((), ())),
            preferred_element_type=jnp.float32,
        )

    def over_blocks(visit):
        for hop in range(hops):

            @pl.loop(0, chip_blocks)
            def _(local):
                block = (chip - hop) * chip_blocks + local
                seen = facts[3 + jnp.maximum(block, 0)]

                @pl.when(
                    (block >= 0) & (block < here) & ((seen == 0) | (seen == segment))
                )
                def _():
                    visit(hop, local)

    diagonal = lax.rem(here, chip_blocks)
    later = lax.broadcasted_iota(jnp.int32, (rows, BLK), 1) > (
        lax.broadcasted_iota(jnp.int32, (rows, BLK), 0) % BLK
    )
    own = jnp.where(later, MASKED, scores(k_refs[0], diagonal))
    score_ref[diagonal] = own
    peak_ref[...] = own

    def first(hop, local):
        found = scores(k_refs[hop], local)
        score_ref[hop * chip_blocks + local] = found
        peak_ref[...] = jnp.maximum(peak_ref[...], found)

    over_blocks(first)
    peak = jnp.max(peak_ref[...], axis=1, keepdims=True)
    peak_ref[...] = jnp.broadcast_to(peak, (rows, BLK))

    def weigh(hop, local):
        probs = jnp.exp2((score_ref[hop * chip_blocks + local] - peak_ref[...]) * factor)
        return probs, jnp.dot(
            probs.astype(jnp.bfloat16),
            v_refs[hop][place(local), :],
            preferred_element_type=jnp.float32,
        )

    total_ref[...], acc_ref[...] = weigh(0, diagonal)

    def second(hop, local):
        probs, mixed = weigh(hop, local)
        total_ref[...] += probs
        acc_ref[...] += mixed

    over_blocks(second)
    total = jnp.sum(total_ref[...], axis=1, keepdims=True)
    mixed = (acc_ref[...] / total).astype(out_ref.dtype)
    for h in range(group):
        out_ref[:, h * HEAD_SIZE : (h + 1) * HEAD_SIZE] = mixed[h * BLK : (h + 1) * BLK]


def attend(facts, queries, keys, values, before):
    hops = len(keys)
    number_of_rows, query_width = queries.shape
    group = query_width // HEAD_SIZE // KEY_VALUE_HEADS
    heads = KEY_VALUE_HEADS // CORES
    row_blocks = number_of_rows // BLK
    width = group * HEAD_SIZE
    rows = group * BLK
    q_spec = pl.BlockSpec((BLK, width), lambda l, r, f: (r, f[0] * heads + l))
    kv_spec = pl.BlockSpec((keys[0].shape[0], HEAD_SIZE), lambda l, r, f: (0, l))
    operands = [facts, queries, *keys, *values]
    in_specs = [q_spec] + [kv_spec] * (2 * hops)
    aliases = {}
    if before is not None:
        aliases = {len(operands): 0}
        operands.append(before)
        in_specs.append(pl.BlockSpec(memory_space=pl.ANY))
    total_blocks = hops * CORES * row_blocks
    pairs = heads * row_blocks * rows * total_blocks * BLK // 2
    return pl.pallas_call(
        functools.partial(attention_kernel, hops, row_blocks, group),
        out_shape=jax.ShapeDtypeStruct(queries.shape, queries.dtype),
        grid_spec=pltpu.PrefetchScalarGridSpec(
            num_scalar_prefetch=1,
            grid=(heads, row_blocks),
            in_specs=in_specs,
            out_specs=q_spec,
            scratch_shapes=[
                pltpu.VMEM((total_blocks, rows, BLK), jnp.float32),
                pltpu.VMEM((rows, BLK), jnp.float32),
                pltpu.VMEM((rows, BLK), jnp.float32),
                pltpu.VMEM((rows, HEAD_SIZE), jnp.float32),
            ],
        ),
        input_output_aliases=aliases,
        cost_estimate=pl.CostEstimate(
            flops=4 * pairs * HEAD_SIZE,
            bytes_accessed=2 * number_of_rows * query_width * 2,
            transcendentals=pairs,
        ),
        name="attend",
    )(*operands)


def layer(
    hidden_in,
    queries,
    key_projection_weight,
    value_projection_weight,
    key_projection_bias,
    value_projection_bias,
    block_segments,
):
    own_tokens = hidden_in[0]
    number_of_rows = own_tokens.shape[0]
    depth, kv_width = key_projection_weight.shape
    dp_size, ctx_size = lax.axis_size("dp"), lax.axis_size("ctx")
    chips = ctx_size // CORES
    my_index = lax.axis_index("ctx")
    core, chip = my_index % CORES, my_index // CORES
    plane = chip % 2
    half_width = kv_width // CORES
    ring = ring_order(dp_size)
    dp_index = lax.axis_index("dp")
    spots = [0] * dp_size
    for spot, index in enumerate(ring):
        spots[index] = spot
    my_spot = jnp.asarray(spots, jnp.int32)[dp_index]
    ring_array = jnp.asarray(ring, jnp.int32)

    def to_sibling(x):
        return lax.ppermute(x, "ctx", [(i, i ^ 1) for i in range(ctx_size)])

    def to_plane(x):
        return lax.ppermute(x, "ctx", [(i, i ^ CORES) for i in range(ctx_size)])

    def to_next_chip(x):
        return lax.ppermute(x, "ctx", [(i, i + CORES) for i in range(ctx_size - CORES)])

    def along_ring(x, step):
        return lax.ppermute(
            x, "dp", [(ring[i], ring[(i + step) % dp_size]) for i in range(dp_size)]
        )

    key_weight = lax.dynamic_slice_in_dim(key_projection_weight, core * half_width, half_width, 1)
    value_weight = lax.dynamic_slice_in_dim(
        value_projection_weight, core * half_width, half_width, 1
    )
    strip = depth // 2
    part = strip // 2
    key_strip = lax.dynamic_slice_in_dim(key_weight, plane * strip, strip, 0)
    sibling_tokens = to_sibling(own_tokens)

    def source_at(distance):
        return ring_array[(my_spot + distance + dp_size) % dp_size]

    half_ring = dp_size // 2

    key_pieces, key_plan, key_blocks = [key_weight], [], []
    for side in range(2):
        key_plan.append(((0, side * strip), (0, side * strip + part)))
        key_blocks.append(dp_index * 2 + side)
    travelling = {1: key_strip, -1: key_strip}
    last = []
    for hop in range(1, half_ring + 1):
        for step in (1, -1):
            piece = travelling[step]
            if hop == half_ring:
                first_row = 0 if step == 1 else part
                piece = piece[first_row : first_row + part]
            piece = along_ring(piece, step)
            travelling[step] = piece
            last.append((len(key_pieces), len(key_pieces) + 1))
            key_pieces += [piece, to_plane(piece)]
            if hop < half_ring:
                for side, at in enumerate(last[-1]):
                    key_plan.append(((at, 0), (at, part)))
                    key_blocks.append(
                        source_at(-step * hop) * 2 + (plane if side == 0 else 1 - plane)
                    )
    for side in range(2):
        key_plan.append(((last[-2][side], 0), (last[-1][side], 0)))
        key_blocks.append(source_at(half_ring) * 2 + (plane if side == 0 else 1 - plane))

    value_pieces, value_plan, value_blocks = [value_weight], [], []
    for side in range(2):
        value_plan.append(((0, side * strip), (0, side * strip + part)))
        value_blocks.append(dp_index * 2 + side)
    travelling = {1: value_weight, -1: value_weight}
    for hop in range(1, half_ring):
        for step in (1, -1):
            piece = along_ring(travelling[step], step)
            travelling[step] = piece
            at = len(value_pieces)
            value_pieces.append(piece)
            for side in range(2):
                value_plan.append(((at, side * strip), (at, side * strip + part)))
                value_blocks.append(source_at(-step * hop) * 2 + side)
    end_pieces = [
        along_ring(travelling[1][:strip], 1),
        along_ring(travelling[-1][strip:], -1),
    ]
    end_plan = [((side, 0), (side, part)) for side in range(2)]
    end_blocks = [source_at(half_ring) * 2 + side for side in range(2)]

    arange = jnp.arange(number_of_rows, dtype=jnp.int32)
    positions = jnp.concatenate(
        [my_index * number_of_rows + arange, (my_index ^ 1) * number_of_rows + arange]
    )
    key_bias = lax.dynamic_slice_in_dim(key_projection_bias, core * half_width, half_width, 0)
    value_bias = lax.dynamic_slice_in_dim(value_projection_bias, core * half_width, half_width, 0)

    def projected(finish, pieces, plan, blocks, extras):
        return project(
            finish,
            strip,
            own_tokens,
            sibling_tokens,
            pieces,
            tuple(plan),
            jnp.stack(blocks).astype(jnp.int32),
            extras,
        )

    key_rows = projected(
        "key", key_pieces, key_plan, key_blocks, [key_bias[None], *rope_tables(positions)]
    )
    value_sum = projected("sum", value_pieces, value_plan, value_blocks, [value_bias[None]])
    value_rows = projected("add", end_pieces, end_plan, end_blocks, [value_sum])

    keys, values = [key_rows], [value_rows]
    for _ in range(chips - 1):
        keys.append(to_next_chip(keys[-1]))
        values.append(to_next_chip(values[-1]))
    sibling_keys = [to_sibling(x) for x in keys]
    sibling_values = [to_sibling(x) for x in values]

    def facts(half):
        return jnp.concatenate([jnp.stack([half, half, my_index]), block_segments[0]])

    own_queries = queries[0]
    attended = attend(facts(core), own_queries, keys, values, None)
    attended = attend(facts(1 - core), own_queries, sibling_keys, sibling_values, attended)
    return attended[None]


def solution(mesh):
    placed = (
        P("dp", "ctx", None),
        P("dp", "ctx", None),
        P("dp", None),
        P("dp", None),
        P(),
        P(),
        P("dp", None),
    )
    return jax.shard_map(
        layer, mesh=mesh, in_specs=placed, out_specs=P("dp", "ctx", None), check_vma=False
    )
```

profile of v0, /device:TPU:12, one launch (start us, length us, event | category | flops | bytes accessed | tf_op | source)
XLA Modules:
  0.0 144.9 jit_solution(448012338976775400)
XLA Ops:
  0.1 1.2 dynamic_slice.69
  1.4 1.6 %collective-permute-start.1 = (bf16[512,256]{1,0:T(8,128)(2,1)S(1)}, bf16[512,256]{1,0:T(8,128)(2,1)S(1)}, u32[]{:S(2)}, u32[]{:S(2)}) collective-permute-start(bf16[512,256]{1,0:T(8,128)(2,1)S(1)} %dynamic_slice.69), channel_id=1, source_target_pairs={{0,8},{8,16},{16,24},{24,28},{28,20},{20,12},{12,4},{4,0},{1,9},{9... | collective-permute-start | bytes 786440 | tf_op jit(solution)/shard_map/ppermute | solution.py:294
  3.5 1.6 %collective-permute-start.20 = (bf16[1024,256]{1,0:T(8,128)(2,1)S(1)}, bf16[1024,256]{1,0:T(8,128)(2,1)S(1)}, u32[]{:S(2)}, u32[]{:S(2)}) collective-permute-start(bf16[1024,256]{1,0:T(8,128)(2,1)S(1)} %constant_dynamic-slice_fusion.refs_0_), channel_id=1, source_target_pairs={{0,8},{8,16},{16,24},{24,28},{28,20},{20,12},{12,4},{4,0},{1,9},{9... | collective-permute-start | bytes 1572872 | tf_op jit(solution)/shard_map/ppermute | solution.py:294
  5.6 5.0 %collective-permute-done.1.refs_1_ = bf16[512,256]{1,0:T(8,128)(2,1)S(1)} collective-permute-done((bf16[512,256]{1,0:T(8,128)(2,1)S(1)}, bf16[512,256]{1,0:T(8,128)(2,1)S(1)}, u32[]{:S(2)}, u32[]{:S(2)}) %collective-permute-start.1) | collective-permute-done | bytes 262176 | tf_op jit(solution)/shard_map/ppermute | solution.py:294
  11.1 1.1 collective-permute-done.3.refs_3_
  12.7 7.1 %collective-permute-done.2.refs_2_ = bf16[512,256]{1,0:T(8,128)(2,1)S(1)} collective-permute-done((bf16[512,256]{1,0:T(8,128)(2,1)S(1)}, bf16[512,256]{1,0:T(8,128)(2,1)S(1)}, u32[]{:S(2)}, u32[]{:S(2)}) %collective-permute-start.2) | collective-permute-done | bytes 262176 | tf_op jit(solution)/shard_map/ppermute | solution.py:288
  19.8 1.6 %collective-permute-start.5 = (bf16[512,256]{1,0:T(8,128)(2,1)S(1)}, bf16[512,256]{1,0:T(8,128)(2,1)}, u32[]{:S(2)}, u32[]{:S(2)}) collective-permute-start(bf16[512,256]{1,0:T(8,128)(2,1)S(1)} %collective-permute-done.1.refs_1_), channel_id=1, source_target_pairs={{0,8},{8,16},{16,24},{24,28},{28,20},{20,12},{12,4},{4,0},{1,9},{9... | collective-permute-start | bytes 786440 | tf_op jit(solution)/shard_map/ppermute | solution.py:294
  21.3 1.9 %collective-permute-done.4.refs_4_ = bf16[512,256]{1,0:T(8,128)(2,1)S(1)} collective-permute-done((bf16[512,256]{1,0:T(8,128)(2,1)S(1)}, bf16[512,256]{1,0:T(8,128)(2,1)S(1)}, u32[]{:S(2)}, u32[]{:S(2)}) %collective-permute-start.4) | collective-permute-done | bytes 262176 | tf_op jit(solution)/shard_map/ppermute | solution.py:288
  23.7 1.6 %collective-permute-start.21 = (bf16[1024,256]{1,0:T(8,128)(2,1)S(1)}, bf16[1024,256]{1,0:T(8,128)(2,1)}, u32[]{:S(2)}, u32[]{:S(2)}) collective-permute-start(bf16[1024,256]{1,0:T(8,128)(2,1)S(1)} %collective-permute-done.20.refs_1_), channel_id=1, source_target_pairs={{0,8},{8,16},{16,24},{24,28},{28,20},{20,12},{12,4},{4,0},{1,9},{9... | collective-permute-start | bytes 1572872 | tf_op jit(solution)/shard_map/ppermute | solution.py:294
  25.8 3.3 %collective-permute-done.5.refs_5_ = bf16[512,256]{1,0:T(8,128)(2,1)} collective-permute-done((bf16[512,256]{1,0:T(8,128)(2,1)S(1)}, bf16[512,256]{1,0:T(8,128)(2,1)}, u32[]{:S(2)}, u32[]{:S(2)}) %collective-permute-start.5) | collective-permute-done | bytes 262176 | tf_op jit(solution)/shard_map/ppermute | solution.py:294
  29.1 1.6 %collective-permute-start.9 = (bf16[512,256]{1,0:T(8,128)(2,1)}, bf16[512,256]{1,0:T(8,128)(2,1)S(1)}, u32[]{:S(2)}, u32[]{:S(2)}) collective-permute-start(bf16[512,256]{1,0:T(8,128)(2,1)} %collective-permute-done.5.refs_5_), channel_id=1, source_target_pairs={{0,8},{8,16},{16,24},{24,28},{28,20},{20,12},{12,4},{4,0},{1,9},{9... | collective-permute-start | bytes 786440 | tf_op jit(solution)/shard_map/ppermute | solution.py:294
  30.6 1.9 %collective-permute-done.7.refs_7_ = bf16[512,256]{1,0:T(8,128)(2,1)} collective-permute-done((bf16[512,256]{1,0:T(8,128)(2,1)S(1)}, bf16[512,256]{1,0:T(8,128)(2,1)}, u32[]{:S(2)}, u32[]{:S(2)}) %collective-permute-start.7) | collective-permute-done | bytes 262176 | tf_op jit(solution)/shard_map/ppermute | solution.py:294
  33.0 10.7 %collective-permute-done.9.refs_9_ = bf16[512,256]{1,0:T(8,128)(2,1)S(1)} collective-permute-done((bf16[512,256]{1,0:T(8,128)(2,1)}, bf16[512,256]{1,0:T(8,128)(2,1)S(1)}, u32[]{:S(2)}, u32[]{:S(2)}) %collective-permute-start.9) | collective-permute-done | bytes 262176 | tf_op jit(solution)/shard_map/ppermute | solution.py:294
  44.2 2.2 %collective-permute-done.11.refs_11_ = bf16[512,256]{1,0:T(8,128)(2,1)S(1)} collective-permute-done((bf16[512,256]{1,0:T(8,128)(2,1)}, bf16[512,256]{1,0:T(8,128)(2,1)S(1)}, u32[]{:S(2)}, u32[]{:S(2)}) %collective-permute-start.11) | collective-permute-done | bytes 262176 | tf_op jit(solution)/shard_map/ppermute | solution.py:294
  46.8 1.6 %collective-permute-start.22 = (bf16[1024,256]{1,0:T(8,128)(2,1)}, bf16[1024,256]{1,0:T(8,128)(2,1)S(1)}, u32[]{:S(2)}, u32[]{:S(2)}) collective-permute-start(bf16[1024,256]{1,0:T(8,128)(2,1)} %collective-permute-done.21.refs_3_), channel_id=1, source_target_pairs={{0,8},{8,16},{16,24},{24,28},{28,20},{20,12},{12,4},{4,0},{1,9},{9... | collective-permute-start | bytes 1572872 | tf_op jit(solution)/shard_map/ppermute | solution.py:294
  49.0 4.0 %collective-permute-done.6.refs_6_ = bf16[512,256]{1,0:T(8,128)(2,1)S(1)} collective-permute-done((bf16[512,256]{1,0:T(8,128)(2,1)}, bf16[512,256]{1,0:T(8,128)(2,1)S(1)}, u32[]{:S(2)}, u32[]{:S(2)}) %collective-permute-start.6) | collective-permute-done | bytes 262176 | tf_op jit(solution)/shard_map/ppermute | solution.py:288
  53.0 1.6 %collective-permute-start.13 = (bf16[256,256]{1,0:T(8,128)(2,1)S(1)}, bf16[256,256]{1,0:T(8,128)(2,1)S(1)}, u32[]{:S(2)}, u32[]{:S(2)}) collective-permute-start(bf16[256,256]{1,0:T(8,128)(2,1)S(1)} %slice.16), channel_id=1, source_target_pairs={{0,8},{8,16},{16,24},{24,28},{28,20},{20,12},{12,4},{4,0},{1,9},{9... | collective-permute-start | bytes 393224 | tf_op jit(solution)/shard_map/ppermute | solution.py:294
  54.5 1.2 collective-permute-done.8.refs_8_
  57.7 3.0 %collective-permute-done.13.refs_13_ = bf16[256,256]{1,0:T(8,128)(2,1)S(1)} collective-permute-done((bf16[256,256]{1,0:T(8,128)(2,1)S(1)}, bf16[256,256]{1,0:T(8,128)(2,1)S(1)}, u32[]{:S(2)}, u32[]{:S(2)}) %collective-permute-start.13) | collective-permute-done | bytes 131104 | tf_op jit(solution)/shard_map/ppermute | solution.py:294
  60.7 1.5 %collective-permute-start.10 = (bf16[512,256]{1,0:T(8,128)(2,1)}, bf16[512,256]{1,0:T(8,128)(2,1)}, u32[]{:S(2)}, u32[]{:S(2)}) collective-permute-start(bf16[512,256]{1,0:T(8,128)(2,1)} %copy-done.5), channel_id=1, source_target_pairs={{0,2},{1,3},{2,0},{3,1},{4,6},{5,7},{6,4},{7,5},{8,10},{9,11},{10,... | collective-permute-start | bytes 786440 | tf_op jit(solution)/shard_map/ppermute | solution.py:288
  62.2 1.4 collective-permute-start.12
  63.6 1.9 %constant_dynamic-slice_fusion.1.refs_0_ = bf16[1024,256]{1,0:T(8,128)(2,1)} fusion(bf16[1024,512]{1,0:T(8,128)(2,1)} %param.11, s32[]{:T(128)S(6)} %select_n.161), kind=kLoop, calls=%fused_computation.13 | loop fusion | bytes 1048580 | tf_op jit(solution)/shard_map/dynamic_slice | solution.py:298
  72.7 1.4 collective-permute-start.16
  82.2 1.6 %collective-permute-start.23 = (bf16[512,256]{1,0:T(8,128)(2,1)S(1)}, bf16[512,256]{1,0:T(8,128)(2,1)S(1)}, u32[]{:S(2)}, u32[]{:S(2)}) collective-permute-start(bf16[512,256]{1,0:T(8,128)(2,1)S(1)} %slice.18), channel_id=1, source_target_pairs={{0,8},{8,16},{16,24},{24,28},{28,20},{20,12},{12,4},{4,0},{1,9},{9... | collective-permute-start | bytes 786440 | tf_op jit(solution)/shard_map/ppermute | solution.py:294
  84.4 8.3 %shard_map.91.refs_1_ = bf16[512,256]{1,0:T(8,128)(2,1)} custom-call(s32[16]{0:T(128)} %stack.117.columns, bf16[256,8192]{1,0:T(8,128)(2,1)} %bitcast.47, bf16[256,8192]{1,0:T(8,128)(2,1)} %collective-permute-done.sibling_ref, bf16[1024,256]{1,0:T(8,128)(2,1)} %constant_dynamic-slice_fusion.1.refs_0_, bf16[512,256]{1,0:T(8,128)(2,1)} %copy-done.9, ...), custom_call_target="tpu_custom_call" | custom-call | flops 2147483648 | bytes 12582912 | tf_op jit(solution)/shard_map/pallas_call | solution.py:104
  92.7 1.3 collective-permute-start.18
  94.0 7.3 %shard_map.92.refs_2_ = f32[512,256]{1,0:T(8,128)} custom-call(s32[14]{0:T(128)} %stack.126.columns, bf16[256,8192]{1,0:T(8,128)(2,1)} %bitcast.48, bf16[256,8192]{1,0:T(8,128)(2,1)} %collective-permute-done.sibling_ref, bf16[1024,256]{1,0:T(8,128)(2,1)} %copy-done.1, bf16[1024,256]{1,0:T(8,128)(2,1)} %copy-done.7, bf16[1024,256]{1,0:T(8,128)(2,1)} %copy-done.8, ...), custom_call_target="tpu_custom_call" | custom-call | flops 1879048192 | bytes 11010048 | tf_op jit(solution)/shard_map/pallas_call | solution.py:104
  102.7 4.4 %shard_map.93.refs_3_ = bf16[512,256]{1,0:T(8,128)(2,1)} custom-call(s32[2]{0:T(128)} %pad_add_fusion.columns, bf16[256,8192]{1,0:T(8,128)(2,1)} %bitcast.49, bf16[256,8192]{1,0:T(8,128)(2,1)} %collective-permute-done.sibling_ref, bf16[512,256]{1,0:T(8,128)(2,1)} %copy-done.15, bf16[512,256]{1,0:T(8,128)(2,1)} %copy-done.16, f32[512,256]{1,0:T(8,128)} %shard_map.92.refs_2_), custom_call_target="tpu_custom_call" | custom-call | flops 268435456 | bytes 1572864 | tf_op jit(solution)/shard_map/pallas_call | solution.py:104
  107.1 1.3 collective-permute-start.29
  109.1 7.2 %collective-permute-done.29.refs_4_ = bf16[512,256]{1,0:T(8,128)(2,1)S(1)} collective-permute-done((bf16[512,256]{1,0:T(8,128)(2,1)}, bf16[512,256]{1,0:T(8,128)(2,1)S(1)}, u32[]{:S(2)}, u32[]{:S(2)}) %collective-permute-start.29) | collective-permute-done | bytes 262176 | tf_op jit(solution)/shard_map/ppermute | solution.py:291
  117.0 13.4 %attend.2.refs_5_ = bf16[256,4096]{1,0:T(8,128)(2,1)} custom-call(s32[11]{0:T(128)} %get-tuple-element.8.facts, bf16[256,4096]{1,0:T(8,128)(2,1)} %bitcast.50, bf16[512,256]{1,0:T(8,128)(2,1)} %shard_map.91.refs_1_, bf16[512,256]{1,0:T(8,128)(2,1)} %collective-permute-done.18.refs_2_, bf16[512,256]{1,0:T(8,128)(2,1)} %shard_map.93.refs_3_, ...), custom_call_target="tpu_custom_call" | custom-call | flops 1073741824 | bytes 4194304 | tf_op jit(solution)/shard_map/attend/pallas_call | solution.py:233
  131.4 13.4 %attend.3 = bf16[256,4096]{1,0:T(8,128)(2,1)} custom-call(s32[11]{0:T(128)} %get-tuple-element.9.facts, bf16[256,4096]{1,0:T(8,128)(2,1)} %bitcast.51, bf16[512,256]{1,0:T(8,128)(2,1)} %copy-done.18, bf16[512,256]{1,0:T(8,128)(2,1)} %copy-done.20, bf16[512,256]{1,0:T(8,128)(2,1)} %copy-done.19, ...), custom_call_target="tpu_custom_call", output_to_operand_aliasing={{}: (6, {})} | custom-call | flops 1073741824 | bytes 4194304 | tf_op jit(solution)/shard_map/attend/pallas_call | solution.py:233
  (112 shorter events, 17.3 us)
Async XLA Ops:
  0.0 84.3 %collective-permute-start = (bf16[256,8192]{1,0:T(8,128)(2,1)}, bf16[256,8192]{1,0:T(8,128)(2,1)}, u32[]{:S(2)}, u32[]{:S(2)}) collective-permute-start(bf16[256,8192]{1,0:T(8,128)(2,1)} %bitcast.46), channel_id=1, source_target_pairs={{0,1},{1,0},{2,3},{3,2},{4,5},{5,4},{6,7},{7,6},{8,9},{9,8},{10,11... | collective-permute-start | bytes 12582920 | tf_op jit(solution)/shard_map/ppermute | solution.py:285
  0.1 79.1 %copy-start.25 = (f32[512]{0:T(512)S(1)}, f32[512]{0:T(512)}, u32[]{:S(2)}) copy-start(f32[512]{0:T(512)} %param.14) | copy-start | bytes 6148
  1.4 9.2 %collective-permute-start.1 = (bf16[512,256]{1,0:T(8,128)(2,1)S(1)}, bf16[512,256]{1,0:T(8,128)(2,1)S(1)}, u32[]{:S(2)}, u32[]{:S(2)}) collective-permute-start(bf16[512,256]{1,0:T(8,128)(2,1)S(1)} %dynamic_slice.69), channel_id=1, source_target_pairs={{0,8},{8,16},{16,24},{24,28},{28,20},{20,12},{12,4},{4,0},{1,9},{9... | collective-permute-start | bytes 786440 | tf_op jit(solution)/shard_map/ppermute | solution.py:294
  3.0 9.2 %collective-permute-start.3 = (bf16[512,256]{1,0:T(8,128)(2,1)S(1)}, bf16[512,256]{1,0:T(8,128)(2,1)S(1)}, u32[]{:S(2)}, u32[]{:S(2)}) collective-permute-start(bf16[512,256]{1,0:T(8,128)(2,1)S(1)} %dynamic_slice.69), channel_id=1, source_target_pairs={{0,4},{8,0},{16,8},{24,16},{28,24},{20,28},{12,20},{4,12},{1,5},{9... | collective-permute-start | bytes 786440 | tf_op jit(solution)/shard_map/ppermute | solution.py:294
  3.5 20.2 %collective-permute-start.20 = (bf16[1024,256]{1,0:T(8,128)(2,1)S(1)}, bf16[1024,256]{1,0:T(8,128)(2,1)S(1)}, u32[]{:S(2)}, u32[]{:S(2)}) collective-permute-start(bf16[1024,256]{1,0:T(8,128)(2,1)S(1)} %constant_dynamic-slice_fusion.refs_0_), channel_id=1, source_target_pairs={{0,8},{8,16},{16,24},{24,28},{28,20},{20,12},{12,4},{4,0},{1,9},{9... | collective-permute-start | bytes 1572872 | tf_op jit(solution)/shard_map/ppermute | solution.py:294
  5.1 20.2 %collective-permute-start.24 = (bf16[1024,256]{1,0:T(8,128)(2,1)S(1)}, bf16[1024,256]{1,0:T(8,128)(2,1)S(1)}, u32[]{:S(2)}, u32[]{:S(2)}) collective-permute-start(bf16[1024,256]{1,0:T(8,128)(2,1)S(1)} %constant_dynamic-slice_fusion.refs_0_), channel_id=1, source_target_pairs={{0,4},{8,0},{16,8},{24,16},{28,24},{20,28},{12,20},{4,12},{1,5},{9... | collective-permute-start | bytes 1572872 | tf_op jit(solution)/shard_map/ppermute | solution.py:294
  10.6 9.2 %collective-permute-start.2 = (bf16[512,256]{1,0:T(8,128)(2,1)S(1)}, bf16[512,256]{1,0:T(8,128)(2,1)S(1)}, u32[]{:S(2)}, u32[]{:S(2)}) collective-permute-start(bf16[512,256]{1,0:T(8,128)(2,1)S(1)} %collective-permute-done.1.refs_1_), channel_id=1, source_target_pairs={{0,2},{1,3},{2,0},{3,1},{4,6},{5,7},{6,4},{7,5},{8,10},{9,11},{10,... | collective-permute-start | bytes 786440 | tf_op jit(solution)/shard_map/ppermute | solution.py:288
  12.2 11.1 %collective-permute-start.4 = (bf16[512,256]{1,0:T(8,128)(2,1)S(1)}, bf16[512,256]{1,0:T(8,128)(2,1)S(1)}, u32[]{:S(2)}, u32[]{:S(2)}) collective-permute-start(bf16[512,256]{1,0:T(8,128)(2,1)S(1)} %collective-permute-done.3.refs_3_), channel_id=1, source_target_pairs={{0,2},{1,3},{2,0},{3,1},{4,6},{5,7},{6,4},{7,5},{8,10},{9,11},{10,... | collective-permute-start | bytes 786440 | tf_op jit(solution)/shard_map/ppermute | solution.py:288
  19.8 9.3 %collective-permute-start.5 = (bf16[512,256]{1,0:T(8,128)(2,1)S(1)}, bf16[512,256]{1,0:T(8,128)(2,1)}, u32[]{:S(2)}, u32[]{:S(2)}) collective-permute-start(bf16[512,256]{1,0:T(8,128)(2,1)S(1)} %collective-permute-done.1.refs_1_), channel_id=1, source_target_pairs={{0,8},{8,16},{16,24},{24,28},{28,20},{20,12},{12,4},{4,0},{1,9},{9... | collective-permute-start | bytes 786440 | tf_op jit(solution)/shard_map/ppermute | solution.py:294
  23.3 9.3 %collective-permute-start.7 = (bf16[512,256]{1,0:T(8,128)(2,1)S(1)}, bf16[512,256]{1,0:T(8,128)(2,1)}, u32[]{:S(2)}, u32[]{:S(2)}) collective-permute-start(bf16[512,256]{1,0:T(8,128)(2,1)S(1)} %collective-permute-done.3.refs_3_), channel_id=1, source_target_pairs={{0,4},{8,0},{16,8},{24,16},{28,24},{20,28},{12,20},{4,12},{1,5},{9... | collective-permute-start | bytes 786440 | tf_op jit(solution)/shard_map/ppermute | solution.py:294
  23.7 23.1 %collective-permute-start.21 = (bf16[1024,256]{1,0:T(8,128)(2,1)S(1)}, bf16[1024,256]{1,0:T(8,128)(2,1)}, u32[]{:S(2)}, u32[]{:S(2)}) collective-permute-start(bf16[1024,256]{1,0:T(8,128)(2,1)S(1)} %collective-permute-done.20.refs_1_), channel_id=1, source_target_pairs={{0,8},{8,16},{16,24},{24,28},{28,20},{20,12},{12,4},{4,0},{1,9},{9... | collective-permute-start | bytes 1572872 | tf_op jit(solution)/shard_map/ppermute | solution.py:294
  25.3 23.2 %collective-permute-start.25 = (bf16[1024,256]{1,0:T(8,128)(2,1)S(1)}, bf16[1024,256]{1,0:T(8,128)(2,1)}, u32[]{:S(2)}, u32[]{:S(2)}) collective-permute-start(bf16[1024,256]{1,0:T(8,128)(2,1)S(1)} %collective-permute-done.24.refs_2_), channel_id=1, source_target_pairs={{0,4},{8,0},{16,8},{24,16},{28,24},{20,28},{12,20},{4,12},{1,5},{9... | collective-permute-start | bytes 1572872 | tf_op jit(solution)/shard_map/ppermute | solution.py:294
  29.1 14.6 %collective-permute-start.9 = (bf16[512,256]{1,0:T(8,128)(2,1)}, bf16[512,256]{1,0:T(8,128)(2,1)S(1)}, u32[]{:S(2)}, u32[]{:S(2)}) collective-permute-start(bf16[512,256]{1,0:T(8,128)(2,1)} %collective-permute-done.5.refs_5_), channel_id=1, source_target_pairs={{0,8},{8,16},{16,24},{24,28},{28,20},{20,12},{12,4},{4,0},{1,9},{9... | collective-permute-start | bytes 786440 | tf_op jit(solution)/shard_map/ppermute | solution.py:294
  32.6 13.8 %collective-permute-start.11 = (bf16[512,256]{1,0:T(8,128)(2,1)}, bf16[512,256]{1,0:T(8,128)(2,1)S(1)}, u32[]{:S(2)}, u32[]{:S(2)}) collective-permute-start(bf16[512,256]{1,0:T(8,128)(2,1)} %collective-permute-done.7.refs_7_), channel_id=1, source_target_pairs={{0,4},{8,0},{16,8},{24,16},{28,24},{20,28},{12,20},{4,12},{1,5},{9... | collective-permute-start | bytes 786440 | tf_op jit(solution)/shard_map/ppermute | solution.py:294
  43.7 9.3 %collective-permute-start.6 = (bf16[512,256]{1,0:T(8,128)(2,1)}, bf16[512,256]{1,0:T(8,128)(2,1)S(1)}, u32[]{:S(2)}, u32[]{:S(2)}) collective-permute-start(bf16[512,256]{1,0:T(8,128)(2,1)} %collective-permute-done.5.refs_5_), channel_id=1, source_target_pairs={{0,2},{1,3},{2,0},{3,1},{4,6},{5,7},{6,4},{7,5},{8,10},{9,11},{10,... | collective-permute-start | bytes 786440 | tf_op jit(solution)/shard_map/ppermute | solution.py:288
  46.3 9.5 %collective-permute-start.8 = (bf16[512,256]{1,0:T(8,128)(2,1)}, bf16[512,256]{1,0:T(8,128)(2,1)S(1)}, u32[]{:S(2)}, u32[]{:S(2)}) collective-permute-start(bf16[512,256]{1,0:T(8,128)(2,1)} %collective-permute-done.7.refs_7_), channel_id=1, source_target_pairs={{0,2},{1,3},{2,0},{3,1},{4,6},{5,7},{6,4},{7,5},{8,10},{9,11},{10,... | collective-permute-start | bytes 786440 | tf_op jit(solution)/shard_map/ppermute | solution.py:288
  46.8 25.1 %collective-permute-start.22 = (bf16[1024,256]{1,0:T(8,128)(2,1)}, bf16[1024,256]{1,0:T(8,128)(2,1)S(1)}, u32[]{:S(2)}, u32[]{:S(2)}) collective-permute-start(bf16[1024,256]{1,0:T(8,128)(2,1)} %collective-permute-done.21.refs_3_), channel_id=1, source_target_pairs={{0,8},{8,16},{16,24},{24,28},{28,20},{20,12},{12,4},{4,0},{1,9},{9... | collective-permute-start | bytes 1572872 | tf_op jit(solution)/shard_map/ppermute | solution.py:294
  48.5 24.2 %collective-permute-start.26 = (bf16[1024,256]{1,0:T(8,128)(2,1)}, bf16[1024,256]{1,0:T(8,128)(2,1)S(1)}, u32[]{:S(2)}, u32[]{:S(2)}) collective-permute-start(bf16[1024,256]{1,0:T(8,128)(2,1)} %collective-permute-done.25.refs_4_), channel_id=1, source_target_pairs={{0,4},{8,0},{16,8},{24,16},{28,24},{20,28},{12,20},{4,12},{1,5},{9... | collective-permute-start | bytes 1572872 | tf_op jit(solution)/shard_map/ppermute | solution.py:294
  53.0 7.7 %collective-permute-start.13 = (bf16[256,256]{1,0:T(8,128)(2,1)S(1)}, bf16[256,256]{1,0:T(8,128)(2,1)S(1)}, u32[]{:S(2)}, u32[]{:S(2)}) collective-permute-start(bf16[256,256]{1,0:T(8,128)(2,1)S(1)} %slice.16), channel_id=1, source_target_pairs={{0,8},{8,16},{16,24},{24,28},{28,20},{20,12},{12,4},{4,0},{1,9},{9... | collective-permute-start | bytes 393224 | tf_op jit(solution)/shard_map/ppermute | solution.py:294
  55.8 6.4 %collective-permute-start.15 = (bf16[256,256]{1,0:T(8,128)(2,1)S(1)}, bf16[256,256]{1,0:T(8,128)(2,1)}, u32[]{:S(2)}, u32[]{:S(2)}) collective-permute-start(bf16[256,256]{1,0:T(8,128)(2,1)S(1)} %slice.17), channel_id=1, source_target_pairs={{0,4},{8,0},{16,8},{24,16},{28,24},{20,28},{12,20},{4,12},{1,5},{9... | collective-permute-start | bytes 393224 | tf_op jit(solution)/shard_map/ppermute | solution.py:294
  60.7 23.6 %collective-permute-start.10 = (bf16[512,256]{1,0:T(8,128)(2,1)}, bf16[512,256]{1,0:T(8,128)(2,1)}, u32[]{:S(2)}, u32[]{:S(2)}) collective-permute-start(bf16[512,256]{1,0:T(8,128)(2,1)} %copy-done.5), channel_id=1, source_target_pairs={{0,2},{1,3},{2,0},{3,1},{4,6},{5,7},{6,4},{7,5},{8,10},{9,11},{10,... | collective-permute-start | bytes 786440 | tf_op jit(solution)/shard_map/ppermute | solution.py:288
  62.2 22.1 %collective-permute-start.12 = (bf16[512,256]{1,0:T(8,128)(2,1)}, bf16[512,256]{1,0:T(8,128)(2,1)}, u32[]{:S(2)}, u32[]{:S(2)}) collective-permute-start(bf16[512,256]{1,0:T(8,128)(2,1)} %copy-done.6), channel_id=1, source_target_pairs={{0,2},{1,3},{2,0},{3,1},{4,6},{5,7},{6,4},{7,5},{8,10},{9,11},{10,... | collective-permute-start | bytes 786440 | tf_op jit(solution)/shard_map/ppermute | solution.py:288
  72.0 10.3 %collective-permute-start.14 = (bf16[256,256]{1,0:T(8,128)(2,1)S(1)}, bf16[256,256]{1,0:T(8,128)(2,1)}, u32[]{:S(2)}, u32[]{:S(2)}) collective-permute-start(bf16[256,256]{1,0:T(8,128)(2,1)S(1)} %collective-permute-done.13.refs_13_), channel_id=1, source_target_pairs={{0,2},{1,3},{2,0},{3,1},{4,6},{5,7},{6,4},{7,5},{8,10},{9,11},{10,... | collective-permute-start | bytes 393224 | tf_op jit(solution)/shard_map/ppermute | solution.py:288
  72.7 11.2 %collective-permute-start.16 = (bf16[256,256]{1,0:T(8,128)(2,1)}, bf16[256,256]{1,0:T(8,128)(2,1)}, u32[]{:S(2)}, u32[]{:S(2)}) collective-permute-start(bf16[256,256]{1,0:T(8,128)(2,1)} %collective-permute-done.15.refs_15_), channel_id=1, source_target_pairs={{0,2},{1,3},{2,0},{3,1},{4,6},{5,7},{6,4},{7,5},{8,10},{9,11},{10,... | collective-permute-start | bytes 393224 | tf_op jit(solution)/shard_map/ppermute | solution.py:288
  82.2 19.1 %collective-permute-start.23 = (bf16[512,256]{1,0:T(8,128)(2,1)S(1)}, bf16[512,256]{1,0:T(8,128)(2,1)S(1)}, u32[]{:S(2)}, u32[]{:S(2)}) collective-permute-start(bf16[512,256]{1,0:T(8,128)(2,1)S(1)} %slice.18), channel_id=1, source_target_pairs={{0,8},{8,16},{16,24},{24,28},{28,20},{20,12},{12,4},{4,0},{1,9},{9... | collective-permute-start | bytes 786440 | tf_op jit(solution)/shard_map/ppermute | solution.py:294
  83.9 17.4 %collective-permute-start.27 = (bf16[512,256]{1,0:T(8,128)(2,1)S(1)}, bf16[512,256]{1,0:T(8,128)(2,1)S(1)}, u32[]{:S(2)}, u32[]{:S(2)}) collective-permute-start(bf16[512,256]{1,0:T(8,128)(2,1)S(1)} %slice.19), channel_id=1, source_target_pairs={{0,4},{8,0},{16,8},{24,16},{28,24},{20,28},{12,20},{4,12},{1,5},{9... | collective-permute-start | bytes 786440 | tf_op jit(solution)/shard_map/ppermute | solution.py:294
  92.7 16.3 %collective-permute-start.18 = (bf16[512,256]{1,0:T(8,128)(2,1)}, bf16[512,256]{1,0:T(8,128)(2,1)}, u32[]{:S(2)}, u32[]{:S(2)}) collective-permute-start(bf16[512,256]{1,0:T(8,128)(2,1)} %shard_map.91.refs_1_), channel_id=1, source_target_pairs={{0,2},{1,3},{4,6},{5,7},{8,10},{9,11},{12,14},{13,15},{16,18},{17,... | collective-permute-start | bytes 786440 | tf_op jit(solution)/shard_map/ppermute | solution.py:291
  107.1 9.2 %collective-permute-start.29 = (bf16[512,256]{1,0:T(8,128)(2,1)}, bf16[512,256]{1,0:T(8,128)(2,1)S(1)}, u32[]{:S(2)}, u32[]{:S(2)}) collective-permute-start(bf16[512,256]{1,0:T(8,128)(2,1)} %shard_map.93.refs_3_), channel_id=1, source_target_pairs={{0,2},{1,3},{4,6},{5,7},{8,10},{9,11},{12,14},{13,15},{16,18},{17,... | collective-permute-start | bytes 786440 | tf_op jit(solution)/shard_map/ppermute | solution.py:291
  108.4 22.0 %collective-permute-start.17 = (bf16[512,256]{1,0:T(8,128)(2,1)S(1)}, bf16[512,256]{1,0:T(8,128)(2,1)S(1)}, u32[]{:S(2)}, u32[]{:S(2)}) collective-permute-start(bf16[512,256]{1,0:T(8,128)(2,1)S(1)} %copy-done.4), channel_id=1, source_target_pairs={{0,1},{1,0},{2,3},{3,2},{4,5},{5,4},{6,7},{7,6},{8,9},{9,8},{10,11... | collective-permute-start | bytes 786440 | tf_op jit(solution)/shard_map/ppermute | solution.py:285
  108.5 21.9 %collective-permute-start.28 = (bf16[512,256]{1,0:T(8,128)(2,1)}, bf16[512,256]{1,0:T(8,128)(2,1)S(1)}, u32[]{:S(2)}, u32[]{:S(2)}) collective-permute-start(bf16[512,256]{1,0:T(8,128)(2,1)} %shard_map.93.refs_3_), channel_id=1, source_target_pairs={{0,1},{1,0},{2,3},{3,2},{4,5},{5,4},{6,7},{7,6},{8,9},{9,8},{10,11... | collective-permute-start | bytes 786440 | tf_op jit(solution)/shard_map/ppermute | solution.py:285
  109.0 21.5 %collective-permute-start.19 = (bf16[512,256]{1,0:T(8,128)(2,1)}, bf16[512,256]{1,0:T(8,128)(2,1)S(1)}, u32[]{:S(2)}, u32[]{:S(2)}) collective-permute-start(bf16[512,256]{1,0:T(8,128)(2,1)} %collective-permute-done.18.refs_2_), channel_id=1, source_target_pairs={{0,1},{1,0},{2,3},{3,2},{4,5},{5,4},{6,7},{7,6},{8,9},{9,8},{10,11... | collective-permute-start | bytes 786440 | tf_op jit(solution)/shard_map/ppermute | solution.py:285
  116.3 14.2 %collective-permute-start.30 = (bf16[512,256]{1,0:T(8,128)(2,1)S(1)}, bf16[512,256]{1,0:T(8,128)(2,1)S(1)}, u32[]{:S(2)}, u32[]{:S(2)}) collective-permute-start(bf16[512,256]{1,0:T(8,128)(2,1)S(1)} %collective-permute-done.29.refs_4_), channel_id=1, source_target_pairs={{0,1},{1,0},{2,3},{3,2},{4,5},{5,4},{6,7},{7,6},{8,9},{9,8},{10,11... | collective-permute-start | bytes 786440 | tf_op jit(solution)/shard_map/ppermute | solution.py:285
  (27 other events, 541.1 us)
where the time goes:
time: 145 us
  waiting for transfers between devices  48.6 us (34%)
  Pallas kernels  46.8 us (32%)
  starting transfers between devices  27.2 us (19%)
  local copies, waits for them, and re-layouts  9.68 us (7%)
  between operations  9.35 us (6%)
  other arithmetic  3.31 us (2%)
    ppermute x16, waiting for transfers between devices, along_ring(): lax.ppermute(x, 'dp', [(ring[i], ring[(i + step) % dp_size]) for i in ran...  27.1 us
    pallas_call x2, Pallas kernels, attend(): pl.pallas_call(functools.partial(attention_kernel, hops, row_blocks, grou...  26.8 us
    pallas_call x3, Pallas kernels, project(): pl.pallas_call(functools.partial(project_kernel, plan, finish), out_shape...  19.9 us
    ppermute x16, starting transfers between devices, along_ring(): lax.ppermute(x, 'dp', [(ring[i], ring[(i + step) % dp_size]) for i in ran...  16.9 us
    ppermute x8, waiting for transfers between devices, to_plane(): return lax.ppermute(x, 'ctx', [(i, i ^ CORES) for i in range(ctx_size)])  14.2 us
    ppermute x2, waiting for transfers between devices, to_next_chip(): lax.ppermute(x, 'ctx', [(i, i + CORES) for i in range(ctx_size - CORES)])  7.22 us
    ppermute x8, starting transfers between devices, to_plane(): return lax.ppermute(x, 'ctx', [(i, i ^ CORES) for i in range(ctx_size)])  7.05 us
  transfers between devices with their start and end apart: 31, of which 12 were waited for; matrix products, arithmetic and copies ran while one was open for 7% of the time, Pallas kernels for 23%

commit v1 on v0

--- a/solution.py
+++ b/solution.py
@@ -14,6 +14,7 @@
 BLK = 128
 MASKED = -1e30
 CORES = 2
+SPARE_VMEM = 4 << 20
 
 rope_base = 1000000.0
 
@@ -35,7 +36,7 @@
     )
 
 
-def project_kernel(plan, finish, columns, own_ref, sibling_ref, *refs):
+def project_kernel(plan, finish, added, columns, own_ref, sibling_ref, *refs):
     operands = 1 + max(part[0] for parts in plan for part in parts)
     piece_refs = refs[:operands]
     extra_refs = refs[operands:-6]
@@ -63,8 +64,9 @@
             part_copy(operand, first_row, at, part).start()
         for half in range(2):
             token_copy(at, half).start()
-    if finish == "add":
+    if added:
         acc_ref[...] = extra_refs[0][...]
+        extra_refs = extra_refs[1:]
     else:
         acc_ref[...] = jnp.zeros_like(acc_ref)
 
@@ -87,13 +89,15 @@
             head = acc_ref[:, lanes] + bias_ref[:, lanes]
             turned = head * cos_ref[...] + pltpu.roll(head, HEAD_SIZE // 2, 1) * sine_ref[...]
             out_ref[:, lanes] = turned.astype(out_ref.dtype)
-    elif finish == "sum":
-        out_ref[...] = acc_ref[...] + extra_refs[0][...]
+    elif finish == "value":
+        out_ref[...] = (acc_ref[...] + extra_refs[0][...]).astype(out_ref.dtype)
     else:
         out_ref[...] = acc_ref[...].astype(out_ref.dtype)
 
 
-def project(finish, strip, own_tokens, sibling_tokens, pieces, plan, columns, extras):
+def project(
+    finish, strip, own_tokens, sibling_tokens, pieces, plan, columns, before, extras
+):
     number_of_rows = own_tokens.shape[0]
     width = pieces[0].shape[1]
     anywhere = pl.BlockSpec(memory_space=pl.ANY)
@@ -101,8 +105,13 @@
     out = jax.ShapeDtypeStruct(
         (chip_rows, width), jnp.float32 if finish == "sum" else jnp.bfloat16
     )
+    added = before is not None
+    if added:
+        extras = [before, *extras]
+    grant = len(plan) * strip * (chip_rows + width) * 2
+    grant += chip_rows * width * (4 + 8 * len(extras) + 8) + SPARE_VMEM
     return pl.pallas_call(
-        functools.partial(project_kernel, plan, finish),
+        functools.partial(project_kernel, plan, finish, added),
         out_shape=out,
         grid_spec=pltpu.PrefetchScalarGridSpec(
             num_scalar_prefetch=1,
@@ -123,6 +132,7 @@
             bytes_accessed=2 * len(plan) * strip * (chip_rows + width),
             transcendentals=0,
         ),
+        compiler_params=pltpu.CompilerParams(vmem_limit_bytes=grant),
     )(columns, own_tokens, sibling_tokens, *pieces, *extras)
 
 
@@ -246,6 +256,11 @@
             ],
         ),
         input_output_aliases=aliases,
+        compiler_params=pltpu.CompilerParams(
+            vmem_limit_bytes=rows * BLK * 4 * (total_blocks + 6)
+            + (BLK * width + hops * keys[0].size) * 8
+            + SPARE_VMEM
+        ),
         cost_estimate=pl.CostEstimate(
             flops=4 * pairs * HEAD_SIZE,
             bytes_accessed=2 * number_of_rows * query_width * 2,
@@ -309,77 +324,98 @@
 
     half_ring = dp_size // 2
 
-    key_pieces, key_plan, key_blocks = [key_weight], [], []
-    for side in range(2):
-        key_plan.append(((0, side * strip), (0, side * strip + part)))
-        key_blocks.append(dp_index * 2 + side)
+    arange = jnp.arange(number_of_rows, dtype=jnp.int32)
+    positions = jnp.concatenate(
+        [my_index * number_of_rows + arange, (my_index ^ 1) * number_of_rows + arange]
+    )
+    key_bias = lax.dynamic_slice_in_dim(key_projection_bias, core * half_width, half_width, 0)
+    value_bias = lax.dynamic_slice_in_dim(value_projection_bias, core * half_width, half_width, 0)
+
+    def projected(finish, strips, before, extras):
+        pieces = []
+
+        def operand(piece):
+            for at, known in enumerate(pieces):
+                if known is piece:
+                    return at
+            pieces.append(piece)
+            return len(pieces) - 1
+
+        plan = tuple(
+            tuple((operand(piece), first_row) for piece, first_row in parts) for parts, _ in strips
+        )
+        columns = jnp.stack([at for _, at in strips]).astype(jnp.int32)
+        return project(
+            finish, strip, own_tokens, sibling_tokens, pieces, plan, columns, before, extras
+        )
+
+    def whole_strip(piece, first_row, at):
+        return (((piece, first_row), (piece, first_row + part)), at)
+
+    own_strips = [
+        [whole_strip(weight, side * strip, dp_index * 2 + side) for side in range(2)]
+        for weight in (key_weight, value_weight)
+    ]
+    sides = [plane, 1 - plane]
+    key_strips = [own_strips[0]]
     travelling = {1: key_strip, -1: key_strip}
-    last = []
     for hop in range(1, half_ring + 1):
+        arrived = {}
         for step in (1, -1):
             piece = travelling[step]
             if hop == half_ring:
                 first_row = 0 if step == 1 else part
                 piece = piece[first_row : first_row + part]
             piece = along_ring(piece, step)
+            other = to_plane(piece)
             travelling[step] = piece
-            last.append((len(key_pieces), len(key_pieces) + 1))
-            key_pieces += [piece, to_plane(piece)]
-            if hop < half_ring:
-                for side, at in enumerate(last[-1]):
-                    key_plan.append(((at, 0), (at, part)))
-                    key_blocks.append(
-                        source_at(-step * hop) * 2 + (plane if side == 0 else 1 - plane)
+            arrived[step] = (piece, other)
+        if hop < half_ring:
+            key_strips.append(
+                [
+                    whole_strip(arrived[step][side], 0, source_at(-step * hop) * 2 + sides[side])
+                    for step in (1, -1)
+                    for side in range(2)
+                ]
+            )
+        else:
+            key_strips.append(
+                [
+                    (
+                        ((arrived[1][side], 0), (arrived[-1][side], 0)),
+                        source_at(hop) * 2 + sides[side],
                     )
-    for side in range(2):
-        key_plan.append(((last[-2][side], 0), (last[-1][side], 0)))
-        key_blocks.append(source_at(half_ring) * 2 + (plane if side == 0 else 1 - plane))
-
-    value_pieces, value_plan, value_blocks = [value_weight], [], []
-    for side in range(2):
-        value_plan.append(((0, side * strip), (0, side * strip + part)))
-        value_blocks.append(dp_index * 2 + side)
-    travelling = {1: value_weight, -1: value_weight}
-    for hop in range(1, half_ring):
-        for step in (1, -1):
-            piece = along_ring(travelling[step], step)
-            travelling[step] = piece
-            at = len(value_pieces)
-            value_pieces.append(piece)
-            for side in range(2):
-                value_plan.append(((at, side * strip), (at, side * strip + part)))
-                value_blocks.append(source_at(-step * hop) * 2 + side)
-    end_pieces = [
-        along_ring(travelling[1][:strip], 1),
-        along_ring(travelling[-1][strip:], -1),
-    ]
-    end_plan = [((side, 0), (side, part)) for side in range(2)]
-    end_blocks = [source_at(half_ring) * 2 + side for side in range(2)]
-
-    arange = jnp.arange(number_of_rows, dtype=jnp.int32)
-    positions = jnp.concatenate(
-        [my_index * number_of_rows + arange, (my_index ^ 1) * number_of_rows + arange]
-    )
-    key_bias = lax.dynamic_slice_in_dim(key_projection_bias, core * half_width, half_width, 0)
-    value_bias = lax.dynamic_slice_in_dim(value_projection_bias, core * half_width, half_width, 0)
-
-    def projected(finish, pieces, plan, blocks, extras):
-        return project(
-            finish,
-            strip,
-            own_tokens,
-            sibling_tokens,
-            pieces,
-            tuple(plan),
-            jnp.stack(blocks).astype(jnp.int32),
-            extras,
-        )
-
+                    for side in range(2)
+                ]
+            )
+
+    value_strips = [own_strips[1]]
+    travelling = {
+        (side, step): value_weight[side * strip : (side + 1) * strip]
+        for side in range(2)
+        for step in (1, -1)
+    }
+    for hop in range(1, half_ring + 1):
+        arrived = []
+        for side in range(2):
+            for step in (1, -1):
+                if hop == half_ring and step != (1, -1)[side]:
+                    continue
+                piece = along_ring(travelling[side, step], step)
+                travelling[side, step] = piece
+                arrived.append(whole_strip(piece, 0, source_at(-step * hop) * 2 + side))
+        value_strips.append(arrived)
+
+    def joined(hops):
+        return [entry for strips in hops for entry in strips]
+
+    key_sum = projected("sum", joined(key_strips[:-2]), None, [])
     key_rows = projected(
-        "key", key_pieces, key_plan, key_blocks, [key_bias[None], *rope_tables(positions)]
-    )
-    value_sum = projected("sum", value_pieces, value_plan, value_blocks, [value_bias[None]])
-    value_rows = projected("add", end_pieces, end_plan, end_blocks, [value_sum])
+        "key", joined(key_strips[-2:]), key_sum, [key_bias[None], *rope_tables(positions)]
+    )
+    value_sum = projected("sum", joined(value_strips[:-2]), None, [])
+    value_sum = projected("sum", value_strips[-2], value_sum, [])
+    value_rows = projected("value", value_strips[-1], value_sum, [value_bias[None]])
 
     keys, values = [key_rows], [value_rows]
     for _ in range(chips - 1):

time: 145 us -> 143 us (0.986)
  waiting for transfers between devices: 48.6 us -> 37.3 us
  starting transfers between devices: 27.2 us -> 32.2 us
  Pallas kernels: 46.8 us -> 48.9 us
  local copies, waits for them, and re-layouts: 9.68 us -> 11.6 us
    ppermute x8, waiting for transfers between devices: 14.2 us -> 0.02 us  [to_plane(): return lax.ppermute(x, 'ctx', [(i, i ^ CORES) for i in range(ctx_size)])]
    ppermute x16 -> x22, starting transfers between devices: 16.9 us -> 22.3 us  [along_ring(): lax.ppermute(x, 'dp', [(ring[i], ring[(i + step) % dp_size]) for i in ran...]
    ppermute x16 -> x22, waiting for transfers between devices: 27.1 us -> 30.4 us  [along_ring(): lax.ppermute(x, 'dp', [(ring[i], ring[(i + step) % dp_size]) for i in ran...]
    pallas_call x3 -> x5, Pallas kernels: 19.9 us -> 22.4 us  [project(): pl.pallas_call(functools.partial(project_kernel, plan, finish, added), ou...]
    unnamed x56 -> x54, local copies, waits for them, and re-layouts: 2.5 us -> 4.61 us
    dynamic_slice x1, local copies, waits for them, and re-layouts: 1.87 us -> 0.03 us  [layer(): lax.dynamic_slice_in_dim(key_projection_weight, core * half_width, half_w...]
  transfers between devices with their start and end apart: 31 -> 37, of which waited for: 12 -> 14; matrix products, arithmetic and copies ran while one was open for 7% -> 6% of each run, Pallas kernels for 23% -> 25%
where the time goes in v1:
time: 143 us; the launch traced here: 142 us
  Pallas kernels  48.9 us (34%)
  waiting for transfers between devices  37.3 us (26%)
  starting transfers between devices  32.2 us (23%)
  local copies, waits for them, and re-layouts  11.6 us (8%)
  between operations  10.4 us (7%)
  other arithmetic  2.07 us (1%)
    ppermute x22, waiting for transfers between devices, along_ring(): lax.ppermute(x, 'dp', [(ring[i], ring[(i + step) % dp_size]) for i in ran...  30.4 us
    pallas_call x2, Pallas kernels, attend(): pl.pallas_call(functools.partial(attention_kernel, hops, row_blocks, grou...  26.5 us
    pallas_call x5, Pallas kernels, project(): pl.pallas_call(functools.partial(project_kernel, plan, finish, added), ou...  22.4 us
    ppermute x22, starting transfers between devices, along_ring(): lax.ppermute(x, 'dp', [(ring[i], ring[(i + step) % dp_size]) for i in ran...  22.3 us
    ppermute x2, waiting for transfers between devices, to_next_chip(): lax.ppermute(x, 'ctx', [(i, i + CORES) for i in range(ctx_size - CORES)])  6.81 us
    ppermute x8, starting transfers between devices, to_plane(): return lax.ppermute(x, 'ctx', [(i, i ^ CORES) for i in range(ctx_size)])  6.28 us
    unnamed x54, local copies, waits for them, and re-layouts  4.61 us
    ppermute x2, starting transfers between devices, to_next_chip(): lax.ppermute(x, 'ctx', [(i, i + CORES) for i in range(ctx_size - CORES)])  2.9 us
  transfers between devices with their start and end apart: 37, of which 14 were waited for; matrix products, arithmetic and copies ran while one was open for 6% of the time, Pallas kernels for 25%

profile of v1, /device:TPU:12, one launch (start us, length us, event | category | flops | bytes accessed | tf_op | source)
XLA Modules:
  0.0 142.5 jit_solution(10969039897363666444)
XLA Ops:
  1.1 1.6 %collective-permute-start.20 = (bf16[512,256]{1,0:T(8,128)(2,1)S(1)}, bf16[512,256]{1,0:T(8,128)(2,1)S(1)}, u32[]{:S(2)}, u32[]{:S(2)}) collective-permute-start(bf16[512,256]{1,0:T(8,128)(2,1)S(1)} %get-tuple-element.6), channel_id=1, source_target_pairs={{0,8},{8,16},{16,24},{24,28},{28,20},{20,12},{12,4},{4,0},{1,9},{9... | collective-permute-start | bytes 786440 | tf_op jit(solution)/shard_map/ppermute | solution.py:309
  3.6 1.6 %collective-permute-start.31 = (bf16[512,256]{1,0:T(8,128)(2,1)S(1)}, bf16[512,256]{1,0:T(8,128)(2,1)S(1)}, u32[]{:S(2)}, u32[]{:S(2)}) collective-permute-start(bf16[512,256]{1,0:T(8,128)(2,1)S(1)} %get-tuple-element.5), channel_id=1, source_target_pairs={{0,8},{8,16},{16,24},{24,28},{28,20},{20,12},{12,4},{4,0},{1,9},{9... | collective-permute-start | bytes 786440 | tf_op jit(solution)/shard_map/ppermute | solution.py:309
  6.3 4.0 %collective-permute-done.20.refs_1_ = bf16[512,256]{1,0:T(8,128)(2,1)S(1)} collective-permute-done((bf16[512,256]{1,0:T(8,128)(2,1)S(1)}, bf16[512,256]{1,0:T(8,128)(2,1)S(1)}, u32[]{:S(2)}, u32[]{:S(2)}) %collective-permute-start.20) | collective-permute-done | bytes 262176 | tf_op jit(solution)/shard_map/ppermute | solution.py:309
  10.3 1.6 %collective-permute-start.1 = (bf16[512,256]{1,0:T(8,128)(2,1)S(1)}, bf16[512,256]{1,0:T(8,128)(2,1)S(1)}, u32[]{:S(2)}, u32[]{:S(2)}) collective-permute-start(bf16[512,256]{1,0:T(8,128)(2,1)S(1)} %dynamic_slice.32), channel_id=1, source_target_pairs={{0,8},{8,16},{16,24},{24,28},{28,20},{20,12},{12,4},{4,0},{1,9},{9... | collective-permute-start | bytes 786440 | tf_op jit(solution)/shard_map/ppermute | solution.py:309
  12.3 5.2 %collective-permute-done.28.refs_2_ = bf16[512,256]{1,0:T(8,128)(2,1)S(1)} collective-permute-done((bf16[512,256]{1,0:T(8,128)(2,1)S(1)}, bf16[512,256]{1,0:T(8,128)(2,1)S(1)}, u32[]{:S(2)}, u32[]{:S(2)}) %collective-permute-start.28) | collective-permute-done | bytes 262176 | tf_op jit(solution)/shard_map/ppermute | solution.py:309
  17.5 1.6 %collective-permute-start.21 = (bf16[512,256]{1,0:T(8,128)(2,1)S(1)}, bf16[512,256]{1,0:T(8,128)(2,1)S(1)}, u32[]{:S(2)}, u32[]{:S(2)}) collective-permute-start(bf16[512,256]{1,0:T(8,128)(2,1)S(1)} %collective-permute-done.20.refs_1_), channel_id=1, source_target_pairs={{0,8},{8,16},{16,24},{24,28},{28,20},{20,12},{12,4},{4,0},{1,9},{9... | collective-permute-start | bytes 786440 | tf_op jit(solution)/shard_map/ppermute | solution.py:309
  19.5 2.0 %collective-permute-done.1.refs_1_ = bf16[512,256]{1,0:T(8,128)(2,1)S(1)} collective-permute-done((bf16[512,256]{1,0:T(8,128)(2,1)S(1)}, bf16[512,256]{1,0:T(8,128)(2,1)S(1)}, u32[]{:S(2)}, u32[]{:S(2)}) %collective-permute-start.1) | collective-permute-done | bytes 262176 | tf_op jit(solution)/shard_map/ppermute | solution.py:309
  23.1 1.6 %collective-permute-start.32 = (bf16[512,256]{1,0:T(8,128)(2,1)S(1)}, bf16[512,256]{1,0:T(8,128)(2,1)}, u32[]{:S(2)}, u32[]{:S(2)}) collective-permute-start(bf16[512,256]{1,0:T(8,128)(2,1)S(1)} %collective-permute-done.31.refs_3_), channel_id=1, source_target_pairs={{0,8},{8,16},{16,24},{24,28},{28,20},{20,12},{12,4},{4,0},{1,9},{9... | collective-permute-start | bytes 786440 | tf_op jit(solution)/shard_map/ppermute | solution.py:309
  24.7 2.5 %collective-permute-done.21.refs_5_ = bf16[512,256]{1,0:T(8,128)(2,1)S(1)} collective-permute-done((bf16[512,256]{1,0:T(8,128)(2,1)S(1)}, bf16[512,256]{1,0:T(8,128)(2,1)S(1)}, u32[]{:S(2)}, u32[]{:S(2)}) %collective-permute-start.21) | collective-permute-done | bytes 262176 | tf_op jit(solution)/shard_map/ppermute | solution.py:309
  27.2 1.6 %collective-permute-start.2 = (bf16[512,256]{1,0:T(8,128)(2,1)S(1)}, bf16[512,256]{1,0:T(8,128)(2,1)}, u32[]{:S(2)}, u32[]{:S(2)}) collective-permute-start(bf16[512,256]{1,0:T(8,128)(2,1)S(1)} %collective-permute-done.1.refs_1_), channel_id=1, source_target_pairs={{0,8},{8,16},{16,24},{24,28},{28,20},{20,12},{12,4},{4,0},{1,9},{9... | collective-permute-start | bytes 786440 | tf_op jit(solution)/shard_map/ppermute | solution.py:309
  29.3 4.4 %collective-permute-done.29.refs_6_ = bf16[512,256]{1,0:T(8,128)(2,1)} collective-permute-done((bf16[512,256]{1,0:T(8,128)(2,1)S(1)}, bf16[512,256]{1,0:T(8,128)(2,1)}, u32[]{:S(2)}, u32[]{:S(2)}) %collective-permute-start.29) | collective-permute-done | bytes 262176 | tf_op jit(solution)/shard_map/ppermute | solution.py:309
  34.8 3.3 %collective-permute-done.2.refs_5_ = bf16[512,256]{1,0:T(8,128)(2,1)} collective-permute-done((bf16[512,256]{1,0:T(8,128)(2,1)S(1)}, bf16[512,256]{1,0:T(8,128)(2,1)}, u32[]{:S(2)}, u32[]{:S(2)}) %collective-permute-start.2) | collective-permute-done | bytes 262176 | tf_op jit(solution)/shard_map/ppermute | solution.py:309
  38.0 1.6 %collective-permute-start.22 = (bf16[512,256]{1,0:T(8,128)(2,1)S(1)}, bf16[512,256]{1,0:T(8,128)(2,1)S(1)}, u32[]{:S(2)}, u32[]{:S(2)}) collective-permute-start(bf16[512,256]{1,0:T(8,128)(2,1)S(1)} %collective-permute-done.21.refs_5_), channel_id=1, source_target_pairs={{0,8},{8,16},{16,24},{24,28},{28,20},{20,12},{12,4},{4,0},{1,9},{9... | collective-permute-start | bytes 786440 | tf_op jit(solution)/shard_map/ppermute | solution.py:309
  39.6 1.7 %collective-permute-done.6.refs_7_ = bf16[512,256]{1,0:T(8,128)(2,1)S(1)} collective-permute-done((bf16[512,256]{1,0:T(8,128)(2,1)S(1)}, bf16[512,256]{1,0:T(8,128)(2,1)S(1)}, u32[]{:S(2)}, u32[]{:S(2)}) %collective-permute-start.6) | collective-permute-done | bytes 262176 | tf_op jit(solution)/shard_map/ppermute | solution.py:309
  41.8 1.6 %collective-permute-start.3 = (bf16[512,256]{1,0:T(8,128)(2,1)}, bf16[512,256]{1,0:T(8,128)(2,1)S(1)}, u32[]{:S(2)}, u32[]{:S(2)}) collective-permute-start(bf16[512,256]{1,0:T(8,128)(2,1)} %collective-permute-done.2.refs_5_), channel_id=1, source_target_pairs={{0,8},{8,16},{16,24},{24,28},{28,20},{20,12},{12,4},{4,0},{1,9},{9... | collective-permute-start | bytes 786440 | tf_op jit(solution)/shard_map/ppermute | solution.py:309
  47.7 3.0 %collective-permute-done.26.refs_3_ = bf16[512,256]{1,0:T(8,128)(2,1)S(1)} collective-permute-done((bf16[512,256]{1,0:T(8,128)(2,1)}, bf16[512,256]{1,0:T(8,128)(2,1)S(1)}, u32[]{:S(2)}, u32[]{:S(2)}) %collective-permute-start.26) | collective-permute-done | bytes 262176 | tf_op jit(solution)/shard_map/ppermute | solution.py:309
  51.5 1.6 %collective-permute-start.33 = (bf16[512,256]{1,0:T(8,128)(2,1)}, bf16[512,256]{1,0:T(8,128)(2,1)}, u32[]{:S(2)}, u32[]{:S(2)}) collective-permute-start(bf16[512,256]{1,0:T(8,128)(2,1)} %collective-permute-done.32.refs_7_), channel_id=1, source_target_pairs={{0,8},{8,16},{16,24},{24,28},{28,20},{20,12},{12,4},{4,0},{1,9},{9... | collective-permute-start | bytes 786440 | tf_op jit(solution)/shard_map/ppermute | solution.py:309
  53.9 2.4 %collective-permute-done.7.refs_2_ = bf16[512,256]{1,0:T(8,128)(2,1)S(1)} collective-permute-done((bf16[512,256]{1,0:T(8,128)(2,1)S(1)}, bf16[512,256]{1,0:T(8,128)(2,1)S(1)}, u32[]{:S(2)}, u32[]{:S(2)}) %collective-permute-start.7) | collective-permute-done | bytes 262176 | tf_op jit(solution)/shard_map/ppermute | solution.py:309
  56.3 1.6 %collective-permute-start.9 = (bf16[256,256]{1,0:T(8,128)(2,1)}, bf16[256,256]{1,0:T(8,128)(2,1)S(1)}, u32[]{:S(2)}, u32[]{:S(2)}) collective-permute-start(bf16[256,256]{1,0:T(8,128)(2,1)} %slice.18), channel_id=1, source_target_pairs={{0,8},{8,16},{16,24},{24,28},{28,20},{20,12},{12,4},{4,0},{1,9},{9... | collective-permute-start | bytes 393224 | tf_op jit(solution)/shard_map/ppermute | solution.py:309
  72.7 1.6 %collective-permute-start.23 = (bf16[512,256]{1,0:T(8,128)(2,1)}, bf16[512,256]{1,0:T(8,128)(2,1)S(1)}, u32[]{:S(2)}, u32[]{:S(2)}) collective-permute-start(bf16[512,256]{1,0:T(8,128)(2,1)} %copy-done.17), channel_id=1, source_target_pairs={{0,8},{8,16},{16,24},{24,28},{28,20},{20,12},{12,4},{4,0},{1,9},{9... | collective-permute-start | bytes 786440 | tf_op jit(solution)/shard_map/ppermute | solution.py:309
  74.8 1.5 %collective-permute-start.4 = (bf16[512,256]{1,0:T(8,128)(2,1)S(1)}, bf16[512,256]{1,0:T(8,128)(2,1)S(1)}, u32[]{:S(2)}, u32[]{:S(2)}) collective-permute-start(bf16[512,256]{1,0:T(8,128)(2,1)S(1)} %collective-permute-done.3.refs_0_), channel_id=1, source_target_pairs={{0,2},{1,3},{2,0},{3,1},{4,6},{5,7},{6,4},{7,5},{8,10},{9,11},{10,... | collective-permute-start | bytes 786440 | tf_op jit(solution)/shard_map/ppermute | solution.py:303
  76.9 2.2 %copy-done = bf16[1,256,8192]{2,1,0:T(8,128)(2,1)S(1)} copy-done((bf16[1,256,8192]{2,1,0:T(8,128)(2,1)S(1)}, bf16[1,256,8192]{2,1,0:T(8,128)(2,1)}, u32[]{:S(2)}) %copy-start) | copy-done | bytes 4194328
  80.7 5.9 %shard_map.93.refs_4_ = f32[512,256]{1,0:T(8,128)S(1)} custom-call(s32[10]{0:T(128)S(1)} %copy-done.19, bf16[256,8192]{1,0:T(8,128)(2,1)S(1)} %bitcast.48, bf16[256,8192]{1,0:T(8,128)(2,1)} %collective-permute-done.sibling_ref, bf16[1024,256]{1,0:T(8,128)(2,1)S(1)} %constant_dynamic-slice_fusion.1.refs_0_, ...), custom_call_target="tpu_custom_call" | custom-call | flops 1342177280 | bytes 7864320 | tf_op jit(solution)/shard_map/pallas_call | solution.py:113
  86.6 3.2 %shard_map.94.refs_2_ = f32[512,256]{1,0:T(8,128)S(1)} custom-call(s32[4]{0:T(128)S(1)} %copy-done.20, bf16[256,8192]{1,0:T(8,128)(2,1)S(1)} %bitcast.49, bf16[256,8192]{1,0:T(8,128)(2,1)} %collective-permute-done.sibling_ref, bf16[512,256]{1,0:T(8,128)(2,1)S(1)} %copy-done.18, bf16[512,256]{1,0:T(8,128)(2,1)} %collective-permute-done.30.refs_1_, ...), custom_call_target="tpu_custom_call" | custom-call | flops 536870912 | bytes 3145728 | tf_op jit(solution)/shard_map/pallas_call | solution.py:113
  89.8 1.6 %collective-permute-start.11 = (bf16[256,256]{1,0:T(8,128)(2,1)S(1)}, bf16[256,256]{1,0:T(8,128)(2,1)S(1)}, u32[]{:S(2)}, u32[]{:S(2)}) collective-permute-start(bf16[256,256]{1,0:T(8,128)(2,1)S(1)} %collective-permute-done.9.refs_4_), channel_id=1, source_target_pairs={{0,2},{1,3},{2,0},{3,1},{4,6},{5,7},{6,4},{7,5},{8,10},{9,11},{10,... | collective-permute-start | bytes 393224 | tf_op jit(solution)/shard_map/ppermute | solution.py:303
  91.9 2.8 %shard_map.95.refs_3_ = bf16[512,256]{1,0:T(8,128)(2,1)S(1)} custom-call(s32[2]{0:T(128)S(1)} %pad_add_fusion.columns, bf16[256,8192]{1,0:T(8,128)(2,1)S(1)} %bitcast.50, bf16[256,8192]{1,0:T(8,128)(2,1)} %collective-permute-done.sibling_ref, bf16[512,256]{1,0:T(8,128)(2,1)S(1)} %collective-permute-done.23.refs_0_, ...), custom_call_target="tpu_custom_call" | custom-call | flops 268435456 | bytes 1572864 | tf_op jit(solution)/shard_map/pallas_call | solution.py:113
  96.2 6.2 %shard_map.91.refs_8_ = f32[512,256]{1,0:T(8,128)S(1)} custom-call(s32[10]{0:T(128)S(1)} %stack.124.columns, bf16[256,8192]{1,0:T(8,128)(2,1)S(1)} %bitcast.51, bf16[256,8192]{1,0:T(8,128)(2,1)} %collective-permute-done.sibling_ref, bf16[1024,256]{1,0:T(8,128)(2,1)S(1)} %constant_dynamic-slice_fusion.2.refs_0_, ...), custom_call_target="tpu_custom_call" | custom-call | flops 1342177280 | bytes 7864320 | tf_op jit(solution)/shard_map/pallas_call | solution.py:113
  102.5 4.4 %shard_map.92.refs_1_ = bf16[512,256]{1,0:T(8,128)(2,1)S(1)} custom-call(s32[6]{0:T(128)S(1)} %stack.113.columns, bf16[256,8192]{1,0:T(8,128)(2,1)S(1)} %bitcast.52, bf16[256,8192]{1,0:T(8,128)(2,1)} %collective-permute-done.sibling_ref, bf16[512,256]{1,0:T(8,128)(2,1)S(1)} %collective-permute-done.3.refs_0_, ...), custom_call_target="tpu_custom_call" | custom-call | flops 805306368 | bytes 4718592 | tf_op jit(solution)/shard_map/pallas_call | solution.py:113
  106.9 1.5 %collective-permute-start.18 = (bf16[512,256]{1,0:T(8,128)(2,1)S(1)}, bf16[512,256]{1,0:T(8,128)(2,1)S(1)}, u32[]{:S(2)}, u32[]{:S(2)}) collective-permute-start(bf16[512,256]{1,0:T(8,128)(2,1)S(1)} %shard_map.92.refs_1_), channel_id=1, source_target_pairs={{0,2},{1,3},{4,6},{5,7},{8,10},{9,11},{12,14},{13,15},{16,18},{17,... | collective-permute-start | bytes 786440 | tf_op jit(solution)/shard_map/ppermute | solution.py:306
  109.0 6.8 %collective-permute-done.18.refs_2_ = bf16[512,256]{1,0:T(8,128)(2,1)S(1)} collective-permute-done((bf16[512,256]{1,0:T(8,128)(2,1)S(1)}, bf16[512,256]{1,0:T(8,128)(2,1)S(1)}, u32[]{:S(2)}, u32[]{:S(2)}) %collective-permute-start.18) | collective-permute-done | bytes 262176 | tf_op jit(solution)/shard_map/ppermute | solution.py:306
  115.9 13.2 %attend.2.refs_5_ = bf16[256,4096]{1,0:T(8,128)(2,1)} custom-call(s32[11]{0:T(128)S(1)} %get-tuple-element.10.facts, bf16[256,4096]{1,0:T(8,128)(2,1)S(1)} %bitcast.53, bf16[512,256]{1,0:T(8,128)(2,1)S(1)} %shard_map.92.refs_1_, bf16[512,256]{1,0:T(8,128)(2,1)S(1)} %collective-permute-done.18.refs_2_, bf16[512,256]{1,0:T(8,128)(2,1)S(1)} %shard_map.95.refs_3_, ...), custom_call_target="tpu_custom_call" | custom-call | flops 1073741824 | bytes 4194304 | tf_op jit(solution)/shard_map/attend/pallas_call | solution.py:243
  129.2 13.2 %attend.3 = bf16[256,4096]{1,0:T(8,128)(2,1)} custom-call(s32[11]{0:T(128)S(1)} %get-tuple-element.11.facts, bf16[256,4096]{1,0:T(8,128)(2,1)S(1)} %bitcast.54, bf16[512,256]{1,0:T(8,128)(2,1)S(1)} %collective-permute-done.17.refs_1_, bf16[512,256]{1,0:T(8,128)(2,1)} %collective-permute-done.19.refs_2_, ...), custom_call_target="tpu_custom_call", output_to_operand_aliasing={{}: (6, {})} | custom-call | flops 1073741824 | bytes 4194304 | tf_op jit(solution)/shard_map/attend/pallas_call | solution.py:243
  (125 shorter events, 23.9 us)
Async XLA Ops:
  0.0 76.4 %collective-permute-start = (bf16[256,8192]{1,0:T(8,128)(2,1)}, bf16[256,8192]{1,0:T(8,128)(2,1)}, u32[]{:S(2)}, u32[]{:S(2)}) collective-permute-start(bf16[256,8192]{1,0:T(8,128)(2,1)} %bitcast.47), channel_id=1, source_target_pairs={{0,1},{1,0},{2,3},{3,2},{4,5},{5,4},{6,7},{7,6},{8,9},{9,8},{10,11... | collective-permute-start | bytes 12582920 | tf_op jit(solution)/shard_map/ppermute | solution.py:300
  1.1 9.2 %collective-permute-start.20 = (bf16[512,256]{1,0:T(8,128)(2,1)S(1)}, bf16[512,256]{1,0:T(8,128)(2,1)S(1)}, u32[]{:S(2)}, u32[]{:S(2)}) collective-permute-start(bf16[512,256]{1,0:T(8,128)(2,1)S(1)} %get-tuple-element.6), channel_id=1, source_target_pairs={{0,8},{8,16},{16,24},{24,28},{28,20},{20,12},{12,4},{4,0},{1,9},{9... | collective-permute-start | bytes 786440 | tf_op jit(solution)/shard_map/ppermute | solution.py:309
  3.1 14.3 %collective-permute-start.28 = (bf16[512,256]{1,0:T(8,128)(2,1)S(1)}, bf16[512,256]{1,0:T(8,128)(2,1)S(1)}, u32[]{:S(2)}, u32[]{:S(2)}) collective-permute-start(bf16[512,256]{1,0:T(8,128)(2,1)S(1)} %get-tuple-element.6), channel_id=1, source_target_pairs={{0,4},{8,0},{16,8},{24,16},{28,24},{20,28},{12,20},{4,12},{1,5},{9... | collective-permute-start | bytes 786440 | tf_op jit(solution)/shard_map/ppermute | solution.py:309
  3.6 15.5 %collective-permute-start.31 = (bf16[512,256]{1,0:T(8,128)(2,1)S(1)}, bf16[512,256]{1,0:T(8,128)(2,1)S(1)}, u32[]{:S(2)}, u32[]{:S(2)}) collective-permute-start(bf16[512,256]{1,0:T(8,128)(2,1)S(1)} %get-tuple-element.5), channel_id=1, source_target_pairs={{0,8},{8,16},{16,24},{24,28},{28,20},{20,12},{12,4},{4,0},{1,9},{9... | collective-permute-start | bytes 786440 | tf_op jit(solution)/shard_map/ppermute | solution.py:309
  10.3 11.2 %collective-permute-start.1 = (bf16[512,256]{1,0:T(8,128)(2,1)S(1)}, bf16[512,256]{1,0:T(8,128)(2,1)S(1)}, u32[]{:S(2)}, u32[]{:S(2)}) collective-permute-start(bf16[512,256]{1,0:T(8,128)(2,1)S(1)} %dynamic_slice.32), channel_id=1, source_target_pairs={{0,8},{8,16},{16,24},{24,28},{28,20},{20,12},{12,4},{4,0},{1,9},{9... | collective-permute-start | bytes 786440 | tf_op jit(solution)/shard_map/ppermute | solution.py:309
  11.9 11.2 %collective-permute-start.5 = (bf16[512,256]{1,0:T(8,128)(2,1)S(1)}, bf16[512,256]{1,0:T(8,128)(2,1)S(1)}, u32[]{:S(2)}, u32[]{:S(2)}) collective-permute-start(bf16[512,256]{1,0:T(8,128)(2,1)S(1)} %dynamic_slice.32), channel_id=1, source_target_pairs={{0,4},{8,0},{16,8},{24,16},{28,24},{20,28},{12,20},{4,12},{1,5},{9... | collective-permute-start | bytes 786440 | tf_op jit(solution)/shard_map/ppermute | solution.py:309
  17.5 9.7 %collective-permute-start.21 = (bf16[512,256]{1,0:T(8,128)(2,1)S(1)}, bf16[512,256]{1,0:T(8,128)(2,1)S(1)}, u32[]{:S(2)}, u32[]{:S(2)}) collective-permute-start(bf16[512,256]{1,0:T(8,128)(2,1)S(1)} %collective-permute-done.20.refs_1_), channel_id=1, source_target_pairs={{0,8},{8,16},{16,24},{24,28},{28,20},{20,12},{12,4},{4,0},{1,9},{9... | collective-permute-start | bytes 786440 | tf_op jit(solution)/shard_map/ppermute | solution.py:309
  19.1 9.8 %collective-permute-start.25 = (bf16[512,256]{1,0:T(8,128)(2,1)S(1)}, bf16[512,256]{1,0:T(8,128)(2,1)}, u32[]{:S(2)}, u32[]{:S(2)}) collective-permute-start(bf16[512,256]{1,0:T(8,128)(2,1)S(1)} %collective-permute-done.24.refs_4_), channel_id=1, source_target_pairs={{0,4},{8,0},{16,8},{24,16},{28,24},{20,28},{12,20},{4,12},{1,5},{9... | collective-permute-start | bytes 786440 | tf_op jit(solution)/shard_map/ppermute | solution.py:309
  21.5 12.2 %collective-permute-start.29 = (bf16[512,256]{1,0:T(8,128)(2,1)S(1)}, bf16[512,256]{1,0:T(8,128)(2,1)}, u32[]{:S(2)}, u32[]{:S(2)}) collective-permute-start(bf16[512,256]{1,0:T(8,128)(2,1)S(1)} %collective-permute-done.28.refs_2_), channel_id=1, source_target_pairs={{0,4},{8,0},{16,8},{24,16},{28,24},{20,28},{12,20},{4,12},{1,5},{9... | collective-permute-start | bytes 786440 | tf_op jit(solution)/shard_map/ppermute | solution.py:309
  23.1 11.1 %collective-permute-start.32 = (bf16[512,256]{1,0:T(8,128)(2,1)S(1)}, bf16[512,256]{1,0:T(8,128)(2,1)}, u32[]{:S(2)}, u32[]{:S(2)}) collective-permute-start(bf16[512,256]{1,0:T(8,128)(2,1)S(1)} %collective-permute-done.31.refs_3_), channel_id=1, source_target_pairs={{0,8},{8,16},{16,24},{24,28},{28,20},{20,12},{12,4},{4,0},{1,9},{9... | collective-permute-start | bytes 786440 | tf_op jit(solution)/shard_map/ppermute | solution.py:309
  27.2 10.9 %collective-permute-start.2 = (bf16[512,256]{1,0:T(8,128)(2,1)S(1)}, bf16[512,256]{1,0:T(8,128)(2,1)}, u32[]{:S(2)}, u32[]{:S(2)}) collective-permute-start(bf16[512,256]{1,0:T(8,128)(2,1)S(1)} %collective-permute-done.1.refs_1_), channel_id=1, source_target_pairs={{0,8},{8,16},{16,24},{24,28},{28,20},{20,12},{12,4},{4,0},{1,9},{9... | collective-permute-start | bytes 786440 | tf_op jit(solution)/shard_map/ppermute | solution.py:309
  28.8 12.9 %collective-permute-start.13 = (bf16[512,256]{1,0:T(8,128)(2,1)S(1)}, bf16[512,256]{1,0:T(8,128)(2,1)S(1)}, u32[]{:S(2)}, u32[]{:S(2)}) collective-permute-start(bf16[512,256]{1,0:T(8,128)(2,1)S(1)} %collective-permute-done.1.refs_1_), channel_id=1, source_target_pairs={{0,2},{1,3},{2,0},{3,1},{4,6},{5,7},{6,4},{7,5},{8,10},{9,11},{10,... | collective-permute-start | bytes 786440 | tf_op jit(solution)/shard_map/ppermute | solution.py:303
  34.2 10.2 %collective-permute-start.14 = (bf16[512,256]{1,0:T(8,128)(2,1)S(1)}, bf16[512,256]{1,0:T(8,128)(2,1)S(1)}, u32[]{:S(2)}, u32[]{:S(2)}) collective-permute-start(bf16[512,256]{1,0:T(8,128)(2,1)S(1)} %collective-permute-done.5.refs_3_), channel_id=1, source_target_pairs={{0,2},{1,3},{2,0},{3,1},{4,6},{5,7},{6,4},{7,5},{8,10},{9,11},{10,... | collective-permute-start | bytes 786440 | tf_op jit(solution)/shard_map/ppermute | solution.py:303
  41.3 9.4 %collective-permute-start.26 = (bf16[512,256]{1,0:T(8,128)(2,1)}, bf16[512,256]{1,0:T(8,128)(2,1)S(1)}, u32[]{:S(2)}, u32[]{:S(2)}) collective-permute-start(bf16[512,256]{1,0:T(8,128)(2,1)} %collective-permute-done.25.refs_8_), channel_id=1, source_target_pairs={{0,4},{8,0},{16,8},{24,16},{28,24},{20,28},{12,20},{4,12},{1,5},{9... | collective-permute-start | bytes 786440 | tf_op jit(solution)/shard_map/ppermute | solution.py:309
  41.8 9.8 %collective-permute-start.3 = (bf16[512,256]{1,0:T(8,128)(2,1)}, bf16[512,256]{1,0:T(8,128)(2,1)S(1)}, u32[]{:S(2)}, u32[]{:S(2)}) collective-permute-start(bf16[512,256]{1,0:T(8,128)(2,1)} %collective-permute-done.2.refs_5_), channel_id=1, source_target_pairs={{0,8},{8,16},{16,24},{24,28},{28,20},{20,12},{12,4},{4,0},{1,9},{9... | collective-permute-start | bytes 786440 | tf_op jit(solution)/shard_map/ppermute | solution.py:309
  45.1 11.2 %collective-permute-start.7 = (bf16[512,256]{1,0:T(8,128)(2,1)S(1)}, bf16[512,256]{1,0:T(8,128)(2,1)S(1)}, u32[]{:S(2)}, u32[]{:S(2)}) collective-permute-start(bf16[512,256]{1,0:T(8,128)(2,1)S(1)} %collective-permute-done.6.refs_7_), channel_id=1, source_target_pairs={{0,4},{8,0},{16,8},{24,16},{28,24},{20,28},{12,20},{4,12},{1,5},{9... | collective-permute-start | bytes 786440 | tf_op jit(solution)/shard_map/ppermute | solution.py:309
  47.2 19.1 %collective-permute-start.30 = (bf16[512,256]{1,0:T(8,128)(2,1)}, bf16[512,256]{1,0:T(8,128)(2,1)}, u32[]{:S(2)}, u32[]{:S(2)}) collective-permute-start(bf16[512,256]{1,0:T(8,128)(2,1)} %collective-permute-done.29.refs_6_), channel_id=1, source_target_pairs={{0,4},{8,0},{16,8},{24,16},{28,24},{20,28},{12,20},{4,12},{1,5},{9... | collective-permute-start | bytes 786440 | tf_op jit(solution)/shard_map/ppermute | solution.py:309
  50.7 22.0 %collective-permute-start.15 = (bf16[512,256]{1,0:T(8,128)(2,1)}, bf16[512,256]{1,0:T(8,128)(2,1)}, u32[]{:S(2)}, u32[]{:S(2)}) collective-permute-start(bf16[512,256]{1,0:T(8,128)(2,1)} %collective-permute-done.2.refs_5_), channel_id=1, source_target_pairs={{0,2},{1,3},{2,0},{3,1},{4,6},{5,7},{6,4},{7,5},{8,10},{9,11},{10,... | collective-permute-start | bytes 786440 | tf_op jit(solution)/shard_map/ppermute | solution.py:303
  51.5 20.6 %collective-permute-start.33 = (bf16[512,256]{1,0:T(8,128)(2,1)}, bf16[512,256]{1,0:T(8,128)(2,1)}, u32[]{:S(2)}, u32[]{:S(2)}) collective-permute-start(bf16[512,256]{1,0:T(8,128)(2,1)} %collective-permute-done.32.refs_7_), channel_id=1, source_target_pairs={{0,8},{8,16},{16,24},{24,28},{28,20},{20,12},{12,4},{4,0},{1,9},{9... | collective-permute-start | bytes 786440 | tf_op jit(solution)/shard_map/ppermute | solution.py:309
  56.3 18.0 %collective-permute-start.9 = (bf16[256,256]{1,0:T(8,128)(2,1)}, bf16[256,256]{1,0:T(8,128)(2,1)S(1)}, u32[]{:S(2)}, u32[]{:S(2)}) collective-permute-start(bf16[256,256]{1,0:T(8,128)(2,1)} %slice.18), channel_id=1, source_target_pairs={{0,8},{8,16},{16,24},{24,28},{28,20},{20,12},{12,4},{4,0},{1,9},{9... | collective-permute-start | bytes 393224 | tf_op jit(solution)/shard_map/ppermute | solution.py:309
  72.2 22.5 %collective-permute-start.16 = (bf16[512,256]{1,0:T(8,128)(2,1)}, bf16[512,256]{1,0:T(8,128)(2,1)S(1)}, u32[]{:S(2)}, u32[]{:S(2)}) collective-permute-start(bf16[512,256]{1,0:T(8,128)(2,1)} %copy-done.11), channel_id=1, source_target_pairs={{0,2},{1,3},{2,0},{3,1},{4,6},{5,7},{6,4},{7,5},{8,10},{9,11},{10,... | collective-permute-start | bytes 786440 | tf_op jit(solution)/shard_map/ppermute | solution.py:303
  72.7 17.1 %collective-permute-start.23 = (bf16[512,256]{1,0:T(8,128)(2,1)}, bf16[512,256]{1,0:T(8,128)(2,1)S(1)}, u32[]{:S(2)}, u32[]{:S(2)}) collective-permute-start(bf16[512,256]{1,0:T(8,128)(2,1)} %copy-done.17), channel_id=1, source_target_pairs={{0,8},{8,16},{16,24},{24,28},{28,20},{20,12},{12,4},{4,0},{1,9},{9... | collective-permute-start | bytes 786440 | tf_op jit(solution)/shard_map/ppermute | solution.py:309
  74.3 17.1 %collective-permute-start.27 = (bf16[512,256]{1,0:T(8,128)(2,1)}, bf16[512,256]{1,0:T(8,128)(2,1)S(1)}, u32[]{:S(2)}, u32[]{:S(2)}) collective-permute-start(bf16[512,256]{1,0:T(8,128)(2,1)} %copy-done.15), channel_id=1, source_target_pairs={{0,4},{8,0},{16,8},{24,16},{28,24},{20,28},{12,20},{4,12},{1,5},{9... | collective-permute-start | bytes 786440 | tf_op jit(solution)/shard_map/ppermute | solution.py:309
  74.8 27.6 %collective-permute-start.4 = (bf16[512,256]{1,0:T(8,128)(2,1)S(1)}, bf16[512,256]{1,0:T(8,128)(2,1)S(1)}, u32[]{:S(2)}, u32[]{:S(2)}) collective-permute-start(bf16[512,256]{1,0:T(8,128)(2,1)S(1)} %collective-permute-done.3.refs_0_), channel_id=1, source_target_pairs={{0,2},{1,3},{2,0},{3,1},{4,6},{5,7},{6,4},{7,5},{8,10},{9,11},{10,... | collective-permute-start | bytes 786440 | tf_op jit(solution)/shard_map/ppermute | solution.py:303
  76.4 26.0 %collective-permute-start.8 = (bf16[512,256]{1,0:T(8,128)(2,1)S(1)}, bf16[512,256]{1,0:T(8,128)(2,1)S(1)}, u32[]{:S(2)}, u32[]{:S(2)}) collective-permute-start(bf16[512,256]{1,0:T(8,128)(2,1)S(1)} %collective-permute-done.7.refs_2_), channel_id=1, source_target_pairs={{0,2},{1,3},{2,0},{3,1},{4,6},{5,7},{6,4},{7,5},{8,10},{9,11},{10,... | collective-permute-start | bytes 786440 | tf_op jit(solution)/shard_map/ppermute | solution.py:303
  89.8 12.6 %collective-permute-start.11 = (bf16[256,256]{1,0:T(8,128)(2,1)S(1)}, bf16[256,256]{1,0:T(8,128)(2,1)S(1)}, u32[]{:S(2)}, u32[]{:S(2)}) collective-permute-start(bf16[256,256]{1,0:T(8,128)(2,1)S(1)} %collective-permute-done.9.refs_4_), channel_id=1, source_target_pairs={{0,2},{1,3},{2,0},{3,1},{4,6},{5,7},{6,4},{7,5},{8,10},{9,11},{10,... | collective-permute-start | bytes 393224 | tf_op jit(solution)/shard_map/ppermute | solution.py:303
  91.4 11.0 %collective-permute-start.12 = (bf16[256,256]{1,0:T(8,128)(2,1)}, bf16[256,256]{1,0:T(8,128)(2,1)S(1)}, u32[]{:S(2)}, u32[]{:S(2)}) collective-permute-start(bf16[256,256]{1,0:T(8,128)(2,1)} %collective-permute-done.10.refs_5_), channel_id=1, source_target_pairs={{0,2},{1,3},{2,0},{3,1},{4,6},{5,7},{6,4},{7,5},{8,10},{9,11},{10,... | collective-permute-start | bytes 393224 | tf_op jit(solution)/shard_map/ppermute | solution.py:303
  94.7 14.3 %collective-permute-start.35 = (bf16[512,256]{1,0:T(8,128)(2,1)S(1)}, bf16[512,256]{1,0:T(8,128)(2,1)}, u32[]{:S(2)}, u32[]{:S(2)}) collective-permute-start(bf16[512,256]{1,0:T(8,128)(2,1)S(1)} %shard_map.95.refs_3_), channel_id=1, source_target_pairs={{0,2},{1,3},{4,6},{5,7},{8,10},{9,11},{12,14},{13,15},{16,18},{17,... | collective-permute-start | bytes 786440 | tf_op jit(solution)/shard_map/ppermute | solution.py:306
  108.4 20.8 %collective-permute-start.34 = (bf16[512,256]{1,0:T(8,128)(2,1)S(1)}, bf16[512,256]{1,0:T(8,128)(2,1)S(1)}, u32[]{:S(2)}, u32[]{:S(2)}) collective-permute-start(bf16[512,256]{1,0:T(8,128)(2,1)S(1)} %shard_map.95.refs_3_), channel_id=1, source_target_pairs={{0,1},{1,0},{2,3},{3,2},{4,5},{5,4},{6,7},{7,6},{8,9},{9,8},{10,11... | collective-permute-start | bytes 786440 | tf_op jit(solution)/shard_map/ppermute | solution.py:300
  108.5 20.7 %collective-permute-start.17 = (bf16[512,256]{1,0:T(8,128)(2,1)S(1)}, bf16[512,256]{1,0:T(8,128)(2,1)S(1)}, u32[]{:S(2)}, u32[]{:S(2)}) collective-permute-start(bf16[512,256]{1,0:T(8,128)(2,1)S(1)} %shard_map.92.refs_1_), channel_id=1, source_target_pairs={{0,1},{1,0},{2,3},{3,2},{4,5},{5,4},{6,7},{7,6},{8,9},{9,8},{10,11... | collective-permute-start | bytes 786440 | tf_op jit(solution)/shard_map/ppermute | solution.py:300
  109.0 20.2 %collective-permute-start.36 = (bf16[512,256]{1,0:T(8,128)(2,1)}, bf16[512,256]{1,0:T(8,128)(2,1)}, u32[]{:S(2)}, u32[]{:S(2)}) collective-permute-start(bf16[512,256]{1,0:T(8,128)(2,1)} %collective-permute-done.35.refs_4_), channel_id=1, source_target_pairs={{0,1},{1,0},{2,3},{3,2},{4,5},{5,4},{6,7},{7,6},{8,9},{9,8},{10,11... | collective-permute-start | bytes 786440 | tf_op jit(solution)/shard_map/ppermute | solution.py:300
  115.8 13.4 %collective-permute-start.19 = (bf16[512,256]{1,0:T(8,128)(2,1)S(1)}, bf16[512,256]{1,0:T(8,128)(2,1)}, u32[]{:S(2)}, u32[]{:S(2)}) collective-permute-start(bf16[512,256]{1,0:T(8,128)(2,1)S(1)} %collective-permute-done.18.refs_2_), channel_id=1, source_target_pairs={{0,1},{1,0},{2,3},{3,2},{4,5},{5,4},{6,7},{7,6},{8,9},{9,8},{10,11... | collective-permute-start | bytes 786440 | tf_op jit(solution)/shard_map/ppermute | solution.py:300
  (32 other events, 376.3 us)

commit v2 on v1

--- a/solution.py
+++ b/solution.py
@@ -100,7 +100,7 @@
 ):
     number_of_rows = own_tokens.shape[0]
     width = pieces[0].shape[1]
-    anywhere = pl.BlockSpec(memory_space=pl.ANY)
+    anywhere = pl.BlockSpec(memory_space=pltpu.MemorySpace.HBM)
     chip_rows = CORES * number_of_rows
     out = jax.ShapeDtypeStruct(
         (chip_rows, width), jnp.float32 if finish == "sum" else jnp.bfloat16
@@ -290,11 +290,7 @@
     half_width = kv_width // CORES
     ring = ring_order(dp_size)
     dp_index = lax.axis_index("dp")
-    spots = [0] * dp_size
-    for spot, index in enumerate(ring):
-        spots[index] = spot
-    my_spot = jnp.asarray(spots, jnp.int32)[dp_index]
-    ring_array = jnp.asarray(ring, jnp.int32)
+    my_spot = jnp.where(dp_index % 2 == 0, dp_index // 2, dp_size - (dp_index + 1) // 2)
 
     def to_sibling(x):
         return lax.ppermute(x, "ctx", [(i, i ^ 1) for i in range(ctx_size)])
@@ -320,7 +316,8 @@
     sibling_tokens = to_sibling(own_tokens)
 
     def source_at(distance):
-        return ring_array[(my_spot + distance + dp_size) % dp_size]
+        spot = (my_spot + distance + dp_size) % dp_size
+        return jnp.where(spot < dp_size // 2, 2 * spot, 2 * (dp_size - spot) - 1)
 
     half_ring = dp_size // 2
 

time: 143 us -> 134 us (0.937)
  between operations: 10.4 us -> 0.45 us
  waiting for transfers between devices: 37.3 us -> 40.3 us
  local copies, waits for them, and re-layouts: 11.6 us -> 10.1 us
    ppermute x22, waiting for transfers between devices: 30.4 us -> 33.2 us  [along_ring(): lax.ppermute(x, 'dp', [(ring[i], ring[(i + step) % dp_size]) for i in ran...]
    unnamed x54 -> x50, local copies, waits for them, and re-layouts: 4.61 us -> 4.51 us
  transfers between devices with their start and end apart: 37 -> 37, of which waited for: 14 -> 16; matrix products, arithmetic and copies ran while one was open for 6% -> 6% of each run, Pallas kernels for 25% -> 27%
where the time goes in v2:
time: 134 us
  Pallas kernels  48.9 us (36%)
  waiting for transfers between devices  40.3 us (30%)
  starting transfers between devices  32 us (24%)
  local copies, waits for them, and re-layouts  10.1 us (8%)
  other arithmetic  2.09 us (2%)
    ppermute x22, waiting for transfers between devices, along_ring(): lax.ppermute(x, 'dp', [(ring[i], ring[(i + step) % dp_size]) for i in ran...  33.2 us
    pallas_call x2, Pallas kernels, attend(): pl.pallas_call(functools.partial(attention_kernel, hops, row_blocks, grou...  26.5 us
    pallas_call x5, Pallas kernels, project(): pl.pallas_call(functools.partial(project_kernel, plan, finish, added), ou...  22.4 us
    ppermute x22, starting transfers between devices, along_ring(): lax.ppermute(x, 'dp', [(ring[i], ring[(i + step) % dp_size]) for i in ran...  22.3 us
    ppermute x2, waiting for transfers between devices, to_next_chip(): lax.ppermute(x, 'ctx', [(i, i + CORES) for i in range(ctx_size - CORES)])  7 us
    ppermute x8, starting transfers between devices, to_plane(): return lax.ppermute(x, 'ctx', [(i, i ^ CORES) for i in range(ctx_size)])  6.27 us
    unnamed x50, local copies, waits for them, and re-layouts  4.51 us
    ppermute x2, starting transfers between devices, to_next_chip(): lax.ppermute(x, 'ctx', [(i, i + CORES) for i in range(ctx_size - CORES)])  2.72 us
  transfers between devices with their start and end apart: 37, of which 16 were waited for; matrix products, arithmetic and copies ran while one was open for 6% of the time, Pallas kernels for 27%

profile of v2, /device:TPU:12, one launch (start us, length us, event | category | flops | bytes accessed | tf_op | source)
XLA Modules:
  0.0 133.8 jit_solution(4153920200355202862)
XLA Ops:
  1.1 1.6 %collective-permute-start.20 = (bf16[512,256]{1,0:T(8,128)(2,1)S(1)}, bf16[512,256]{1,0:T(8,128)(2,1)S(1)}, u32[]{:S(2)}, u32[]{:S(2)}) collective-permute-start(bf16[512,256]{1,0:T(8,128)(2,1)S(1)} %get-tuple-element.6), channel_id=1, source_target_pairs={{0,8},{8,16},{16,24},{24,28},{28,20},{20,12},{12,4},{4,0},{1,9},{9... | collective-permute-start | bytes 786440 | tf_op jit(solution)/shard_map/ppermute | solution.py:305
  3.6 1.6 %collective-permute-start.31 = (bf16[512,256]{1,0:T(8,128)(2,1)S(1)}, bf16[512,256]{1,0:T(8,128)(2,1)S(1)}, u32[]{:S(2)}, u32[]{:S(2)}) collective-permute-start(bf16[512,256]{1,0:T(8,128)(2,1)S(1)} %get-tuple-element.5), channel_id=1, source_target_pairs={{0,8},{8,16},{16,24},{24,28},{28,20},{20,12},{12,4},{4,0},{1,9},{9... | collective-permute-start | bytes 786440 | tf_op jit(solution)/shard_map/ppermute | solution.py:305
  6.3 4.0 %collective-permute-done.20.refs_1_ = bf16[512,256]{1,0:T(8,128)(2,1)S(1)} collective-permute-done((bf16[512,256]{1,0:T(8,128)(2,1)S(1)}, bf16[512,256]{1,0:T(8,128)(2,1)S(1)}, u32[]{:S(2)}, u32[]{:S(2)}) %collective-permute-start.20) | collective-permute-done | bytes 262176 | tf_op jit(solution)/shard_map/ppermute | solution.py:305
  10.3 1.6 %collective-permute-start.1 = (bf16[512,256]{1,0:T(8,128)(2,1)S(1)}, bf16[512,256]{1,0:T(8,128)(2,1)S(1)}, u32[]{:S(2)}, u32[]{:S(2)}) collective-permute-start(bf16[512,256]{1,0:T(8,128)(2,1)S(1)} %dynamic_slice.15), channel_id=1, source_target_pairs={{0,8},{8,16},{16,24},{24,28},{28,20},{20,12},{12,4},{4,0},{1,9},{9... | collective-permute-start | bytes 786440 | tf_op jit(solution)/shard_map/ppermute | solution.py:305
  12.3 5.2 %collective-permute-done.28.refs_2_ = bf16[512,256]{1,0:T(8,128)(2,1)S(1)} collective-permute-done((bf16[512,256]{1,0:T(8,128)(2,1)S(1)}, bf16[512,256]{1,0:T(8,128)(2,1)S(1)}, u32[]{:S(2)}, u32[]{:S(2)}) %collective-permute-start.28) | collective-permute-done | bytes 262176 | tf_op jit(solution)/shard_map/ppermute | solution.py:305
  17.5 1.6 %collective-permute-start.21 = (bf16[512,256]{1,0:T(8,128)(2,1)S(1)}, bf16[512,256]{1,0:T(8,128)(2,1)S(1)}, u32[]{:S(2)}, u32[]{:S(2)}) collective-permute-start(bf16[512,256]{1,0:T(8,128)(2,1)S(1)} %collective-permute-done.20.refs_1_), channel_id=1, source_target_pairs={{0,8},{8,16},{16,24},{24,28},{28,20},{20,12},{12,4},{4,0},{1,9},{9... | collective-permute-start | bytes 786440 | tf_op jit(solution)/shard_map/ppermute | solution.py:305
  19.5 2.0 %collective-permute-done.1.refs_1_ = bf16[512,256]{1,0:T(8,128)(2,1)S(1)} collective-permute-done((bf16[512,256]{1,0:T(8,128)(2,1)S(1)}, bf16[512,256]{1,0:T(8,128)(2,1)S(1)}, u32[]{:S(2)}, u32[]{:S(2)}) %collective-permute-start.1) | collective-permute-done | bytes 262176 | tf_op jit(solution)/shard_map/ppermute | solution.py:305
  23.1 1.6 %collective-permute-start.32 = (bf16[512,256]{1,0:T(8,128)(2,1)S(1)}, bf16[512,256]{1,0:T(8,128)(2,1)}, u32[]{:S(2)}, u32[]{:S(2)}) collective-permute-start(bf16[512,256]{1,0:T(8,128)(2,1)S(1)} %collective-permute-done.31.refs_3_), channel_id=1, source_target_pairs={{0,8},{8,16},{16,24},{24,28},{28,20},{20,12},{12,4},{4,0},{1,9},{9... | collective-permute-start | bytes 786440 | tf_op jit(solution)/shard_map/ppermute | solution.py:305
  24.7 2.5 %collective-permute-done.21.refs_5_ = bf16[512,256]{1,0:T(8,128)(2,1)S(1)} collective-permute-done((bf16[512,256]{1,0:T(8,128)(2,1)S(1)}, bf16[512,256]{1,0:T(8,128)(2,1)S(1)}, u32[]{:S(2)}, u32[]{:S(2)}) %collective-permute-start.21) | collective-permute-done | bytes 262176 | tf_op jit(solution)/shard_map/ppermute | solution.py:305
  27.2 1.6 %collective-permute-start.2 = (bf16[512,256]{1,0:T(8,128)(2,1)S(1)}, bf16[512,256]{1,0:T(8,128)(2,1)}, u32[]{:S(2)}, u32[]{:S(2)}) collective-permute-start(bf16[512,256]{1,0:T(8,128)(2,1)S(1)} %collective-permute-done.1.refs_1_), channel_id=1, source_target_pairs={{0,8},{8,16},{16,24},{24,28},{28,20},{20,12},{12,4},{4,0},{1,9},{9... | collective-permute-start | bytes 786440 | tf_op jit(solution)/shard_map/ppermute | solution.py:305
  29.3 4.4 %collective-permute-done.29.refs_6_ = bf16[512,256]{1,0:T(8,128)(2,1)} collective-permute-done((bf16[512,256]{1,0:T(8,128)(2,1)S(1)}, bf16[512,256]{1,0:T(8,128)(2,1)}, u32[]{:S(2)}, u32[]{:S(2)}) %collective-permute-start.29) | collective-permute-done | bytes 262176 | tf_op jit(solution)/shard_map/ppermute | solution.py:305
  34.8 3.3 %collective-permute-done.2.refs_5_ = bf16[512,256]{1,0:T(8,128)(2,1)} collective-permute-done((bf16[512,256]{1,0:T(8,128)(2,1)S(1)}, bf16[512,256]{1,0:T(8,128)(2,1)}, u32[]{:S(2)}, u32[]{:S(2)}) %collective-permute-start.2) | collective-permute-done | bytes 262176 | tf_op jit(solution)/shard_map/ppermute | solution.py:305
  38.0 1.6 %collective-permute-start.22 = (bf16[512,256]{1,0:T(8,128)(2,1)S(1)}, bf16[512,256]{1,0:T(8,128)(2,1)S(1)}, u32[]{:S(2)}, u32[]{:S(2)}) collective-permute-start(bf16[512,256]{1,0:T(8,128)(2,1)S(1)} %collective-permute-done.21.refs_5_), channel_id=1, source_target_pairs={{0,8},{8,16},{16,24},{24,28},{28,20},{20,12},{12,4},{4,0},{1,9},{9... | collective-permute-start | bytes 786440 | tf_op jit(solution)/shard_map/ppermute | solution.py:305
  39.6 1.7 %collective-permute-done.6.refs_7_ = bf16[512,256]{1,0:T(8,128)(2,1)S(1)} collective-permute-done((bf16[512,256]{1,0:T(8,128)(2,1)S(1)}, bf16[512,256]{1,0:T(8,128)(2,1)S(1)}, u32[]{:S(2)}, u32[]{:S(2)}) %collective-permute-start.6) | collective-permute-done | bytes 262176 | tf_op jit(solution)/shard_map/ppermute | solution.py:305
  41.8 1.6 %collective-permute-start.3 = (bf16[512,256]{1,0:T(8,128)(2,1)}, bf16[512,256]{1,0:T(8,128)(2,1)S(1)}, u32[]{:S(2)}, u32[]{:S(2)}) collective-permute-start(bf16[512,256]{1,0:T(8,128)(2,1)} %collective-permute-done.2.refs_5_), channel_id=1, source_target_pairs={{0,8},{8,16},{16,24},{24,28},{28,20},{20,12},{12,4},{4,0},{1,9},{9... | collective-permute-start | bytes 786440 | tf_op jit(solution)/shard_map/ppermute | solution.py:305
  47.7 3.0 %collective-permute-done.26.refs_3_ = bf16[512,256]{1,0:T(8,128)(2,1)S(1)} collective-permute-done((bf16[512,256]{1,0:T(8,128)(2,1)}, bf16[512,256]{1,0:T(8,128)(2,1)S(1)}, u32[]{:S(2)}, u32[]{:S(2)}) %collective-permute-start.26) | collective-permute-done | bytes 262176 | tf_op jit(solution)/shard_map/ppermute | solution.py:305
  51.5 1.6 %collective-permute-start.33 = (bf16[512,256]{1,0:T(8,128)(2,1)}, bf16[512,256]{1,0:T(8,128)(2,1)}, u32[]{:S(2)}, u32[]{:S(2)}) collective-permute-start(bf16[512,256]{1,0:T(8,128)(2,1)} %collective-permute-done.32.refs_7_), channel_id=1, source_target_pairs={{0,8},{8,16},{16,24},{24,28},{28,20},{20,12},{12,4},{4,0},{1,9},{9... | collective-permute-start | bytes 786440 | tf_op jit(solution)/shard_map/ppermute | solution.py:305
  53.9 2.4 %collective-permute-done.7.refs_2_ = bf16[512,256]{1,0:T(8,128)(2,1)S(1)} collective-permute-done((bf16[512,256]{1,0:T(8,128)(2,1)S(1)}, bf16[512,256]{1,0:T(8,128)(2,1)S(1)}, u32[]{:S(2)}, u32[]{:S(2)}) %collective-permute-start.7) | collective-permute-done | bytes 262176 | tf_op jit(solution)/shard_map/ppermute | solution.py:305
  56.3 1.6 %collective-permute-start.9 = (bf16[256,256]{1,0:T(8,128)(2,1)}, bf16[256,256]{1,0:T(8,128)(2,1)S(1)}, u32[]{:S(2)}, u32[]{:S(2)}) collective-permute-start(bf16[256,256]{1,0:T(8,128)(2,1)} %slice.18), channel_id=1, source_target_pairs={{0,8},{8,16},{16,24},{24,28},{28,20},{20,12},{12,4},{4,0},{1,9},{9... | collective-permute-start | bytes 393224 | tf_op jit(solution)/shard_map/ppermute | solution.py:305
  62.2 1.6 %collective-permute-start.23 = (bf16[512,256]{1,0:T(8,128)(2,1)}, bf16[512,256]{1,0:T(8,128)(2,1)S(1)}, u32[]{:S(2)}, u32[]{:S(2)}) collective-permute-start(bf16[512,256]{1,0:T(8,128)(2,1)} %copy-done.17), channel_id=1, source_target_pairs={{0,8},{8,16},{16,24},{24,28},{28,20},{20,12},{12,4},{4,0},{1,9},{9... | collective-permute-start | bytes 786440 | tf_op jit(solution)/shard_map/ppermute | solution.py:305
  64.3 2.0 %collective-permute-done.10.refs_5_ = bf16[256,256]{1,0:T(8,128)(2,1)} collective-permute-done((bf16[256,256]{1,0:T(8,128)(2,1)}, bf16[256,256]{1,0:T(8,128)(2,1)}, u32[]{:S(2)}, u32[]{:S(2)}) %collective-permute-start.10) | collective-permute-done | bytes 131104 | tf_op jit(solution)/shard_map/ppermute | solution.py:305
  66.3 2.0 %collective-permute-start.8 = (bf16[512,256]{1,0:T(8,128)(2,1)S(1)}, bf16[512,256]{1,0:T(8,128)(2,1)S(1)}, u32[]{:S(2)}, u32[]{:S(2)}) collective-permute-start(bf16[512,256]{1,0:T(8,128)(2,1)S(1)} %collective-permute-done.7.refs_2_), channel_id=1, source_target_pairs={{0,2},{1,3},{2,0},{3,1},{4,6},{5,7},{6,4},{7,5},{8,10},{9,11},{10,... | collective-permute-start | bytes 786440 | tf_op jit(solution)/shard_map/ppermute | solution.py:299
  68.3 2.2 %copy-done = bf16[1,256,8192]{2,1,0:T(8,128)(2,1)S(1)} copy-done((bf16[1,256,8192]{2,1,0:T(8,128)(2,1)S(1)}, bf16[1,256,8192]{2,1,0:T(8,128)(2,1)}, u32[]{:S(2)}) %copy-start) | copy-done | bytes 4194328
  72.0 5.9 %shard_map.75.refs_4_ = f32[512,256]{1,0:T(8,128)S(1)} custom-call(s32[10]{0:T(128)S(1)} %copy-done.19, bf16[256,8192]{1,0:T(8,128)(2,1)S(1)} %bitcast.40, bf16[256,8192]{1,0:T(8,128)(2,1)} %collective-permute-done.sibling_ref, bf16[1024,256]{1,0:T(8,128)(2,1)S(1)} %constant_dynamic-slice_fusion.1.refs_0_, ...), custom_call_target="tpu_custom_call" | custom-call | flops 1342177280 | bytes 7864320 | tf_op jit(solution)/shard_map/pallas_call | solution.py:113
  77.9 3.2 %shard_map.76.refs_2_ = f32[512,256]{1,0:T(8,128)S(1)} custom-call(s32[4]{0:T(128)S(1)} %pad_add_fusion.1.columns, bf16[256,8192]{1,0:T(8,128)(2,1)S(1)} %bitcast.41, bf16[256,8192]{1,0:T(8,128)(2,1)} %collective-permute-done.sibling_ref, bf16[512,256]{1,0:T(8,128)(2,1)S(1)} %copy-done.18, bf16[512,256]{1,0:T(8,128)(2,1)} %collective-permute-done.30.refs_1_, ...), custom_call_target="tpu_custom_call" | custom-call | flops 536870912 | bytes 3145728 | tf_op jit(solution)/shard_map/pallas_call | solution.py:113
  81.2 2.0 %collective-permute-start.12 = (bf16[256,256]{1,0:T(8,128)(2,1)}, bf16[256,256]{1,0:T(8,128)(2,1)S(1)}, u32[]{:S(2)}, u32[]{:S(2)}) collective-permute-start(bf16[256,256]{1,0:T(8,128)(2,1)} %collective-permute-done.10.refs_5_), channel_id=1, source_target_pairs={{0,2},{1,3},{2,0},{3,1},{4,6},{5,7},{6,4},{7,5},{8,10},{9,11},{10,... | collective-permute-start | bytes 393224 | tf_op jit(solution)/shard_map/ppermute | solution.py:299
  83.2 2.8 %shard_map.77.refs_3_ = bf16[512,256]{1,0:T(8,128)(2,1)S(1)} custom-call(s32[2]{0:T(128)S(1)} %copy-done.20, bf16[256,8192]{1,0:T(8,128)(2,1)S(1)} %bitcast.42, bf16[256,8192]{1,0:T(8,128)(2,1)} %collective-permute-done.sibling_ref, bf16[512,256]{1,0:T(8,128)(2,1)S(1)} %collective-permute-done.23.refs_0_, ...), custom_call_target="tpu_custom_call" | custom-call | flops 268435456 | bytes 1572864 | tf_op jit(solution)/shard_map/pallas_call | solution.py:113
  87.5 6.2 %shard_map.73.refs_8_ = f32[512,256]{1,0:T(8,128)S(1)} custom-call(s32[10]{0:T(128)S(1)} %stack.138.columns, bf16[256,8192]{1,0:T(8,128)(2,1)S(1)} %bitcast.43, bf16[256,8192]{1,0:T(8,128)(2,1)} %collective-permute-done.sibling_ref, bf16[1024,256]{1,0:T(8,128)(2,1)S(1)} %constant_dynamic-slice_fusion.2.refs_0_, ...), custom_call_target="tpu_custom_call" | custom-call | flops 1342177280 | bytes 7864320 | tf_op jit(solution)/shard_map/pallas_call | solution.py:113
  93.8 4.4 %shard_map.74.refs_1_ = bf16[512,256]{1,0:T(8,128)(2,1)S(1)} custom-call(s32[6]{0:T(128)S(1)} %stack.127.columns, bf16[256,8192]{1,0:T(8,128)(2,1)S(1)} %bitcast.44, bf16[256,8192]{1,0:T(8,128)(2,1)} %collective-permute-done.sibling_ref, bf16[512,256]{1,0:T(8,128)(2,1)S(1)} %collective-permute-done.3.refs_0_, ...), custom_call_target="tpu_custom_call" | custom-call | flops 805306368 | bytes 4718592 | tf_op jit(solution)/shard_map/pallas_call | solution.py:113
  100.2 7.0 %collective-permute-done.18.refs_2_ = bf16[512,256]{1,0:T(8,128)(2,1)S(1)} collective-permute-done((bf16[512,256]{1,0:T(8,128)(2,1)S(1)}, bf16[512,256]{1,0:T(8,128)(2,1)S(1)}, u32[]{:S(2)}, u32[]{:S(2)}) %collective-permute-start.18) | collective-permute-done | bytes 262176 | tf_op jit(solution)/shard_map/ppermute | solution.py:302
  107.2 13.3 %attend.2.refs_5_ = bf16[256,4096]{1,0:T(8,128)(2,1)} custom-call(s32[11]{0:T(128)S(1)} %get-tuple-element.10.facts, bf16[256,4096]{1,0:T(8,128)(2,1)S(1)} %bitcast.45, bf16[512,256]{1,0:T(8,128)(2,1)S(1)} %shard_map.74.refs_1_, bf16[512,256]{1,0:T(8,128)(2,1)S(1)} %collective-permute-done.18.refs_2_, bf16[512,256]{1,0:T(8,128)(2,1)S(1)} %shard_map.77.refs_3_, ...), custom_call_target="tpu_custom_call" | custom-call | flops 1073741824 | bytes 4194304 | tf_op jit(solution)/shard_map/attend/pallas_call | solution.py:243
  120.5 13.2 %attend.3 = bf16[256,4096]{1,0:T(8,128)(2,1)} custom-call(s32[11]{0:T(128)S(1)} %get-tuple-element.11.facts, bf16[256,4096]{1,0:T(8,128)(2,1)S(1)} %bitcast.46, bf16[512,256]{1,0:T(8,128)(2,1)S(1)} %collective-permute-done.17.refs_1_, bf16[512,256]{1,0:T(8,128)(2,1)} %collective-permute-done.19.refs_2_, ...), custom_call_target="tpu_custom_call", output_to_operand_aliasing={{}: (6, {})} | custom-call | flops 1073741824 | bytes 4194304 | tf_op jit(solution)/shard_map/attend/pallas_call | solution.py:243
  (119 shorter events, 23.5 us)
Async XLA Ops:
  0.0 66.3 %collective-permute-start = (bf16[256,8192]{1,0:T(8,128)(2,1)}, bf16[256,8192]{1,0:T(8,128)(2,1)}, u32[]{:S(2)}, u32[]{:S(2)}) collective-permute-start(bf16[256,8192]{1,0:T(8,128)(2,1)} %bitcast.39), channel_id=1, source_target_pairs={{0,1},{1,0},{2,3},{3,2},{4,5},{5,4},{6,7},{7,6},{8,9},{9,8},{10,11... | collective-permute-start | bytes 12582920 | tf_op jit(solution)/shard_map/ppermute | solution.py:296
  1.1 9.2 %collective-permute-start.20 = (bf16[512,256]{1,0:T(8,128)(2,1)S(1)}, bf16[512,256]{1,0:T(8,128)(2,1)S(1)}, u32[]{:S(2)}, u32[]{:S(2)}) collective-permute-start(bf16[512,256]{1,0:T(8,128)(2,1)S(1)} %get-tuple-element.6), channel_id=1, source_target_pairs={{0,8},{8,16},{16,24},{24,28},{28,20},{20,12},{12,4},{4,0},{1,9},{9... | collective-permute-start | bytes 786440 | tf_op jit(solution)/shard_map/ppermute | solution.py:305
  2.7 9.2 %collective-permute-start.24 = (bf16[512,256]{1,0:T(8,128)(2,1)S(1)}, bf16[512,256]{1,0:T(8,128)(2,1)S(1)}, u32[]{:S(2)}, u32[]{:S(2)}) collective-permute-start(bf16[512,256]{1,0:T(8,128)(2,1)S(1)} %get-tuple-element.5), channel_id=1, source_target_pairs={{0,4},{8,0},{16,8},{24,16},{28,24},{20,28},{12,20},{4,12},{1,5},{9... | collective-permute-start | bytes 786440 | tf_op jit(solution)/shard_map/ppermute | solution.py:305
  3.1 14.3 %collective-permute-start.28 = (bf16[512,256]{1,0:T(8,128)(2,1)S(1)}, bf16[512,256]{1,0:T(8,128)(2,1)S(1)}, u32[]{:S(2)}, u32[]{:S(2)}) collective-permute-start(bf16[512,256]{1,0:T(8,128)(2,1)S(1)} %get-tuple-element.6), channel_id=1, source_target_pairs={{0,4},{8,0},{16,8},{24,16},{28,24},{20,28},{12,20},{4,12},{1,5},{9... | collective-permute-start | bytes 786440 | tf_op jit(solution)/shard_map/ppermute | solution.py:305
  3.6 15.5 %collective-permute-start.31 = (bf16[512,256]{1,0:T(8,128)(2,1)S(1)}, bf16[512,256]{1,0:T(8,128)(2,1)S(1)}, u32[]{:S(2)}, u32[]{:S(2)}) collective-permute-start(bf16[512,256]{1,0:T(8,128)(2,1)S(1)} %get-tuple-element.5), channel_id=1, source_target_pairs={{0,8},{8,16},{16,24},{24,28},{28,20},{20,12},{12,4},{4,0},{1,9},{9... | collective-permute-start | bytes 786440 | tf_op jit(solution)/shard_map/ppermute | solution.py:305
  10.3 11.2 %collective-permute-start.1 = (bf16[512,256]{1,0:T(8,128)(2,1)S(1)}, bf16[512,256]{1,0:T(8,128)(2,1)S(1)}, u32[]{:S(2)}, u32[]{:S(2)}) collective-permute-start(bf16[512,256]{1,0:T(8,128)(2,1)S(1)} %dynamic_slice.15), channel_id=1, source_target_pairs={{0,8},{8,16},{16,24},{24,28},{28,20},{20,12},{12,4},{4,0},{1,9},{9... | collective-permute-start | bytes 786440 | tf_op jit(solution)/shard_map/ppermute | solution.py:305
  11.9 11.2 %collective-permute-start.5 = (bf16[512,256]{1,0:T(8,128)(2,1)S(1)}, bf16[512,256]{1,0:T(8,128)(2,1)S(1)}, u32[]{:S(2)}, u32[]{:S(2)}) collective-permute-start(bf16[512,256]{1,0:T(8,128)(2,1)S(1)} %dynamic_slice.15), channel_id=1, source_target_pairs={{0,4},{8,0},{16,8},{24,16},{28,24},{20,28},{12,20},{4,12},{1,5},{9... | collective-permute-start | bytes 786440 | tf_op jit(solution)/shard_map/ppermute | solution.py:305
  17.5 9.7 %collective-permute-start.21 = (bf16[512,256]{1,0:T(8,128)(2,1)S(1)}, bf16[512,256]{1,0:T(8,128)(2,1)S(1)}, u32[]{:S(2)}, u32[]{:S(2)}) collective-permute-start(bf16[512,256]{1,0:T(8,128)(2,1)S(1)} %collective-permute-done.20.refs_1_), channel_id=1, source_target_pairs={{0,8},{8,16},{16,24},{24,28},{28,20},{20,12},{12,4},{4,0},{1,9},{9... | collective-permute-start | bytes 786440 | tf_op jit(solution)/shard_map/ppermute | solution.py:305
  19.1 9.8 %collective-permute-start.25 = (bf16[512,256]{1,0:T(8,128)(2,1)S(1)}, bf16[512,256]{1,0:T(8,128)(2,1)}, u32[]{:S(2)}, u32[]{:S(2)}) collective-permute-start(bf16[512,256]{1,0:T(8,128)(2,1)S(1)} %collective-permute-done.24.refs_4_), channel_id=1, source_target_pairs={{0,4},{8,0},{16,8},{24,16},{28,24},{20,28},{12,20},{4,12},{1,5},{9... | collective-permute-start | bytes 786440 | tf_op jit(solution)/shard_map/ppermute | solution.py:305
  21.5 12.2 %collective-permute-start.29 = (bf16[512,256]{1,0:T(8,128)(2,1)S(1)}, bf16[512,256]{1,0:T(8,128)(2,1)}, u32[]{:S(2)}, u32[]{:S(2)}) collective-permute-start(bf16[512,256]{1,0:T(8,128)(2,1)S(1)} %collective-permute-done.28.refs_2_), channel_id=1, source_target_pairs={{0,4},{8,0},{16,8},{24,16},{28,24},{20,28},{12,20},{4,12},{1,5},{9... | collective-permute-start | bytes 786440 | tf_op jit(solution)/shard_map/ppermute | solution.py:305
  23.1 11.1 %collective-permute-start.32 = (bf16[512,256]{1,0:T(8,128)(2,1)S(1)}, bf16[512,256]{1,0:T(8,128)(2,1)}, u32[]{:S(2)}, u32[]{:S(2)}) collective-permute-start(bf16[512,256]{1,0:T(8,128)(2,1)S(1)} %collective-permute-done.31.refs_3_), channel_id=1, source_target_pairs={{0,8},{8,16},{16,24},{24,28},{28,20},{20,12},{12,4},{4,0},{1,9},{9... | collective-permute-start | bytes 786440 | tf_op jit(solution)/shard_map/ppermute | solution.py:305
  27.2 10.9 %collective-permute-start.2 = (bf16[512,256]{1,0:T(8,128)(2,1)S(1)}, bf16[512,256]{1,0:T(8,128)(2,1)}, u32[]{:S(2)}, u32[]{:S(2)}) collective-permute-start(bf16[512,256]{1,0:T(8,128)(2,1)S(1)} %collective-permute-done.1.refs_1_), channel_id=1, source_target_pairs={{0,8},{8,16},{16,24},{24,28},{28,20},{20,12},{12,4},{4,0},{1,9},{9... | collective-permute-start | bytes 786440 | tf_op jit(solution)/shard_map/ppermute | solution.py:305
  28.8 12.9 %collective-permute-start.13 = (bf16[512,256]{1,0:T(8,128)(2,1)S(1)}, bf16[512,256]{1,0:T(8,128)(2,1)S(1)}, u32[]{:S(2)}, u32[]{:S(2)}) collective-permute-start(bf16[512,256]{1,0:T(8,128)(2,1)S(1)} %collective-permute-done.1.refs_1_), channel_id=1, source_target_pairs={{0,2},{1,3},{2,0},{3,1},{4,6},{5,7},{6,4},{7,5},{8,10},{9,11},{10,... | collective-permute-start | bytes 786440 | tf_op jit(solution)/shard_map/ppermute | solution.py:299
  34.2 10.2 %collective-permute-start.14 = (bf16[512,256]{1,0:T(8,128)(2,1)S(1)}, bf16[512,256]{1,0:T(8,128)(2,1)S(1)}, u32[]{:S(2)}, u32[]{:S(2)}) collective-permute-start(bf16[512,256]{1,0:T(8,128)(2,1)S(1)} %collective-permute-done.5.refs_3_), channel_id=1, source_target_pairs={{0,2},{1,3},{2,0},{3,1},{4,6},{5,7},{6,4},{7,5},{8,10},{9,11},{10,... | collective-permute-start | bytes 786440 | tf_op jit(solution)/shard_map/ppermute | solution.py:299
  41.3 9.4 %collective-permute-start.26 = (bf16[512,256]{1,0:T(8,128)(2,1)}, bf16[512,256]{1,0:T(8,128)(2,1)S(1)}, u32[]{:S(2)}, u32[]{:S(2)}) collective-permute-start(bf16[512,256]{1,0:T(8,128)(2,1)} %collective-permute-done.25.refs_8_), channel_id=1, source_target_pairs={{0,4},{8,0},{16,8},{24,16},{28,24},{20,28},{12,20},{4,12},{1,5},{9... | collective-permute-start | bytes 786440 | tf_op jit(solution)/shard_map/ppermute | solution.py:305
  41.8 9.8 %collective-permute-start.3 = (bf16[512,256]{1,0:T(8,128)(2,1)}, bf16[512,256]{1,0:T(8,128)(2,1)S(1)}, u32[]{:S(2)}, u32[]{:S(2)}) collective-permute-start(bf16[512,256]{1,0:T(8,128)(2,1)} %collective-permute-done.2.refs_5_), channel_id=1, source_target_pairs={{0,8},{8,16},{16,24},{24,28},{28,20},{20,12},{12,4},{4,0},{1,9},{9... | collective-permute-start | bytes 786440 | tf_op jit(solution)/shard_map/ppermute | solution.py:305
  45.1 11.2 %collective-permute-start.7 = (bf16[512,256]{1,0:T(8,128)(2,1)S(1)}, bf16[512,256]{1,0:T(8,128)(2,1)S(1)}, u32[]{:S(2)}, u32[]{:S(2)}) collective-permute-start(bf16[512,256]{1,0:T(8,128)(2,1)S(1)} %collective-permute-done.6.refs_7_), channel_id=1, source_target_pairs={{0,4},{8,0},{16,8},{24,16},{28,24},{20,28},{12,20},{4,12},{1,5},{9... | collective-permute-start | bytes 786440 | tf_op jit(solution)/shard_map/ppermute | solution.py:305
  47.2 12.4 %collective-permute-start.30 = (bf16[512,256]{1,0:T(8,128)(2,1)}, bf16[512,256]{1,0:T(8,128)(2,1)}, u32[]{:S(2)}, u32[]{:S(2)}) collective-permute-start(bf16[512,256]{1,0:T(8,128)(2,1)} %collective-permute-done.29.refs_6_), channel_id=1, source_target_pairs={{0,4},{8,0},{16,8},{24,16},{28,24},{20,28},{12,20},{4,12},{1,5},{9... | collective-permute-start | bytes 786440 | tf_op jit(solution)/shard_map/ppermute | solution.py:305
  50.7 11.5 %collective-permute-start.15 = (bf16[512,256]{1,0:T(8,128)(2,1)}, bf16[512,256]{1,0:T(8,128)(2,1)}, u32[]{:S(2)}, u32[]{:S(2)}) collective-permute-start(bf16[512,256]{1,0:T(8,128)(2,1)} %collective-permute-done.2.refs_5_), channel_id=1, source_target_pairs={{0,2},{1,3},{2,0},{3,1},{4,6},{5,7},{6,4},{7,5},{8,10},{9,11},{10,... | collective-permute-start | bytes 786440 | tf_op jit(solution)/shard_map/ppermute | solution.py:299
  51.5 10.1 %collective-permute-start.33 = (bf16[512,256]{1,0:T(8,128)(2,1)}, bf16[512,256]{1,0:T(8,128)(2,1)}, u32[]{:S(2)}, u32[]{:S(2)}) collective-permute-start(bf16[512,256]{1,0:T(8,128)(2,1)} %collective-permute-done.32.refs_7_), channel_id=1, source_target_pairs={{0,8},{8,16},{16,24},{24,28},{28,20},{20,12},{12,4},{4,0},{1,9},{9... | collective-permute-start | bytes 786440 | tf_op jit(solution)/shard_map/ppermute | solution.py:305
  61.6 24.4 %collective-permute-start.16 = (bf16[512,256]{1,0:T(8,128)(2,1)}, bf16[512,256]{1,0:T(8,128)(2,1)S(1)}, u32[]{:S(2)}, u32[]{:S(2)}) collective-permute-start(bf16[512,256]{1,0:T(8,128)(2,1)} %copy-done.11), channel_id=1, source_target_pairs={{0,2},{1,3},{2,0},{3,1},{4,6},{5,7},{6,4},{7,5},{8,10},{9,11},{10,... | collective-permute-start | bytes 786440 | tf_op jit(solution)/shard_map/ppermute | solution.py:299
  62.2 18.9 %collective-permute-start.23 = (bf16[512,256]{1,0:T(8,128)(2,1)}, bf16[512,256]{1,0:T(8,128)(2,1)S(1)}, u32[]{:S(2)}, u32[]{:S(2)}) collective-permute-start(bf16[512,256]{1,0:T(8,128)(2,1)} %copy-done.17), channel_id=1, source_target_pairs={{0,8},{8,16},{16,24},{24,28},{28,20},{20,12},{12,4},{4,0},{1,9},{9... | collective-permute-start | bytes 786440 | tf_op jit(solution)/shard_map/ppermute | solution.py:305
  63.7 17.5 %collective-permute-start.27 = (bf16[512,256]{1,0:T(8,128)(2,1)}, bf16[512,256]{1,0:T(8,128)(2,1)S(1)}, u32[]{:S(2)}, u32[]{:S(2)}) collective-permute-start(bf16[512,256]{1,0:T(8,128)(2,1)} %copy-done.15), channel_id=1, source_target_pairs={{0,4},{8,0},{16,8},{24,16},{28,24},{20,28},{12,20},{4,12},{1,5},{9... | collective-permute-start | bytes 786440 | tf_op jit(solution)/shard_map/ppermute | solution.py:305
  66.3 27.5 %collective-permute-start.4 = (bf16[512,256]{1,0:T(8,128)(2,1)S(1)}, bf16[512,256]{1,0:T(8,128)(2,1)S(1)}, u32[]{:S(2)}, u32[]{:S(2)}) collective-permute-start(bf16[512,256]{1,0:T(8,128)(2,1)S(1)} %collective-permute-done.3.refs_0_), channel_id=1, source_target_pairs={{0,2},{1,3},{2,0},{3,1},{4,6},{5,7},{6,4},{7,5},{8,10},{9,11},{10,... | collective-permute-start | bytes 786440 | tf_op jit(solution)/shard_map/ppermute | solution.py:299
  66.3 27.5 %collective-permute-start.8 = (bf16[512,256]{1,0:T(8,128)(2,1)S(1)}, bf16[512,256]{1,0:T(8,128)(2,1)S(1)}, u32[]{:S(2)}, u32[]{:S(2)}) collective-permute-start(bf16[512,256]{1,0:T(8,128)(2,1)S(1)} %collective-permute-done.7.refs_2_), channel_id=1, source_target_pairs={{0,2},{1,3},{2,0},{3,1},{4,6},{5,7},{6,4},{7,5},{8,10},{9,11},{10,... | collective-permute-start | bytes 786440 | tf_op jit(solution)/shard_map/ppermute | solution.py:299
  81.1 12.6 %collective-permute-start.11 = (bf16[256,256]{1,0:T(8,128)(2,1)S(1)}, bf16[256,256]{1,0:T(8,128)(2,1)S(1)}, u32[]{:S(2)}, u32[]{:S(2)}) collective-permute-start(bf16[256,256]{1,0:T(8,128)(2,1)S(1)} %collective-permute-done.9.refs_4_), channel_id=1, source_target_pairs={{0,2},{1,3},{2,0},{3,1},{4,6},{5,7},{6,4},{7,5},{8,10},{9,11},{10,... | collective-permute-start | bytes 393224 | tf_op jit(solution)/shard_map/ppermute | solution.py:299
  81.2 12.5 %collective-permute-start.12 = (bf16[256,256]{1,0:T(8,128)(2,1)}, bf16[256,256]{1,0:T(8,128)(2,1)S(1)}, u32[]{:S(2)}, u32[]{:S(2)}) collective-permute-start(bf16[256,256]{1,0:T(8,128)(2,1)} %collective-permute-done.10.refs_5_), channel_id=1, source_target_pairs={{0,2},{1,3},{2,0},{3,1},{4,6},{5,7},{6,4},{7,5},{8,10},{9,11},{10,... | collective-permute-start | bytes 393224 | tf_op jit(solution)/shard_map/ppermute | solution.py:299
  86.0 14.1 %collective-permute-start.35 = (bf16[512,256]{1,0:T(8,128)(2,1)S(1)}, bf16[512,256]{1,0:T(8,128)(2,1)}, u32[]{:S(2)}, u32[]{:S(2)}) collective-permute-start(bf16[512,256]{1,0:T(8,128)(2,1)S(1)} %shard_map.77.refs_3_), channel_id=1, source_target_pairs={{0,2},{1,3},{4,6},{5,7},{8,10},{9,11},{12,14},{13,15},{16,18},{17,... | collective-permute-start | bytes 786440 | tf_op jit(solution)/shard_map/ppermute | solution.py:302
  99.5 21.0 %collective-permute-start.34 = (bf16[512,256]{1,0:T(8,128)(2,1)S(1)}, bf16[512,256]{1,0:T(8,128)(2,1)S(1)}, u32[]{:S(2)}, u32[]{:S(2)}) collective-permute-start(bf16[512,256]{1,0:T(8,128)(2,1)S(1)} %shard_map.77.refs_3_), channel_id=1, source_target_pairs={{0,1},{1,0},{2,3},{3,2},{4,5},{5,4},{6,7},{7,6},{8,9},{9,8},{10,11... | collective-permute-start | bytes 786440 | tf_op jit(solution)/shard_map/ppermute | solution.py:296
  99.6 20.9 %collective-permute-start.17 = (bf16[512,256]{1,0:T(8,128)(2,1)S(1)}, bf16[512,256]{1,0:T(8,128)(2,1)S(1)}, u32[]{:S(2)}, u32[]{:S(2)}) collective-permute-start(bf16[512,256]{1,0:T(8,128)(2,1)S(1)} %shard_map.74.refs_1_), channel_id=1, source_target_pairs={{0,1},{1,0},{2,3},{3,2},{4,5},{5,4},{6,7},{7,6},{8,9},{9,8},{10,11... | collective-permute-start | bytes 786440 | tf_op jit(solution)/shard_map/ppermute | solution.py:296
  100.1 20.4 %collective-permute-start.36 = (bf16[512,256]{1,0:T(8,128)(2,1)}, bf16[512,256]{1,0:T(8,128)(2,1)}, u32[]{:S(2)}, u32[]{:S(2)}) collective-permute-start(bf16[512,256]{1,0:T(8,128)(2,1)} %collective-permute-done.35.refs_4_), channel_id=1, source_target_pairs={{0,1},{1,0},{2,3},{3,2},{4,5},{5,4},{6,7},{7,6},{8,9},{9,8},{10,11... | collective-permute-start | bytes 786440 | tf_op jit(solution)/shard_map/ppermute | solution.py:296
  107.2 13.4 %collective-permute-start.19 = (bf16[512,256]{1,0:T(8,128)(2,1)S(1)}, bf16[512,256]{1,0:T(8,128)(2,1)}, u32[]{:S(2)}, u32[]{:S(2)}) collective-permute-start(bf16[512,256]{1,0:T(8,128)(2,1)S(1)} %collective-permute-done.18.refs_2_), channel_id=1, source_target_pairs={{0,1},{1,0},{2,3},{3,2},{4,5},{5,4},{6,7},{7,6},{8,9},{9,8},{10,11... | collective-permute-start | bytes 786440 | tf_op jit(solution)/shard_map/ppermute | solution.py:296
  (30 other events, 293.9 us)

commit v3 on v2

--- a/solution.py
+++ b/solution.py
@@ -14,7 +14,9 @@
 BLK = 128
 MASKED = -1e30
 CORES = 2
+CHUNK = 2 * BLK
 SPARE_VMEM = 4 << 20
+MOST_VMEM = 67043328
 
 rope_base = 1000000.0
 
@@ -108,8 +110,7 @@
     added = before is not None
     if added:
         extras = [before, *extras]
-    grant = len(plan) * strip * (chip_rows + width) * 2
-    grant += chip_rows * width * (4 + 8 * len(extras) + 8) + SPARE_VMEM
+    grant = MOST_VMEM - (3 << 19) * (finish == "value" or (added and finish == "sum"))
     return pl.pallas_call(
         functools.partial(project_kernel, plan, finish, added),
         out_shape=out,
@@ -136,138 +137,247 @@
     )(columns, own_tokens, sibling_tokens, *pieces, *extras)
 
 
-def attention_kernel(hops, row_blocks, group, facts, *refs):
-    q_ref = refs[0]
-    k_refs = refs[1 : 1 + hops]
-    v_refs = refs[1 + hops : 1 + 2 * hops]
-    out_ref, score_ref, peak_ref, total_ref, acc_ref = refs[-5:]
-    chip_blocks = CORES * row_blocks
-    row_block = pl.program_id(1)
-    source_core, ctx_index = facts[1], facts[2]
-    chip = ctx_index // CORES
-    here = ctx_index * row_blocks + row_block
-    segment = facts[3 + here]
+class Blocks:
+    def __init__(self, facts, hops, row_blocks, row_block):
+        self.row_blocks, self.source_core = row_blocks, facts[1]
+        per_chip = CORES * row_blocks
+        chip = facts[2] // CORES
+        here = facts[2] * row_blocks + row_block
+        segment = facts[3 + here]
+        self.diagonal = lax.rem(here, per_chip)
+        self.entries, slot = [], jnp.int32(0)
+        for hop in range(hops):
+            for local in range(per_chip):
+                block = (chip - hop) * per_chip + local
+                seen = facts[3 + jnp.maximum(block, 0)]
+                allowed = (block >= 0) & (block < here) & ((seen == 0) | (seen == segment))
+                self.entries.append((hop, local, allowed, slot))
+                slot = slot + jnp.where(allowed, 1, 0)
+        self.odd = lax.rem(slot, 2) == 1
+        self.free_slot = slot
+        self.chunks = (slot + 2) // 2
+
+    def place(self, local):
+        core = local // self.row_blocks
+        slot = jnp.where(core == self.source_core, 0, self.row_blocks)
+        slot = slot + lax.rem(local, self.row_blocks)
+        return pl.ds(pl.multiple_of(slot * BLK, BLK), BLK)
+
+    def gather(self, refs, chosen_ref):
+        def slot_rows(slot):
+            return pl.ds(pl.multiple_of(slot * BLK, BLK), BLK)
+
+        for hop, local, allowed, slot in self.entries:
+
+            @pl.when(allowed)
+            def _(hop=hop, local=local, slot=slot):
+                chosen_ref[slot_rows(slot), :] = refs[hop][self.place(jnp.int32(local)), :]
+
+        @pl.when(jnp.logical_not(self.odd))
+        def _():
+            chosen_ref[slot_rows(self.free_slot), :] = jnp.zeros((BLK, HEAD_SIZE), jnp.bfloat16)
+
+        chosen_ref[slot_rows(2 * self.chunks - 1), :] = refs[0][self.place(self.diagonal), :]
+
+
+def chunk_rows(chunk):
+    return pl.ds(pl.multiple_of(chunk * CHUNK, CHUNK), CHUNK)
+
+
+def score_kernel(hops, row_blocks, group, facts, q_ref, *refs):
+    k_refs = refs[:hops]
+    probs_ref, inverse_ref, chosen_ref, score_ref, peak_ref, total_ref = refs[hops:]
+    blocks = Blocks(facts, hops, row_blocks, pl.program_id(1))
+    blocks.gather(k_refs, chosen_ref)
     factor = math.log2(math.e) / math.sqrt(HEAD_SIZE)
     rows = group * BLK
 
-    def place(local):
-        core = local // row_blocks
-        slot = jnp.where(core == source_core, 0, row_blocks) + local % row_blocks
-        return pl.ds(pl.multiple_of(slot * BLK, BLK), BLK)
-
-    def queries():
-        return jnp.concatenate(
-            [q_ref[:, h * HEAD_SIZE : (h + 1) * HEAD_SIZE] for h in range(group)], axis=0
-        )
-
-    def scores(k_ref, local):
+    def scores(chunk):
+        heads = [q_ref[:, h * HEAD_SIZE : (h + 1) * HEAD_SIZE] for h in range(group)]
         return lax.dot_general(
-            queries(),
-            k_ref[place(local), :],
+            jnp.concatenate(heads, axis=0),
+            chosen_ref[chunk_rows(chunk), :],
             (((1,), (1,)), ((), ())),
             preferred_element_type=jnp.float32,
         )
 
-    def over_blocks(visit):
-        for hop in range(hops):
-
-            @pl.loop(0, chip_blocks)
-            def _(local):
-                block = (chip - hop) * chip_blocks + local
-                seen = facts[3 + jnp.maximum(block, 0)]
-
-                @pl.when(
-                    (block >= 0) & (block < here) & ((seen == 0) | (seen == segment))
-                )
-                def _():
-                    visit(hop, local)
-
-    diagonal = lax.rem(here, chip_blocks)
-    later = lax.broadcasted_iota(jnp.int32, (rows, BLK), 1) > (
-        lax.broadcasted_iota(jnp.int32, (rows, BLK), 0) % BLK
-    )
-    own = jnp.where(later, MASKED, scores(k_refs[0], diagonal))
-    score_ref[diagonal] = own
-    peak_ref[...] = own
-
-    def first(hop, local):
-        found = scores(k_refs[hop], local)
-        score_ref[hop * chip_blocks + local] = found
-        peak_ref[...] = jnp.maximum(peak_ref[...], found)
-
-    over_blocks(first)
-    peak = jnp.max(peak_ref[...], axis=1, keepdims=True)
-    peak_ref[...] = jnp.broadcast_to(peak, (rows, BLK))
-
-    def weigh(hop, local):
-        probs = jnp.exp2((score_ref[hop * chip_blocks + local] - peak_ref[...]) * factor)
-        return probs, jnp.dot(
-            probs.astype(jnp.bfloat16),
-            v_refs[hop][place(local), :],
+    last = blocks.chunks - 1
+    column = lax.broadcasted_iota(jnp.int32, (rows, CHUNK), 1)
+    row = lax.broadcasted_iota(jnp.int32, (rows, CHUNK), 0) % BLK
+    first_column = jnp.where(blocks.odd, 0, BLK)
+    found = jnp.where(
+        (column >= first_column) & (column - BLK <= row), scores(last), MASKED
+    )
+    score_ref[last] = found
+    peak_ref[...] = jnp.maximum(found[:, :BLK], found[:, BLK:])
+
+    @pl.loop(0, last)
+    def _(chunk):
+        found = scores(chunk)
+        score_ref[chunk] = found
+        peak_ref[...] = jnp.maximum(
+            peak_ref[...], jnp.maximum(found[:, :BLK], found[:, BLK:])
+        )
+
+    peak_ref[...] = jnp.broadcast_to(
+        jnp.max(peak_ref[...], axis=1, keepdims=True), (rows, BLK)
+    )
+    total_ref[...] = jnp.zeros_like(total_ref)
+
+    @pl.loop(0, blocks.chunks)
+    def _(chunk):
+        peak = peak_ref[...]
+        total = total_ref[...]
+        for first in range(0, CHUNK, BLK):
+            lanes = slice(first, first + BLK)
+            probs = jnp.exp2((score_ref[chunk, :, lanes] - peak) * factor)
+            probs_ref[0, chunk, :, lanes] = probs.astype(probs_ref.dtype)
+            total = total + probs
+        total_ref[...] = total
+
+    inverse_ref[0] = jnp.broadcast_to(
+        1.0 / jnp.sum(total_ref[...], axis=1, keepdims=True), (rows, BLK)
+    )
+
+
+def mix_kernel(hops, row_blocks, group, facts, probs_ref, inverse_ref, *refs):
+    v_refs = refs[:hops]
+    out_ref, chosen_ref, held_ref, acc_ref, sems = refs[-5:]
+    head, row_block = pl.program_id(0), pl.program_id(1)
+    step = head * row_blocks + row_block
+    steps = pl.num_programs(0) * row_blocks
+    blocks = Blocks(facts, hops, row_blocks, row_block)
+
+    def fetch(at, chunk):
+        side = lax.rem(at, 2)
+        return pltpu.make_async_copy(
+            probs_ref.at[at, chunk], held_ref.at[side, chunk], sems.at[side, chunk]
+        )
+
+    @pl.when(step == 0)
+    def _():
+        @pl.loop(0, blocks.chunks)
+        def _(chunk):
+            fetch(step, chunk).start()
+
+    @pl.when(step + 1 < steps)
+    def _():
+        coming = Blocks(facts, hops, row_blocks, lax.rem(row_block + 1, row_blocks))
+
+        @pl.loop(0, coming.chunks)
+        def _(chunk):
+            fetch(step + 1, chunk).start()
+
+    blocks.gather(v_refs, chosen_ref)
+    acc_ref[...] = jnp.zeros_like(acc_ref)
+
+    @pl.loop(0, blocks.chunks)
+    def _(chunk):
+        fetch(step, chunk).wait()
+        acc_ref[...] += jnp.dot(
+            held_ref[lax.rem(step, 2), chunk],
+            chosen_ref[chunk_rows(chunk), :],
             preferred_element_type=jnp.float32,
         )
 
-    total_ref[...], acc_ref[...] = weigh(0, diagonal)
-
-    def second(hop, local):
-        probs, mixed = weigh(hop, local)
-        total_ref[...] += probs
-        acc_ref[...] += mixed
-
-    over_blocks(second)
-    total = jnp.sum(total_ref[...], axis=1, keepdims=True)
-    mixed = (acc_ref[...] / total).astype(out_ref.dtype)
+    mixed = (acc_ref[...] * inverse_ref[0]).astype(out_ref.dtype)
     for h in range(group):
         out_ref[:, h * HEAD_SIZE : (h + 1) * HEAD_SIZE] = mixed[h * BLK : (h + 1) * BLK]
 
 
-def attend(facts, queries, keys, values, before):
-    hops = len(keys)
-    number_of_rows, query_width = queries.shape
-    group = query_width // HEAD_SIZE // KEY_VALUE_HEADS
-    heads = KEY_VALUE_HEADS // CORES
-    row_blocks = number_of_rows // BLK
-    width = group * HEAD_SIZE
-    rows = group * BLK
-    q_spec = pl.BlockSpec((BLK, width), lambda l, r, f: (r, f[0] * heads + l))
-    kv_spec = pl.BlockSpec((keys[0].shape[0], HEAD_SIZE), lambda l, r, f: (0, l))
-    operands = [facts, queries, *keys, *values]
-    in_specs = [q_spec] + [kv_spec] * (2 * hops)
-    aliases = {}
-    if before is not None:
-        aliases = {len(operands): 0}
-        operands.append(before)
-        in_specs.append(pl.BlockSpec(memory_space=pl.ANY))
-    total_blocks = hops * CORES * row_blocks
-    pairs = heads * row_blocks * rows * total_blocks * BLK // 2
-    return pl.pallas_call(
-        functools.partial(attention_kernel, hops, row_blocks, group),
-        out_shape=jax.ShapeDtypeStruct(queries.shape, queries.dtype),
-        grid_spec=pltpu.PrefetchScalarGridSpec(
-            num_scalar_prefetch=1,
-            grid=(heads, row_blocks),
-            in_specs=in_specs,
-            out_specs=q_spec,
-            scratch_shapes=[
-                pltpu.VMEM((total_blocks, rows, BLK), jnp.float32),
-                pltpu.VMEM((rows, BLK), jnp.float32),
-                pltpu.VMEM((rows, BLK), jnp.float32),
-                pltpu.VMEM((rows, HEAD_SIZE), jnp.float32),
-            ],
-        ),
-        input_output_aliases=aliases,
-        compiler_params=pltpu.CompilerParams(
-            vmem_limit_bytes=rows * BLK * 4 * (total_blocks + 6)
-            + (BLK * width + hops * keys[0].size) * 8
-            + SPARE_VMEM
-        ),
-        cost_estimate=pl.CostEstimate(
-            flops=4 * pairs * HEAD_SIZE,
-            bytes_accessed=2 * number_of_rows * query_width * 2,
-            transcendentals=pairs,
-        ),
-        name="attend",
-    )(*operands)
+class Attention:
+    def __init__(self, facts, queries, hops):
+        self.facts, self.queries, self.hops = facts, queries, hops
+        self.rows, query_width = queries.shape
+        self.group = query_width // HEAD_SIZE // KEY_VALUE_HEADS
+        self.heads = KEY_VALUE_HEADS // CORES
+        self.row_blocks = self.rows // BLK
+        self.stacked = self.group * BLK
+        self.chunks = hops * CORES * self.row_blocks * BLK // CHUNK
+        self.q_spec = pl.BlockSpec(
+            (BLK, self.group * HEAD_SIZE), lambda l, r, f: (r, f[0] * self.heads + l)
+        )
+        self.kv_spec = pl.BlockSpec((CORES * self.rows, HEAD_SIZE), lambda l, r, f: (0, l))
+        self.inverse_spec = pl.BlockSpec(
+            (1, self.stacked, BLK), lambda l, r, f: (l * self.row_blocks + r, 0, 0)
+        )
+        self.pairs = self.heads * self.row_blocks * self.stacked * self.chunks * CHUNK // 2
+        self.block_bytes = self.stacked * BLK * 4
+
+    def scores(self, keys):
+        count = self.heads * self.row_blocks
+        probs = jax.ShapeDtypeStruct(
+            (count, self.chunks, self.stacked, CHUNK), jnp.bfloat16
+        )
+        return pl.pallas_call(
+            functools.partial(score_kernel, self.hops, self.row_blocks, self.group),
+            out_shape=(
+                probs,
+                jax.ShapeDtypeStruct((count, self.stacked, BLK), jnp.float32),
+            ),
+            grid_spec=pltpu.PrefetchScalarGridSpec(
+                num_scalar_prefetch=1,
+                grid=(self.heads, self.row_blocks),
+                in_specs=[self.q_spec] + [self.kv_spec] * self.hops,
+                out_specs=(
+                    pl.BlockSpec(
+                        (1, *probs.shape[1:]), lambda l, r, f: (l * self.row_blocks + r, 0, 0, 0)
+                    ),
+                    self.inverse_spec,
+                ),
+                scratch_shapes=[
+                    pltpu.VMEM((self.chunks * CHUNK, HEAD_SIZE), jnp.bfloat16),
+                    pltpu.VMEM((self.chunks, self.stacked, CHUNK), jnp.float32),
+                    pltpu.VMEM((self.stacked, BLK), jnp.float32),
+                    pltpu.VMEM((self.stacked, BLK), jnp.float32),
+                ],
+            ),
+            compiler_params=pltpu.CompilerParams(
+                vmem_limit_bytes=self.block_bytes * (4 * self.chunks + 8) + SPARE_VMEM
+            ),
+            cost_estimate=pl.CostEstimate(
+                flops=2 * self.pairs * HEAD_SIZE,
+                bytes_accessed=self.queries.size + self.pairs * 4,
+                transcendentals=self.pairs,
+            ),
+            name="score",
+        )(self.facts, self.queries, *keys)
+
+    def mix(self, probs, inverse, values, before):
+        operands = [self.facts, probs, inverse, *values]
+        in_specs = [pl.BlockSpec(memory_space=pl.ANY), self.inverse_spec]
+        in_specs += [self.kv_spec] * self.hops
+        aliases = {}
+        if before is not None:
+            aliases = {len(operands): 0}
+            operands.append(before)
+            in_specs.append(pl.BlockSpec(memory_space=pl.ANY))
+        return pl.pallas_call(
+            functools.partial(mix_kernel, self.hops, self.row_blocks, self.group),
+            out_shape=jax.ShapeDtypeStruct(self.queries.shape, self.queries.dtype),
+            grid_spec=pltpu.PrefetchScalarGridSpec(
+                num_scalar_prefetch=1,
+                grid=(self.heads, self.row_blocks),
+                in_specs=in_specs,
+                out_specs=self.q_spec,
+                scratch_shapes=[
+                    pltpu.VMEM((self.chunks * CHUNK, HEAD_SIZE), jnp.bfloat16),
+                    pltpu.VMEM((2, *probs.shape[1:]), jnp.bfloat16),
+                    pltpu.VMEM((self.stacked, HEAD_SIZE), jnp.float32),
+                    pltpu.SemaphoreType.DMA((2, self.chunks)),
+                ],
+            ),
+            input_output_aliases=aliases,
+            compiler_params=pltpu.CompilerParams(
+                vmem_limit_bytes=self.block_bytes * (2 * self.chunks + 8) + SPARE_VMEM
+            ),
+            cost_estimate=pl.CostEstimate(
+                flops=2 * self.pairs * HEAD_SIZE,
+                bytes_accessed=self.queries.size + self.pairs * 4,
+                transcendentals=0,
+            ),
+            name="mix",
+        )(*operands)
 
 
 def layer(
@@ -415,18 +525,21 @@
     value_rows = projected("value", value_strips[-1], value_sum, [value_bias[None]])
 
     keys, values = [key_rows], [value_rows]
-    for _ in range(chips - 1):
+    for _ in range(1, chips):
         keys.append(to_next_chip(keys[-1]))
         values.append(to_next_chip(values[-1]))
     sibling_keys = [to_sibling(x) for x in keys]
     sibling_values = [to_sibling(x) for x in values]
 
-    def facts(half):
-        return jnp.concatenate([jnp.stack([half, half, my_index]), block_segments[0]])
-
-    own_queries = queries[0]
-    attended = attend(facts(core), own_queries, keys, values, None)
-    attended = attend(facts(1 - core), own_queries, sibling_keys, sibling_values, attended)
+    def attention(half):
+        facts = jnp.concatenate([jnp.stack([half, half, my_index]), block_segments[0]])
+        return Attention(facts, queries[0], chips)
+
+    near, far = attention(core), attention(1 - core)
+    near_weights = near.scores(keys)
+    far_weights = far.scores(sibling_keys)
+    attended = near.mix(*near_weights, values, None)
+    attended = far.mix(*far_weights, sibling_values, attended)
     return attended[None]
 
 

time: 134 us -> 145 us (1.082)
  the two profiles are of different devices: /device:TPU:12 before, /device:TPU:5 now
where the time goes in v3:
time: 145 us; the launch traced here: 144 us
  Pallas kernels  56.2 us (39%)
  starting transfers between devices  41.2 us (28%)
  waiting for transfers between devices  32.4 us (22%)
  local copies, waits for them, and re-layouts  9.71 us (7%)
  other arithmetic  3.98 us (3%)
    pallas_call x5, Pallas kernels, project(): pl.pallas_call(functools.partial(project_kernel, plan, finish, added), ou...  26.4 us
    ppermute x22, waiting for transfers between devices, along_ring(): lax.ppermute(x, 'dp', [(ring[i], ring[(i + step) % dp_size]) for i in ran...  22.5 us
    ppermute x22, starting transfers between devices, along_ring(): lax.ppermute(x, 'dp', [(ring[i], ring[(i + step) % dp_size]) for i in ran...  18.1 us
    pallas_call x2, Pallas kernels, scores(): pl.pallas_call(functools.partial(score_kernel, self.hops, self.row_blocks...  17.4 us
    ppermute x5, starting transfers between devices, to_sibling(): return lax.ppermute(x, 'ctx', [(i, i ^ 1) for i in range(ctx_size)])  14.7 us
    pallas_call x2, Pallas kernels, mix(): pl.pallas_call(functools.partial(mix_kernel, self.hops, self.row_blocks,...  12.5 us
    ppermute x8, waiting for transfers between devices, to_plane(): return lax.ppermute(x, 'ctx', [(i, i ^ CORES) for i in range(ctx_size)])  9.91 us
    ppermute x8, starting transfers between devices, to_plane(): return lax.ppermute(x, 'ctx', [(i, i ^ CORES) for i in range(ctx_size)])  5.49 us
  transfers between devices with their start and end apart: 37, of which 11 were waited for; matrix products, arithmetic and copies ran while one was open for 8% of the time, Pallas kernels for 35%

profile of v3, /device:TPU:5, one launch (start us, length us, event | category | flops | bytes accessed | tf_op | source)
XLA Modules:
  0.0 144.1 jit_solution(16723674876842168731)
XLA Ops:
  1.8 1.3 collective-permute-start.1
  4.4 1.3 collective-permute-start.20
  5.9 3.8 %collective-permute-done.1.refs_1_ = bf16[512,256]{1,0:T(8,128)(2,1)S(1)} collective-permute-done((bf16[512,256]{1,0:T(8,128)(2,1)S(1)}, bf16[512,256]{1,0:T(8,128)(2,1)S(1)}, u32[]{:S(2)}, u32[]{:S(2)}) %collective-permute-start.1) | collective-permute-done | bytes 262176 | tf_op jit(solution)/shard_map/ppermute | solution.py:415
  12.0 3.2 %collective-permute-done.20.refs_1_ = bf16[512,256]{1,0:T(8,128)(2,1)S(1)} collective-permute-done((bf16[512,256]{1,0:T(8,128)(2,1)S(1)}, bf16[512,256]{1,0:T(8,128)(2,1)S(1)}, u32[]{:S(2)}, u32[]{:S(2)}) %collective-permute-start.20) | collective-permute-done | bytes 262176 | tf_op jit(solution)/shard_map/ppermute | solution.py:415
  15.2 1.3 collective-permute-start.2
  16.7 5.2 %collective-permute-done.28.refs_2_ = bf16[512,256]{1,0:T(8,128)(2,1)S(1)} collective-permute-done((bf16[512,256]{1,0:T(8,128)(2,1)S(1)}, bf16[512,256]{1,0:T(8,128)(2,1)S(1)}, u32[]{:S(2)}, u32[]{:S(2)}) %collective-permute-start.28) | collective-permute-done | bytes 262176 | tf_op jit(solution)/shard_map/ppermute | solution.py:415
  23.3 3.2 %collective-permute-done.2.refs_5_ = bf16[512,256]{1,0:T(8,128)(2,1)} collective-permute-done((bf16[512,256]{1,0:T(8,128)(2,1)S(1)}, bf16[512,256]{1,0:T(8,128)(2,1)}, u32[]{:S(2)}, u32[]{:S(2)}) %collective-permute-start.2) | collective-permute-done | bytes 262176 | tf_op jit(solution)/shard_map/ppermute | solution.py:415
  26.5 1.3 collective-permute-start.21
  29.3 4.0 %collective-permute-done.14.refs_4_ = bf16[512,256]{1,0:T(8,128)(2,1)} collective-permute-done((bf16[512,256]{1,0:T(8,128)(2,1)}, bf16[512,256]{1,0:T(8,128)(2,1)}, u32[]{:S(2)}, u32[]{:S(2)}) %collective-permute-start.14) | collective-permute-done | bytes 262176 | tf_op jit(solution)/shard_map/ppermute | solution.py:409
  33.3 1.3 collective-permute-start.32
  34.6 1.3 collective-permute-start.3
  37.1 2.9 %collective-permute-done.29.refs_6_ = bf16[512,256]{1,0:T(8,128)(2,1)S(1)} collective-permute-done((bf16[512,256]{1,0:T(8,128)(2,1)S(1)}, bf16[512,256]{1,0:T(8,128)(2,1)S(1)}, u32[]{:S(2)}, u32[]{:S(2)}) %collective-permute-start.29) | collective-permute-done | bytes 262176 | tf_op jit(solution)/shard_map/ppermute | solution.py:415
  41.5 2.3 %collective-permute-done.3.refs_0_ = bf16[512,256]{1,0:T(8,128)(2,1)S(1)} collective-permute-done((bf16[512,256]{1,0:T(8,128)(2,1)}, bf16[512,256]{1,0:T(8,128)(2,1)S(1)}, u32[]{:S(2)}, u32[]{:S(2)}) %collective-permute-start.3) | collective-permute-done | bytes 262176 | tf_op jit(solution)/shard_map/ppermute | solution.py:415
  43.8 1.3 collective-permute-start.22
  48.8 1.3 collective-permute-start.9
  53.0 1.5 %collective-permute-done.9.refs_4_ = bf16[256,256]{1,0:T(8,128)(2,1)S(1)} collective-permute-done((bf16[256,256]{1,0:T(8,128)(2,1)S(1)}, bf16[256,256]{1,0:T(8,128)(2,1)S(1)}, u32[]{:S(2)}, u32[]{:S(2)}) %collective-permute-start.9) | collective-permute-done | bytes 131104 | tf_op jit(solution)/shard_map/ppermute | solution.py:415
  60.1 3.0 %collective-permute-done.11.refs_6_ = bf16[256,256]{1,0:T(8,128)(2,1)S(1)} collective-permute-done((bf16[256,256]{1,0:T(8,128)(2,1)S(1)}, bf16[256,256]{1,0:T(8,128)(2,1)S(1)}, u32[]{:S(2)}, u32[]{:S(2)}) %collective-permute-start.11) | collective-permute-done | bytes 131104 | tf_op jit(solution)/shard_map/ppermute | solution.py:409
  63.1 2.9 %collective-permute-done.12.refs_7_ = bf16[256,256]{1,0:T(8,128)(2,1)S(1)} collective-permute-done((bf16[256,256]{1,0:T(8,128)(2,1)S(1)}, bf16[256,256]{1,0:T(8,128)(2,1)S(1)}, u32[]{:S(2)}, u32[]{:S(2)}) %collective-permute-start.12) | collective-permute-done | bytes 131104 | tf_op jit(solution)/shard_map/ppermute | solution.py:409
  67.2 1.3 collective-permute-start.23
  68.8 5.6 %shard_map.73.refs_8_ = f32[512,256]{1,0:T(8,128)} custom-call(s32[10]{0:T(128)} %stack.138.columns, bf16[256,8192]{1,0:T(8,128)(2,1)} %bitcast.42, bf16[256,8192]{1,0:T(8,128)(2,1)} %collective-permute-done.sibling_ref, bf16[1024,256]{1,0:T(8,128)(2,1)} %constant_dynamic-slice_fusion.2.refs_0_, bf16[512,256]{1,0:T(8,128)(2,1)} %copy-done.10, ...), custom_call_target="tpu_custom_call" | custom-call | flops 1342177280 | bytes 7864320 | tf_op jit(solution)/shard_map/pallas_call | solution.py:114
  74.4 5.8 %shard_map.74.refs_0_ = bf16[512,256]{1,0:T(8,128)(2,1)} custom-call(s32[6]{0:T(128)} %stack.127.columns, bf16[256,8192]{1,0:T(8,128)(2,1)} %bitcast.43, bf16[256,8192]{1,0:T(8,128)(2,1)} %collective-permute-done.sibling_ref, bf16[512,256]{1,0:T(8,128)(2,1)} %copy-done.4, bf16[512,256]{1,0:T(8,128)(2,1)} %copy-done.13, ...), custom_call_target="tpu_custom_call" | custom-call | flops 805306368 | bytes 4718592 | tf_op jit(solution)/shard_map/pallas_call | solution.py:114
  81.5 5.6 %shard_map.75.refs_4_ = f32[512,256]{1,0:T(8,128)} custom-call(s32[10]{0:T(128)} %stack.155.columns, bf16[256,8192]{1,0:T(8,128)(2,1)} %bitcast.44, bf16[256,8192]{1,0:T(8,128)(2,1)} %collective-permute-done.sibling_ref, bf16[1024,256]{1,0:T(8,128)(2,1)} %constant_dynamic-slice_fusion.1.refs_0_, bf16[512,256]{1,0:T(8,128)(2,1)} %copy-done.6, ...), custom_call_target="tpu_custom_call" | custom-call | flops 1342177280 | bytes 7864320 | tf_op jit(solution)/shard_map/pallas_call | solution.py:114
  87.1 5.0 %shard_map.76.refs_2_ = f32[512,256]{1,0:T(8,128)} custom-call(s32[4]{0:T(128)} %pad_add_fusion.1.columns, bf16[256,8192]{1,0:T(8,128)(2,1)} %bitcast.45, bf16[256,8192]{1,0:T(8,128)(2,1)} %collective-permute-done.sibling_ref, bf16[512,256]{1,0:T(8,128)(2,1)} %collective-permute-done.22.refs_0_, bf16[512,256]{1,0:T(8,128)(2,1)} %collective-permute-done.30.refs_1_, ...), custom_call_target="tpu_custom_call" | custom-call | flops 536870912 | bytes 3145728 | tf_op jit(solution)/shard_map/pallas_call | solution.py:114
  92.2 4.5 %shard_map.77.refs_0_ = bf16[512,256]{1,0:T(8,128)(2,1)} custom-call(s32[2]{0:T(128)} %pad_add_fusion.columns, bf16[256,8192]{1,0:T(8,128)(2,1)} %bitcast.46, bf16[256,8192]{1,0:T(8,128)(2,1)} %collective-permute-done.sibling_ref, bf16[512,256]{1,0:T(8,128)(2,1)} %collective-permute-done.23.refs_0_, bf16[512,256]{1,0:T(8,128)(2,1)} %collective-permute-done.27.refs_1_, ...), custom_call_target="tpu_custom_call" | custom-call | flops 268435456 | bytes 1572864 | tf_op jit(solution)/shard_map/pallas_call | solution.py:114
  96.6 1.6 %collective-permute-start.35 = (bf16[512,256]{1,0:T(8,128)(2,1)}, bf16[512,256]{1,0:T(8,128)(2,1)S(1)}, u32[]{:S(2)}, u32[]{:S(2)}) collective-permute-start(bf16[512,256]{1,0:T(8,128)(2,1)} %shard_map.77.refs_0_), channel_id=1, source_target_pairs={{0,2},{1,3},{4,6},{5,7},{8,10},{9,11},{12,14},{13,15},{16,18},{17,... | collective-permute-start | bytes 786440 | tf_op jit(solution)/shard_map/ppermute | solution.py:412
  98.3 6.4 %collective-permute-start.17 = (bf16[512,256]{1,0:T(8,128)(2,1)S(1)}, bf16[512,256]{1,0:T(8,128)(2,1)S(1)}, u32[]{:S(2)}, u32[]{:S(2)}) collective-permute-start(bf16[512,256]{1,0:T(8,128)(2,1)S(1)} %copy-done.1), channel_id=1, source_target_pairs={{0,1},{1,0},{2,3},{3,2},{4,5},{5,4},{6,7},{7,6},{8,9},{9,8},{10,11... | collective-permute-start | bytes 786440 | tf_op jit(solution)/shard_map/ppermute | solution.py:406
  105.2 7.1 %collective-permute-start.36 = (bf16[512,256]{1,0:T(8,128)(2,1)S(1)}, bf16[512,256]{1,0:T(8,128)(2,1)S(1)}, u32[]{:S(2)}, u32[]{:S(2)}) collective-permute-start(bf16[512,256]{1,0:T(8,128)(2,1)S(1)} %collective-permute-done.35.refs_1_), channel_id=1, source_target_pairs={{0,1},{1,0},{2,3},{3,2},{4,5},{5,4},{6,7},{7,6},{8,9},{9,8},{10,11... | collective-permute-start | bytes 786440 | tf_op jit(solution)/shard_map/ppermute | solution.py:406
  112.4 1.6 %copy-done.2 = bf16[1,256,4096]{2,1,0:T(8,128)(2,1)S(1)} copy-done((bf16[1,256,4096]{2,1,0:T(8,128)(2,1)S(1)}, bf16[1,256,4096]{2,1,0:T(8,128)(2,1)}, u32[]{:S(2)}) %copy-start.2) | copy-done | bytes 2097176
  114.0 9.1 %score.3 = (bf16[4,4,1024,256]{3,2,1,0:T(8,128)(2,1)S(1)}, f32[4,1024,128]{2,1,0:T(8,128)S(1)}) custom-call(s32[11]{0:T(128)S(1)} %get-tuple-element.18.facts, bf16[256,4096]{1,0:T(8,128)(2,1)S(1)} %bitcast.39, bf16[512,256]{1,0:T(8,128)(2,1)S(1)} %copy-done.1, bf16[512,256]{1,0:T(8,128)(2,1)} %collective-permute-done.18.refs_1_), custom_call_target="tpu_custom_call" | custom-call | flops 536870912 | bytes 9437184 | tf_op jit(solution)/shard_map/score/pallas_call | solution.py:312
  123.1 6.2 %mix.2.refs_2_ = bf16[256,4096]{1,0:T(8,128)(2,1)} custom-call(s32[11]{0:T(128)S(1)} %get-tuple-element.18.facts, bf16[4,4,1024,256]{3,2,1,0:T(8,128)(2,1)S(1)} %get-tuple-element.11.probs_ref, f32[4,1024,128]{2,1,0:T(8,128)S(1)} %get-tuple-element.12.inverse_ref, bf16[512,256]{1,0:T(8,128)(2,1)S(1)} %copy-done, ...), custom_call_target="tpu_custom_call" | custom-call | flops 536870912 | bytes 9437184 | tf_op jit(solution)/shard_map/mix/pallas_call | solution.py:355
  129.3 8.3 %score.2 = (bf16[4,4,1024,256]{3,2,1,0:T(8,128)(2,1)S(1)}, f32[4,1024,128]{2,1,0:T(8,128)S(1)}) custom-call(s32[11]{0:T(128)S(1)} %get-tuple-element.19.facts, bf16[256,4096]{1,0:T(8,128)(2,1)S(1)} %bitcast.40, bf16[512,256]{1,0:T(8,128)(2,1)S(1)} %collective-permute-done.17.refs_0_, bf16[512,256]{1,0:T(8,128)(2,1)S(1)} %collective-permute-done.19.refs_1_), custom_call_target="tpu_custom_call" | custom-call | flops 536870912 | bytes 9437184 | tf_op jit(solution)/shard_map/score/pallas_call | solution.py:312
  137.7 6.3 %mix.3 = bf16[256,4096]{1,0:T(8,128)(2,1)} custom-call(s32[11]{0:T(128)S(1)} %get-tuple-element.19.facts, bf16[4,4,1024,256]{3,2,1,0:T(8,128)(2,1)S(1)} %get-tuple-element.9.probs_ref, f32[4,1024,128]{2,1,0:T(8,128)S(1)} %get-tuple-element.10.inverse_ref, bf16[512,256]{1,0:T(8,128)(2,1)S(1)} %collective-permute-done.34.refs_0_, ...), custom_call_target="tpu_custom_call", output_to_operand_aliasing={{}: (5, {})} | custom-call | flops 536870912 | bytes 9437184 | tf_op jit(solution)/shard_map/mix/pallas_call | solution.py:355
  (113 shorter events, 26.8 us)
Async XLA Ops:
  0.0 68.6 %collective-permute-start = (bf16[256,8192]{1,0:T(8,128)(2,1)}, bf16[256,8192]{1,0:T(8,128)(2,1)}, u32[]{:S(2)}, u32[]{:S(2)}) collective-permute-start(bf16[256,8192]{1,0:T(8,128)(2,1)} %bitcast.41), channel_id=1, source_target_pairs={{0,1},{1,0},{2,3},{3,2},{4,5},{5,4},{6,7},{7,6},{8,9},{9,8},{10,11... | collective-permute-start | bytes 12582920 | tf_op jit(solution)/shard_map/ppermute | solution.py:406
  1.8 7.9 %collective-permute-start.1 = (bf16[512,256]{1,0:T(8,128)(2,1)S(1)}, bf16[512,256]{1,0:T(8,128)(2,1)S(1)}, u32[]{:S(2)}, u32[]{:S(2)}) collective-permute-start(bf16[512,256]{1,0:T(8,128)(2,1)S(1)} %dynamic_slice.15), channel_id=1, source_target_pairs={{0,8},{8,16},{16,24},{24,28},{28,20},{20,12},{12,4},{4,0},{1,9},{9... | collective-permute-start | bytes 786440 | tf_op jit(solution)/shard_map/ppermute | solution.py:415
  3.2 7.7 %collective-permute-start.5 = (bf16[512,256]{1,0:T(8,128)(2,1)S(1)}, bf16[512,256]{1,0:T(8,128)(2,1)}, u32[]{:S(2)}, u32[]{:S(2)}) collective-permute-start(bf16[512,256]{1,0:T(8,128)(2,1)S(1)} %dynamic_slice.15), channel_id=1, source_target_pairs={{0,4},{8,0},{16,8},{24,16},{28,24},{20,28},{12,20},{4,12},{1,5},{9... | collective-permute-start | bytes 786440 | tf_op jit(solution)/shard_map/ppermute | solution.py:415
  4.4 10.8 %collective-permute-start.20 = (bf16[512,256]{1,0:T(8,128)(2,1)S(1)}, bf16[512,256]{1,0:T(8,128)(2,1)S(1)}, u32[]{:S(2)}, u32[]{:S(2)}) collective-permute-start(bf16[512,256]{1,0:T(8,128)(2,1)S(1)} %get-tuple-element.14), channel_id=1, source_target_pairs={{0,8},{8,16},{16,24},{24,28},{28,20},{20,12},{12,4},{4,0},{1,9},{9... | collective-permute-start | bytes 786440 | tf_op jit(solution)/shard_map/ppermute | solution.py:415
  5.8 10.7 %collective-permute-start.24 = (bf16[512,256]{1,0:T(8,128)(2,1)S(1)}, bf16[512,256]{1,0:T(8,128)(2,1)S(1)}, u32[]{:S(2)}, u32[]{:S(2)}) collective-permute-start(bf16[512,256]{1,0:T(8,128)(2,1)S(1)} %get-tuple-element.13), channel_id=1, source_target_pairs={{0,4},{8,0},{16,8},{24,16},{28,24},{20,28},{12,20},{4,12},{1,5},{9... | collective-permute-start | bytes 786440 | tf_op jit(solution)/shard_map/ppermute | solution.py:415
  9.7 12.1 %collective-permute-start.28 = (bf16[512,256]{1,0:T(8,128)(2,1)S(1)}, bf16[512,256]{1,0:T(8,128)(2,1)S(1)}, u32[]{:S(2)}, u32[]{:S(2)}) collective-permute-start(bf16[512,256]{1,0:T(8,128)(2,1)S(1)} %get-tuple-element.14), channel_id=1, source_target_pairs={{0,4},{8,0},{16,8},{24,16},{28,24},{20,28},{12,20},{4,12},{1,5},{9... | collective-permute-start | bytes 786440 | tf_op jit(solution)/shard_map/ppermute | solution.py:415
  10.9 11.3 %collective-permute-start.31 = (bf16[512,256]{1,0:T(8,128)(2,1)S(1)}, bf16[512,256]{1,0:T(8,128)(2,1)S(1)}, u32[]{:S(2)}, u32[]{:S(2)}) collective-permute-start(bf16[512,256]{1,0:T(8,128)(2,1)S(1)} %get-tuple-element.13), channel_id=1, source_target_pairs={{0,8},{8,16},{16,24},{24,28},{28,20},{20,12},{12,4},{4,0},{1,9},{9... | collective-permute-start | bytes 786440 | tf_op jit(solution)/shard_map/ppermute | solution.py:415
  15.2 11.3 %collective-permute-start.2 = (bf16[512,256]{1,0:T(8,128)(2,1)S(1)}, bf16[512,256]{1,0:T(8,128)(2,1)}, u32[]{:S(2)}, u32[]{:S(2)}) collective-permute-start(bf16[512,256]{1,0:T(8,128)(2,1)S(1)} %collective-permute-done.1.refs_1_), channel_id=1, source_target_pairs={{0,8},{8,16},{16,24},{24,28},{28,20},{20,12},{12,4},{4,0},{1,9},{9... | collective-permute-start | bytes 786440 | tf_op jit(solution)/shard_map/ppermute | solution.py:415
  16.5 11.3 %collective-permute-start.6 = (bf16[512,256]{1,0:T(8,128)(2,1)}, bf16[512,256]{1,0:T(8,128)(2,1)}, u32[]{:S(2)}, u32[]{:S(2)}) collective-permute-start(bf16[512,256]{1,0:T(8,128)(2,1)} %collective-permute-done.5.refs_3_), channel_id=1, source_target_pairs={{0,4},{8,0},{16,8},{24,16},{28,24},{20,28},{12,20},{4,12},{1,5},{9... | collective-permute-start | bytes 786440 | tf_op jit(solution)/shard_map/ppermute | solution.py:415
  22.2 11.1 %collective-permute-start.14 = (bf16[512,256]{1,0:T(8,128)(2,1)}, bf16[512,256]{1,0:T(8,128)(2,1)}, u32[]{:S(2)}, u32[]{:S(2)}) collective-permute-start(bf16[512,256]{1,0:T(8,128)(2,1)} %collective-permute-done.5.refs_3_), channel_id=1, source_target_pairs={{0,2},{1,3},{2,0},{3,1},{4,6},{5,7},{6,4},{7,5},{8,10},{9,11},{10,... | collective-permute-start | bytes 786440 | tf_op jit(solution)/shard_map/ppermute | solution.py:409
  26.5 8.0 %collective-permute-start.21 = (bf16[512,256]{1,0:T(8,128)(2,1)S(1)}, bf16[512,256]{1,0:T(8,128)(2,1)}, u32[]{:S(2)}, u32[]{:S(2)}) collective-permute-start(bf16[512,256]{1,0:T(8,128)(2,1)S(1)} %collective-permute-done.20.refs_1_), channel_id=1, source_target_pairs={{0,8},{8,16},{16,24},{24,28},{28,20},{20,12},{12,4},{4,0},{1,9},{9... | collective-permute-start | bytes 786440 | tf_op jit(solution)/shard_map/ppermute | solution.py:415
  27.8 8.0 %collective-permute-start.25 = (bf16[512,256]{1,0:T(8,128)(2,1)S(1)}, bf16[512,256]{1,0:T(8,128)(2,1)}, u32[]{:S(2)}, u32[]{:S(2)}) collective-permute-start(bf16[512,256]{1,0:T(8,128)(2,1)S(1)} %collective-permute-done.24.refs_4_), channel_id=1, source_target_pairs={{0,4},{8,0},{16,8},{24,16},{28,24},{20,28},{12,20},{4,12},{1,5},{9... | collective-permute-start | bytes 786440 | tf_op jit(solution)/shard_map/ppermute | solution.py:415
  28.0 12.0 %collective-permute-start.29 = (bf16[512,256]{1,0:T(8,128)(2,1)S(1)}, bf16[512,256]{1,0:T(8,128)(2,1)S(1)}, u32[]{:S(2)}, u32[]{:S(2)}) collective-permute-start(bf16[512,256]{1,0:T(8,128)(2,1)S(1)} %collective-permute-done.28.refs_2_), channel_id=1, source_target_pairs={{0,4},{8,0},{16,8},{24,16},{28,24},{20,28},{12,20},{4,12},{1,5},{9... | collective-permute-start | bytes 786440 | tf_op jit(solution)/shard_map/ppermute | solution.py:415
  33.3 7.0 %collective-permute-start.32 = (bf16[512,256]{1,0:T(8,128)(2,1)S(1)}, bf16[512,256]{1,0:T(8,128)(2,1)S(1)}, u32[]{:S(2)}, u32[]{:S(2)}) collective-permute-start(bf16[512,256]{1,0:T(8,128)(2,1)S(1)} %collective-permute-done.31.refs_3_), channel_id=1, source_target_pairs={{0,8},{8,16},{16,24},{24,28},{28,20},{20,12},{12,4},{4,0},{1,9},{9... | collective-permute-start | bytes 786440 | tf_op jit(solution)/shard_map/ppermute | solution.py:415
  34.6 9.3 %collective-permute-start.3 = (bf16[512,256]{1,0:T(8,128)(2,1)}, bf16[512,256]{1,0:T(8,128)(2,1)S(1)}, u32[]{:S(2)}, u32[]{:S(2)}) collective-permute-start(bf16[512,256]{1,0:T(8,128)(2,1)} %collective-permute-done.2.refs_5_), channel_id=1, source_target_pairs={{0,8},{8,16},{16,24},{24,28},{28,20},{20,12},{12,4},{4,0},{1,9},{9... | collective-permute-start | bytes 786440 | tf_op jit(solution)/shard_map/ppermute | solution.py:415
  35.9 10.1 %collective-permute-start.7 = (bf16[512,256]{1,0:T(8,128)(2,1)}, bf16[512,256]{1,0:T(8,128)(2,1)}, u32[]{:S(2)}, u32[]{:S(2)}) collective-permute-start(bf16[512,256]{1,0:T(8,128)(2,1)} %collective-permute-done.6.refs_7_), channel_id=1, source_target_pairs={{0,4},{8,0},{16,8},{24,16},{28,24},{20,28},{12,20},{4,12},{1,5},{9... | collective-permute-start | bytes 786440 | tf_op jit(solution)/shard_map/ppermute | solution.py:415
  40.0 8.8 %collective-permute-start.15 = (bf16[512,256]{1,0:T(8,128)(2,1)}, bf16[512,256]{1,0:T(8,128)(2,1)}, u32[]{:S(2)}, u32[]{:S(2)}) collective-permute-start(bf16[512,256]{1,0:T(8,128)(2,1)} %collective-permute-done.2.refs_5_), channel_id=1, source_target_pairs={{0,2},{1,3},{2,0},{3,1},{4,6},{5,7},{6,4},{7,5},{8,10},{9,11},{10,... | collective-permute-start | bytes 786440 | tf_op jit(solution)/shard_map/ppermute | solution.py:409
  40.3 9.9 %collective-permute-start.16 = (bf16[512,256]{1,0:T(8,128)(2,1)}, bf16[512,256]{1,0:T(8,128)(2,1)}, u32[]{:S(2)}, u32[]{:S(2)}) collective-permute-start(bf16[512,256]{1,0:T(8,128)(2,1)} %collective-permute-done.6.refs_7_), channel_id=1, source_target_pairs={{0,2},{1,3},{2,0},{3,1},{4,6},{5,7},{6,4},{7,5},{8,10},{9,11},{10,... | collective-permute-start | bytes 786440 | tf_op jit(solution)/shard_map/ppermute | solution.py:409
  50.4 16.8 %collective-permute-start.4 = (bf16[512,256]{1,0:T(8,128)(2,1)S(1)}, bf16[512,256]{1,0:T(8,128)(2,1)S(1)}, u32[]{:S(2)}, u32[]{:S(2)}) collective-permute-start(bf16[512,256]{1,0:T(8,128)(2,1)S(1)} %collective-permute-done.3.refs_0_), channel_id=1, source_target_pairs={{0,2},{1,3},{2,0},{3,1},{4,6},{5,7},{6,4},{7,5},{8,10},{9,11},{10,... | collective-permute-start | bytes 786440 | tf_op jit(solution)/shard_map/ppermute | solution.py:409
  51.9 22.5 %collective-permute-start.8 = (bf16[512,256]{1,0:T(8,128)(2,1)}, bf16[512,256]{1,0:T(8,128)(2,1)}, u32[]{:S(2)}, u32[]{:S(2)}) collective-permute-start(bf16[512,256]{1,0:T(8,128)(2,1)} %collective-permute-done.7.refs_2_), channel_id=1, source_target_pairs={{0,2},{1,3},{2,0},{3,1},{4,6},{5,7},{6,4},{7,5},{8,10},{9,11},{10,... | collective-permute-start | bytes 786440 | tf_op jit(solution)/shard_map/ppermute | solution.py:409
  54.5 8.6 %collective-permute-start.11 = (bf16[256,256]{1,0:T(8,128)(2,1)S(1)}, bf16[256,256]{1,0:T(8,128)(2,1)S(1)}, u32[]{:S(2)}, u32[]{:S(2)}) collective-permute-start(bf16[256,256]{1,0:T(8,128)(2,1)S(1)} %collective-permute-done.9.refs_4_), channel_id=1, source_target_pairs={{0,2},{1,3},{2,0},{3,1},{4,6},{5,7},{6,4},{7,5},{8,10},{9,11},{10,... | collective-permute-start | bytes 393224 | tf_op jit(solution)/shard_map/ppermute | solution.py:409
  55.1 11.0 %collective-permute-start.12 = (bf16[256,256]{1,0:T(8,128)(2,1)S(1)}, bf16[256,256]{1,0:T(8,128)(2,1)S(1)}, u32[]{:S(2)}, u32[]{:S(2)}) collective-permute-start(bf16[256,256]{1,0:T(8,128)(2,1)S(1)} %collective-permute-done.10.refs_5_), channel_id=1, source_target_pairs={{0,2},{1,3},{2,0},{3,1},{4,6},{5,7},{6,4},{7,5},{8,10},{9,11},{10,... | collective-permute-start | bytes 393224 | tf_op jit(solution)/shard_map/ppermute | solution.py:409
  63.1 24.0 %collective-permute-start.30 = (bf16[512,256]{1,0:T(8,128)(2,1)}, bf16[512,256]{1,0:T(8,128)(2,1)}, u32[]{:S(2)}, u32[]{:S(2)}) collective-permute-start(bf16[512,256]{1,0:T(8,128)(2,1)} %copy-done.11), channel_id=1, source_target_pairs={{0,4},{8,0},{16,8},{24,16},{28,24},{20,28},{12,20},{4,12},{1,5},{9... | collective-permute-start | bytes 786440 | tf_op jit(solution)/shard_map/ppermute | solution.py:415
  66.0 21.1 %collective-permute-start.33 = (bf16[512,256]{1,0:T(8,128)(2,1)}, bf16[512,256]{1,0:T(8,128)(2,1)}, u32[]{:S(2)}, u32[]{:S(2)}) collective-permute-start(bf16[512,256]{1,0:T(8,128)(2,1)} %copy-done.12), channel_id=1, source_target_pairs={{0,8},{8,16},{16,24},{24,28},{28,20},{20,12},{12,4},{4,0},{1,9},{9... | collective-permute-start | bytes 786440 | tf_op jit(solution)/shard_map/ppermute | solution.py:415
  67.2 24.9 %collective-permute-start.23 = (bf16[512,256]{1,0:T(8,128)(2,1)}, bf16[512,256]{1,0:T(8,128)(2,1)}, u32[]{:S(2)}, u32[]{:S(2)}) collective-permute-start(bf16[512,256]{1,0:T(8,128)(2,1)} %collective-permute-done.22.refs_0_), channel_id=1, source_target_pairs={{0,8},{8,16},{16,24},{24,28},{28,20},{20,12},{12,4},{4,0},{1,9},{9... | collective-permute-start | bytes 786440 | tf_op jit(solution)/shard_map/ppermute | solution.py:415
  68.6 23.5 %collective-permute-start.27 = (bf16[512,256]{1,0:T(8,128)(2,1)}, bf16[512,256]{1,0:T(8,128)(2,1)}, u32[]{:S(2)}, u32[]{:S(2)}) collective-permute-start(bf16[512,256]{1,0:T(8,128)(2,1)} %collective-permute-done.26.refs_3_), channel_id=1, source_target_pairs={{0,4},{8,0},{16,8},{24,16},{28,24},{20,28},{12,20},{4,12},{1,5},{9... | collective-permute-start | bytes 786440 | tf_op jit(solution)/shard_map/ppermute | solution.py:415
  80.2 24.5 %collective-permute-start.18 = (bf16[512,256]{1,0:T(8,128)(2,1)}, bf16[512,256]{1,0:T(8,128)(2,1)}, u32[]{:S(2)}, u32[]{:S(2)}) collective-permute-start(bf16[512,256]{1,0:T(8,128)(2,1)} %shard_map.74.refs_0_), channel_id=1, source_target_pairs={{0,2},{1,3},{4,6},{5,7},{8,10},{9,11},{12,14},{13,15},{16,18},{17,... | collective-permute-start | bytes 786440 | tf_op jit(solution)/shard_map/ppermute | solution.py:412
  96.6 8.6 %collective-permute-start.35 = (bf16[512,256]{1,0:T(8,128)(2,1)}, bf16[512,256]{1,0:T(8,128)(2,1)S(1)}, u32[]{:S(2)}, u32[]{:S(2)}) collective-permute-start(bf16[512,256]{1,0:T(8,128)(2,1)} %shard_map.77.refs_0_), channel_id=1, source_target_pairs={{0,2},{1,3},{4,6},{5,7},{8,10},{9,11},{12,14},{13,15},{16,18},{17,... | collective-permute-start | bytes 786440 | tf_op jit(solution)/shard_map/ppermute | solution.py:412
  98.3 31.0 %collective-permute-start.17 = (bf16[512,256]{1,0:T(8,128)(2,1)S(1)}, bf16[512,256]{1,0:T(8,128)(2,1)S(1)}, u32[]{:S(2)}, u32[]{:S(2)}) collective-permute-start(bf16[512,256]{1,0:T(8,128)(2,1)S(1)} %copy-done.1), channel_id=1, source_target_pairs={{0,1},{1,0},{2,3},{3,2},{4,5},{5,4},{6,7},{7,6},{8,9},{9,8},{10,11... | collective-permute-start | bytes 786440 | tf_op jit(solution)/shard_map/ppermute | solution.py:406
  104.7 24.6 %collective-permute-start.19 = (bf16[512,256]{1,0:T(8,128)(2,1)}, bf16[512,256]{1,0:T(8,128)(2,1)S(1)}, u32[]{:S(2)}, u32[]{:S(2)}) collective-permute-start(bf16[512,256]{1,0:T(8,128)(2,1)} %collective-permute-done.18.refs_1_), channel_id=1, source_target_pairs={{0,1},{1,0},{2,3},{3,2},{4,5},{5,4},{6,7},{7,6},{8,9},{9,8},{10,11... | collective-permute-start | bytes 786440 | tf_op jit(solution)/shard_map/ppermute | solution.py:406
  104.8 32.8 %collective-permute-start.34 = (bf16[512,256]{1,0:T(8,128)(2,1)}, bf16[512,256]{1,0:T(8,128)(2,1)S(1)}, u32[]{:S(2)}, u32[]{:S(2)}) collective-permute-start(bf16[512,256]{1,0:T(8,128)(2,1)} %shard_map.77.refs_0_), channel_id=1, source_target_pairs={{0,1},{1,0},{2,3},{3,2},{4,5},{5,4},{6,7},{7,6},{8,9},{9,8},{10,11... | collective-permute-start | bytes 786440 | tf_op jit(solution)/shard_map/ppermute | solution.py:406
  105.2 32.4 %collective-permute-start.36 = (bf16[512,256]{1,0:T(8,128)(2,1)S(1)}, bf16[512,256]{1,0:T(8,128)(2,1)S(1)}, u32[]{:S(2)}, u32[]{:S(2)}) collective-permute-start(bf16[512,256]{1,0:T(8,128)(2,1)S(1)} %collective-permute-done.35.refs_1_), channel_id=1, source_target_pairs={{0,1},{1,0},{2,3},{3,2},{4,5},{5,4},{6,7},{7,6},{8,9},{9,8},{10,11... | collective-permute-start | bytes 786440 | tf_op jit(solution)/shard_map/ppermute | solution.py:406
  (26 other events, 522.6 us)

commit v4 on v3

--- a/solution.py
+++ b/solution.py
@@ -17,6 +17,7 @@
 CHUNK = 2 * BLK
 SPARE_VMEM = 4 << 20
 MOST_VMEM = 67043328
+LEFT_VMEM = 3 << 20
 
 rope_base = 1000000.0
 
@@ -110,7 +111,7 @@
     added = before is not None
     if added:
         extras = [before, *extras]
-    grant = MOST_VMEM - (3 << 19) * (finish == "value" or (added and finish == "sum"))
+    grant = MOST_VMEM - LEFT_VMEM
     return pl.pallas_call(
         functools.partial(project_kernel, plan, finish, added),
         out_shape=out,
@@ -137,6 +138,81 @@
     )(columns, own_tokens, sibling_tokens, *pieces, *extras)
 
 
+def partial_kernel(copies, shards, facts, own_ref, sibling_ref, *refs):
+    piece_refs = refs[:-7]
+    key_ref, value_ref, token_ref, weight_ref, acc_ref, token_sems, weight_sems = refs[-7:]
+    number_of_rows, depth = own_ref.shape[0], weight_ref.shape[1]
+    width = weight_ref.shape[2] // 2
+    for operand, shard, first_row, side, lane in copies:
+        piece_ref = piece_refs[operand]
+        row = first_row
+        if side >= 0:
+            row = pl.multiple_of((facts[0] if side == 0 else 1 - facts[0]) * (depth // 2), depth // 2)
+        pltpu.make_async_copy(
+            piece_ref,
+            weight_ref.at[shard, pl.ds(row, piece_ref.shape[0]), pl.ds(lane, width)],
+            weight_sems.at[shard],
+        ).start()
+    for shard in range(shards):
+        columns = pl.ds(pl.multiple_of(facts[1 + shard] * depth, depth), depth)
+        for half, tokens_ref in enumerate((own_ref, sibling_ref)):
+            pltpu.make_async_copy(
+                tokens_ref.at[:, columns],
+                token_ref.at[shard, pl.ds(half * number_of_rows, number_of_rows), :],
+                token_sems.at[shard],
+            ).start()
+    acc_ref[...] = jnp.zeros_like(acc_ref)
+
+    @pl.loop(0, shards)
+    def _(shard):
+        pltpu.make_async_copy(
+            weight_ref.at[shard], weight_ref.at[shard], weight_sems.at[shard]
+        ).wait()
+        pltpu.make_async_copy(
+            token_ref.at[shard], token_ref.at[shard], token_sems.at[shard]
+        ).wait()
+        acc_ref[...] += jnp.dot(
+            token_ref[shard], weight_ref[shard], preferred_element_type=jnp.float32
+        )
+
+    key_ref[...] = acc_ref[:, :width]
+    value_ref[...] = acc_ref[:, width:]
+
+
+def project_partial(own_tokens, sibling_tokens, pieces, copies, sources, plane, depth):
+    shards = len(sources)
+    chip_rows = CORES * own_tokens.shape[0]
+    width = pieces[0].shape[1]
+    facts = jnp.stack([plane, *sources]).astype(jnp.int32)
+    out = jax.ShapeDtypeStruct((chip_rows, width), jnp.float32)
+    out_spec = pl.BlockSpec(out.shape, lambda p, b: (0, 0))
+    anywhere = pl.BlockSpec(memory_space=pltpu.MemorySpace.HBM)
+    return pl.pallas_call(
+        functools.partial(partial_kernel, tuple(copies), shards),
+        out_shape=(out, out),
+        grid_spec=pltpu.PrefetchScalarGridSpec(
+            num_scalar_prefetch=1,
+            grid=(1,),
+            in_specs=[anywhere] * (2 + len(pieces)),
+            out_specs=(out_spec, out_spec),
+            scratch_shapes=[
+                pltpu.VMEM((shards, chip_rows, depth), jnp.bfloat16),
+                pltpu.VMEM((shards, depth, 2 * width), jnp.bfloat16),
+                pltpu.VMEM((chip_rows, 2 * width), jnp.float32),
+                pltpu.SemaphoreType.DMA((shards,)),
+                pltpu.SemaphoreType.DMA((shards,)),
+            ],
+        ),
+        compiler_params=pltpu.CompilerParams(vmem_limit_bytes=MOST_VMEM - LEFT_VMEM),
+        cost_estimate=pl.CostEstimate(
+            flops=4 * shards * depth * chip_rows * width,
+            bytes_accessed=2 * shards * depth * (chip_rows + 2 * width),
+            transcendentals=0,
+        ),
+        name="project_partial",
+    )(facts, own_tokens, sibling_tokens, *pieces)
+
+
 class Blocks:
     def __init__(self, facts, hops, row_blocks, row_block):
         self.row_blocks, self.source_core = row_blocks, facts[1]
@@ -184,19 +260,14 @@
     return pl.ds(pl.multiple_of(chunk * CHUNK, CHUNK), CHUNK)
 
 
-def score_kernel(hops, row_blocks, group, facts, q_ref, *refs):
-    k_refs = refs[:hops]
-    probs_ref, inverse_ref, chosen_ref, score_ref, peak_ref, total_ref = refs[hops:]
-    blocks = Blocks(facts, hops, row_blocks, pl.program_id(1))
-    blocks.gather(k_refs, chosen_ref)
-    factor = math.log2(math.e) / math.sqrt(HEAD_SIZE)
+def find_scores(blocks, group, q_ref, key_ref, score_ref, peak_ref):
     rows = group * BLK
 
     def scores(chunk):
         heads = [q_ref[:, h * HEAD_SIZE : (h + 1) * HEAD_SIZE] for h in range(group)]
         return lax.dot_general(
             jnp.concatenate(heads, axis=0),
-            chosen_ref[chunk_rows(chunk), :],
+            key_ref[chunk_rows(chunk), :],
             (((1,), (1,)), ((), ())),
             preferred_element_type=jnp.float32,
         )
@@ -222,22 +293,60 @@
     peak_ref[...] = jnp.broadcast_to(
         jnp.max(peak_ref[...], axis=1, keepdims=True), (rows, BLK)
     )
+
+
+def weights_of(chunk, score_ref, peak_ref, total_ref):
+    factor = math.log2(math.e) / math.sqrt(HEAD_SIZE)
+    peak, total, halves = peak_ref[...], total_ref[...], []
+    for first in range(0, CHUNK, BLK):
+        probs = jnp.exp2((score_ref[chunk, :, first : first + BLK] - peak) * factor)
+        halves.append(probs.astype(jnp.bfloat16))
+        total = total + probs
+    total_ref[...] = total
+    return halves
+
+
+def score_kernel(hops, row_blocks, group, facts, q_ref, *refs):
+    k_refs = refs[:hops]
+    probs_ref, inverse_ref, key_ref, score_ref, peak_ref, total_ref = refs[hops:]
+    blocks = Blocks(facts, hops, row_blocks, pl.program_id(1))
+    blocks.gather(k_refs, key_ref)
+    find_scores(blocks, group, q_ref, key_ref, score_ref, peak_ref)
     total_ref[...] = jnp.zeros_like(total_ref)
 
     @pl.loop(0, blocks.chunks)
     def _(chunk):
-        peak = peak_ref[...]
-        total = total_ref[...]
-        for first in range(0, CHUNK, BLK):
-            lanes = slice(first, first + BLK)
-            probs = jnp.exp2((score_ref[chunk, :, lanes] - peak) * factor)
-            probs_ref[0, chunk, :, lanes] = probs.astype(probs_ref.dtype)
-            total = total + probs
-        total_ref[...] = total
+        halves = weights_of(chunk, score_ref, peak_ref, total_ref)
+        for at, half in enumerate(halves):
+            probs_ref[0, chunk, :, at * BLK : (at + 1) * BLK] = half
 
     inverse_ref[0] = jnp.broadcast_to(
-        1.0 / jnp.sum(total_ref[...], axis=1, keepdims=True), (rows, BLK)
-    )
+        1.0 / jnp.sum(total_ref[...], axis=1, keepdims=True), (group * BLK, BLK)
+    )
+
+
+def attend_kernel(hops, row_blocks, group, facts, q_ref, *refs):
+    k_refs, v_refs = refs[:hops], refs[hops : 2 * hops]
+    out_ref, key_ref, value_ref, score_ref, peak_ref, total_ref, acc_ref = refs[-7:]
+    blocks = Blocks(facts, hops, row_blocks, pl.program_id(1))
+    blocks.gather(k_refs, key_ref)
+    find_scores(blocks, group, q_ref, key_ref, score_ref, peak_ref)
+    blocks.gather(v_refs, value_ref)
+    total_ref[...] = jnp.zeros_like(total_ref)
+    acc_ref[...] = jnp.zeros_like(acc_ref)
+
+    @pl.loop(0, blocks.chunks)
+    def _(chunk):
+        halves = weights_of(chunk, score_ref, peak_ref, total_ref)
+        acc_ref[...] += jnp.dot(
+            jnp.concatenate(halves, axis=1),
+            value_ref[chunk_rows(chunk), :],
+            preferred_element_type=jnp.float32,
+        )
+
+    mixed = (acc_ref[...] / jnp.sum(total_ref[...], axis=1, keepdims=True)).astype(out_ref.dtype)
+    for h in range(group):
+        out_ref[:, h * HEAD_SIZE : (h + 1) * HEAD_SIZE] = mixed[h * BLK : (h + 1) * BLK]
 
 
 def mix_kernel(hops, row_blocks, group, facts, probs_ref, inverse_ref, *refs):
@@ -302,7 +411,10 @@
             (1, self.stacked, BLK), lambda l, r, f: (l * self.row_blocks + r, 0, 0)
         )
         self.pairs = self.heads * self.row_blocks * self.stacked * self.chunks * CHUNK // 2
-        self.block_bytes = self.stacked * BLK * 4
+        count = self.heads * self.row_blocks
+        block_bytes = self.stacked * BLK * 4
+        kept = block_bytes * count * (self.chunks + 1) + (2 << 20)
+        self.grant = max(MOST_VMEM - kept, block_bytes * (4 * self.chunks + 8) + SPARE_VMEM)
 
     def scores(self, keys):
         count = self.heads * self.row_blocks
@@ -333,7 +445,7 @@
                 ],
             ),
             compiler_params=pltpu.CompilerParams(
-                vmem_limit_bytes=self.block_bytes * (4 * self.chunks + 8) + SPARE_VMEM
+                vmem_limit_bytes=self.grant
             ),
             cost_estimate=pl.CostEstimate(
                 flops=2 * self.pairs * HEAD_SIZE,
@@ -342,6 +454,45 @@
             ),
             name="score",
         )(self.facts, self.queries, *keys)
+
+    def attend(self, keys, values, before):
+        operands = [self.facts, self.queries, *keys, *values]
+        in_specs = [self.q_spec] + [self.kv_spec] * (2 * self.hops)
+        aliases = {}
+        if before is not None:
+            aliases = {len(operands): 0}
+            operands.append(before)
+            in_specs.append(pl.BlockSpec(memory_space=pl.ANY))
+        chosen = pltpu.VMEM((self.chunks * CHUNK, HEAD_SIZE), jnp.bfloat16)
+        tall = pltpu.VMEM((self.stacked, BLK), jnp.float32)
+        return pl.pallas_call(
+            functools.partial(attend_kernel, self.hops, self.row_blocks, self.group),
+            out_shape=jax.ShapeDtypeStruct(self.queries.shape, self.queries.dtype),
+            grid_spec=pltpu.PrefetchScalarGridSpec(
+                num_scalar_prefetch=1,
+                grid=(self.heads, self.row_blocks),
+                in_specs=in_specs,
+                out_specs=self.q_spec,
+                scratch_shapes=[
+                    chosen,
+                    chosen,
+                    pltpu.VMEM((self.chunks, self.stacked, CHUNK), jnp.float32),
+                    tall,
+                    tall,
+                    tall,
+                ],
+            ),
+            input_output_aliases=aliases,
+            compiler_params=pltpu.CompilerParams(
+                vmem_limit_bytes=MOST_VMEM - LEFT_VMEM
+            ),
+            cost_estimate=pl.CostEstimate(
+                flops=4 * self.pairs * HEAD_SIZE,
+                bytes_accessed=2 * self.queries.size,
+                transcendentals=self.pairs,
+            ),
+            name="attend",
+        )(*operands)
 
     def mix(self, probs, inverse, values, before):
         operands = [self.facts, probs, inverse, *values]
@@ -369,7 +520,7 @@
             ),
             input_output_aliases=aliases,
             compiler_params=pltpu.CompilerParams(
-                vmem_limit_bytes=self.block_bytes * (2 * self.chunks + 8) + SPARE_VMEM
+                vmem_limit_bytes=self.grant
             ),
             cost_estimate=pl.CostEstimate(
                 flops=2 * self.pairs * HEAD_SIZE,
@@ -464,6 +615,7 @@
         for weight in (key_weight, value_weight)
     ]
     sides = [plane, 1 - plane]
+    key_arrived, value_arrived = {}, {}
     key_strips = [own_strips[0]]
     travelling = {1: key_strip, -1: key_strip}
     for hop in range(1, half_ring + 1):
@@ -477,6 +629,7 @@
             other = to_plane(piece)
             travelling[step] = piece
             arrived[step] = (piece, other)
+            key_arrived[hop, step] = (piece, other)
         if hop < half_ring:
             key_strips.append(
                 [
@@ -510,17 +663,31 @@
                     continue
                 piece = along_ring(travelling[side, step], step)
                 travelling[side, step] = piece
+                value_arrived[hop, step, side] = piece
                 arrived.append(whole_strip(piece, 0, source_at(-step * hop) * 2 + side))
         value_strips.append(arrived)
 
     def joined(hops):
         return [entry for strips in hops for entry in strips]
 
-    key_sum = projected("sum", joined(key_strips[:-2]), None, [])
+    early = half_ring - 2
+    sources = [source_at(distance) for distance in range(-early, early + 1)]
+    pieces, copies = [key_weight, value_weight], [(0, early, 0, -1, 0), (1, early, 0, -1, half_width)]
+    for hop in range(1, early + 1):
+        for step in (1, -1):
+            shard = early - step * hop
+            for side, piece in enumerate(key_arrived[hop, step]):
+                copies.append((len(pieces), shard, 0, side, 0))
+                pieces.append(piece)
+            for side in range(2):
+                copies.append((len(pieces), shard, side * strip, -1, half_width))
+                pieces.append(value_arrived[hop, step, side])
+    key_sum, value_sum = project_partial(
+        own_tokens, sibling_tokens, pieces, copies, sources, plane, depth
+    )
     key_rows = projected(
         "key", joined(key_strips[-2:]), key_sum, [key_bias[None], *rope_tables(positions)]
     )
-    value_sum = projected("sum", joined(value_strips[:-2]), None, [])
     value_sum = projected("sum", value_strips[-2], value_sum, [])
     value_rows = projected("value", value_strips[-1], value_sum, [value_bias[None]])
 
@@ -537,9 +704,8 @@
 
     near, far = attention(core), attention(1 - core)
     near_weights = near.scores(keys)
-    far_weights = far.scores(sibling_keys)
     attended = near.mix(*near_weights, values, None)
-    attended = far.mix(*far_weights, sibling_values, attended)
+    attended = far.attend(sibling_keys, sibling_values, attended)
     return attended[None]
 
 

time: 145 us -> 142 us (0.979)
  the two profiles are of different devices: /device:TPU:5 before, /device:TPU:31 now
where the time goes in v4:
time: 142 us
  Pallas kernels  53 us (37%)
  waiting for transfers between devices  39.7 us (28%)
  starting transfers between devices  34 us (24%)
  local copies, waits for them, and re-layouts  10 us (7%)
  other arithmetic  4.57 us (3%)
    ppermute x22, waiting for transfers between devices, along_ring(): lax.ppermute(x, 'dp', [(ring[i], ring[(i + step) % dp_size]) for i in ran...  30.9 us
    pallas_call x3, Pallas kernels, project(): pl.pallas_call(functools.partial(project_kernel, plan, finish, added), ou...  15.2 us
    ppermute x5, starting transfers between devices, to_sibling(): return lax.ppermute(x, 'ctx', [(i, i ^ 1) for i in range(ctx_size)])  14.8 us
    ppermute x22, starting transfers between devices, along_ring(): lax.ppermute(x, 'dp', [(ring[i], ring[(i + step) % dp_size]) for i in ran...  12 us
    pallas_call x1, Pallas kernels, attend(): pl.pallas_call(functools.partial(attend_kernel, self.hops, self.row_block...  11.6 us
    pallas_call x1, Pallas kernels, scores(): pl.pallas_call(functools.partial(score_kernel, self.hops, self.row_blocks...  10.3 us
    ppermute x8, waiting for transfers between devices, to_plane(): return lax.ppermute(x, 'ctx', [(i, i ^ CORES) for i in range(ctx_size)])  8.82 us
    pallas_call x1, Pallas kernels, project_partial(): pl.pallas_call(functools.partial(partial_kernel, tuple(copies), shards),...  8.22 us
  transfers between devices with their start and end apart: 37, of which 12 were waited for; matrix products, arithmetic and copies ran while one was open for 8% of the time, Pallas kernels for 29%

profile of v4, /device:TPU:31, one launch (start us, length us, event | category | flops | bytes accessed | tf_op | source)
XLA Modules:
  0.0 141.9 jit_solution(10065056229252452750)
XLA Ops:
  0.7 1.1 dynamic_slice.15
  2.0 1.3 collective-permute-start.5
  3.3 1.1 fusion.1
  4.8 4.7 %collective-permute-done.1.refs_2_ = bf16[512,256]{1,0:T(8,128)(2,1)S(1)} collective-permute-done((bf16[512,256]{1,0:T(8,128)(2,1)S(1)}, bf16[512,256]{1,0:T(8,128)(2,1)S(1)}, u32[]{:S(2)}, u32[]{:S(2)}) %collective-permute-start.1) | collective-permute-done | bytes 262176 | tf_op jit(solution)/shard_map/ppermute | solution.py:566
  9.7 0.9 collective-permute-start.18
  10.7 4.5 %collective-permute-done.14.refs_4_ = bf16[512,256]{1,0:T(8,128)(2,1)S(1)} collective-permute-done((bf16[512,256]{1,0:T(8,128)(2,1)S(1)}, bf16[512,256]{1,0:T(8,128)(2,1)S(1)}, u32[]{:S(2)}, u32[]{:S(2)}) %collective-permute-start.14) | collective-permute-done | bytes 262176 | tf_op jit(solution)/shard_map/ppermute | solution.py:566
  15.4 5.4 %collective-permute-done.15.refs_5_ = bf16[512,256]{1,0:T(8,128)(2,1)} collective-permute-done((bf16[512,256]{1,0:T(8,128)(2,1)S(1)}, bf16[512,256]{1,0:T(8,128)(2,1)}, u32[]{:S(2)}, u32[]{:S(2)}) %collective-permute-start.15) | collective-permute-done | bytes 262176 | tf_op jit(solution)/shard_map/ppermute | solution.py:566
  21.3 1.2 collective-permute-start.16
  22.5 3.9 %collective-permute-done.2.refs_10_ = bf16[512,256]{1,0:T(8,128)(2,1)} collective-permute-done((bf16[512,256]{1,0:T(8,128)(2,1)S(1)}, bf16[512,256]{1,0:T(8,128)(2,1)}, u32[]{:S(2)}, u32[]{:S(2)}) %collective-permute-start.2) | collective-permute-done | bytes 262176 | tf_op jit(solution)/shard_map/ppermute | solution.py:566
  27.1 1.3 collective-permute-start.23
  28.4 4.1 %collective-permute-done.16.refs_7_ = bf16[512,256]{1,0:T(8,128)(2,1)} collective-permute-done((bf16[512,256]{1,0:T(8,128)(2,1)S(1)}, bf16[512,256]{1,0:T(8,128)(2,1)}, u32[]{:S(2)}, u32[]{:S(2)}) %collective-permute-start.16) | collective-permute-done | bytes 262176 | tf_op jit(solution)/shard_map/ppermute | solution.py:560
  32.6 1.2 collective-permute-start.3
  34.1 4.7 %collective-permute-done.21.refs_13_ = bf16[512,256]{1,0:T(8,128)(2,1)S(1)} collective-permute-done((bf16[512,256]{1,0:T(8,128)(2,1)}, bf16[512,256]{1,0:T(8,128)(2,1)S(1)}, u32[]{:S(2)}, u32[]{:S(2)}) %collective-permute-start.21) | collective-permute-done | bytes 262176 | tf_op jit(solution)/shard_map/ppermute | solution.py:566
  39.3 5.1 %collective-permute-done.3.refs_0_ = bf16[512,256]{1,0:T(8,128)(2,1)S(1)} collective-permute-done((bf16[512,256]{1,0:T(8,128)(2,1)}, bf16[512,256]{1,0:T(8,128)(2,1)S(1)}, u32[]{:S(2)}, u32[]{:S(2)}) %collective-permute-start.3) | collective-permute-done | bytes 262176 | tf_op jit(solution)/shard_map/ppermute | solution.py:566
  44.6 1.0 fusion
  49.6 3.4 %collective-permute-done.22.refs_15_ = bf16[512,256]{1,0:T(8,128)(2,1)S(1)} collective-permute-done((bf16[512,256]{1,0:T(8,128)(2,1)}, bf16[512,256]{1,0:T(8,128)(2,1)S(1)}, u32[]{:S(2)}, u32[]{:S(2)}) %collective-permute-start.22) | collective-permute-done | bytes 262176 | tf_op jit(solution)/shard_map/ppermute | solution.py:560
  56.6 1.7 %collective-permute-done.10.refs_5_ = bf16[256,256]{1,0:T(8,128)(2,1)S(1)} collective-permute-done((bf16[256,256]{1,0:T(8,128)(2,1)S(1)}, bf16[256,256]{1,0:T(8,128)(2,1)S(1)}, u32[]{:S(2)}, u32[]{:S(2)}) %collective-permute-start.10) | collective-permute-done | bytes 131104 | tf_op jit(solution)/shard_map/ppermute | solution.py:566
  59.4 1.0 collective-permute-start.8
  64.0 1.3 collective-permute-done.12.refs_7_
  65.3 1.1 collective-permute-start.33
  66.5 1.4 collective-permute-start.31
  67.9 8.2 %project_partial.1 = (f32[512,256]{1,0:T(8,128)}, f32[512,256]{1,0:T(8,128)}) custom-call(s32[6]{0:T(128)} %stack.93.facts, bf16[256,8192]{1,0:T(8,128)(2,1)} %bitcast.28, bf16[256,8192]{1,0:T(8,128)(2,1)} %collective-permute-done.sibling_ref, bf16[1024,256]{1,0:T(8,128)(2,1)} %constant_dynamic-slice_fusion.2.refs_0_, ...), custom_call_target="tpu_custom_call" | custom-call | flops 2684354560 | bytes 10485760 | tf_op jit(solution)/shard_map/project_partial/pallas_call | solution.py:190
  76.9 5.8 %shard_map.73.refs_0_ = bf16[512,256]{1,0:T(8,128)(2,1)} custom-call(s32[6]{0:T(128)} %stack.86.columns, bf16[256,8192]{1,0:T(8,128)(2,1)} %bitcast.29, bf16[256,8192]{1,0:T(8,128)(2,1)} %collective-permute-done.sibling_ref, bf16[512,256]{1,0:T(8,128)(2,1)} %copy-done.3, bf16[512,256]{1,0:T(8,128)(2,1)} %copy-done.17, bf16[512,256]{1,0:T(8,128)(2,1)} %copy-done.4, ...), custom_call_target="tpu_custom_call" | custom-call | flops 805306368 | bytes 4718592 | tf_op jit(solution)/shard_map/pallas_call | solution.py:115
  82.7 1.3 collective-permute-start.26
  84.8 5.0 %shard_map.74.refs_2_ = f32[512,256]{1,0:T(8,128)} custom-call(s32[4]{0:T(128)} %pad_add_fusion.1.columns, bf16[256,8192]{1,0:T(8,128)(2,1)} %bitcast.30, bf16[256,8192]{1,0:T(8,128)(2,1)} %collective-permute-done.sibling_ref, bf16[512,256]{1,0:T(8,128)(2,1)} %copy-done.21, bf16[512,256]{1,0:T(8,128)(2,1)} %copy-done.22, bf16[512,256]{1,0:T(8,128)(2,1)} %copy-done.23, ...), custom_call_target="tpu_custom_call" | custom-call | flops 536870912 | bytes 3145728 | tf_op jit(solution)/shard_map/pallas_call | solution.py:115
  90.6 4.4 %shard_map.75.refs_0_ = bf16[512,256]{1,0:T(8,128)(2,1)} custom-call(s32[2]{0:T(128)} %pad_add_fusion.columns, bf16[256,8192]{1,0:T(8,128)(2,1)} %bitcast.31, bf16[256,8192]{1,0:T(8,128)(2,1)} %collective-permute-done.sibling_ref, bf16[512,256]{1,0:T(8,128)(2,1)} %copy-done.19, bf16[512,256]{1,0:T(8,128)(2,1)} %copy-done.20, f32[512,256]{1,0:T(8,128)} %shard_map.74.refs_2_, ...), custom_call_target="tpu_custom_call" | custom-call | flops 268435456 | bytes 1572864 | tf_op jit(solution)/shard_map/pallas_call | solution.py:115
  95.1 1.4 %collective-permute-start.35 = (bf16[512,256]{1,0:T(8,128)(2,1)}, bf16[512,256]{1,0:T(8,128)(2,1)S(1)}, u32[]{:S(2)}, u32[]{:S(2)}) collective-permute-start(bf16[512,256]{1,0:T(8,128)(2,1)} %shard_map.75.refs_0_), channel_id=1, source_target_pairs={{0,2},{1,3},{4,6},{5,7},{8,10},{9,11},{12,14},{13,15},{16,18},{17,... | collective-permute-start | bytes 786440 | tf_op jit(solution)/shard_map/ppermute | solution.py:563
  96.5 7.0 %collective-permute-start.25 = (bf16[512,256]{1,0:T(8,128)(2,1)S(1)}, bf16[512,256]{1,0:T(8,128)(2,1)S(1)}, u32[]{:S(2)}, u32[]{:S(2)}) collective-permute-start(bf16[512,256]{1,0:T(8,128)(2,1)S(1)} %copy-done.1), channel_id=1, source_target_pairs={{0,1},{1,0},{2,3},{3,2},{4,5},{5,4},{6,7},{7,6},{8,9},{9,8},{10,11... | collective-permute-start | bytes 786440 | tf_op jit(solution)/shard_map/ppermute | solution.py:557
  104.0 6.6 %collective-permute-start.36 = (bf16[512,256]{1,0:T(8,128)(2,1)S(1)}, bf16[512,256]{1,0:T(8,128)(2,1)S(1)}, u32[]{:S(2)}, u32[]{:S(2)}) collective-permute-start(bf16[512,256]{1,0:T(8,128)(2,1)S(1)} %collective-permute-done.35.refs_1_), channel_id=1, source_target_pairs={{0,1},{1,0},{2,3},{3,2},{4,5},{5,4},{6,7},{7,6},{8,9},{9,8},{10,11... | collective-permute-start | bytes 786440 | tf_op jit(solution)/shard_map/ppermute | solution.py:557
  111.3 10.3 %score.1 = (bf16[4,4,1024,256]{3,2,1,0:T(8,128)(2,1)}, f32[4,1024,128]{2,1,0:T(8,128)}) custom-call(s32[11]{0:T(128)S(1)} %get-tuple-element.18.facts, bf16[256,4096]{1,0:T(8,128)(2,1)} %bitcast.32, bf16[512,256]{1,0:T(8,128)(2,1)S(1)} %copy-done.1, bf16[512,256]{1,0:T(8,128)(2,1)S(1)} %collective-permute-done.26.refs_1_), custom_call_target="tpu_custom_call" | custom-call | flops 536870912 | bytes 9437184 | tf_op jit(solution)/shard_map/score/pallas_call | solution.py:424
  121.5 7.7 %mix.1.refs_4_ = bf16[256,4096]{1,0:T(8,128)(2,1)} custom-call(s32[11]{0:T(128)S(1)} %get-tuple-element.18.facts, bf16[4,4,1024,256]{3,2,1,0:T(8,128)(2,1)} %get-tuple-element.11.probs_ref, f32[4,1024,128]{2,1,0:T(8,128)} %get-tuple-element.12.inverse_ref, bf16[512,256]{1,0:T(8,128)(2,1)S(1)} %copy-done, bf16[512,256]{1,0:T(8,128)(2,1)S(1)} %collective-permute-done.35.refs_1_), custom_call_target="tpu_custom_call" | custom-call | flops 536870912 | bytes 9437184 | tf_op jit(solution)/shard_map/mix/pallas_call | solution.py:506
  130.3 11.6 %attend.1 = bf16[256,4096]{1,0:T(8,128)(2,1)} custom-call(s32[11]{0:T(128)} %get-tuple-element.19.facts, bf16[256,4096]{1,0:T(8,128)(2,1)} %bitcast.33, bf16[512,256]{1,0:T(8,128)(2,1)} %copy-done.24, bf16[512,256]{1,0:T(8,128)(2,1)} %copy-done.26, bf16[512,256]{1,0:T(8,128)(2,1)} %copy-done.25, ...), custom_call_target="tpu_custom_call", output_to_operand_aliasing={{}: (6, {})} | custom-call | flops 1073741824 | bytes 2097152 | tf_op jit(solution)/shard_map/attend/pallas_call | solution.py:468
  (138 shorter events, 20.5 us)
Async XLA Ops:
  0.0 66.5 %collective-permute-start = (bf16[256,8192]{1,0:T(8,128)(2,1)}, bf16[256,8192]{1,0:T(8,128)(2,1)}, u32[]{:S(2)}, u32[]{:S(2)}) collective-permute-start(bf16[256,8192]{1,0:T(8,128)(2,1)} %bitcast.27), channel_id=1, source_target_pairs={{0,1},{1,0},{2,3},{3,2},{4,5},{5,4},{6,7},{7,6},{8,9},{9,8},{10,11... | collective-permute-start | bytes 12582920 | tf_op jit(solution)/shard_map/ppermute | solution.py:557
  1.8 7.7 %collective-permute-start.1 = (bf16[512,256]{1,0:T(8,128)(2,1)S(1)}, bf16[512,256]{1,0:T(8,128)(2,1)S(1)}, u32[]{:S(2)}, u32[]{:S(2)}) collective-permute-start(bf16[512,256]{1,0:T(8,128)(2,1)S(1)} %dynamic_slice.15), channel_id=1, source_target_pairs={{0,8},{8,16},{16,24},{24,28},{28,20},{20,12},{12,4},{4,0},{1,9},{9... | collective-permute-start | bytes 786440 | tf_op jit(solution)/shard_map/ppermute | solution.py:566
  2.0 7.7 %collective-permute-start.5 = (bf16[512,256]{1,0:T(8,128)(2,1)S(1)}, bf16[512,256]{1,0:T(8,128)(2,1)S(1)}, u32[]{:S(2)}, u32[]{:S(2)}) collective-permute-start(bf16[512,256]{1,0:T(8,128)(2,1)S(1)} %dynamic_slice.15), channel_id=1, source_target_pairs={{0,4},{8,0},{16,8},{24,16},{28,24},{20,28},{12,20},{4,12},{1,5},{9... | collective-permute-start | bytes 786440 | tf_op jit(solution)/shard_map/ppermute | solution.py:566
  4.4 10.8 %collective-permute-start.14 = (bf16[512,256]{1,0:T(8,128)(2,1)S(1)}, bf16[512,256]{1,0:T(8,128)(2,1)S(1)}, u32[]{:S(2)}, u32[]{:S(2)}) collective-permute-start(bf16[512,256]{1,0:T(8,128)(2,1)S(1)} %get-tuple-element.14), channel_id=1, source_target_pairs={{0,8},{8,16},{16,24},{24,28},{28,20},{20,12},{12,4},{4,0},{1,9},{9... | collective-permute-start | bytes 786440 | tf_op jit(solution)/shard_map/ppermute | solution.py:566
  4.6 16.2 %collective-permute-start.15 = (bf16[512,256]{1,0:T(8,128)(2,1)S(1)}, bf16[512,256]{1,0:T(8,128)(2,1)}, u32[]{:S(2)}, u32[]{:S(2)}) collective-permute-start(bf16[512,256]{1,0:T(8,128)(2,1)S(1)} %get-tuple-element.13), channel_id=1, source_target_pairs={{0,8},{8,16},{16,24},{24,28},{28,20},{20,12},{12,4},{4,0},{1,9},{9... | collective-permute-start | bytes 786440 | tf_op jit(solution)/shard_map/ppermute | solution.py:566
  9.5 11.6 %collective-permute-start.17 = (bf16[512,256]{1,0:T(8,128)(2,1)S(1)}, bf16[512,256]{1,0:T(8,128)(2,1)}, u32[]{:S(2)}, u32[]{:S(2)}) collective-permute-start(bf16[512,256]{1,0:T(8,128)(2,1)S(1)} %get-tuple-element.14), channel_id=1, source_target_pairs={{0,4},{8,0},{16,8},{24,16},{28,24},{20,28},{12,20},{4,12},{1,5},{9... | collective-permute-start | bytes 786440 | tf_op jit(solution)/shard_map/ppermute | solution.py:566
  9.7 11.6 %collective-permute-start.18 = (bf16[512,256]{1,0:T(8,128)(2,1)S(1)}, bf16[512,256]{1,0:T(8,128)(2,1)S(1)}, u32[]{:S(2)}, u32[]{:S(2)}) collective-permute-start(bf16[512,256]{1,0:T(8,128)(2,1)S(1)} %get-tuple-element.13), channel_id=1, source_target_pairs={{0,4},{8,0},{16,8},{24,16},{28,24},{20,28},{12,20},{4,12},{1,5},{9... | collective-permute-start | bytes 786440 | tf_op jit(solution)/shard_map/ppermute | solution.py:566
  15.2 11.2 %collective-permute-start.2 = (bf16[512,256]{1,0:T(8,128)(2,1)S(1)}, bf16[512,256]{1,0:T(8,128)(2,1)}, u32[]{:S(2)}, u32[]{:S(2)}) collective-permute-start(bf16[512,256]{1,0:T(8,128)(2,1)S(1)} %collective-permute-done.1.refs_2_), channel_id=1, source_target_pairs={{0,8},{8,16},{16,24},{24,28},{28,20},{20,12},{12,4},{4,0},{1,9},{9... | collective-permute-start | bytes 786440 | tf_op jit(solution)/shard_map/ppermute | solution.py:566
  21.3 11.2 %collective-permute-start.16 = (bf16[512,256]{1,0:T(8,128)(2,1)S(1)}, bf16[512,256]{1,0:T(8,128)(2,1)}, u32[]{:S(2)}, u32[]{:S(2)}) collective-permute-start(bf16[512,256]{1,0:T(8,128)(2,1)S(1)} %collective-permute-done.5.refs_6_), channel_id=1, source_target_pairs={{0,2},{1,3},{2,0},{3,1},{4,6},{5,7},{6,4},{7,5},{8,10},{9,11},{10,... | collective-permute-start | bytes 786440 | tf_op jit(solution)/shard_map/ppermute | solution.py:560
  26.4 7.4 %collective-permute-start.20 = (bf16[512,256]{1,0:T(8,128)(2,1)S(1)}, bf16[512,256]{1,0:T(8,128)(2,1)}, u32[]{:S(2)}, u32[]{:S(2)}) collective-permute-start(bf16[512,256]{1,0:T(8,128)(2,1)S(1)} %collective-permute-done.14.refs_4_), channel_id=1, source_target_pairs={{0,8},{8,16},{16,24},{24,28},{28,20},{20,12},{12,4},{4,0},{1,9},{9... | collective-permute-start | bytes 786440 | tf_op jit(solution)/shard_map/ppermute | solution.py:566
  27.0 11.8 %collective-permute-start.21 = (bf16[512,256]{1,0:T(8,128)(2,1)}, bf16[512,256]{1,0:T(8,128)(2,1)S(1)}, u32[]{:S(2)}, u32[]{:S(2)}) collective-permute-start(bf16[512,256]{1,0:T(8,128)(2,1)} %collective-permute-done.15.refs_5_), channel_id=1, source_target_pairs={{0,8},{8,16},{16,24},{24,28},{28,20},{20,12},{12,4},{4,0},{1,9},{9... | collective-permute-start | bytes 786440 | tf_op jit(solution)/shard_map/ppermute | solution.py:566
  27.1 11.9 %collective-permute-start.23 = (bf16[512,256]{1,0:T(8,128)(2,1)}, bf16[512,256]{1,0:T(8,128)(2,1)S(1)}, u32[]{:S(2)}, u32[]{:S(2)}) collective-permute-start(bf16[512,256]{1,0:T(8,128)(2,1)} %collective-permute-done.17.refs_8_), channel_id=1, source_target_pairs={{0,4},{8,0},{16,8},{24,16},{28,24},{20,28},{12,20},{4,12},{1,5},{9... | collective-permute-start | bytes 786440 | tf_op jit(solution)/shard_map/ppermute | solution.py:566
  32.6 11.9 %collective-permute-start.3 = (bf16[512,256]{1,0:T(8,128)(2,1)}, bf16[512,256]{1,0:T(8,128)(2,1)S(1)}, u32[]{:S(2)}, u32[]{:S(2)}) collective-permute-start(bf16[512,256]{1,0:T(8,128)(2,1)} %collective-permute-done.2.refs_10_), channel_id=1, source_target_pairs={{0,8},{8,16},{16,24},{24,28},{28,20},{20,12},{12,4},{4,0},{1,9},{9... | collective-permute-start | bytes 786440 | tf_op jit(solution)/shard_map/ppermute | solution.py:566
  33.8 11.9 %collective-permute-start.7 = (bf16[512,256]{1,0:T(8,128)(2,1)}, bf16[512,256]{1,0:T(8,128)(2,1)S(1)}, u32[]{:S(2)}, u32[]{:S(2)}) collective-permute-start(bf16[512,256]{1,0:T(8,128)(2,1)} %copy-done.10), channel_id=1, source_target_pairs={{0,4},{8,0},{16,8},{24,16},{28,24},{20,28},{12,20},{4,12},{1,5},{9... | collective-permute-start | bytes 786440 | tf_op jit(solution)/shard_map/ppermute | solution.py:566
  38.8 9.3 %collective-permute-start.24 = (bf16[512,256]{1,0:T(8,128)(2,1)}, bf16[512,256]{1,0:T(8,128)(2,1)}, u32[]{:S(2)}, u32[]{:S(2)}) collective-permute-start(bf16[512,256]{1,0:T(8,128)(2,1)} %copy-done.9), channel_id=1, source_target_pairs={{0,4},{8,0},{16,8},{24,16},{28,24},{20,28},{12,20},{4,12},{1,5},{9... | collective-permute-start | bytes 786440 | tf_op jit(solution)/shard_map/ppermute | solution.py:566
  39.1 10.0 %collective-permute-start.19 = (bf16[512,256]{1,0:T(8,128)(2,1)}, bf16[512,256]{1,0:T(8,128)(2,1)S(1)}, u32[]{:S(2)}, u32[]{:S(2)}) collective-permute-start(bf16[512,256]{1,0:T(8,128)(2,1)} %collective-permute-done.2.refs_10_), channel_id=1, source_target_pairs={{0,2},{1,3},{2,0},{3,1},{4,6},{5,7},{6,4},{7,5},{8,10},{9,11},{10,... | collective-permute-start | bytes 786440 | tf_op jit(solution)/shard_map/ppermute | solution.py:560
  44.4 8.5 %collective-permute-start.22 = (bf16[512,256]{1,0:T(8,128)(2,1)}, bf16[512,256]{1,0:T(8,128)(2,1)S(1)}, u32[]{:S(2)}, u32[]{:S(2)}) collective-permute-start(bf16[512,256]{1,0:T(8,128)(2,1)} %copy-done.10), channel_id=1, source_target_pairs={{0,2},{1,3},{2,0},{3,1},{4,6},{5,7},{6,4},{7,5},{8,10},{9,11},{10,... | collective-permute-start | bytes 786440 | tf_op jit(solution)/shard_map/ppermute | solution.py:560
  45.7 8.4 %collective-permute-start.28 = (bf16[512,256]{1,0:T(8,128)(2,1)}, bf16[512,256]{1,0:T(8,128)(2,1)S(1)}, u32[]{:S(2)}, u32[]{:S(2)}) collective-permute-start(bf16[512,256]{1,0:T(8,128)(2,1)} %collective-permute-done.20.refs_12_), channel_id=1, source_target_pairs={{0,8},{8,16},{16,24},{24,28},{28,20},{20,12},{12,4},{4,0},{1,9},{9... | collective-permute-start | bytes 786440 | tf_op jit(solution)/shard_map/ppermute | solution.py:566
  48.1 11.3 %collective-permute-start.30 = (bf16[512,256]{1,0:T(8,128)(2,1)}, bf16[512,256]{1,0:T(8,128)(2,1)}, u32[]{:S(2)}, u32[]{:S(2)}) collective-permute-start(bf16[512,256]{1,0:T(8,128)(2,1)} %collective-permute-done.24.refs_17_), channel_id=1, source_target_pairs={{0,4},{8,0},{16,8},{24,16},{28,24},{20,28},{12,20},{4,12},{1,5},{9... | collective-permute-start | bytes 786440 | tf_op jit(solution)/shard_map/ppermute | solution.py:566
  54.1 12.4 %collective-permute-start.4 = (bf16[512,256]{1,0:T(8,128)(2,1)S(1)}, bf16[512,256]{1,0:T(8,128)(2,1)S(1)}, u32[]{:S(2)}, u32[]{:S(2)}) collective-permute-start(bf16[512,256]{1,0:T(8,128)(2,1)S(1)} %collective-permute-done.3.refs_0_), channel_id=1, source_target_pairs={{0,2},{1,3},{2,0},{3,1},{4,6},{5,7},{6,4},{7,5},{8,10},{9,11},{10,... | collective-permute-start | bytes 786440 | tf_op jit(solution)/shard_map/ppermute | solution.py:560
  55.7 7.7 %collective-permute-start.11 = (bf16[256,256]{1,0:T(8,128)(2,1)S(1)}, bf16[256,256]{1,0:T(8,128)(2,1)S(1)}, u32[]{:S(2)}, u32[]{:S(2)}) collective-permute-start(bf16[256,256]{1,0:T(8,128)(2,1)S(1)} %collective-permute-done.9.refs_4_), channel_id=1, source_target_pairs={{0,2},{1,3},{2,0},{3,1},{4,6},{5,7},{6,4},{7,5},{8,10},{9,11},{10,... | collective-permute-start | bytes 393224 | tf_op jit(solution)/shard_map/ppermute | solution.py:560
  59.4 16.8 %collective-permute-start.8 = (bf16[512,256]{1,0:T(8,128)(2,1)S(1)}, bf16[512,256]{1,0:T(8,128)(2,1)S(1)}, u32[]{:S(2)}, u32[]{:S(2)}) collective-permute-start(bf16[512,256]{1,0:T(8,128)(2,1)S(1)} %collective-permute-done.7.refs_2_), channel_id=1, source_target_pairs={{0,2},{1,3},{2,0},{3,1},{4,6},{5,7},{6,4},{7,5},{8,10},{9,11},{10,... | collective-permute-start | bytes 786440 | tf_op jit(solution)/shard_map/ppermute | solution.py:560
  63.5 20.5 %collective-permute-start.32 = (bf16[512,256]{1,0:T(8,128)(2,1)S(1)}, bf16[512,256]{1,0:T(8,128)(2,1)S(1)}, u32[]{:S(2)}, u32[]{:S(2)}) collective-permute-start(bf16[512,256]{1,0:T(8,128)(2,1)S(1)} %copy-done.14), channel_id=1, source_target_pairs={{0,4},{8,0},{16,8},{24,16},{28,24},{20,28},{12,20},{4,12},{1,5},{9... | collective-permute-start | bytes 786440 | tf_op jit(solution)/shard_map/ppermute | solution.py:566
  65.3 18.7 %collective-permute-start.33 = (bf16[512,256]{1,0:T(8,128)(2,1)S(1)}, bf16[512,256]{1,0:T(8,128)(2,1)S(1)}, u32[]{:S(2)}, u32[]{:S(2)}) collective-permute-start(bf16[512,256]{1,0:T(8,128)(2,1)S(1)} %copy-done.12), channel_id=1, source_target_pairs={{0,8},{8,16},{16,24},{24,28},{28,20},{20,12},{12,4},{4,0},{1,9},{9... | collective-permute-start | bytes 786440 | tf_op jit(solution)/shard_map/ppermute | solution.py:566
  66.4 23.3 %collective-permute-start.29 = (bf16[512,256]{1,0:T(8,128)(2,1)}, bf16[512,256]{1,0:T(8,128)(2,1)S(1)}, u32[]{:S(2)}, u32[]{:S(2)}) collective-permute-start(bf16[512,256]{1,0:T(8,128)(2,1)} %copy-done.21), channel_id=1, source_target_pairs={{0,8},{8,16},{16,24},{24,28},{28,20},{20,12},{12,4},{4,0},{1,9},{9... | collective-permute-start | bytes 786440 | tf_op jit(solution)/shard_map/ppermute | solution.py:566
  66.5 23.3 %collective-permute-start.31 = (bf16[512,256]{1,0:T(8,128)(2,1)}, bf16[512,256]{1,0:T(8,128)(2,1)S(1)}, u32[]{:S(2)}, u32[]{:S(2)}) collective-permute-start(bf16[512,256]{1,0:T(8,128)(2,1)} %collective-permute-done.30.refs_3_), channel_id=1, source_target_pairs={{0,4},{8,0},{16,8},{24,16},{28,24},{20,28},{12,20},{4,12},{1,5},{9... | collective-permute-start | bytes 786440 | tf_op jit(solution)/shard_map/ppermute | solution.py:566
  82.7 20.9 %collective-permute-start.26 = (bf16[512,256]{1,0:T(8,128)(2,1)}, bf16[512,256]{1,0:T(8,128)(2,1)S(1)}, u32[]{:S(2)}, u32[]{:S(2)}) collective-permute-start(bf16[512,256]{1,0:T(8,128)(2,1)} %shard_map.73.refs_0_), channel_id=1, source_target_pairs={{0,2},{1,3},{4,6},{5,7},{8,10},{9,11},{12,14},{13,15},{16,18},{17,... | collective-permute-start | bytes 786440 | tf_op jit(solution)/shard_map/ppermute | solution.py:563
  95.1 8.9 %collective-permute-start.35 = (bf16[512,256]{1,0:T(8,128)(2,1)}, bf16[512,256]{1,0:T(8,128)(2,1)S(1)}, u32[]{:S(2)}, u32[]{:S(2)}) collective-permute-start(bf16[512,256]{1,0:T(8,128)(2,1)} %shard_map.75.refs_0_), channel_id=1, source_target_pairs={{0,2},{1,3},{4,6},{5,7},{8,10},{9,11},{12,14},{13,15},{16,18},{17,... | collective-permute-start | bytes 786440 | tf_op jit(solution)/shard_map/ppermute | solution.py:563
  96.5 32.8 %collective-permute-start.25 = (bf16[512,256]{1,0:T(8,128)(2,1)S(1)}, bf16[512,256]{1,0:T(8,128)(2,1)S(1)}, u32[]{:S(2)}, u32[]{:S(2)}) collective-permute-start(bf16[512,256]{1,0:T(8,128)(2,1)S(1)} %copy-done.1), channel_id=1, source_target_pairs={{0,1},{1,0},{2,3},{3,2},{4,5},{5,4},{6,7},{7,6},{8,9},{9,8},{10,11... | collective-permute-start | bytes 786440 | tf_op jit(solution)/shard_map/ppermute | solution.py:557
  103.5 25.8 %collective-permute-start.34 = (bf16[512,256]{1,0:T(8,128)(2,1)}, bf16[512,256]{1,0:T(8,128)(2,1)S(1)}, u32[]{:S(2)}, u32[]{:S(2)}) collective-permute-start(bf16[512,256]{1,0:T(8,128)(2,1)} %shard_map.75.refs_0_), channel_id=1, source_target_pairs={{0,1},{1,0},{2,3},{3,2},{4,5},{5,4},{6,7},{7,6},{8,9},{9,8},{10,11... | collective-permute-start | bytes 786440 | tf_op jit(solution)/shard_map/ppermute | solution.py:557
  103.6 25.7 %collective-permute-start.27 = (bf16[512,256]{1,0:T(8,128)(2,1)S(1)}, bf16[512,256]{1,0:T(8,128)(2,1)S(1)}, u32[]{:S(2)}, u32[]{:S(2)}) collective-permute-start(bf16[512,256]{1,0:T(8,128)(2,1)S(1)} %collective-permute-done.26.refs_1_), channel_id=1, source_target_pairs={{0,1},{1,0},{2,3},{3,2},{4,5},{5,4},{6,7},{7,6},{8,9},{9,8},{10,11... | collective-permute-start | bytes 786440 | tf_op jit(solution)/shard_map/ppermute | solution.py:557
  104.0 25.3 %collective-permute-start.36 = (bf16[512,256]{1,0:T(8,128)(2,1)S(1)}, bf16[512,256]{1,0:T(8,128)(2,1)S(1)}, u32[]{:S(2)}, u32[]{:S(2)}) collective-permute-start(bf16[512,256]{1,0:T(8,128)(2,1)S(1)} %collective-permute-done.35.refs_1_), channel_id=1, source_target_pairs={{0,1},{1,0},{2,3},{3,2},{4,5},{5,4},{6,7},{7,6},{8,9},{9,8},{10,11... | collective-permute-start | bytes 786440 | tf_op jit(solution)/shard_map/ppermute | solution.py:557
  (40 other events, 505.1 us)

commit v5 on v3

v5 whole, which is shorter than its diff:
```python
import functools
import math

import jax
import jax.numpy as jnp
from jax import lax
from jax.experimental import pallas as pl
from jax.experimental.pallas import tpu as pltpu
from jax.sharding import PartitionSpec as P


HEAD_SIZE = 128
KEY_VALUE_HEADS = 4
BLK = 128
MASKED = -1e30
CORES = 2
CHUNK = 2 * BLK
MOST_VMEM = 67043328
LEFT_VMEM = 3 << 20

rope_base = 1000000.0


def ring_order(count):
    return list(range(0, count, 2)) + list(range(count - 1, 0, -2))


def rope_tables(token_positions):
    half_dim = HEAD_SIZE // 2
    frequency = rope_base ** (
        -(jnp.arange(half_dim, dtype=jnp.float32) * 2.0 / HEAD_SIZE)
    )
    angles = token_positions.astype(jnp.float32)[:, None] * frequency[None, :]
    cos_part, sine_part = jnp.cos(angles), jnp.sin(angles)
    return jnp.concatenate([cos_part, cos_part, -sine_part, sine_part], axis=1)


def main_kernel(copies, early, late, facts, own_ref, sibling_ref, bias_hbm, table_hbm, *refs):
    piece_refs = refs[:-10]
    key_ref, value_ref, token_ref, weight_ref, acc_ref = refs[-10:-5]
    bias_ref, table_ref, token_sems, weight_sems, other_sems = refs[-5:]
    number_of_rows, depth = own_ref.shape[0], weight_ref.shape[1]
    width = weight_ref.shape[2] // 2
    strip = depth // 2
    others = [
        pltpu.make_async_copy(bias_hbm, bias_ref, other_sems.at[0]),
        pltpu.make_async_copy(table_hbm, table_ref, other_sems.at[1]),
    ]
    for shard in range(early + late):
        for operand, at, side, offset, lane in copies:
            if at != shard:
                continue
            row = offset
            if side >= 0:
                plane = facts[0] if side == 0 else 1 - facts[0]
                row = pl.multiple_of(plane * strip + offset, strip // 2)
            pltpu.make_async_copy(
                piece_refs[operand],
                weight_ref.at[
                    shard, pl.ds(row, piece_refs[operand].shape[0]), pl.ds(lane, width)
                ],
                weight_sems.at[shard],
            ).start()
        columns = pl.ds(pl.multiple_of(facts[1 + shard] * depth, depth), depth)
        for half, tokens_ref in enumerate((own_ref, sibling_ref)):
            pltpu.make_async_copy(
                tokens_ref.at[:, columns],
                token_ref.at[shard, pl.ds(half * number_of_rows, number_of_rows), :],
                token_sems.at[shard],
            ).start()
    for copy in others:
        copy.start()
    acc_ref[...] = jnp.zeros_like(acc_ref)

    def add_shard(shard, lanes):
        strips = weight_ref.at[shard, :, pl.ds(0, lanes)]
        pltpu.make_async_copy(strips, strips, weight_sems.at[shard]).wait()
        pltpu.make_async_copy(
            token_ref.at[shard], token_ref.at[shard], token_sems.at[shard]
        ).wait()
        acc_ref[:, :lanes] += jnp.dot(
            token_ref[shard], weight_ref[shard, :, :lanes], preferred_element_type=jnp.float32
        )

    @pl.loop(0, early)
    def _(shard):
        add_shard(shard, 2 * width)

    for copy in others:
        copy.wait()
    value_ref[...] = acc_ref[:, width:] + bias_ref[:, width:]

    @pl.loop(early, early + late)
    def _(shard):
        add_shard(shard, width)

    for first in range(0, width, HEAD_SIZE):
        lanes = slice(first, first + HEAD_SIZE)
        head = acc_ref[:, lanes] + bias_ref[:, lanes]
        turned = head * table_ref[:, :HEAD_SIZE]
        turned += pltpu.roll(head, HEAD_SIZE // 2, 1) * table_ref[:, HEAD_SIZE:]
        key_ref[:, lanes] = turned.astype(key_ref.dtype)


def project_main(own_tokens, sibling_tokens, bias, table, pieces, copies, sources, early, plane):
    shards = len(sources)
    depth = own_tokens.shape[1] // shards
    chip_rows = CORES * own_tokens.shape[0]
    width = pieces[0].shape[1]
    facts = jnp.stack([plane, *sources]).astype(jnp.int32)
    out_spec = pl.BlockSpec((chip_rows, width), lambda p, b: (0, 0))
    anywhere = pl.BlockSpec(memory_space=pltpu.MemorySpace.HBM)
    return pl.pallas_call(
        functools.partial(main_kernel, tuple(copies), early, shards - early),
        out_shape=(
            jax.ShapeDtypeStruct((chip_rows, width), jnp.bfloat16),
            jax.ShapeDtypeStruct((chip_rows, width), jnp.float32),
        ),
        grid_spec=pltpu.PrefetchScalarGridSpec(
            num_scalar_prefetch=1,
            grid=(1,),
            in_specs=[anywhere] * (4 + len(pieces)),
            out_specs=(out_spec, out_spec),
            scratch_shapes=[
                pltpu.VMEM((shards, chip_rows, depth), jnp.bfloat16),
                pltpu.VMEM((shards, depth, 2 * width), jnp.bfloat16),
                pltpu.VMEM((chip_rows, 2 * width), jnp.float32),
                pltpu.VMEM(bias.shape, jnp.float32),
                pltpu.VMEM(table.shape, jnp.float32),
                pltpu.SemaphoreType.DMA((shards,)),
                pltpu.SemaphoreType.DMA((shards,)),
                pltpu.SemaphoreType.DMA((2,)),
            ],
        ),
        compiler_params=pltpu.CompilerParams(vmem_limit_bytes=MOST_VMEM - LEFT_VMEM),
        cost_estimate=pl.CostEstimate(
            flops=2 * (shards + early) * depth * chip_rows * width,
            bytes_accessed=2 * shards * depth * (chip_rows + width),
            transcendentals=0,
        ),
        name="project_main",
    )(facts, own_tokens, sibling_tokens, bias, table, *pieces)


class Blocks:
    def __init__(self, facts, hops, row_blocks, row_block):
        self.row_blocks, self.source_core = row_blocks, facts[1]
        per_chip = CORES * row_blocks
        chip = facts[2] // CORES
        here = facts[2] * row_blocks + row_block
        segment = facts[3 + here]
        self.diagonal = lax.rem(here, per_chip)
        self.entries, slot = [], jnp.int32(0)
        for hop in range(hops):
            for local in range(per_chip):
                block = (chip - hop) * per_chip + local
                seen = facts[3 + jnp.maximum(block, 0)]
                allowed = (block >= 0) & (block < here) & ((seen == 0) | (seen == segment))
                self.entries.append((hop, local, allowed, slot))
                slot = slot + jnp.where(allowed, 1, 0)
        self.odd = lax.rem(slot, 2) == 1
        self.free_slot = slot
        self.chunks = (slot + 2) // 2

    def place(self, local):
        core = local // self.row_blocks
        slot = jnp.where(core == self.source_core, 0, self.row_blocks)
        slot = slot + lax.rem(local, self.row_blocks)
        return pl.ds(pl.multiple_of(slot * BLK, BLK), BLK)

    def gather(self, refs, chosen_ref):
        def slot_rows(slot):
            return pl.ds(pl.multiple_of(slot * BLK, BLK), BLK)

        for hop, local, allowed, slot in self.entries:

            @pl.when(allowed)
            def _(hop=hop, local=local, slot=slot):
                chosen_ref[slot_rows(slot), :] = refs[hop][self.place(jnp.int32(local)), :]

        @pl.when(jnp.logical_not(self.odd))
        def _():
            chosen_ref[slot_rows(self.free_slot), :] = jnp.zeros((BLK, HEAD_SIZE), jnp.bfloat16)

        chosen_ref[slot_rows(2 * self.chunks - 1), :] = refs[0][self.place(self.diagonal), :]


def chunk_rows(chunk):
    return pl.ds(pl.multiple_of(chunk * CHUNK, CHUNK), CHUNK)


def find_scores(blocks, group, q_ref, key_ref, score_ref, peak_ref):
    rows = group * BLK

    def scores(chunk):
        heads = [q_ref[:, h * HEAD_SIZE : (h + 1) * HEAD_SIZE] for h in range(group)]
        return lax.dot_general(
            jnp.concatenate(heads, axis=0),
            key_ref[chunk_rows(chunk), :],
            (((1,), (1,)), ((), ())),
            preferred_element_type=jnp.float32,
        )

    last = blocks.chunks - 1
    column = lax.broadcasted_iota(jnp.int32, (rows, CHUNK), 1)
    row = lax.broadcasted_iota(jnp.int32, (rows, CHUNK), 0) % BLK
    first_column = jnp.where(blocks.odd, 0, BLK)
    found = jnp.where(
        (column >= first_column) & (column - BLK <= row), scores(last), MASKED
    )
    score_ref[last] = found
    peak_ref[...] = jnp.maximum(found[:, :BLK], found[:, BLK:])

    @pl.loop(0, last)
    def _(chunk):
        found = scores(chunk)
        score_ref[chunk] = found
        peak_ref[...] = jnp.maximum(
            peak_ref[...], jnp.maximum(found[:, :BLK], found[:, BLK:])
        )

    peak_ref[...] = jnp.broadcast_to(
        jnp.max(peak_ref[...], axis=1, keepdims=True), (rows, BLK)
    )


def weights_of(chunk, score_ref, peak_ref, total_ref):
    factor = math.log2(math.e) / math.sqrt(HEAD_SIZE)
    peak, total, halves = peak_ref[...], total_ref[...], []
    for first in range(0, CHUNK, BLK):
        probs = jnp.exp2((score_ref[chunk, :, first : first + BLK] - peak) * factor)
        halves.append(probs.astype(jnp.bfloat16))
        total = total + probs
    total_ref[...] = total
    return halves


def attend_kernel(hops, row_blocks, group, facts, q_ref, *refs):
    k_refs, v_refs = refs[:hops], refs[hops : 2 * hops]
    out_ref, key_ref, value_ref, score_ref, peak_ref, total_ref, acc_ref = refs[-7:]
    blocks = Blocks(facts, hops, row_blocks, pl.program_id(1))
    blocks.gather(k_refs, key_ref)
    find_scores(blocks, group, q_ref, key_ref, score_ref, peak_ref)
    blocks.gather(v_refs, value_ref)
    total_ref[...] = jnp.zeros_like(total_ref)
    acc_ref[...] = jnp.zeros_like(acc_ref)

    @pl.loop(0, blocks.chunks)
    def _(chunk):
        halves = weights_of(chunk, score_ref, peak_ref, total_ref)
        acc_ref[...] += jnp.dot(
            jnp.concatenate(halves, axis=1),
            value_ref[chunk_rows(chunk), :],
            preferred_element_type=jnp.float32,
        )

    mixed = (acc_ref[...] / jnp.sum(total_ref[...], axis=1, keepdims=True)).astype(out_ref.dtype)
    for h in range(group):
        out_ref[:, h * HEAD_SIZE : (h + 1) * HEAD_SIZE] = mixed[h * BLK : (h + 1) * BLK]


class Attention:
    def __init__(self, facts, queries, hops):
        self.facts, self.queries, self.hops = facts, queries, hops
        self.rows, query_width = queries.shape
        self.group = query_width // HEAD_SIZE // KEY_VALUE_HEADS
        self.heads = KEY_VALUE_HEADS // CORES
        self.row_blocks = self.rows // BLK
        self.stacked = self.group * BLK
        self.chunks = hops * CORES * self.row_blocks * BLK // CHUNK
        self.q_spec = pl.BlockSpec(
            (BLK, self.group * HEAD_SIZE), lambda l, r, f: (r, f[0] * self.heads + l)
        )
        self.kv_spec = pl.BlockSpec((CORES * self.rows, HEAD_SIZE), lambda l, r, f: (0, l))
        self.pairs = self.heads * self.row_blocks * self.stacked * self.chunks * CHUNK // 2

    def attend(self, keys, values, before):
        operands = [self.facts, self.queries, *keys, *values]
        in_specs = [self.q_spec] + [self.kv_spec] * (2 * self.hops)
        aliases = {}
        if before is not None:
            aliases = {len(operands): 0}
            operands.append(before)
            in_specs.append(pl.BlockSpec(memory_space=pl.ANY))
        chosen = pltpu.VMEM((self.chunks * CHUNK, HEAD_SIZE), jnp.bfloat16)
        tall = pltpu.VMEM((self.stacked, BLK), jnp.float32)
        return pl.pallas_call(
            functools.partial(attend_kernel, self.hops, self.row_blocks, self.group),
            out_shape=jax.ShapeDtypeStruct(self.queries.shape, self.queries.dtype),
            grid_spec=pltpu.PrefetchScalarGridSpec(
                num_scalar_prefetch=1,
                grid=(self.heads, self.row_blocks),
                in_specs=in_specs,
                out_specs=self.q_spec,
                scratch_shapes=[
                    chosen,
                    chosen,
                    pltpu.VMEM((self.chunks, self.stacked, CHUNK), jnp.float32),
                    tall,
                    tall,
                    tall,
                ],
            ),
            input_output_aliases=aliases,
            compiler_params=pltpu.CompilerParams(
                vmem_limit_bytes=MOST_VMEM - LEFT_VMEM
            ),
            cost_estimate=pl.CostEstimate(
                flops=4 * self.pairs * HEAD_SIZE,
                bytes_accessed=2 * self.queries.size,
                transcendentals=self.pairs,
            ),
            name="attend",
        )(*operands)


def layer(
    hidden_in,
    queries,
    key_projection_weight,
    value_projection_weight,
    key_projection_bias,
    value_projection_bias,
    block_segments,
):
    own_tokens = hidden_in[0]
    number_of_rows = own_tokens.shape[0]
    depth, kv_width = key_projection_weight.shape
    dp_size, ctx_size = lax.axis_size("dp"), lax.axis_size("ctx")
    chips = ctx_size // CORES
    my_index = lax.axis_index("ctx")
    core, chip = my_index % CORES, my_index // CORES
    plane = chip % 2
    half_width = kv_width // CORES
    ring = ring_order(dp_size)
    dp_index = lax.axis_index("dp")
    my_spot = jnp.where(dp_index % 2 == 0, dp_index // 2, dp_size - (dp_index + 1) // 2)

    def to_sibling(x):
        return lax.ppermute(x, "ctx", [(i, i ^ 1) for i in range(ctx_size)])

    def to_plane(x):
        return lax.ppermute(x, "ctx", [(i, i ^ CORES) for i in range(ctx_size)])

    def to_next_chip(x):
        return lax.ppermute(x, "ctx", [(i, i + CORES) for i in range(ctx_size - CORES)])

    def along_ring(x, step):
        return lax.ppermute(
            x, "dp", [(ring[i], ring[(i + step) % dp_size]) for i in range(dp_size)]
        )

    key_weight = lax.dynamic_slice_in_dim(key_projection_weight, core * half_width, half_width, 1)
    value_weight = lax.dynamic_slice_in_dim(
        value_projection_weight, core * half_width, half_width, 1
    )
    strip = depth // 2
    part = strip // 2
    key_strip = lax.dynamic_slice_in_dim(key_weight, plane * strip, strip, 0)
    sibling_tokens = to_sibling(own_tokens)

    def source_at(distance):
        spot = (my_spot + distance + dp_size) % dp_size
        return jnp.where(spot < dp_size // 2, 2 * spot, 2 * (dp_size - spot) - 1)

    half_ring = dp_size // 2

    arange = jnp.arange(number_of_rows, dtype=jnp.int32)
    positions = jnp.concatenate(
        [my_index * number_of_rows + arange, (my_index ^ 1) * number_of_rows + arange]
    )
    key_bias = lax.dynamic_slice_in_dim(key_projection_bias, core * half_width, half_width, 0)
    value_bias = lax.dynamic_slice_in_dim(value_projection_bias, core * half_width, half_width, 0)

    key_arrived, value_arrived = {}, {}
    travelling = {1: key_strip, -1: key_strip}
    for hop in range(1, half_ring + 1):
        for step in (1, -1):
            piece = travelling[step]
            if hop == half_ring:
                first_row = 0 if step == 1 else part
                piece = piece[first_row : first_row + part]
            piece = along_ring(piece, step)
            other = to_plane(piece)
            travelling[step] = piece
            key_arrived[hop, step] = (piece, other)

    travelling = {
        (side, step): value_weight[side * strip : (side + 1) * strip]
        for side in range(2)
        for step in (1, -1)
    }
    for hop in range(1, half_ring + 1):
        for side in range(2):
            for step in (1, -1):
                if hop == half_ring and step != (1, -1)[side]:
                    continue
                piece = along_ring(travelling[side, step], step)
                travelling[side, step] = piece
                value_arrived[hop, step, side] = piece

    early = half_ring - 2
    distances = list(range(-early, early + 1)) + [-half_ring + 1, half_ring - 1, half_ring]
    pieces = [key_weight, value_weight]
    copies = [(0, early, -1, 0, 0), (1, early, -1, 0, half_width)]
    for hop in range(1, half_ring + 1):
        for step in (1, -1):
            shard = distances.index(half_ring if hop == half_ring else -step * hop)
            offset = part if hop == half_ring and step == -1 else 0
            for side, piece in enumerate(key_arrived[hop, step]):
                copies.append((len(pieces), shard, side, offset, 0))
                pieces.append(piece)
            if hop <= early:
                for side in range(2):
                    copies.append((len(pieces), shard, -1, side * strip, half_width))
                    pieces.append(value_arrived[hop, step, side])
    key_rows, value_proj = project_main(
        own_tokens,
        sibling_tokens,
        jnp.concatenate([key_bias, value_bias])[None],
        rope_tables(positions),
        pieces,
        copies,
        [source_at(distance) for distance in distances],
        2 * early + 1,
        plane,
    )

    def picked(source):
        return jnp.concatenate(
            [
                lax.dynamic_slice_in_dim(tokens, source * depth, depth, 1)
                for tokens in (own_tokens, sibling_tokens)
            ],
            axis=0,
        )

    def late_product(columns, side, piece):
        return jnp.dot(
            columns[:, side * strip : (side + 1) * strip],
            piece,
            preferred_element_type=jnp.float32,
        )

    columns = {hop: picked(source_at(hop)) for hop in distances[-3:]}
    for step in (1, -1):
        for side in range(2):
            hop = half_ring - 1
            value_proj += late_product(columns[-step * hop], side, value_arrived[hop, step, side])
    for side, step in enumerate((1, -1)):
        value_proj += late_product(columns[half_ring], side, value_arrived[half_ring, step, side])
    value_rows = value_proj.astype(jnp.bfloat16)

    keys, values = [key_rows], [value_rows]
    for hop in range(1, chips):
        keys.append(to_next_chip(keys[-1]))
        values.append(to_next_chip(values[-1]))
    sibling_keys = [to_sibling(x) for x in keys]
    sibling_values = [to_sibling(x) for x in values]

    def attention(half):
        facts = jnp.concatenate([jnp.stack([half, half, my_index]), block_segments[0]])
        return Attention(facts, queries[0], chips)

    near, far = attention(core), attention(1 - core)
    attended = near.attend(keys, values, None)
    attended = far.attend(sibling_keys, sibling_values, attended)
    return attended[None]


def solution(mesh):
    placed = (
        P("dp", "ctx", None),
        P("dp", "ctx", None),
        P("dp", None),
        P("dp", None),
        P(),
        P(),
        P("dp", None),
    )
    return jax.shard_map(
        layer, mesh=mesh, in_specs=placed, out_specs=P("dp", "ctx", None), check_vma=False
    )
```

time: 145 us -> 133 us (0.917)
  Pallas kernels: 56.2 us -> 32.2 us
  waiting for transfers between devices: 32.4 us -> 38.1 us
  matrix products: 0 us -> 3.77 us
  starting transfers between devices: 41.2 us -> 43.7 us
  local copies, waits for them, and re-layouts: 9.71 us -> 11.3 us
    pallas_call x9 -> x3, Pallas kernels: 56.2 us -> 32.2 us  [the longest x2 23.2 us: attend(): pl.pallas_call(functools.partial(attend_kernel, self.hops, self.row_block...]
    ppermute x8, waiting for transfers between devices: 9.91 us -> 16.2 us  [to_plane(): return lax.ppermute(x, 'ctx', [(i, i ^ CORES) for i in range(ctx_size)])]
    ppermute x22, starting transfers between devices: 18.1 us -> 22.3 us  [along_ring(): lax.ppermute(x, 'dp', [(ring[i], ring[(i + step) % dp_size]) for i in ran...]
    dot_general x0 -> x6, matrix products: none -> 3.77 us  [late_product(): jnp.dot(columns[:, side * strip:(side + 1) * strip], piece, preferred_ele...]
    dynamic_slice x1 -> x2, local copies, waits for them, and re-layouts: 0.83 us -> 3.01 us  [picked(): lax.dynamic_slice_in_dim(tokens, source * depth, depth, 1)]
  transfers between devices with their start and end apart: 37 -> 37, of which waited for: 11 -> 12; matrix products, arithmetic and copies ran while one was open for 8% -> 13% of each run, Pallas kernels for 35% -> 16%
where the time goes in v5:
time: 133 us
  starting transfers between devices  43.7 us (33%)
  waiting for transfers between devices  38.1 us (29%)
  Pallas kernels  32.2 us (24%)
  local copies, waits for them, and re-layouts  11.3 us (8%)
  matrix products  3.77 us (3%)
  other arithmetic  3.28 us (2%)
    pallas_call x2, Pallas kernels, attend(): pl.pallas_call(functools.partial(attend_kernel, self.hops, self.row_block...  23.2 us
    ppermute x22, starting transfers between devices, along_ring(): lax.ppermute(x, 'dp', [(ring[i], ring[(i + step) % dp_size]) for i in ran...  22.3 us
    ppermute x22, waiting for transfers between devices, along_ring(): lax.ppermute(x, 'dp', [(ring[i], ring[(i + step) % dp_size]) for i in ran...  21.4 us
    ppermute x8, waiting for transfers between devices, to_plane(): return lax.ppermute(x, 'ctx', [(i, i ^ CORES) for i in range(ctx_size)])  16.2 us
    ppermute x5, starting transfers between devices, to_sibling(): return lax.ppermute(x, 'ctx', [(i, i ^ 1) for i in range(ctx_size)])  13.8 us
    pallas_call x1, Pallas kernels, project_main(): pl.pallas_call(functools.partial(main_kernel, tuple(copies), early, shard...  9.05 us
    ppermute x8, starting transfers between devices, to_plane(): return lax.ppermute(x, 'ctx', [(i, i ^ CORES) for i in range(ctx_size)])  5.03 us
    dot_general x6, matrix products, late_product(): jnp.dot(columns[:, side * strip:(side + 1) * strip], piece, preferred_ele...  3.77 us
  transfers between devices with their start and end apart: 37, of which 12 were waited for; matrix products, arithmetic and copies ran while one was open for 13% of the time, Pallas kernels for 16%

profile of v5, /device:TPU:5, one launch (start us, length us, event | category | flops | bytes accessed | tf_op | source)
XLA Modules:
  0.0 132.8 jit_solution(13838619494625693537)
XLA Ops:
  1.8 1.3 %collective-permute-start.1 = (bf16[512,256]{1,0:T(8,128)(2,1)S(1)}, bf16[512,256]{1,0:T(8,128)(2,1)S(1)}, u32[]{:S(2)}, u32[]{:S(2)}) collective-permute-start(bf16[512,256]{1,0:T(8,128)(2,1)S(1)} %dynamic_slice.43), channel_id=1, source_target_pairs={{0,8},{8,16},{16,24},{24,28},{28,20},{20,12},{12,4},{4,0},{1,9},{9... | collective-permute-start | bytes 786440 | tf_op jit(solution)/shard_map/ppermute | solution.py:349
  4.4 1.3 %collective-permute-start.3 = (bf16[512,256]{1,0:T(8,128)(2,1)S(1)}, bf16[512,256]{1,0:T(8,128)(2,1)S(1)}, u32[]{:S(2)}, u32[]{:S(2)}) collective-permute-start(bf16[512,256]{1,0:T(8,128)(2,1)S(1)} %get-tuple-element.16), channel_id=1, source_target_pairs={{0,8},{8,16},{16,24},{24,28},{28,20},{20,12},{12,4},{4,0},{1,9},{9... | collective-permute-start | bytes 786440 | tf_op jit(solution)/shard_map/ppermute | solution.py:349
  5.7 1.3 collective-permute-start.4
  7.0 2.5 %collective-permute-done.1.refs_2_ = bf16[512,256]{1,0:T(8,128)(2,1)S(1)} collective-permute-done((bf16[512,256]{1,0:T(8,128)(2,1)S(1)}, bf16[512,256]{1,0:T(8,128)(2,1)S(1)}, u32[]{:S(2)}, u32[]{:S(2)}) %collective-permute-start.1) | collective-permute-done | bytes 262176 | tf_op jit(solution)/shard_map/ppermute | solution.py:349
  10.8 1.3 collective-permute-start.8
  12.1 3.1 %collective-permute-done.3.refs_4_ = bf16[512,256]{1,0:T(8,128)(2,1)S(1)} collective-permute-done((bf16[512,256]{1,0:T(8,128)(2,1)S(1)}, bf16[512,256]{1,0:T(8,128)(2,1)S(1)}, u32[]{:S(2)}, u32[]{:S(2)}) %collective-permute-start.3) | collective-permute-done | bytes 262176 | tf_op jit(solution)/shard_map/ppermute | solution.py:349
  15.2 1.3 collective-permute-start.9
  16.5 4.3 %collective-permute-done.4.refs_5_ = bf16[512,256]{1,0:T(8,128)(2,1)S(1)} collective-permute-done((bf16[512,256]{1,0:T(8,128)(2,1)S(1)}, bf16[512,256]{1,0:T(8,128)(2,1)S(1)}, u32[]{:S(2)}, u32[]{:S(2)}) %collective-permute-start.4) | collective-permute-done | bytes 262176 | tf_op jit(solution)/shard_map/ppermute | solution.py:349
  22.3 1.3 collective-permute-start.12
  23.6 2.9 %collective-permute-done.9.refs_10_ = bf16[512,256]{1,0:T(8,128)(2,1)} collective-permute-done((bf16[512,256]{1,0:T(8,128)(2,1)S(1)}, bf16[512,256]{1,0:T(8,128)(2,1)}, u32[]{:S(2)}, u32[]{:S(2)}) %collective-permute-start.9) | collective-permute-done | bytes 262176 | tf_op jit(solution)/shard_map/ppermute | solution.py:349
  27.8 1.3 collective-permute-start.16
  29.1 3.1 %collective-permute-done.11.refs_12_ = bf16[512,256]{1,0:T(8,128)(2,1)} collective-permute-done((bf16[512,256]{1,0:T(8,128)(2,1)S(1)}, bf16[512,256]{1,0:T(8,128)(2,1)}, u32[]{:S(2)}, u32[]{:S(2)}) %collective-permute-start.11) | collective-permute-done | bytes 262176 | tf_op jit(solution)/shard_map/ppermute | solution.py:349
  32.4 5.4 %collective-permute-done.12.refs_13_ = bf16[512,256]{1,0:T(8,128)(2,1)S(1)} collective-permute-done((bf16[512,256]{1,0:T(8,128)(2,1)S(1)}, bf16[512,256]{1,0:T(8,128)(2,1)S(1)}, u32[]{:S(2)}, u32[]{:S(2)}) %collective-permute-start.12) | collective-permute-done | bytes 262176 | tf_op jit(solution)/shard_map/ppermute | solution.py:349
  38.0 1.3 collective-permute-start.17
  39.8 1.5 %dynamic-slice_bitcast_fusion.2 = (bf16[256,1024]{1,0:T(8,128)(2,1)S(1)}, bf16[256,1024]{1,0:T(8,128)(2,1)S(1)}, bf16[256,1024]{1,0:T(8,128)(2,1)S(1)}) fusion(bf16[1,256,8192]{2,1,0:T(8,128)(2,1)} %param.7, s32[]{:T(128)S(6)} %select_n.145, s32[]{:T(128)S(6)} %select_n.147, s32[]{:T(128)S(6)} %select_n.146), kind=kLoop, calls=%fused_computation.26 | loop fusion | bytes 3145740 | tf_op jit(solution)/shard_map/dynamic_slice | solution.py:432
  42.4 2.5 %collective-permute-done.6.refs_7_ = bf16[512,256]{1,0:T(8,128)(2,1)S(1)} collective-permute-done((bf16[512,256]{1,0:T(8,128)(2,1)S(1)}, bf16[512,256]{1,0:T(8,128)(2,1)S(1)}, u32[]{:S(2)}, u32[]{:S(2)}) %collective-permute-start.6) | collective-permute-done | bytes 262176 | tf_op jit(solution)/shard_map/ppermute | solution.py:343
  50.4 1.3 collective-permute-start.21
  51.8 4.3 %collective-permute-done.14.refs_15_ = bf16[512,256]{1,0:T(8,128)(2,1)} collective-permute-done((bf16[512,256]{1,0:T(8,128)(2,1)}, bf16[512,256]{1,0:T(8,128)(2,1)}, u32[]{:S(2)}, u32[]{:S(2)}) %collective-permute-start.14) | collective-permute-done | bytes 262176 | tf_op jit(solution)/shard_map/ppermute | solution.py:343
  65.0 6.7 %collective-permute-done.22.refs_23_ = bf16[256,256]{1,0:T(8,128)(2,1)S(1)} collective-permute-done((bf16[256,256]{1,0:T(8,128)(2,1)S(1)}, bf16[256,256]{1,0:T(8,128)(2,1)S(1)}, u32[]{:S(2)}, u32[]{:S(2)}) %collective-permute-start.22) | collective-permute-done | bytes 131104 | tf_op jit(solution)/shard_map/ppermute | solution.py:343
  72.1 2.3 %collective-permute-done.24.refs_25_ = bf16[256,256]{1,0:T(8,128)(2,1)S(1)} collective-permute-done((bf16[256,256]{1,0:T(8,128)(2,1)}, bf16[256,256]{1,0:T(8,128)(2,1)S(1)}, u32[]{:S(2)}, u32[]{:S(2)}) %collective-permute-start.24) | collective-permute-done | bytes 131104 | tf_op jit(solution)/shard_map/ppermute | solution.py:343
  74.4 1.3 collective-permute-start.30
  75.7 1.3 collective-permute-start.33
  77.2 9.0 %project_main.1 = (bf16[512,256]{1,0:T(8,128)(2,1)}, f32[512,256]{1,0:T(8,128)}) custom-call(s32[9]{0:T(128)} %stack.53.facts, bf16[256,8192]{1,0:T(8,128)(2,1)} %bitcast.32, bf16[256,8192]{1,0:T(8,128)(2,1)} %collective-permute-done.sibling_ref, f32[1,512]{1,0:T(1,128)} %bitcast.33, f32[512,256]{1,0:T(8,128)} %pad_maximum_fusion.6.table_hbm, ...), custom_call_target="tpu_custom_call" | custom-call | flops 3489660928 | bytes 12582912 | tf_op jit(solution)/shard_map/project_main/pallas_call | solution.py:113
  86.2 1.5 %constant_dynamic-slice_fusion.3 = (bf16[256,1024]{1,0:T(8,128)(2,1)S(1)}, bf16[256,1024]{1,0:T(8,128)(2,1)S(1)}, bf16[256,1024]{1,0:T(8,128)(2,1)S(1)}) fusion(bf16[256,8192]{1,0:T(8,128)(2,1)} %collective-permute-done.sibling_ref, s32[]{:T(128)S(6)} %select_n.145, s32[]{:T(128)S(6)} %select_n.147, s32[]{:T(128)S(6)} %select_n.146), kind=kLoop, calls=%fused_computation.33 | loop fusion | bytes 3145740 | tf_op jit(solution)/shard_map/dynamic_slice | solution.py:432
  89.7 1.3 fusion.5
  91.7 1.3 collective-permute-start.35
  93.0 1.3 collective-permute-start.26
  94.3 3.9 %collective-permute-start.34 = (bf16[512,256]{1,0:T(8,128)(2,1)S(1)}, bf16[512,256]{1,0:T(8,128)(2,1)S(1)}, u32[]{:S(2)}, u32[]{:S(2)}) collective-permute-start(bf16[512,256]{1,0:T(8,128)(2,1)S(1)} %fusion.1.refs_2_), channel_id=1, source_target_pairs={{0,1},{1,0},{2,3},{3,2},{4,5},{5,4},{6,7},{7,6},{8,9},{9,8},{10,11... | collective-permute-start | bytes 786440 | tf_op jit(solution)/shard_map/ppermute | solution.py:340
  98.8 6.3 %collective-permute-start.36 = (bf16[512,256]{1,0:T(8,128)(2,1)S(1)}, bf16[512,256]{1,0:T(8,128)(2,1)S(1)}, u32[]{:S(2)}, u32[]{:S(2)}) collective-permute-start(bf16[512,256]{1,0:T(8,128)(2,1)S(1)} %collective-permute-done.35.refs_3_), channel_id=1, source_target_pairs={{0,1},{1,0},{2,3},{3,2},{4,5},{5,4},{6,7},{7,6},{8,9},{9,8},{10,11... | collective-permute-start | bytes 786440 | tf_op jit(solution)/shard_map/ppermute | solution.py:340
  105.1 2.8 %collective-permute-start.27 = (bf16[512,256]{1,0:T(8,128)(2,1)S(1)}, bf16[512,256]{1,0:T(8,128)(2,1)S(1)}, u32[]{:S(2)}, u32[]{:S(2)}) collective-permute-start(bf16[512,256]{1,0:T(8,128)(2,1)S(1)} %collective-permute-done.26.refs_1_), channel_id=1, source_target_pairs={{0,1},{1,0},{2,3},{3,2},{4,5},{5,4},{6,7},{7,6},{8,9},{9,8},{10,11... | collective-permute-start | bytes 786440 | tf_op jit(solution)/shard_map/ppermute | solution.py:340
  108.6 11.6 %attend.2.refs_4_ = bf16[256,4096]{1,0:T(8,128)(2,1)} custom-call(s32[11]{0:T(128)} %get-tuple-element.20.facts, bf16[256,4096]{1,0:T(8,128)(2,1)} %bitcast.29, bf16[512,256]{1,0:T(8,128)(2,1)} %get-tuple-element.7.refs_0_, bf16[512,256]{1,0:T(8,128)(2,1)} %copy-done.16, bf16[512,256]{1,0:T(8,128)(2,1)} %copy-done.1, bf16[512,256]{1,0:T(8,128)(2,1)} %copy-done.15), custom_call_target="tpu_custom_call" | custom-call | flops 1073741824 | bytes 2097152 | tf_op jit(solution)/shard_map/attend/pallas_call | solution.py:287
  121.2 11.6 %attend.3 = bf16[256,4096]{1,0:T(8,128)(2,1)} custom-call(s32[11]{0:T(128)} %get-tuple-element.21.facts, bf16[256,4096]{1,0:T(8,128)(2,1)} %bitcast.30, bf16[512,256]{1,0:T(8,128)(2,1)} %copy-done.18, bf16[512,256]{1,0:T(8,128)(2,1)} %copy-done.20, bf16[512,256]{1,0:T(8,128)(2,1)} %copy-done.17, ...), custom_call_target="tpu_custom_call", output_to_operand_aliasing={{}: (6, {})} | custom-call | flops 1073741824 | bytes 2097152 | tf_op jit(solution)/shard_map/attend/pallas_call | solution.py:287
  (122 shorter events, 28.8 us)
Async XLA Ops:
  0.0 77.1 %collective-permute-start = (bf16[256,8192]{1,0:T(8,128)(2,1)}, bf16[256,8192]{1,0:T(8,128)(2,1)}, u32[]{:S(2)}, u32[]{:S(2)}) collective-permute-start(bf16[256,8192]{1,0:T(8,128)(2,1)} %bitcast.31), channel_id=1, source_target_pairs={{0,1},{1,0},{2,3},{3,2},{4,5},{5,4},{6,7},{7,6},{8,9},{9,8},{10,11... | collective-permute-start | bytes 12582920 | tf_op jit(solution)/shard_map/ppermute | solution.py:340
  1.8 7.8 %collective-permute-start.1 = (bf16[512,256]{1,0:T(8,128)(2,1)S(1)}, bf16[512,256]{1,0:T(8,128)(2,1)S(1)}, u32[]{:S(2)}, u32[]{:S(2)}) collective-permute-start(bf16[512,256]{1,0:T(8,128)(2,1)S(1)} %dynamic_slice.43), channel_id=1, source_target_pairs={{0,8},{8,16},{16,24},{24,28},{28,20},{20,12},{12,4},{4,0},{1,9},{9... | collective-permute-start | bytes 786440 | tf_op jit(solution)/shard_map/ppermute | solution.py:349
  3.2 7.6 %collective-permute-start.5 = (bf16[512,256]{1,0:T(8,128)(2,1)S(1)}, bf16[512,256]{1,0:T(8,128)(2,1)S(1)}, u32[]{:S(2)}, u32[]{:S(2)}) collective-permute-start(bf16[512,256]{1,0:T(8,128)(2,1)S(1)} %dynamic_slice.43), channel_id=1, source_target_pairs={{0,4},{8,0},{16,8},{24,16},{28,24},{20,28},{12,20},{4,12},{1,5},{9... | collective-permute-start | bytes 786440 | tf_op jit(solution)/shard_map/ppermute | solution.py:349
  4.4 10.8 %collective-permute-start.3 = (bf16[512,256]{1,0:T(8,128)(2,1)S(1)}, bf16[512,256]{1,0:T(8,128)(2,1)S(1)}, u32[]{:S(2)}, u32[]{:S(2)}) collective-permute-start(bf16[512,256]{1,0:T(8,128)(2,1)S(1)} %get-tuple-element.16), channel_id=1, source_target_pairs={{0,8},{8,16},{16,24},{24,28},{28,20},{20,12},{12,4},{4,0},{1,9},{9... | collective-permute-start | bytes 786440 | tf_op jit(solution)/shard_map/ppermute | solution.py:349
  5.7 15.1 %collective-permute-start.4 = (bf16[512,256]{1,0:T(8,128)(2,1)S(1)}, bf16[512,256]{1,0:T(8,128)(2,1)S(1)}, u32[]{:S(2)}, u32[]{:S(2)}) collective-permute-start(bf16[512,256]{1,0:T(8,128)(2,1)S(1)} %get-tuple-element.15), channel_id=1, source_target_pairs={{0,8},{8,16},{16,24},{24,28},{28,20},{20,12},{12,4},{4,0},{1,9},{9... | collective-permute-start | bytes 786440 | tf_op jit(solution)/shard_map/ppermute | solution.py:349
  9.6 12.4 %collective-permute-start.7 = (bf16[512,256]{1,0:T(8,128)(2,1)S(1)}, bf16[512,256]{1,0:T(8,128)(2,1)S(1)}, u32[]{:S(2)}, u32[]{:S(2)}) collective-permute-start(bf16[512,256]{1,0:T(8,128)(2,1)S(1)} %get-tuple-element.16), channel_id=1, source_target_pairs={{0,4},{8,0},{16,8},{24,16},{28,24},{20,28},{12,20},{4,12},{1,5},{9... | collective-permute-start | bytes 786440 | tf_op jit(solution)/shard_map/ppermute | solution.py:349
  10.8 11.5 %collective-permute-start.8 = (bf16[512,256]{1,0:T(8,128)(2,1)S(1)}, bf16[512,256]{1,0:T(8,128)(2,1)S(1)}, u32[]{:S(2)}, u32[]{:S(2)}) collective-permute-start(bf16[512,256]{1,0:T(8,128)(2,1)S(1)} %get-tuple-element.15), channel_id=1, source_target_pairs={{0,4},{8,0},{16,8},{24,16},{28,24},{20,28},{12,20},{4,12},{1,5},{9... | collective-permute-start | bytes 786440 | tf_op jit(solution)/shard_map/ppermute | solution.py:349
  15.2 11.3 %collective-permute-start.9 = (bf16[512,256]{1,0:T(8,128)(2,1)S(1)}, bf16[512,256]{1,0:T(8,128)(2,1)}, u32[]{:S(2)}, u32[]{:S(2)}) collective-permute-start(bf16[512,256]{1,0:T(8,128)(2,1)S(1)} %collective-permute-done.1.refs_2_), channel_id=1, source_target_pairs={{0,8},{8,16},{16,24},{24,28},{28,20},{20,12},{12,4},{4,0},{1,9},{9... | collective-permute-start | bytes 786440 | tf_op jit(solution)/shard_map/ppermute | solution.py:349
  22.0 10.1 %collective-permute-start.11 = (bf16[512,256]{1,0:T(8,128)(2,1)S(1)}, bf16[512,256]{1,0:T(8,128)(2,1)}, u32[]{:S(2)}, u32[]{:S(2)}) collective-permute-start(bf16[512,256]{1,0:T(8,128)(2,1)S(1)} %collective-permute-done.3.refs_4_), channel_id=1, source_target_pairs={{0,8},{8,16},{16,24},{24,28},{28,20},{20,12},{12,4},{4,0},{1,9},{9... | collective-permute-start | bytes 786440 | tf_op jit(solution)/shard_map/ppermute | solution.py:349
  22.3 15.5 %collective-permute-start.12 = (bf16[512,256]{1,0:T(8,128)(2,1)S(1)}, bf16[512,256]{1,0:T(8,128)(2,1)S(1)}, u32[]{:S(2)}, u32[]{:S(2)}) collective-permute-start(bf16[512,256]{1,0:T(8,128)(2,1)S(1)} %collective-permute-done.4.refs_5_), channel_id=1, source_target_pairs={{0,8},{8,16},{16,24},{24,28},{28,20},{20,12},{12,4},{4,0},{1,9},{9... | collective-permute-start | bytes 786440 | tf_op jit(solution)/shard_map/ppermute | solution.py:349
  26.5 11.5 %collective-permute-start.15 = (bf16[512,256]{1,0:T(8,128)(2,1)S(1)}, bf16[512,256]{1,0:T(8,128)(2,1)S(1)}, u32[]{:S(2)}, u32[]{:S(2)}) collective-permute-start(bf16[512,256]{1,0:T(8,128)(2,1)S(1)} %collective-permute-done.7.refs_8_), channel_id=1, source_target_pairs={{0,4},{8,0},{16,8},{24,16},{28,24},{20,28},{12,20},{4,12},{1,5},{9... | collective-permute-start | bytes 786440 | tf_op jit(solution)/shard_map/ppermute | solution.py:349
  27.8 11.6 %collective-permute-start.16 = (bf16[512,256]{1,0:T(8,128)(2,1)S(1)}, bf16[512,256]{1,0:T(8,128)(2,1)}, u32[]{:S(2)}, u32[]{:S(2)}) collective-permute-start(bf16[512,256]{1,0:T(8,128)(2,1)S(1)} %collective-permute-done.8.refs_9_), channel_id=1, source_target_pairs={{0,4},{8,0},{16,8},{24,16},{28,24},{20,28},{12,20},{4,12},{1,5},{9... | collective-permute-start | bytes 786440 | tf_op jit(solution)/shard_map/ppermute | solution.py:349
  32.2 9.1 %collective-permute-start.2 = (bf16[512,256]{1,0:T(8,128)(2,1)S(1)}, bf16[512,256]{1,0:T(8,128)(2,1)S(1)}, u32[]{:S(2)}, u32[]{:S(2)}) collective-permute-start(bf16[512,256]{1,0:T(8,128)(2,1)S(1)} %collective-permute-done.1.refs_2_), channel_id=1, source_target_pairs={{0,2},{1,3},{2,0},{3,1},{4,6},{5,7},{6,4},{7,5},{8,10},{9,11},{10,... | collective-permute-start | bytes 786440 | tf_op jit(solution)/shard_map/ppermute | solution.py:343
  38.0 7.4 %collective-permute-start.17 = (bf16[512,256]{1,0:T(8,128)(2,1)}, bf16[512,256]{1,0:T(8,128)(2,1)}, u32[]{:S(2)}, u32[]{:S(2)}) collective-permute-start(bf16[512,256]{1,0:T(8,128)(2,1)} %collective-permute-done.9.refs_10_), channel_id=1, source_target_pairs={{0,8},{8,16},{16,24},{24,28},{28,20},{20,12},{12,4},{4,0},{1,9},{9... | collective-permute-start | bytes 786440 | tf_op jit(solution)/shard_map/ppermute | solution.py:349
  41.3 9.1 %collective-permute-start.10 = (bf16[512,256]{1,0:T(8,128)(2,1)}, bf16[512,256]{1,0:T(8,128)(2,1)}, u32[]{:S(2)}, u32[]{:S(2)}) collective-permute-start(bf16[512,256]{1,0:T(8,128)(2,1)} %collective-permute-done.9.refs_10_), channel_id=1, source_target_pairs={{0,2},{1,3},{2,0},{3,1},{4,6},{5,7},{6,4},{7,5},{8,10},{9,11},{10,... | collective-permute-start | bytes 786440 | tf_op jit(solution)/shard_map/ppermute | solution.py:343
  44.9 11.2 %collective-permute-start.14 = (bf16[512,256]{1,0:T(8,128)(2,1)}, bf16[512,256]{1,0:T(8,128)(2,1)}, u32[]{:S(2)}, u32[]{:S(2)}) collective-permute-start(bf16[512,256]{1,0:T(8,128)(2,1)} %collective-permute-done.13.refs_14_), channel_id=1, source_target_pairs={{0,2},{1,3},{2,0},{3,1},{4,6},{5,7},{6,4},{7,5},{8,10},{9,11},{10,... | collective-permute-start | bytes 786440 | tf_op jit(solution)/shard_map/ppermute | solution.py:343
  45.4 11.8 %collective-permute-start.31 = (bf16[512,256]{1,0:T(8,128)(2,1)}, bf16[512,256]{1,0:T(8,128)(2,1)}, u32[]{:S(2)}, u32[]{:S(2)}) collective-permute-start(bf16[512,256]{1,0:T(8,128)(2,1)} %collective-permute-done.16.refs_17_), channel_id=1, source_target_pairs={{0,4},{8,0},{16,8},{24,16},{28,24},{20,28},{12,20},{4,12},{1,5},{9... | collective-permute-start | bytes 786440 | tf_op jit(solution)/shard_map/ppermute | solution.py:349
  46.3 11.1 %collective-permute-start.28 = (bf16[512,256]{1,0:T(8,128)(2,1)}, bf16[512,256]{1,0:T(8,128)(2,1)S(1)}, u32[]{:S(2)}, u32[]{:S(2)}) collective-permute-start(bf16[512,256]{1,0:T(8,128)(2,1)} %collective-permute-done.11.refs_12_), channel_id=1, source_target_pairs={{0,8},{8,16},{16,24},{24,28},{28,20},{20,12},{12,4},{4,0},{1,9},{9... | collective-permute-start | bytes 786440 | tf_op jit(solution)/shard_map/ppermute | solution.py:349
  50.4 10.8 %collective-permute-start.21 = (bf16[256,256]{1,0:T(8,128)(2,1)S(1)}, bf16[256,256]{1,0:T(8,128)(2,1)S(1)}, u32[]{:S(2)}, u32[]{:S(2)}) collective-permute-start(bf16[256,256]{1,0:T(8,128)(2,1)S(1)} %slice.42), channel_id=1, source_target_pairs={{0,8},{8,16},{16,24},{24,28},{28,20},{20,12},{12,4},{4,0},{1,9},{9... | collective-permute-start | bytes 393224 | tf_op jit(solution)/shard_map/ppermute | solution.py:349
  57.2 18.5 %collective-permute-start.18 = (bf16[512,256]{1,0:T(8,128)(2,1)}, bf16[512,256]{1,0:T(8,128)(2,1)}, u32[]{:S(2)}, u32[]{:S(2)}) collective-permute-start(bf16[512,256]{1,0:T(8,128)(2,1)} %collective-permute-done.17.refs_18_), channel_id=1, source_target_pairs={{0,2},{1,3},{2,0},{3,1},{4,6},{5,7},{6,4},{7,5},{8,10},{9,11},{10,... | collective-permute-start | bytes 786440 | tf_op jit(solution)/shard_map/ppermute | solution.py:343
  57.4 19.5 %collective-permute-start.20 = (bf16[512,256]{1,0:T(8,128)(2,1)}, bf16[512,256]{1,0:T(8,128)(2,1)}, u32[]{:S(2)}, u32[]{:S(2)}) collective-permute-start(bf16[512,256]{1,0:T(8,128)(2,1)} %collective-permute-done.19.refs_20_), channel_id=1, source_target_pairs={{0,2},{1,3},{2,0},{3,1},{4,6},{5,7},{6,4},{7,5},{8,10},{9,11},{10,... | collective-permute-start | bytes 786440 | tf_op jit(solution)/shard_map/ppermute | solution.py:343
  61.3 10.4 %collective-permute-start.22 = (bf16[256,256]{1,0:T(8,128)(2,1)S(1)}, bf16[256,256]{1,0:T(8,128)(2,1)S(1)}, u32[]{:S(2)}, u32[]{:S(2)}) collective-permute-start(bf16[256,256]{1,0:T(8,128)(2,1)S(1)} %collective-permute-done.21.refs_22_), channel_id=1, source_target_pairs={{0,2},{1,3},{2,0},{3,1},{4,6},{5,7},{6,4},{7,5},{8,10},{9,11},{10,... | collective-permute-start | bytes 393224 | tf_op jit(solution)/shard_map/ppermute | solution.py:343
  61.5 12.9 %collective-permute-start.24 = (bf16[256,256]{1,0:T(8,128)(2,1)}, bf16[256,256]{1,0:T(8,128)(2,1)S(1)}, u32[]{:S(2)}, u32[]{:S(2)}) collective-permute-start(bf16[256,256]{1,0:T(8,128)(2,1)} %collective-permute-done.23.refs_24_), channel_id=1, source_target_pairs={{0,2},{1,3},{2,0},{3,1},{4,6},{5,7},{6,4},{7,5},{8,10},{9,11},{10,... | collective-permute-start | bytes 393224 | tf_op jit(solution)/shard_map/ppermute | solution.py:343
  71.7 16.4 %collective-permute-start.29 = (bf16[512,256]{1,0:T(8,128)(2,1)}, bf16[512,256]{1,0:T(8,128)(2,1)S(1)}, u32[]{:S(2)}, u32[]{:S(2)}) collective-permute-start(bf16[512,256]{1,0:T(8,128)(2,1)} %copy-done.10), channel_id=1, source_target_pairs={{0,8},{8,16},{16,24},{24,28},{28,20},{20,12},{12,4},{4,0},{1,9},{9... | collective-permute-start | bytes 786440 | tf_op jit(solution)/shard_map/ppermute | solution.py:349
  74.4 15.3 %collective-permute-start.30 = (bf16[512,256]{1,0:T(8,128)(2,1)}, bf16[512,256]{1,0:T(8,128)(2,1)}, u32[]{:S(2)}, u32[]{:S(2)}) collective-permute-start(bf16[512,256]{1,0:T(8,128)(2,1)} %copy-done.9), channel_id=1, source_target_pairs={{0,4},{8,0},{16,8},{24,16},{28,24},{20,28},{12,20},{4,12},{1,5},{9... | collective-permute-start | bytes 786440 | tf_op jit(solution)/shard_map/ppermute | solution.py:349
  75.7 15.3 %collective-permute-start.33 = (bf16[512,256]{1,0:T(8,128)(2,1)}, bf16[512,256]{1,0:T(8,128)(2,1)S(1)}, u32[]{:S(2)}, u32[]{:S(2)}) collective-permute-start(bf16[512,256]{1,0:T(8,128)(2,1)} %collective-permute-done.31), channel_id=1, source_target_pairs={{0,4},{8,0},{16,8},{24,16},{28,24},{20,28},{12,20},{4,12},{1,5},{9... | collective-permute-start | bytes 786440 | tf_op jit(solution)/shard_map/ppermute | solution.py:349
  77.0 14.3 %collective-permute-start.32 = (bf16[512,256]{1,0:T(8,128)(2,1)}, bf16[512,256]{1,0:T(8,128)(2,1)S(1)}, u32[]{:S(2)}, u32[]{:S(2)}) collective-permute-start(bf16[512,256]{1,0:T(8,128)(2,1)} %copy-done.25), channel_id=1, source_target_pairs={{0,8},{8,16},{16,24},{24,28},{28,20},{20,12},{12,4},{4,0},{1,9},{9... | collective-permute-start | bytes 786440 | tf_op jit(solution)/shard_map/ppermute | solution.py:349
  93.0 12.1 %collective-permute-start.26 = (bf16[512,256]{1,0:T(8,128)(2,1)S(1)}, bf16[512,256]{1,0:T(8,128)(2,1)S(1)}, u32[]{:S(2)}, u32[]{:S(2)}) collective-permute-start(bf16[512,256]{1,0:T(8,128)(2,1)S(1)} %copy-done.14), channel_id=1, source_target_pairs={{0,2},{1,3},{4,6},{5,7},{8,10},{9,11},{12,14},{13,15},{16,18},{17,... | collective-permute-start | bytes 786440 | tf_op jit(solution)/shard_map/ppermute | solution.py:346
  94.3 25.9 %collective-permute-start.34 = (bf16[512,256]{1,0:T(8,128)(2,1)S(1)}, bf16[512,256]{1,0:T(8,128)(2,1)S(1)}, u32[]{:S(2)}, u32[]{:S(2)}) collective-permute-start(bf16[512,256]{1,0:T(8,128)(2,1)S(1)} %fusion.1.refs_2_), channel_id=1, source_target_pairs={{0,1},{1,0},{2,3},{3,2},{4,5},{5,4},{6,7},{7,6},{8,9},{9,8},{10,11... | collective-permute-start | bytes 786440 | tf_op jit(solution)/shard_map/ppermute | solution.py:340
  98.2 22.0 %collective-permute-start.25 = (bf16[512,256]{1,0:T(8,128)(2,1)S(1)}, bf16[512,256]{1,0:T(8,128)(2,1)S(1)}, u32[]{:S(2)}, u32[]{:S(2)}) collective-permute-start(bf16[512,256]{1,0:T(8,128)(2,1)S(1)} %copy-done.14), channel_id=1, source_target_pairs={{0,1},{1,0},{2,3},{3,2},{4,5},{5,4},{6,7},{7,6},{8,9},{9,8},{10,11... | collective-permute-start | bytes 786440 | tf_op jit(solution)/shard_map/ppermute | solution.py:340
  98.8 21.4 %collective-permute-start.36 = (bf16[512,256]{1,0:T(8,128)(2,1)S(1)}, bf16[512,256]{1,0:T(8,128)(2,1)S(1)}, u32[]{:S(2)}, u32[]{:S(2)}) collective-permute-start(bf16[512,256]{1,0:T(8,128)(2,1)S(1)} %collective-permute-done.35.refs_3_), channel_id=1, source_target_pairs={{0,1},{1,0},{2,3},{3,2},{4,5},{5,4},{6,7},{7,6},{8,9},{9,8},{10,11... | collective-permute-start | bytes 786440 | tf_op jit(solution)/shard_map/ppermute | solution.py:340
  105.1 15.1 %collective-permute-start.27 = (bf16[512,256]{1,0:T(8,128)(2,1)S(1)}, bf16[512,256]{1,0:T(8,128)(2,1)S(1)}, u32[]{:S(2)}, u32[]{:S(2)}) collective-permute-start(bf16[512,256]{1,0:T(8,128)(2,1)S(1)} %collective-permute-done.26.refs_1_), channel_id=1, source_target_pairs={{0,1},{1,0},{2,3},{3,2},{4,5},{5,4},{6,7},{7,6},{8,9},{9,8},{10,11... | collective-permute-start | bytes 786440 | tf_op jit(solution)/shard_map/ppermute | solution.py:340
  (32 other events, 409.4 us)

commit v6 on v5

--- a/solution.py
+++ b/solution.py
@@ -16,7 +16,7 @@
 CORES = 2
 CHUNK = 2 * BLK
 MOST_VMEM = 67043328
-LEFT_VMEM = 3 << 20
+LEFT_VMEM = (4 << 20) - (1 << 16)
 
 rope_base = 1000000.0
 
@@ -180,7 +180,9 @@
 
         @pl.when(jnp.logical_not(self.odd))
         def _():
-            chosen_ref[slot_rows(self.free_slot), :] = jnp.zeros((BLK, HEAD_SIZE), jnp.bfloat16)
+            chosen_ref[slot_rows(self.free_slot), :] = jnp.zeros(
+                (BLK, chosen_ref.shape[1]), chosen_ref.dtype
+            )
 
         chosen_ref[slot_rows(2 * self.chunks - 1), :] = refs[0][self.place(self.diagonal), :]
 
@@ -238,10 +240,16 @@
 def attend_kernel(hops, row_blocks, group, facts, q_ref, *refs):
     k_refs, v_refs = refs[:hops], refs[hops : 2 * hops]
     out_ref, key_ref, value_ref, score_ref, peak_ref, total_ref, acc_ref = refs[-7:]
-    blocks = Blocks(facts, hops, row_blocks, pl.program_id(1))
-    blocks.gather(k_refs, key_ref)
-    find_scores(blocks, group, q_ref, key_ref, score_ref, peak_ref)
-    blocks.gather(v_refs, value_ref)
+    blocks = Blocks(facts, hops, row_blocks, pl.program_id(0))
+    head = pl.program_id(1)
+    lanes = pl.ds(pl.multiple_of(head * HEAD_SIZE, HEAD_SIZE), HEAD_SIZE)
+
+    @pl.when(head == 0)
+    def _():
+        blocks.gather(k_refs, key_ref)
+        blocks.gather(v_refs, value_ref)
+
+    find_scores(blocks, group, q_ref, key_ref.at[:, lanes], score_ref, peak_ref)
     total_ref[...] = jnp.zeros_like(total_ref)
     acc_ref[...] = jnp.zeros_like(acc_ref)
 
@@ -250,7 +258,7 @@
         halves = weights_of(chunk, score_ref, peak_ref, total_ref)
         acc_ref[...] += jnp.dot(
             jnp.concatenate(halves, axis=1),
-            value_ref[chunk_rows(chunk), :],
+            value_ref[chunk_rows(chunk), lanes],
             preferred_element_type=jnp.float32,
         )
 
@@ -269,9 +277,11 @@
         self.stacked = self.group * BLK
         self.chunks = hops * CORES * self.row_blocks * BLK // CHUNK
         self.q_spec = pl.BlockSpec(
-            (BLK, self.group * HEAD_SIZE), lambda l, r, f: (r, f[0] * self.heads + l)
-        )
-        self.kv_spec = pl.BlockSpec((CORES * self.rows, HEAD_SIZE), lambda l, r, f: (0, l))
+            (BLK, self.group * HEAD_SIZE), lambda r, l, f: (r, f[0] * self.heads + l)
+        )
+        self.kv_spec = pl.BlockSpec(
+            (CORES * self.rows, self.heads * HEAD_SIZE), lambda r, l, f: (0, 0)
+        )
         self.pairs = self.heads * self.row_blocks * self.stacked * self.chunks * CHUNK // 2
 
     def attend(self, keys, values, before):
@@ -282,14 +292,14 @@
             aliases = {len(operands): 0}
             operands.append(before)
             in_specs.append(pl.BlockSpec(memory_space=pl.ANY))
-        chosen = pltpu.VMEM((self.chunks * CHUNK, HEAD_SIZE), jnp.bfloat16)
+        chosen = pltpu.VMEM((self.chunks * CHUNK, self.heads * HEAD_SIZE), jnp.bfloat16)
         tall = pltpu.VMEM((self.stacked, BLK), jnp.float32)
         return pl.pallas_call(
             functools.partial(attend_kernel, self.hops, self.row_blocks, self.group),
             out_shape=jax.ShapeDtypeStruct(self.queries.shape, self.queries.dtype),
             grid_spec=pltpu.PrefetchScalarGridSpec(
                 num_scalar_prefetch=1,
-                grid=(self.heads, self.row_blocks),
+                grid=(self.row_blocks, self.heads),
                 in_specs=in_specs,
                 out_specs=self.q_spec,
                 scratch_shapes=[
@@ -414,11 +424,12 @@
                 for side in range(2):
                     copies.append((len(pieces), shard, -1, side * strip, half_width))
                     pieces.append(value_arrived[hop, step, side])
+    table = rope_tables(positions)
     key_rows, value_proj = project_main(
         own_tokens,
         sibling_tokens,
         jnp.concatenate([key_bias, value_bias])[None],
-        rope_tables(positions),
+        table,
         pieces,
         copies,
         [source_at(distance) for distance in distances],

time: 133 us -> 131 us (0.985)
  waiting for transfers between devices: 38.1 us -> 39.5 us
  local copies, waits for them, and re-layouts: 11.3 us -> 9.92 us
    ppermute x8, waiting for transfers between devices: 16.2 us -> 17.6 us  [to_plane(): return lax.ppermute(x, 'ctx', [(i, i ^ CORES) for i in range(ctx_size)])]
  transfers between devices with their start and end apart: 37 -> 37, of which waited for: 12 -> 12; matrix products, arithmetic and copies ran while one was open for 13% -> 11% of each run, Pallas kernels for 16% -> 15%
where the time goes in v6:
time: 131 us
  starting transfers between devices  43.7 us (33%)
  waiting for transfers between devices  39.5 us (30%)
  Pallas kernels  31.2 us (24%)
  local copies, waits for them, and re-layouts  9.92 us (8%)
  other arithmetic  3.24 us (2%)
  matrix products  2.77 us (2%)
    ppermute x22, starting transfers between devices, along_ring(): lax.ppermute(x, 'dp', [(ring[i], ring[(i + step) % dp_size]) for i in ran...  22.3 us
    pallas_call x2, Pallas kernels, attend(): pl.pallas_call(functools.partial(attend_kernel, self.hops, self.row_block...  22.1 us
    ppermute x22, waiting for transfers between devices, along_ring(): lax.ppermute(x, 'dp', [(ring[i], ring[(i + step) % dp_size]) for i in ran...  21.4 us
    ppermute x8, waiting for transfers between devices, to_plane(): return lax.ppermute(x, 'ctx', [(i, i ^ CORES) for i in range(ctx_size)])  17.6 us
    ppermute x5, starting transfers between devices, to_sibling(): return lax.ppermute(x, 'ctx', [(i, i ^ 1) for i in range(ctx_size)])  13.8 us
    pallas_call x1, Pallas kernels, project_main(): pl.pallas_call(functools.partial(main_kernel, tuple(copies), early, shard...  9.04 us
    ppermute x8, starting transfers between devices, to_plane(): return lax.ppermute(x, 'ctx', [(i, i ^ CORES) for i in range(ctx_size)])  5.05 us
    dynamic_slice x2, local copies, waits for them, and re-layouts, picked(): lax.dynamic_slice_in_dim(tokens, source * depth, depth, 1)  2.98 us
  transfers between devices with their start and end apart: 37, of which 12 were waited for; matrix products, arithmetic and copies ran while one was open for 11% of the time, Pallas kernels for 15%

profile of v6, /device:TPU:5, one launch (start us, length us, event | category | flops | bytes accessed | tf_op | source)
XLA Modules:
  0.0 130.7 jit_solution(12056866014868626427)
XLA Ops:
  1.8 1.3 %collective-permute-start.1 = (bf16[512,256]{1,0:T(8,128)(2,1)S(1)}, bf16[512,256]{1,0:T(8,128)(2,1)S(1)}, u32[]{:S(2)}, u32[]{:S(2)}) collective-permute-start(bf16[512,256]{1,0:T(8,128)(2,1)S(1)} %dynamic_slice.43), channel_id=1, source_target_pairs={{0,8},{8,16},{16,24},{24,28},{28,20},{20,12},{12,4},{4,0},{1,9},{9... | collective-permute-start | bytes 786440 | tf_op jit(solution)/shard_map/ppermute | solution.py:359
  4.4 1.3 %collective-permute-start.3 = (bf16[512,256]{1,0:T(8,128)(2,1)S(1)}, bf16[512,256]{1,0:T(8,128)(2,1)S(1)}, u32[]{:S(2)}, u32[]{:S(2)}) collective-permute-start(bf16[512,256]{1,0:T(8,128)(2,1)S(1)} %get-tuple-element.16), channel_id=1, source_target_pairs={{0,8},{8,16},{16,24},{24,28},{28,20},{20,12},{12,4},{4,0},{1,9},{9... | collective-permute-start | bytes 786440 | tf_op jit(solution)/shard_map/ppermute | solution.py:359
  5.8 1.3 collective-permute-start.4
  7.1 2.5 %collective-permute-done.1.refs_2_ = bf16[512,256]{1,0:T(8,128)(2,1)S(1)} collective-permute-done((bf16[512,256]{1,0:T(8,128)(2,1)S(1)}, bf16[512,256]{1,0:T(8,128)(2,1)S(1)}, u32[]{:S(2)}, u32[]{:S(2)}) %collective-permute-start.1) | collective-permute-done | bytes 262176 | tf_op jit(solution)/shard_map/ppermute | solution.py:359
  10.8 1.3 collective-permute-start.8
  12.1 3.1 %collective-permute-done.3.refs_4_ = bf16[512,256]{1,0:T(8,128)(2,1)S(1)} collective-permute-done((bf16[512,256]{1,0:T(8,128)(2,1)S(1)}, bf16[512,256]{1,0:T(8,128)(2,1)S(1)}, u32[]{:S(2)}, u32[]{:S(2)}) %collective-permute-start.3) | collective-permute-done | bytes 262176 | tf_op jit(solution)/shard_map/ppermute | solution.py:359
  15.2 1.3 collective-permute-start.9
  16.5 4.3 %collective-permute-done.4.refs_5_ = bf16[512,256]{1,0:T(8,128)(2,1)S(1)} collective-permute-done((bf16[512,256]{1,0:T(8,128)(2,1)S(1)}, bf16[512,256]{1,0:T(8,128)(2,1)S(1)}, u32[]{:S(2)}, u32[]{:S(2)}) %collective-permute-start.4) | collective-permute-done | bytes 262176 | tf_op jit(solution)/shard_map/ppermute | solution.py:359
  22.3 1.3 collective-permute-start.12
  23.6 2.9 %collective-permute-done.9.refs_10_ = bf16[512,256]{1,0:T(8,128)(2,1)} collective-permute-done((bf16[512,256]{1,0:T(8,128)(2,1)S(1)}, bf16[512,256]{1,0:T(8,128)(2,1)}, u32[]{:S(2)}, u32[]{:S(2)}) %collective-permute-start.9) | collective-permute-done | bytes 262176 | tf_op jit(solution)/shard_map/ppermute | solution.py:359
  27.8 1.3 collective-permute-start.16
  29.1 3.1 %collective-permute-done.11.refs_12_ = bf16[512,256]{1,0:T(8,128)(2,1)} collective-permute-done((bf16[512,256]{1,0:T(8,128)(2,1)S(1)}, bf16[512,256]{1,0:T(8,128)(2,1)}, u32[]{:S(2)}, u32[]{:S(2)}) %collective-permute-start.11) | collective-permute-done | bytes 262176 | tf_op jit(solution)/shard_map/ppermute | solution.py:359
  32.4 5.4 %collective-permute-done.12.refs_13_ = bf16[512,256]{1,0:T(8,128)(2,1)S(1)} collective-permute-done((bf16[512,256]{1,0:T(8,128)(2,1)S(1)}, bf16[512,256]{1,0:T(8,128)(2,1)S(1)}, u32[]{:S(2)}, u32[]{:S(2)}) %collective-permute-start.12) | collective-permute-done | bytes 262176 | tf_op jit(solution)/shard_map/ppermute | solution.py:359
  38.1 1.3 collective-permute-start.17
  39.8 1.5 %dynamic-slice_bitcast_fusion.2 = (bf16[256,1024]{1,0:T(8,128)(2,1)S(1)}, bf16[256,1024]{1,0:T(8,128)(2,1)S(1)}, bf16[256,1024]{1,0:T(8,128)(2,1)S(1)}) fusion(bf16[1,256,8192]{2,1,0:T(8,128)(2,1)} %param.7, s32[]{:T(128)S(6)} %select_n.145, s32[]{:T(128)S(6)} %select_n.147, s32[]{:T(128)S(6)} %select_n.146), kind=kLoop, calls=%fused_computation.26 | loop fusion | bytes 3145740 | tf_op jit(solution)/shard_map/dynamic_slice | solution.py:443
  42.4 2.5 %collective-permute-done.6.refs_7_ = bf16[512,256]{1,0:T(8,128)(2,1)S(1)} collective-permute-done((bf16[512,256]{1,0:T(8,128)(2,1)S(1)}, bf16[512,256]{1,0:T(8,128)(2,1)S(1)}, u32[]{:S(2)}, u32[]{:S(2)}) %collective-permute-start.6) | collective-permute-done | bytes 262176 | tf_op jit(solution)/shard_map/ppermute | solution.py:353
  50.5 1.3 %collective-permute-start.21 = (bf16[256,256]{1,0:T(8,128)(2,1)S(1)}, bf16[256,256]{1,0:T(8,128)(2,1)S(1)}, u32[]{:S(2)}, u32[]{:S(2)}) collective-permute-start(bf16[256,256]{1,0:T(8,128)(2,1)S(1)} %slice.42), channel_id=1, source_target_pairs={{0,8},{8,16},{16,24},{24,28},{28,20},{20,12},{12,4},{4,0},{1,9},{9... | collective-permute-start | bytes 393224 | tf_op jit(solution)/shard_map/ppermute | solution.py:359
  51.8 4.3 %collective-permute-done.14.refs_15_ = bf16[512,256]{1,0:T(8,128)(2,1)} collective-permute-done((bf16[512,256]{1,0:T(8,128)(2,1)}, bf16[512,256]{1,0:T(8,128)(2,1)}, u32[]{:S(2)}, u32[]{:S(2)}) %collective-permute-start.14) | collective-permute-done | bytes 262176 | tf_op jit(solution)/shard_map/ppermute | solution.py:353
  63.7 8.0 %collective-permute-done.22.refs_23_ = bf16[256,256]{1,0:T(8,128)(2,1)S(1)} collective-permute-done((bf16[256,256]{1,0:T(8,128)(2,1)S(1)}, bf16[256,256]{1,0:T(8,128)(2,1)S(1)}, u32[]{:S(2)}, u32[]{:S(2)}) %collective-permute-start.22) | collective-permute-done | bytes 131104 | tf_op jit(solution)/shard_map/ppermute | solution.py:353
  72.1 2.3 %collective-permute-done.24.refs_25_ = bf16[256,256]{1,0:T(8,128)(2,1)S(1)} collective-permute-done((bf16[256,256]{1,0:T(8,128)(2,1)}, bf16[256,256]{1,0:T(8,128)(2,1)S(1)}, u32[]{:S(2)}, u32[]{:S(2)}) %collective-permute-start.24) | collective-permute-done | bytes 131104 | tf_op jit(solution)/shard_map/ppermute | solution.py:353
  74.4 1.3 collective-permute-start.30
  75.7 1.3 collective-permute-start.33
  77.2 9.0 %project_main.1 = (bf16[512,256]{1,0:T(8,128)(2,1)}, f32[512,256]{1,0:T(8,128)}) custom-call(s32[9]{0:T(128)} %stack.53.facts, bf16[256,8192]{1,0:T(8,128)(2,1)} %bitcast.32, bf16[256,8192]{1,0:T(8,128)(2,1)} %collective-permute-done.sibling_ref, f32[1,512]{1,0:T(1,128)} %bitcast.33, f32[512,256]{1,0:T(8,128)} %pad_maximum_fusion.6.table_hbm, ...), custom_call_target="tpu_custom_call" | custom-call | flops 3489660928 | bytes 12582912 | tf_op jit(solution)/shard_map/project_main/pallas_call | solution.py:113
  86.2 1.5 %constant_dynamic-slice_fusion.3 = (bf16[256,1024]{1,0:T(8,128)(2,1)S(1)}, bf16[256,1024]{1,0:T(8,128)(2,1)S(1)}, bf16[256,1024]{1,0:T(8,128)(2,1)S(1)}) fusion(bf16[256,8192]{1,0:T(8,128)(2,1)} %collective-permute-done.sibling_ref, s32[]{:T(128)S(6)} %select_n.145, s32[]{:T(128)S(6)} %select_n.147, s32[]{:T(128)S(6)} %select_n.146), kind=kLoop, calls=%fused_computation.33 | loop fusion | bytes 3145740 | tf_op jit(solution)/shard_map/dynamic_slice | solution.py:443
  88.4 1.2 fusion.12
  90.7 1.3 collective-permute-start.35
  92.0 1.3 collective-permute-start.26
  93.3 3.9 %collective-permute-start.34 = (bf16[512,256]{1,0:T(8,128)(2,1)S(1)}, bf16[512,256]{1,0:T(8,128)(2,1)S(1)}, u32[]{:S(2)}, u32[]{:S(2)}) collective-permute-start(bf16[512,256]{1,0:T(8,128)(2,1)S(1)} %fusion.1.refs_2_), channel_id=1, source_target_pairs={{0,1},{1,0},{2,3},{3,2},{4,5},{5,4},{6,7},{7,6},{8,9},{9,8},{10,11... | collective-permute-start | bytes 786440 | tf_op jit(solution)/shard_map/ppermute | solution.py:350
  97.8 6.3 %collective-permute-start.36 = (bf16[512,256]{1,0:T(8,128)(2,1)S(1)}, bf16[512,256]{1,0:T(8,128)(2,1)S(1)}, u32[]{:S(2)}, u32[]{:S(2)}) collective-permute-start(bf16[512,256]{1,0:T(8,128)(2,1)S(1)} %collective-permute-done.35.refs_3_), channel_id=1, source_target_pairs={{0,1},{1,0},{2,3},{3,2},{4,5},{5,4},{6,7},{7,6},{8,9},{9,8},{10,11... | collective-permute-start | bytes 786440 | tf_op jit(solution)/shard_map/ppermute | solution.py:350
  104.1 2.8 %collective-permute-start.27 = (bf16[512,256]{1,0:T(8,128)(2,1)S(1)}, bf16[512,256]{1,0:T(8,128)(2,1)S(1)}, u32[]{:S(2)}, u32[]{:S(2)}) collective-permute-start(bf16[512,256]{1,0:T(8,128)(2,1)S(1)} %collective-permute-done.26.refs_1_), channel_id=1, source_target_pairs={{0,1},{1,0},{2,3},{3,2},{4,5},{5,4},{6,7},{7,6},{8,9},{9,8},{10,11... | collective-permute-start | bytes 786440 | tf_op jit(solution)/shard_map/ppermute | solution.py:350
  107.5 11.1 %attend.2.refs_4_ = bf16[256,4096]{1,0:T(8,128)(2,1)} custom-call(s32[11]{0:T(128)} %get-tuple-element.20.facts, bf16[256,4096]{1,0:T(8,128)(2,1)} %bitcast.29, bf16[512,256]{1,0:T(8,128)(2,1)} %get-tuple-element.7.refs_0_, bf16[512,256]{1,0:T(8,128)(2,1)} %copy-done.16, bf16[512,256]{1,0:T(8,128)(2,1)} %copy-done.1, bf16[512,256]{1,0:T(8,128)(2,1)} %copy-done.15), custom_call_target="tpu_custom_call" | custom-call | flops 1073741824 | bytes 2097152 | tf_op jit(solution)/shard_map/attend/pallas_call | solution.py:297
  119.6 11.1 %attend.3 = bf16[256,4096]{1,0:T(8,128)(2,1)} custom-call(s32[11]{0:T(128)} %get-tuple-element.21.facts, bf16[256,4096]{1,0:T(8,128)(2,1)} %bitcast.30, bf16[512,256]{1,0:T(8,128)(2,1)} %copy-done.18, bf16[512,256]{1,0:T(8,128)(2,1)} %copy-done.20, bf16[512,256]{1,0:T(8,128)(2,1)} %copy-done.17, ...), custom_call_target="tpu_custom_call", output_to_operand_aliasing={{}: (6, {})} | custom-call | flops 1073741824 | bytes 2097152 | tf_op jit(solution)/shard_map/attend/pallas_call | solution.py:297
  (126 shorter events, 26.5 us)
Async XLA Ops:
  0.0 77.2 %collective-permute-start = (bf16[256,8192]{1,0:T(8,128)(2,1)}, bf16[256,8192]{1,0:T(8,128)(2,1)}, u32[]{:S(2)}, u32[]{:S(2)}) collective-permute-start(bf16[256,8192]{1,0:T(8,128)(2,1)} %bitcast.31), channel_id=1, source_target_pairs={{0,1},{1,0},{2,3},{3,2},{4,5},{5,4},{6,7},{7,6},{8,9},{9,8},{10,11... | collective-permute-start | bytes 12582920 | tf_op jit(solution)/shard_map/ppermute | solution.py:350
  1.8 7.8 %collective-permute-start.1 = (bf16[512,256]{1,0:T(8,128)(2,1)S(1)}, bf16[512,256]{1,0:T(8,128)(2,1)S(1)}, u32[]{:S(2)}, u32[]{:S(2)}) collective-permute-start(bf16[512,256]{1,0:T(8,128)(2,1)S(1)} %dynamic_slice.43), channel_id=1, source_target_pairs={{0,8},{8,16},{16,24},{24,28},{28,20},{20,12},{12,4},{4,0},{1,9},{9... | collective-permute-start | bytes 786440 | tf_op jit(solution)/shard_map/ppermute | solution.py:359
  3.2 7.6 %collective-permute-start.5 = (bf16[512,256]{1,0:T(8,128)(2,1)S(1)}, bf16[512,256]{1,0:T(8,128)(2,1)S(1)}, u32[]{:S(2)}, u32[]{:S(2)}) collective-permute-start(bf16[512,256]{1,0:T(8,128)(2,1)S(1)} %dynamic_slice.43), channel_id=1, source_target_pairs={{0,4},{8,0},{16,8},{24,16},{28,24},{20,28},{12,20},{4,12},{1,5},{9... | collective-permute-start | bytes 786440 | tf_op jit(solution)/shard_map/ppermute | solution.py:359
  4.4 10.8 %collective-permute-start.3 = (bf16[512,256]{1,0:T(8,128)(2,1)S(1)}, bf16[512,256]{1,0:T(8,128)(2,1)S(1)}, u32[]{:S(2)}, u32[]{:S(2)}) collective-permute-start(bf16[512,256]{1,0:T(8,128)(2,1)S(1)} %get-tuple-element.16), channel_id=1, source_target_pairs={{0,8},{8,16},{16,24},{24,28},{28,20},{20,12},{12,4},{4,0},{1,9},{9... | collective-permute-start | bytes 786440 | tf_op jit(solution)/shard_map/ppermute | solution.py:359
  5.8 15.1 %collective-permute-start.4 = (bf16[512,256]{1,0:T(8,128)(2,1)S(1)}, bf16[512,256]{1,0:T(8,128)(2,1)S(1)}, u32[]{:S(2)}, u32[]{:S(2)}) collective-permute-start(bf16[512,256]{1,0:T(8,128)(2,1)S(1)} %get-tuple-element.15), channel_id=1, source_target_pairs={{0,8},{8,16},{16,24},{24,28},{28,20},{20,12},{12,4},{4,0},{1,9},{9... | collective-permute-start | bytes 786440 | tf_op jit(solution)/shard_map/ppermute | solution.py:359
  9.6 12.4 %collective-permute-start.7 = (bf16[512,256]{1,0:T(8,128)(2,1)S(1)}, bf16[512,256]{1,0:T(8,128)(2,1)S(1)}, u32[]{:S(2)}, u32[]{:S(2)}) collective-permute-start(bf16[512,256]{1,0:T(8,128)(2,1)S(1)} %get-tuple-element.16), channel_id=1, source_target_pairs={{0,4},{8,0},{16,8},{24,16},{28,24},{20,28},{12,20},{4,12},{1,5},{9... | collective-permute-start | bytes 786440 | tf_op jit(solution)/shard_map/ppermute | solution.py:359
  10.8 11.5 %collective-permute-start.8 = (bf16[512,256]{1,0:T(8,128)(2,1)S(1)}, bf16[512,256]{1,0:T(8,128)(2,1)S(1)}, u32[]{:S(2)}, u32[]{:S(2)}) collective-permute-start(bf16[512,256]{1,0:T(8,128)(2,1)S(1)} %get-tuple-element.15), channel_id=1, source_target_pairs={{0,4},{8,0},{16,8},{24,16},{28,24},{20,28},{12,20},{4,12},{1,5},{9... | collective-permute-start | bytes 786440 | tf_op jit(solution)/shard_map/ppermute | solution.py:359
  15.2 11.3 %collective-permute-start.9 = (bf16[512,256]{1,0:T(8,128)(2,1)S(1)}, bf16[512,256]{1,0:T(8,128)(2,1)}, u32[]{:S(2)}, u32[]{:S(2)}) collective-permute-start(bf16[512,256]{1,0:T(8,128)(2,1)S(1)} %collective-permute-done.1.refs_2_), channel_id=1, source_target_pairs={{0,8},{8,16},{16,24},{24,28},{28,20},{20,12},{12,4},{4,0},{1,9},{9... | collective-permute-start | bytes 786440 | tf_op jit(solution)/shard_map/ppermute | solution.py:359
  22.1 10.1 %collective-permute-start.11 = (bf16[512,256]{1,0:T(8,128)(2,1)S(1)}, bf16[512,256]{1,0:T(8,128)(2,1)}, u32[]{:S(2)}, u32[]{:S(2)}) collective-permute-start(bf16[512,256]{1,0:T(8,128)(2,1)S(1)} %collective-permute-done.3.refs_4_), channel_id=1, source_target_pairs={{0,8},{8,16},{16,24},{24,28},{28,20},{20,12},{12,4},{4,0},{1,9},{9... | collective-permute-start | bytes 786440 | tf_op jit(solution)/shard_map/ppermute | solution.py:359
  22.3 15.5 %collective-permute-start.12 = (bf16[512,256]{1,0:T(8,128)(2,1)S(1)}, bf16[512,256]{1,0:T(8,128)(2,1)S(1)}, u32[]{:S(2)}, u32[]{:S(2)}) collective-permute-start(bf16[512,256]{1,0:T(8,128)(2,1)S(1)} %collective-permute-done.4.refs_5_), channel_id=1, source_target_pairs={{0,8},{8,16},{16,24},{24,28},{28,20},{20,12},{12,4},{4,0},{1,9},{9... | collective-permute-start | bytes 786440 | tf_op jit(solution)/shard_map/ppermute | solution.py:359
  26.6 11.5 %collective-permute-start.15 = (bf16[512,256]{1,0:T(8,128)(2,1)S(1)}, bf16[512,256]{1,0:T(8,128)(2,1)S(1)}, u32[]{:S(2)}, u32[]{:S(2)}) collective-permute-start(bf16[512,256]{1,0:T(8,128)(2,1)S(1)} %collective-permute-done.7.refs_8_), channel_id=1, source_target_pairs={{0,4},{8,0},{16,8},{24,16},{28,24},{20,28},{12,20},{4,12},{1,5},{9... | collective-permute-start | bytes 786440 | tf_op jit(solution)/shard_map/ppermute | solution.py:359
  27.8 11.6 %collective-permute-start.16 = (bf16[512,256]{1,0:T(8,128)(2,1)S(1)}, bf16[512,256]{1,0:T(8,128)(2,1)}, u32[]{:S(2)}, u32[]{:S(2)}) collective-permute-start(bf16[512,256]{1,0:T(8,128)(2,1)S(1)} %collective-permute-done.8.refs_9_), channel_id=1, source_target_pairs={{0,4},{8,0},{16,8},{24,16},{28,24},{20,28},{12,20},{4,12},{1,5},{9... | collective-permute-start | bytes 786440 | tf_op jit(solution)/shard_map/ppermute | solution.py:359
  32.2 9.1 %collective-permute-start.2 = (bf16[512,256]{1,0:T(8,128)(2,1)S(1)}, bf16[512,256]{1,0:T(8,128)(2,1)S(1)}, u32[]{:S(2)}, u32[]{:S(2)}) collective-permute-start(bf16[512,256]{1,0:T(8,128)(2,1)S(1)} %collective-permute-done.1.refs_2_), channel_id=1, source_target_pairs={{0,2},{1,3},{2,0},{3,1},{4,6},{5,7},{6,4},{7,5},{8,10},{9,11},{10,... | collective-permute-start | bytes 786440 | tf_op jit(solution)/shard_map/ppermute | solution.py:353
  38.1 7.4 %collective-permute-start.17 = (bf16[512,256]{1,0:T(8,128)(2,1)}, bf16[512,256]{1,0:T(8,128)(2,1)}, u32[]{:S(2)}, u32[]{:S(2)}) collective-permute-start(bf16[512,256]{1,0:T(8,128)(2,1)} %collective-permute-done.9.refs_10_), channel_id=1, source_target_pairs={{0,8},{8,16},{16,24},{24,28},{28,20},{20,12},{12,4},{4,0},{1,9},{9... | collective-permute-start | bytes 786440 | tf_op jit(solution)/shard_map/ppermute | solution.py:359
  41.3 9.1 %collective-permute-start.10 = (bf16[512,256]{1,0:T(8,128)(2,1)}, bf16[512,256]{1,0:T(8,128)(2,1)}, u32[]{:S(2)}, u32[]{:S(2)}) collective-permute-start(bf16[512,256]{1,0:T(8,128)(2,1)} %collective-permute-done.9.refs_10_), channel_id=1, source_target_pairs={{0,2},{1,3},{2,0},{3,1},{4,6},{5,7},{6,4},{7,5},{8,10},{9,11},{10,... | collective-permute-start | bytes 786440 | tf_op jit(solution)/shard_map/ppermute | solution.py:353
  44.9 11.2 %collective-permute-start.14 = (bf16[512,256]{1,0:T(8,128)(2,1)}, bf16[512,256]{1,0:T(8,128)(2,1)}, u32[]{:S(2)}, u32[]{:S(2)}) collective-permute-start(bf16[512,256]{1,0:T(8,128)(2,1)} %collective-permute-done.13.refs_14_), channel_id=1, source_target_pairs={{0,2},{1,3},{2,0},{3,1},{4,6},{5,7},{6,4},{7,5},{8,10},{9,11},{10,... | collective-permute-start | bytes 786440 | tf_op jit(solution)/shard_map/ppermute | solution.py:353
  45.4 11.8 %collective-permute-start.31 = (bf16[512,256]{1,0:T(8,128)(2,1)}, bf16[512,256]{1,0:T(8,128)(2,1)}, u32[]{:S(2)}, u32[]{:S(2)}) collective-permute-start(bf16[512,256]{1,0:T(8,128)(2,1)} %collective-permute-done.16.refs_17_), channel_id=1, source_target_pairs={{0,4},{8,0},{16,8},{24,16},{28,24},{20,28},{12,20},{4,12},{1,5},{9... | collective-permute-start | bytes 786440 | tf_op jit(solution)/shard_map/ppermute | solution.py:359
  46.3 11.1 %collective-permute-start.28 = (bf16[512,256]{1,0:T(8,128)(2,1)}, bf16[512,256]{1,0:T(8,128)(2,1)S(1)}, u32[]{:S(2)}, u32[]{:S(2)}) collective-permute-start(bf16[512,256]{1,0:T(8,128)(2,1)} %collective-permute-done.11.refs_12_), channel_id=1, source_target_pairs={{0,8},{8,16},{16,24},{24,28},{28,20},{20,12},{12,4},{4,0},{1,9},{9... | collective-permute-start | bytes 786440 | tf_op jit(solution)/shard_map/ppermute | solution.py:359
  50.5 9.5 %collective-permute-start.21 = (bf16[256,256]{1,0:T(8,128)(2,1)S(1)}, bf16[256,256]{1,0:T(8,128)(2,1)S(1)}, u32[]{:S(2)}, u32[]{:S(2)}) collective-permute-start(bf16[256,256]{1,0:T(8,128)(2,1)S(1)} %slice.42), channel_id=1, source_target_pairs={{0,8},{8,16},{16,24},{24,28},{28,20},{20,12},{12,4},{4,0},{1,9},{9... | collective-permute-start | bytes 393224 | tf_op jit(solution)/shard_map/ppermute | solution.py:359
  57.2 18.5 %collective-permute-start.18 = (bf16[512,256]{1,0:T(8,128)(2,1)}, bf16[512,256]{1,0:T(8,128)(2,1)}, u32[]{:S(2)}, u32[]{:S(2)}) collective-permute-start(bf16[512,256]{1,0:T(8,128)(2,1)} %collective-permute-done.17.refs_18_), channel_id=1, source_target_pairs={{0,2},{1,3},{2,0},{3,1},{4,6},{5,7},{6,4},{7,5},{8,10},{9,11},{10,... | collective-permute-start | bytes 786440 | tf_op jit(solution)/shard_map/ppermute | solution.py:353
  57.5 19.5 %collective-permute-start.20 = (bf16[512,256]{1,0:T(8,128)(2,1)}, bf16[512,256]{1,0:T(8,128)(2,1)}, u32[]{:S(2)}, u32[]{:S(2)}) collective-permute-start(bf16[512,256]{1,0:T(8,128)(2,1)} %collective-permute-done.19.refs_20_), channel_id=1, source_target_pairs={{0,2},{1,3},{2,0},{3,1},{4,6},{5,7},{6,4},{7,5},{8,10},{9,11},{10,... | collective-permute-start | bytes 786440 | tf_op jit(solution)/shard_map/ppermute | solution.py:353
  59.9 11.8 %collective-permute-start.22 = (bf16[256,256]{1,0:T(8,128)(2,1)S(1)}, bf16[256,256]{1,0:T(8,128)(2,1)S(1)}, u32[]{:S(2)}, u32[]{:S(2)}) collective-permute-start(bf16[256,256]{1,0:T(8,128)(2,1)S(1)} %collective-permute-done.21.refs_22_), channel_id=1, source_target_pairs={{0,2},{1,3},{2,0},{3,1},{4,6},{5,7},{6,4},{7,5},{8,10},{9,11},{10,... | collective-permute-start | bytes 393224 | tf_op jit(solution)/shard_map/ppermute | solution.py:353
  60.2 14.2 %collective-permute-start.24 = (bf16[256,256]{1,0:T(8,128)(2,1)}, bf16[256,256]{1,0:T(8,128)(2,1)S(1)}, u32[]{:S(2)}, u32[]{:S(2)}) collective-permute-start(bf16[256,256]{1,0:T(8,128)(2,1)} %collective-permute-done.23.refs_24_), channel_id=1, source_target_pairs={{0,2},{1,3},{2,0},{3,1},{4,6},{5,7},{6,4},{7,5},{8,10},{9,11},{10,... | collective-permute-start | bytes 393224 | tf_op jit(solution)/shard_map/ppermute | solution.py:353
  71.7 16.4 %collective-permute-start.29 = (bf16[512,256]{1,0:T(8,128)(2,1)}, bf16[512,256]{1,0:T(8,128)(2,1)S(1)}, u32[]{:S(2)}, u32[]{:S(2)}) collective-permute-start(bf16[512,256]{1,0:T(8,128)(2,1)} %copy-done.10), channel_id=1, source_target_pairs={{0,8},{8,16},{16,24},{24,28},{28,20},{20,12},{12,4},{4,0},{1,9},{9... | collective-permute-start | bytes 786440 | tf_op jit(solution)/shard_map/ppermute | solution.py:359
  74.4 15.3 %collective-permute-start.30 = (bf16[512,256]{1,0:T(8,128)(2,1)}, bf16[512,256]{1,0:T(8,128)(2,1)S(1)}, u32[]{:S(2)}, u32[]{:S(2)}) collective-permute-start(bf16[512,256]{1,0:T(8,128)(2,1)} %copy-done.9), channel_id=1, source_target_pairs={{0,4},{8,0},{16,8},{24,16},{28,24},{20,28},{12,20},{4,12},{1,5},{9... | collective-permute-start | bytes 786440 | tf_op jit(solution)/shard_map/ppermute | solution.py:359
  75.7 14.3 %collective-permute-start.33 = (bf16[512,256]{1,0:T(8,128)(2,1)}, bf16[512,256]{1,0:T(8,128)(2,1)S(1)}, u32[]{:S(2)}, u32[]{:S(2)}) collective-permute-start(bf16[512,256]{1,0:T(8,128)(2,1)} %collective-permute-done.31), channel_id=1, source_target_pairs={{0,4},{8,0},{16,8},{24,16},{28,24},{20,28},{12,20},{4,12},{1,5},{9... | collective-permute-start | bytes 786440 | tf_op jit(solution)/shard_map/ppermute | solution.py:359
  77.0 13.3 %collective-permute-start.32 = (bf16[512,256]{1,0:T(8,128)(2,1)}, bf16[512,256]{1,0:T(8,128)(2,1)S(1)}, u32[]{:S(2)}, u32[]{:S(2)}) collective-permute-start(bf16[512,256]{1,0:T(8,128)(2,1)} %copy-done.27), channel_id=1, source_target_pairs={{0,8},{8,16},{16,24},{24,28},{28,20},{20,12},{12,4},{4,0},{1,9},{9... | collective-permute-start | bytes 786440 | tf_op jit(solution)/shard_map/ppermute | solution.py:359
  92.0 12.1 %collective-permute-start.26 = (bf16[512,256]{1,0:T(8,128)(2,1)S(1)}, bf16[512,256]{1,0:T(8,128)(2,1)S(1)}, u32[]{:S(2)}, u32[]{:S(2)}) collective-permute-start(bf16[512,256]{1,0:T(8,128)(2,1)S(1)} %copy-done.14), channel_id=1, source_target_pairs={{0,2},{1,3},{4,6},{5,7},{8,10},{9,11},{12,14},{13,15},{16,18},{17,... | collective-permute-start | bytes 786440 | tf_op jit(solution)/shard_map/ppermute | solution.py:356
  93.3 25.3 %collective-permute-start.34 = (bf16[512,256]{1,0:T(8,128)(2,1)S(1)}, bf16[512,256]{1,0:T(8,128)(2,1)S(1)}, u32[]{:S(2)}, u32[]{:S(2)}) collective-permute-start(bf16[512,256]{1,0:T(8,128)(2,1)S(1)} %fusion.1.refs_2_), channel_id=1, source_target_pairs={{0,1},{1,0},{2,3},{3,2},{4,5},{5,4},{6,7},{7,6},{8,9},{9,8},{10,11... | collective-permute-start | bytes 786440 | tf_op jit(solution)/shard_map/ppermute | solution.py:350
  97.2 21.4 %collective-permute-start.25 = (bf16[512,256]{1,0:T(8,128)(2,1)S(1)}, bf16[512,256]{1,0:T(8,128)(2,1)S(1)}, u32[]{:S(2)}, u32[]{:S(2)}) collective-permute-start(bf16[512,256]{1,0:T(8,128)(2,1)S(1)} %copy-done.14), channel_id=1, source_target_pairs={{0,1},{1,0},{2,3},{3,2},{4,5},{5,4},{6,7},{7,6},{8,9},{9,8},{10,11... | collective-permute-start | bytes 786440 | tf_op jit(solution)/shard_map/ppermute | solution.py:350
  97.8 20.8 %collective-permute-start.36 = (bf16[512,256]{1,0:T(8,128)(2,1)S(1)}, bf16[512,256]{1,0:T(8,128)(2,1)S(1)}, u32[]{:S(2)}, u32[]{:S(2)}) collective-permute-start(bf16[512,256]{1,0:T(8,128)(2,1)S(1)} %collective-permute-done.35.refs_3_), channel_id=1, source_target_pairs={{0,1},{1,0},{2,3},{3,2},{4,5},{5,4},{6,7},{7,6},{8,9},{9,8},{10,11... | collective-permute-start | bytes 786440 | tf_op jit(solution)/shard_map/ppermute | solution.py:350
  104.1 14.6 %collective-permute-start.27 = (bf16[512,256]{1,0:T(8,128)(2,1)S(1)}, bf16[512,256]{1,0:T(8,128)(2,1)S(1)}, u32[]{:S(2)}, u32[]{:S(2)}) collective-permute-start(bf16[512,256]{1,0:T(8,128)(2,1)S(1)} %collective-permute-done.26.refs_1_), channel_id=1, source_target_pairs={{0,1},{1,0},{2,3},{3,2},{4,5},{5,4},{6,7},{7,6},{8,9},{9,8},{10,11... | collective-permute-start | bytes 786440 | tf_op jit(solution)/shard_map/ppermute | solution.py:350
  (34 other events, 522.7 us)

commit v7 on v6

--- a/solution.py
+++ b/solution.py
@@ -15,6 +15,7 @@
 MASKED = -1e30
 CORES = 2
 CHUNK = 2 * BLK
+PART = 2
 MOST_VMEM = 67043328
 LEFT_VMEM = (4 << 20) - (1 << 16)
 
@@ -144,17 +145,17 @@
 
 class Blocks:
     def __init__(self, facts, hops, row_blocks, row_block):
-        self.row_blocks, self.source_core = row_blocks, facts[1]
+        self.row_blocks = row_blocks
         per_chip = CORES * row_blocks
-        chip = facts[2] // CORES
-        here = facts[2] * row_blocks + row_block
-        segment = facts[3 + here]
+        chip = facts[1] // CORES
+        here = facts[1] * row_blocks + row_block
+        segment = facts[2 + here]
         self.diagonal = lax.rem(here, per_chip)
         self.entries, slot = [], jnp.int32(0)
         for hop in range(hops):
             for local in range(per_chip):
                 block = (chip - hop) * per_chip + local
-                seen = facts[3 + jnp.maximum(block, 0)]
+                seen = facts[2 + jnp.maximum(block, 0)]
                 allowed = (block >= 0) & (block < here) & ((seen == 0) | (seen == segment))
                 self.entries.append((hop, local, allowed, slot))
                 slot = slot + jnp.where(allowed, 1, 0)
@@ -162,13 +163,13 @@
         self.free_slot = slot
         self.chunks = (slot + 2) // 2
 
-    def place(self, local):
+    def place(self, local, source_core):
         core = local // self.row_blocks
-        slot = jnp.where(core == self.source_core, 0, self.row_blocks)
+        slot = jnp.where(core == source_core, 0, self.row_blocks)
         slot = slot + lax.rem(local, self.row_blocks)
         return pl.ds(pl.multiple_of(slot * BLK, BLK), BLK)
 
-    def gather(self, refs, chosen_ref):
+    def gather(self, refs, source_core, chosen_ref):
         def slot_rows(slot):
             return pl.ds(pl.multiple_of(slot * BLK, BLK), BLK)
 
@@ -176,7 +177,9 @@
 
             @pl.when(allowed)
             def _(hop=hop, local=local, slot=slot):
-                chosen_ref[slot_rows(slot), :] = refs[hop][self.place(jnp.int32(local)), :]
+                chosen_ref[slot_rows(slot), :] = refs[hop][
+                    self.place(jnp.int32(local), source_core), :
+                ]
 
         @pl.when(jnp.logical_not(self.odd))
         def _():
@@ -184,7 +187,9 @@
                 (BLK, chosen_ref.shape[1]), chosen_ref.dtype
             )
 
-        chosen_ref[slot_rows(2 * self.chunks - 1), :] = refs[0][self.place(self.diagonal), :]
+        chosen_ref[slot_rows(2 * self.chunks - 1), :] = refs[0][
+            self.place(self.diagonal, source_core), :
+        ]
 
 
 def chunk_rows(chunk):
@@ -192,136 +197,240 @@
 
 
 def find_scores(blocks, group, q_ref, key_ref, score_ref, peak_ref):
-    rows = group * BLK
-
-    def scores(chunk):
-        heads = [q_ref[:, h * HEAD_SIZE : (h + 1) * HEAD_SIZE] for h in range(group)]
-        return lax.dot_general(
-            jnp.concatenate(heads, axis=0),
-            key_ref[chunk_rows(chunk), :],
-            (((1,), (1,)), ((), ())),
-            preferred_element_type=jnp.float32,
-        )
+    factor = math.log2(math.e) / math.sqrt(HEAD_SIZE)
+
+    def parts_of(chunk):
+        keys = key_ref[chunk_rows(chunk), :]
+        for first in range(0, group, PART):
+            heads = [
+                q_ref[:, h * HEAD_SIZE : (h + 1) * HEAD_SIZE] for h in range(first, first + PART)
+            ]
+            found = lax.dot_general(
+                jnp.concatenate(heads, axis=0),
+                keys,
+                (((1,), (1,)), ((), ())),
+                preferred_element_type=jnp.float32,
+            )
+            yield slice(first * BLK, (first + PART) * BLK), found * factor
 
     last = blocks.chunks - 1
-    column = lax.broadcasted_iota(jnp.int32, (rows, CHUNK), 1)
-    row = lax.broadcasted_iota(jnp.int32, (rows, CHUNK), 0) % BLK
+    column = lax.broadcasted_iota(jnp.int32, (PART * BLK, CHUNK), 1)
+    row = lax.broadcasted_iota(jnp.int32, (PART * BLK, CHUNK), 0) % BLK
     first_column = jnp.where(blocks.odd, 0, BLK)
-    found = jnp.where(
-        (column >= first_column) & (column - BLK <= row), scores(last), MASKED
-    )
-    score_ref[last] = found
-    peak_ref[...] = jnp.maximum(found[:, :BLK], found[:, BLK:])
+    for rows, found in parts_of(last):
+        found = jnp.where((column >= first_column) & (column - BLK <= row), found, MASKED)
+        score_ref[last, rows, :] = found
+        peak_ref[rows, :] = jnp.maximum(found[:, :BLK], found[:, BLK:])
 
     @pl.loop(0, last)
     def _(chunk):
-        found = scores(chunk)
-        score_ref[chunk] = found
-        peak_ref[...] = jnp.maximum(
-            peak_ref[...], jnp.maximum(found[:, :BLK], found[:, BLK:])
-        )
+        for rows, found in parts_of(chunk):
+            score_ref[chunk, rows, :] = found
+            peak_ref[rows, :] = jnp.maximum(
+                peak_ref[rows, :], jnp.maximum(found[:, :BLK], found[:, BLK:])
+            )
 
     peak_ref[...] = jnp.broadcast_to(
-        jnp.max(peak_ref[...], axis=1, keepdims=True), (rows, BLK)
-    )
-
-
-def weights_of(chunk, score_ref, peak_ref, total_ref):
-    factor = math.log2(math.e) / math.sqrt(HEAD_SIZE)
-    peak, total, halves = peak_ref[...], total_ref[...], []
-    for first in range(0, CHUNK, BLK):
-        probs = jnp.exp2((score_ref[chunk, :, first : first + BLK] - peak) * factor)
-        halves.append(probs.astype(jnp.bfloat16))
-        total = total + probs
-    total_ref[...] = total
-    return halves
-
-
-def attend_kernel(hops, row_blocks, group, facts, q_ref, *refs):
-    k_refs, v_refs = refs[:hops], refs[hops : 2 * hops]
-    out_ref, key_ref, value_ref, score_ref, peak_ref, total_ref, acc_ref = refs[-7:]
+        jnp.max(peak_ref[...], axis=1, keepdims=True), peak_ref.shape
+    )
+
+
+def score_kernel(hops, row_blocks, group, facts, q_ref, *refs):
+    k_refs = refs[:hops]
+    probs_ref, inverse_ref, key_ref, score_ref, peak_ref, total_ref = refs[hops:]
     blocks = Blocks(facts, hops, row_blocks, pl.program_id(0))
     head = pl.program_id(1)
     lanes = pl.ds(pl.multiple_of(head * HEAD_SIZE, HEAD_SIZE), HEAD_SIZE)
 
     @pl.when(head == 0)
     def _():
-        blocks.gather(k_refs, key_ref)
-        blocks.gather(v_refs, value_ref)
+        blocks.gather(k_refs, facts[0], key_ref)
 
     find_scores(blocks, group, q_ref, key_ref.at[:, lanes], score_ref, peak_ref)
     total_ref[...] = jnp.zeros_like(total_ref)
-    acc_ref[...] = jnp.zeros_like(acc_ref)
 
     @pl.loop(0, blocks.chunks)
     def _(chunk):
-        halves = weights_of(chunk, score_ref, peak_ref, total_ref)
-        acc_ref[...] += jnp.dot(
-            jnp.concatenate(halves, axis=1),
-            value_ref[chunk_rows(chunk), lanes],
-            preferred_element_type=jnp.float32,
-        )
-
-    mixed = (acc_ref[...] / jnp.sum(total_ref[...], axis=1, keepdims=True)).astype(out_ref.dtype)
-    for h in range(group):
-        out_ref[:, h * HEAD_SIZE : (h + 1) * HEAD_SIZE] = mixed[h * BLK : (h + 1) * BLK]
+        peak, total = peak_ref[...], total_ref[...]
+        for column in range(0, CHUNK, BLK):
+            probs = jnp.exp2(score_ref[chunk, :, column : column + BLK] - peak)
+            probs_ref[0, chunk, :, column : column + BLK] = probs.astype(jnp.bfloat16)
+            total = total + probs
+        total_ref[...] = total
+
+    inverse_ref[0] = jnp.broadcast_to(
+        1.0 / jnp.sum(total_ref[...], axis=1, keepdims=True), total_ref.shape
+    )
+
+
+def attend_kernel(hops, row_blocks, group, heads, facts, q_ref, probs_hbm, inverse_ref, *refs):
+    near_values, far_keys, far_values = (refs[at * hops : (at + 1) * hops] for at in range(3))
+    out_ref, key_ref, value_ref, score_ref, peak_ref, total_ref, acc_ref = refs[3 * hops : -2]
+    held_ref, sems = refs[-2:]
+    row_block, head = pl.program_id(0), pl.program_id(1)
+    blocks = Blocks(facts, hops, row_blocks, row_block)
+    lanes = pl.ds(pl.multiple_of(lax.rem(head, heads) * HEAD_SIZE, HEAD_SIZE), HEAD_SIZE)
+
+    def fetch(rows_of, at, chunk):
+        return pltpu.make_async_copy(
+            probs_hbm.at[rows_of * heads + at, chunk], held_ref.at[at, chunk], sems.at[at, chunk]
+        )
+
+    def fetch_row_block(rows_of):
+        for at in range(heads):
+
+            @pl.loop(0, Blocks(facts, hops, row_blocks, rows_of).chunks)
+            def _(chunk):
+                fetch(rows_of, at, chunk).start()
+
+    @pl.when((row_block == 0) & (head == 0))
+    def _():
+        fetch_row_block(row_block)
+
+    @pl.when((row_block + 1 < row_blocks) & (head == heads))
+    def _():
+        fetch_row_block(lax.rem(row_block + 1, row_blocks))
+
+    @pl.when(head == 0)
+    def _():
+        blocks.gather(near_values, facts[0], value_ref)
+
+    @pl.when(head == heads)
+    def _():
+        blocks.gather(far_keys, 1 - facts[0], key_ref)
+        blocks.gather(far_values, 1 - facts[0], value_ref)
+
+    def store(mixed):
+        mixed = mixed.astype(out_ref.dtype)
+        for h in range(group):
+            out_ref[:, h * HEAD_SIZE : (h + 1) * HEAD_SIZE] = mixed[h * BLK : (h + 1) * BLK]
+
+    acc_ref[...] = jnp.zeros_like(acc_ref)
+
+    @pl.when(head < heads)
+    def _():
+        @pl.loop(0, blocks.chunks)
+        def _(chunk):
+            fetch(row_block, head, chunk).wait()
+            acc_ref[...] += jnp.dot(
+                held_ref[head, chunk],
+                value_ref[chunk_rows(chunk), lanes],
+                preferred_element_type=jnp.float32,
+            )
+
+        store(acc_ref[...] * inverse_ref[0])
+
+    @pl.when(head >= heads)
+    def _():
+        find_scores(blocks, group, q_ref, key_ref.at[:, lanes], score_ref, peak_ref)
+        total_ref[...] = jnp.zeros_like(total_ref)
+
+        @pl.loop(0, blocks.chunks)
+        def _(chunk):
+            values = value_ref[chunk_rows(chunk), lanes]
+            for first in range(0, group * BLK, PART * BLK):
+                rows = slice(first, first + PART * BLK)
+                peak, total, halves = peak_ref[rows, :], total_ref[rows, :], []
+                for column in range(0, CHUNK, BLK):
+                    found = score_ref[chunk, rows, column : column + BLK]
+                    probs = jnp.exp2(found - peak)
+                    halves.append(probs.astype(jnp.bfloat16))
+                    total = total + probs
+                total_ref[rows, :] = total
+                acc_ref[rows, :] += jnp.dot(
+                    jnp.concatenate(halves, axis=1), values, preferred_element_type=jnp.float32
+                )
+
+        store(acc_ref[...] / jnp.sum(total_ref[...], axis=1, keepdims=True))
 
 
 class Attention:
     def __init__(self, facts, queries, hops):
         self.facts, self.queries, self.hops = facts, queries, hops
-        self.rows, query_width = queries.shape
+        number_of_rows, query_width = queries.shape
         self.group = query_width // HEAD_SIZE // KEY_VALUE_HEADS
-        self.heads = KEY_VALUE_HEADS // CORES
-        self.row_blocks = self.rows // BLK
+        self.heads = heads = KEY_VALUE_HEADS // CORES
+        self.row_blocks = number_of_rows // BLK
         self.stacked = self.group * BLK
         self.chunks = hops * CORES * self.row_blocks * BLK // CHUNK
         self.q_spec = pl.BlockSpec(
-            (BLK, self.group * HEAD_SIZE), lambda r, l, f: (r, f[0] * self.heads + l)
+            (BLK, self.group * HEAD_SIZE),
+            lambda r, l, f: (r, jnp.where(l < heads, f[0], 1 - f[0]) * heads + lax.rem(l, heads)),
         )
         self.kv_spec = pl.BlockSpec(
-            (CORES * self.rows, self.heads * HEAD_SIZE), lambda r, l, f: (0, 0)
-        )
-        self.pairs = self.heads * self.row_blocks * self.stacked * self.chunks * CHUNK // 2
-
-    def attend(self, keys, values, before):
-        operands = [self.facts, self.queries, *keys, *values]
-        in_specs = [self.q_spec] + [self.kv_spec] * (2 * self.hops)
-        aliases = {}
-        if before is not None:
-            aliases = {len(operands): 0}
-            operands.append(before)
-            in_specs.append(pl.BlockSpec(memory_space=pl.ANY))
-        chosen = pltpu.VMEM((self.chunks * CHUNK, self.heads * HEAD_SIZE), jnp.bfloat16)
-        tall = pltpu.VMEM((self.stacked, BLK), jnp.float32)
+            (CORES * number_of_rows, heads * HEAD_SIZE), lambda r, l, f: (0, 0)
+        )
+        self.chosen = pltpu.VMEM((self.chunks * CHUNK, heads * HEAD_SIZE), jnp.bfloat16)
+        self.scores = pltpu.VMEM((self.chunks, self.stacked, CHUNK), jnp.float32)
+        self.tall = pltpu.VMEM((self.stacked, BLK), jnp.float32)
+        count = heads * self.row_blocks
+        self.probs = jax.ShapeDtypeStruct(
+            (count, self.chunks, self.stacked, CHUNK), jnp.bfloat16
+        )
+        self.inverse = jax.ShapeDtypeStruct((count, self.stacked, BLK), jnp.float32)
+        self.pairs = count * self.stacked * self.chunks * CHUNK // 2
+
+    def call(self, kernel, heads, out_shape, in_specs, out_specs, scratch, operands):
         return pl.pallas_call(
-            functools.partial(attend_kernel, self.hops, self.row_blocks, self.group),
-            out_shape=jax.ShapeDtypeStruct(self.queries.shape, self.queries.dtype),
+            kernel,
+            out_shape=out_shape,
             grid_spec=pltpu.PrefetchScalarGridSpec(
                 num_scalar_prefetch=1,
-                grid=(self.row_blocks, self.heads),
-                in_specs=in_specs,
-                out_specs=self.q_spec,
-                scratch_shapes=[
-                    chosen,
-                    chosen,
-                    pltpu.VMEM((self.chunks, self.stacked, CHUNK), jnp.float32),
-                    tall,
-                    tall,
-                    tall,
-                ],
+                grid=(self.row_blocks, heads),
+                in_specs=[self.q_spec] + in_specs,
+                out_specs=out_specs,
+                scratch_shapes=scratch,
             ),
-            input_output_aliases=aliases,
-            compiler_params=pltpu.CompilerParams(
-                vmem_limit_bytes=MOST_VMEM - LEFT_VMEM
-            ),
+            compiler_params=pltpu.CompilerParams(vmem_limit_bytes=MOST_VMEM - LEFT_VMEM),
             cost_estimate=pl.CostEstimate(
                 flops=4 * self.pairs * HEAD_SIZE,
                 bytes_accessed=2 * self.queries.size,
                 transcendentals=self.pairs,
             ),
-            name="attend",
-        )(*operands)
+        )(self.facts, self.queries, *operands)
+
+    def score(self, keys):
+        heads, rows = self.heads, self.row_blocks
+        return self.call(
+            functools.partial(score_kernel, self.hops, rows, self.group),
+            heads,
+            (self.probs, self.inverse),
+            [self.kv_spec] * self.hops,
+            (
+                pl.BlockSpec((1, *self.probs.shape[1:]), lambda r, l, f: (r * heads + l, 0, 0, 0)),
+                pl.BlockSpec((1, self.stacked, BLK), lambda r, l, f: (r * heads + l, 0, 0)),
+            ),
+            [self.chosen, self.scores, self.tall, self.tall],
+            keys,
+        )
+
+    def attend(self, probs, inverse, values, far_keys, far_values):
+        heads = self.heads
+        return self.call(
+            functools.partial(attend_kernel, self.hops, self.row_blocks, self.group, heads),
+            KEY_VALUE_HEADS,
+            jax.ShapeDtypeStruct(self.queries.shape, self.queries.dtype),
+            [
+                pl.BlockSpec(memory_space=pltpu.MemorySpace.HBM),
+                pl.BlockSpec(
+                    (1, self.stacked, BLK),
+                    lambda r, l, f: (r * heads + jnp.minimum(l, heads - 1), 0, 0),
+                ),
+            ]
+            + [self.kv_spec] * (3 * self.hops),
+            self.q_spec,
+            [
+                self.chosen,
+                self.chosen,
+                self.scores,
+                self.tall,
+                self.tall,
+                self.tall,
+                pltpu.VMEM((heads, *self.probs.shape[1:]), jnp.bfloat16),
+                pltpu.SemaphoreType.DMA((heads, self.chunks)),
+            ],
+            [probs, inverse, *values, *far_keys, *far_values],
+        )
 
 
 def layer(
@@ -469,13 +578,10 @@
     sibling_keys = [to_sibling(x) for x in keys]
     sibling_values = [to_sibling(x) for x in values]
 
-    def attention(half):
-        facts = jnp.concatenate([jnp.stack([half, half, my_index]), block_segments[0]])
-        return Attention(facts, queries[0], chips)
-
-    near, far = attention(core), attention(1 - core)
-    attended = near.attend(keys, values, None)
-    attended = far.attend(sibling_keys, sibling_values, attended)
+    facts = jnp.concatenate([jnp.stack([core, my_index]), block_segments[0]])
+    attention = Attention(facts, queries[0], chips)
+    probs, inverse = attention.score(keys)
+    attended = attention.attend(probs, inverse, values, sibling_keys, sibling_values)
     return attended[None]
 
 

time: 131 us -> 139 us (1.061)
  Pallas kernels: 31.2 us -> 36.6 us
  matrix products: 2.77 us -> 4.72 us
    pallas_call x2, Pallas kernels: 22.1 us -> 27.7 us  [call(): pl.pallas_call(kernel, out_shape=out_shape, grid_spec=pltpu.PrefetchScala...]
    dot_general x6, matrix products: 2.77 us -> 4.72 us  [late_product(): jnp.dot(columns[:, side * strip:(side + 1) * strip], piece, preferred_ele...]
  transfers between devices with their start and end apart: 37 -> 37, of which waited for: 12 -> 12; matrix products, arithmetic and copies ran while one was open for 11% -> 12% of each run, Pallas kernels for 15% -> 14%
where the time goes in v7:
time: 139 us; the launch traced here: 138 us
  starting transfers between devices  43.9 us (32%)
  waiting for transfers between devices  39.3 us (28%)
  Pallas kernels  36.6 us (26%)
  local copies, waits for them, and re-layouts  9.89 us (7%)
  matrix products  4.72 us (3%)
  other arithmetic  3.24 us (2%)
    pallas_call x2, Pallas kernels, call(): pl.pallas_call(kernel, out_shape=out_shape, grid_spec=pltpu.PrefetchScala...  27.7 us
    ppermute x22, starting transfers between devices, along_ring(): lax.ppermute(x, 'dp', [(ring[i], ring[(i + step) % dp_size]) for i in ran...  22.3 us
    ppermute x22, waiting for transfers between devices, along_ring(): lax.ppermute(x, 'dp', [(ring[i], ring[(i + step) % dp_size]) for i in ran...  21.4 us
    ppermute x8, waiting for transfers between devices, to_plane(): return lax.ppermute(x, 'ctx', [(i, i ^ CORES) for i in range(ctx_size)])  17.6 us
    ppermute x5, starting transfers between devices, to_sibling(): return lax.ppermute(x, 'ctx', [(i, i ^ 1) for i in range(ctx_size)])  13.8 us
    pallas_call x1, Pallas kernels, project_main(): pl.pallas_call(functools.partial(main_kernel, tuple(copies), early, shard...  8.92 us
    ppermute x8, starting transfers between devices, to_plane(): return lax.ppermute(x, 'ctx', [(i, i ^ CORES) for i in range(ctx_size)])  5.05 us
    dot_general x6, matrix products, late_product(): jnp.dot(columns[:, side * strip:(side + 1) * strip], piece, preferred_ele...  4.72 us
  transfers between devices with their start and end apart: 37, of which 12 were waited for; matrix products, arithmetic and copies ran while one was open for 12% of the time, Pallas kernels for 14%

profile of v7, /device:TPU:5, one launch (start us, length us, event | category | flops | bytes accessed | tf_op | source)
XLA Modules:
  0.0 138.2 jit_solution(6723084904393518150)
XLA Ops:
  1.8 1.3 collective-permute-start.1
  4.4 1.3 collective-permute-start.3
  5.8 1.3 collective-permute-start.4
  7.1 2.5 %collective-permute-done.1.refs_2_ = bf16[512,256]{1,0:T(8,128)(2,1)S(1)} collective-permute-done((bf16[512,256]{1,0:T(8,128)(2,1)S(1)}, bf16[512,256]{1,0:T(8,128)(2,1)S(1)}, u32[]{:S(2)}, u32[]{:S(2)}) %collective-permute-start.1) | collective-permute-done | bytes 262176 | tf_op jit(solution)/shard_map/ppermute | solution.py:468
  10.8 1.3 collective-permute-start.8
  12.1 3.1 %collective-permute-done.3.refs_4_ = bf16[512,256]{1,0:T(8,128)(2,1)S(1)} collective-permute-done((bf16[512,256]{1,0:T(8,128)(2,1)S(1)}, bf16[512,256]{1,0:T(8,128)(2,1)S(1)}, u32[]{:S(2)}, u32[]{:S(2)}) %collective-permute-start.3) | collective-permute-done | bytes 262176 | tf_op jit(solution)/shard_map/ppermute | solution.py:468
  15.2 1.3 collective-permute-start.9
  16.5 4.3 %collective-permute-done.4.refs_5_ = bf16[512,256]{1,0:T(8,128)(2,1)S(1)} collective-permute-done((bf16[512,256]{1,0:T(8,128)(2,1)S(1)}, bf16[512,256]{1,0:T(8,128)(2,1)S(1)}, u32[]{:S(2)}, u32[]{:S(2)}) %collective-permute-start.4) | collective-permute-done | bytes 262176 | tf_op jit(solution)/shard_map/ppermute | solution.py:468
  22.3 1.3 collective-permute-start.12
  23.6 2.9 %collective-permute-done.9.refs_10_ = bf16[512,256]{1,0:T(8,128)(2,1)} collective-permute-done((bf16[512,256]{1,0:T(8,128)(2,1)S(1)}, bf16[512,256]{1,0:T(8,128)(2,1)}, u32[]{:S(2)}, u32[]{:S(2)}) %collective-permute-start.9) | collective-permute-done | bytes 262176 | tf_op jit(solution)/shard_map/ppermute | solution.py:468
  27.8 1.3 collective-permute-start.16
  29.1 3.1 %collective-permute-done.11.refs_12_ = bf16[512,256]{1,0:T(8,128)(2,1)} collective-permute-done((bf16[512,256]{1,0:T(8,128)(2,1)S(1)}, bf16[512,256]{1,0:T(8,128)(2,1)}, u32[]{:S(2)}, u32[]{:S(2)}) %collective-permute-start.11) | collective-permute-done | bytes 262176 | tf_op jit(solution)/shard_map/ppermute | solution.py:468
  32.4 5.4 %collective-permute-done.12.refs_13_ = bf16[512,256]{1,0:T(8,128)(2,1)S(1)} collective-permute-done((bf16[512,256]{1,0:T(8,128)(2,1)S(1)}, bf16[512,256]{1,0:T(8,128)(2,1)S(1)}, u32[]{:S(2)}, u32[]{:S(2)}) %collective-permute-start.12) | collective-permute-done | bytes 262176 | tf_op jit(solution)/shard_map/ppermute | solution.py:468
  39.8 1.5 %dynamic-slice_bitcast_fusion.2 = (bf16[256,1024]{1,0:T(8,128)(2,1)S(1)}, bf16[256,1024]{1,0:T(8,128)(2,1)S(1)}, bf16[256,1024]{1,0:T(8,128)(2,1)S(1)}) fusion(bf16[1,256,8192]{2,1,0:T(8,128)(2,1)} %param.7, s32[]{:T(128)S(6)} %select_n.145, s32[]{:T(128)S(6)} %select_n.147, s32[]{:T(128)S(6)} %select_n.146), kind=kLoop, calls=%fused_computation.26 | loop fusion | bytes 3145740 | tf_op jit(solution)/shard_map/dynamic_slice | solution.py:552
  42.4 2.5 %collective-permute-done.6.refs_7_ = bf16[512,256]{1,0:T(8,128)(2,1)S(1)} collective-permute-done((bf16[512,256]{1,0:T(8,128)(2,1)S(1)}, bf16[512,256]{1,0:T(8,128)(2,1)S(1)}, u32[]{:S(2)}, u32[]{:S(2)}) %collective-permute-start.6) | collective-permute-done | bytes 262176 | tf_op jit(solution)/shard_map/ppermute | solution.py:462
  50.5 1.3 collective-permute-start.21
  51.8 4.3 %collective-permute-done.14.refs_15_ = bf16[512,256]{1,0:T(8,128)(2,1)} collective-permute-done((bf16[512,256]{1,0:T(8,128)(2,1)}, bf16[512,256]{1,0:T(8,128)(2,1)}, u32[]{:S(2)}, u32[]{:S(2)}) %collective-permute-start.14) | collective-permute-done | bytes 262176 | tf_op jit(solution)/shard_map/ppermute | solution.py:462
  63.7 8.0 %collective-permute-done.22.refs_23_ = bf16[256,256]{1,0:T(8,128)(2,1)S(1)} collective-permute-done((bf16[256,256]{1,0:T(8,128)(2,1)S(1)}, bf16[256,256]{1,0:T(8,128)(2,1)S(1)}, u32[]{:S(2)}, u32[]{:S(2)}) %collective-permute-start.22) | collective-permute-done | bytes 131104 | tf_op jit(solution)/shard_map/ppermute | solution.py:462
  72.1 2.3 %collective-permute-done.24.refs_25_ = bf16[256,256]{1,0:T(8,128)(2,1)S(1)} collective-permute-done((bf16[256,256]{1,0:T(8,128)(2,1)}, bf16[256,256]{1,0:T(8,128)(2,1)S(1)}, u32[]{:S(2)}, u32[]{:S(2)}) %collective-permute-start.24) | collective-permute-done | bytes 131104 | tf_op jit(solution)/shard_map/ppermute | solution.py:462
  74.4 1.3 collective-permute-start.28
  75.7 1.3 collective-permute-start.31
  77.2 8.9 %project_main.1 = (bf16[512,256]{1,0:T(8,128)(2,1)}, f32[512,256]{1,0:T(8,128)}) custom-call(s32[9]{0:T(128)} %stack.47.facts, bf16[256,8192]{1,0:T(8,128)(2,1)} %bitcast.29, bf16[256,8192]{1,0:T(8,128)(2,1)} %collective-permute-done.sibling_ref, f32[1,512]{1,0:T(1,128)} %bitcast.32, f32[512,256]{1,0:T(8,128)} %pad_maximum_fusion.6.table_hbm, ...), custom_call_target="tpu_custom_call" | custom-call | flops 3489660928 | bytes 12582912 | tf_op jit(solution)/shard_map/project_main/pallas_call | solution.py:114
  86.1 1.5 %constant_dynamic-slice_fusion.3 = (bf16[256,1024]{1,0:T(8,128)(2,1)S(1)}, bf16[256,1024]{1,0:T(8,128)(2,1)S(1)}, bf16[256,1024]{1,0:T(8,128)(2,1)S(1)}) fusion(bf16[256,8192]{1,0:T(8,128)(2,1)} %collective-permute-done.sibling_ref, s32[]{:T(128)S(6)} %select_n.145, s32[]{:T(128)S(6)} %select_n.147, s32[]{:T(128)S(6)} %select_n.146), kind=kLoop, calls=%fused_computation.33 | loop fusion | bytes 3145740 | tf_op jit(solution)/shard_map/dynamic_slice | solution.py:552
  87.6 1.3 fusion.8
  90.5 1.3 fusion.5
  92.5 1.3 collective-permute-start.32
  93.8 1.5 %collective-permute-start.25 = (bf16[512,256]{1,0:T(8,128)(2,1)S(1)}, bf16[512,256]{1,0:T(8,128)(2,1)S(1)}, u32[]{:S(2)}, u32[]{:S(2)}) collective-permute-start(bf16[512,256]{1,0:T(8,128)(2,1)S(1)} %copy-done.26), channel_id=1, source_target_pairs={{0,2},{1,3},{4,6},{5,7},{8,10},{9,11},{12,14},{13,15},{16,18},{17,... | collective-permute-start | bytes 786440 | tf_op jit(solution)/shard_map/ppermute | solution.py:465
  95.3 3.9 %collective-permute-start.35 = (bf16[512,256]{1,0:T(8,128)(2,1)S(1)}, bf16[512,256]{1,0:T(8,128)(2,1)S(1)}, u32[]{:S(2)}, u32[]{:S(2)}) collective-permute-start(bf16[512,256]{1,0:T(8,128)(2,1)S(1)} %fusion.1.refs_0_), channel_id=1, source_target_pairs={{0,1},{1,0},{2,3},{3,2},{4,5},{5,4},{6,7},{7,6},{8,9},{9,8},{10,11... | collective-permute-start | bytes 786440 | tf_op jit(solution)/shard_map/ppermute | solution.py:459
  99.6 6.3 %collective-permute-start.36 = (bf16[512,256]{1,0:T(8,128)(2,1)S(1)}, bf16[512,256]{1,0:T(8,128)(2,1)S(1)}, u32[]{:S(2)}, u32[]{:S(2)}) collective-permute-start(bf16[512,256]{1,0:T(8,128)(2,1)S(1)} %collective-permute-done.32.refs_1_), channel_id=1, source_target_pairs={{0,1},{1,0},{2,3},{3,2},{4,5},{5,4},{6,7},{7,6},{8,9},{9,8},{10,11... | collective-permute-start | bytes 786440 | tf_op jit(solution)/shard_map/ppermute | solution.py:459
  105.9 2.8 %collective-permute-start.34 = (bf16[512,256]{1,0:T(8,128)(2,1)S(1)}, bf16[512,256]{1,0:T(8,128)(2,1)S(1)}, u32[]{:S(2)}, u32[]{:S(2)}) collective-permute-start(bf16[512,256]{1,0:T(8,128)(2,1)S(1)} %collective-permute-done.25.refs_1_), channel_id=1, source_target_pairs={{0,1},{1,0},{2,3},{3,2},{4,5},{5,4},{6,7},{7,6},{8,9},{9,8},{10,11... | collective-permute-start | bytes 786440 | tf_op jit(solution)/shard_map/ppermute | solution.py:459
  109.3 10.3 %shard_map.73 = (bf16[4,4,1024,256]{3,2,1,0:T(8,128)(2,1)}, f32[4,1024,128]{2,1,0:T(8,128)}) custom-call(s32[10]{0:T(128)} %pad_add_fusion.facts, bf16[256,4096]{1,0:T(8,128)(2,1)} %bitcast.30, bf16[512,256]{1,0:T(8,128)(2,1)} %get-tuple-element.9.refs_0_, bf16[512,256]{1,0:T(8,128)(2,1)} %copy-done.27), custom_call_target="tpu_custom_call" | custom-call | flops 1073741824 | bytes 2097152 | tf_op jit(solution)/shard_map/pallas_call | solution.py:374
  120.6 17.4 %shard_map.74 = bf16[256,4096]{1,0:T(8,128)(2,1)} custom-call(s32[10]{0:T(128)} %pad_add_fusion.facts, bf16[256,4096]{1,0:T(8,128)(2,1)} %bitcast.31, bf16[4,4,1024,256]{3,2,1,0:T(8,128)(2,1)} %get-tuple-element.10.probs_hbm, f32[4,1024,128]{2,1,0:T(8,128)} %get-tuple-element.11.inverse_ref, bf16[512,256]{1,0:T(8,128)(2,1)} %copy-done, ...), custom_call_target="tpu_custom_call" | custom-call | flops 1073741824 | bytes 2097152 | tf_op jit(solution)/shard_map/pallas_call | solution.py:374
  (124 shorter events, 28.2 us)
Async XLA Ops:
  0.0 77.2 %collective-permute-start = (bf16[256,8192]{1,0:T(8,128)(2,1)}, bf16[256,8192]{1,0:T(8,128)(2,1)}, u32[]{:S(2)}, u32[]{:S(2)}) collective-permute-start(bf16[256,8192]{1,0:T(8,128)(2,1)} %bitcast.28), channel_id=1, source_target_pairs={{0,1},{1,0},{2,3},{3,2},{4,5},{5,4},{6,7},{7,6},{8,9},{9,8},{10,11... | collective-permute-start | bytes 12582920 | tf_op jit(solution)/shard_map/ppermute | solution.py:459
  1.8 7.8 %collective-permute-start.1 = (bf16[512,256]{1,0:T(8,128)(2,1)S(1)}, bf16[512,256]{1,0:T(8,128)(2,1)S(1)}, u32[]{:S(2)}, u32[]{:S(2)}) collective-permute-start(bf16[512,256]{1,0:T(8,128)(2,1)S(1)} %dynamic_slice.43), channel_id=1, source_target_pairs={{0,8},{8,16},{16,24},{24,28},{28,20},{20,12},{12,4},{4,0},{1,9},{9... | collective-permute-start | bytes 786440 | tf_op jit(solution)/shard_map/ppermute | solution.py:468
  3.2 7.6 %collective-permute-start.5 = (bf16[512,256]{1,0:T(8,128)(2,1)S(1)}, bf16[512,256]{1,0:T(8,128)(2,1)S(1)}, u32[]{:S(2)}, u32[]{:S(2)}) collective-permute-start(bf16[512,256]{1,0:T(8,128)(2,1)S(1)} %dynamic_slice.43), channel_id=1, source_target_pairs={{0,4},{8,0},{16,8},{24,16},{28,24},{20,28},{12,20},{4,12},{1,5},{9... | collective-permute-start | bytes 786440 | tf_op jit(solution)/shard_map/ppermute | solution.py:468
  4.4 10.8 %collective-permute-start.3 = (bf16[512,256]{1,0:T(8,128)(2,1)S(1)}, bf16[512,256]{1,0:T(8,128)(2,1)S(1)}, u32[]{:S(2)}, u32[]{:S(2)}) collective-permute-start(bf16[512,256]{1,0:T(8,128)(2,1)S(1)} %get-tuple-element.20), channel_id=1, source_target_pairs={{0,8},{8,16},{16,24},{24,28},{28,20},{20,12},{12,4},{4,0},{1,9},{9... | collective-permute-start | bytes 786440 | tf_op jit(solution)/shard_map/ppermute | solution.py:468
  5.8 15.1 %collective-permute-start.4 = (bf16[512,256]{1,0:T(8,128)(2,1)S(1)}, bf16[512,256]{1,0:T(8,128)(2,1)S(1)}, u32[]{:S(2)}, u32[]{:S(2)}) collective-permute-start(bf16[512,256]{1,0:T(8,128)(2,1)S(1)} %get-tuple-element.19), channel_id=1, source_target_pairs={{0,8},{8,16},{16,24},{24,28},{28,20},{20,12},{12,4},{4,0},{1,9},{9... | collective-permute-start | bytes 786440 | tf_op jit(solution)/shard_map/ppermute | solution.py:468
  9.6 12.4 %collective-permute-start.7 = (bf16[512,256]{1,0:T(8,128)(2,1)S(1)}, bf16[512,256]{1,0:T(8,128)(2,1)S(1)}, u32[]{:S(2)}, u32[]{:S(2)}) collective-permute-start(bf16[512,256]{1,0:T(8,128)(2,1)S(1)} %get-tuple-element.20), channel_id=1, source_target_pairs={{0,4},{8,0},{16,8},{24,16},{28,24},{20,28},{12,20},{4,12},{1,5},{9... | collective-permute-start | bytes 786440 | tf_op jit(solution)/shard_map/ppermute | solution.py:468
  10.8 11.5 %collective-permute-start.8 = (bf16[512,256]{1,0:T(8,128)(2,1)S(1)}, bf16[512,256]{1,0:T(8,128)(2,1)S(1)}, u32[]{:S(2)}, u32[]{:S(2)}) collective-permute-start(bf16[512,256]{1,0:T(8,128)(2,1)S(1)} %get-tuple-element.19), channel_id=1, source_target_pairs={{0,4},{8,0},{16,8},{24,16},{28,24},{20,28},{12,20},{4,12},{1,5},{9... | collective-permute-start | bytes 786440 | tf_op jit(solution)/shard_map/ppermute | solution.py:468
  15.2 11.3 %collective-permute-start.9 = (bf16[512,256]{1,0:T(8,128)(2,1)S(1)}, bf16[512,256]{1,0:T(8,128)(2,1)}, u32[]{:S(2)}, u32[]{:S(2)}) collective-permute-start(bf16[512,256]{1,0:T(8,128)(2,1)S(1)} %collective-permute-done.1.refs_2_), channel_id=1, source_target_pairs={{0,8},{8,16},{16,24},{24,28},{28,20},{20,12},{12,4},{4,0},{1,9},{9... | collective-permute-start | bytes 786440 | tf_op jit(solution)/shard_map/ppermute | solution.py:468
  22.1 10.1 %collective-permute-start.11 = (bf16[512,256]{1,0:T(8,128)(2,1)S(1)}, bf16[512,256]{1,0:T(8,128)(2,1)}, u32[]{:S(2)}, u32[]{:S(2)}) collective-permute-start(bf16[512,256]{1,0:T(8,128)(2,1)S(1)} %collective-permute-done.3.refs_4_), channel_id=1, source_target_pairs={{0,8},{8,16},{16,24},{24,28},{28,20},{20,12},{12,4},{4,0},{1,9},{9... | collective-permute-start | bytes 786440 | tf_op jit(solution)/shard_map/ppermute | solution.py:468
  22.3 15.5 %collective-permute-start.12 = (bf16[512,256]{1,0:T(8,128)(2,1)S(1)}, bf16[512,256]{1,0:T(8,128)(2,1)S(1)}, u32[]{:S(2)}, u32[]{:S(2)}) collective-permute-start(bf16[512,256]{1,0:T(8,128)(2,1)S(1)} %collective-permute-done.4.refs_5_), channel_id=1, source_target_pairs={{0,8},{8,16},{16,24},{24,28},{28,20},{20,12},{12,4},{4,0},{1,9},{9... | collective-permute-start | bytes 786440 | tf_op jit(solution)/shard_map/ppermute | solution.py:468
  26.6 11.5 %collective-permute-start.15 = (bf16[512,256]{1,0:T(8,128)(2,1)S(1)}, bf16[512,256]{1,0:T(8,128)(2,1)S(1)}, u32[]{:S(2)}, u32[]{:S(2)}) collective-permute-start(bf16[512,256]{1,0:T(8,128)(2,1)S(1)} %collective-permute-done.7.refs_8_), channel_id=1, source_target_pairs={{0,4},{8,0},{16,8},{24,16},{28,24},{20,28},{12,20},{4,12},{1,5},{9... | collective-permute-start | bytes 786440 | tf_op jit(solution)/shard_map/ppermute | solution.py:468
  27.8 11.6 %collective-permute-start.16 = (bf16[512,256]{1,0:T(8,128)(2,1)S(1)}, bf16[512,256]{1,0:T(8,128)(2,1)}, u32[]{:S(2)}, u32[]{:S(2)}) collective-permute-start(bf16[512,256]{1,0:T(8,128)(2,1)S(1)} %collective-permute-done.8.refs_9_), channel_id=1, source_target_pairs={{0,4},{8,0},{16,8},{24,16},{28,24},{20,28},{12,20},{4,12},{1,5},{9... | collective-permute-start | bytes 786440 | tf_op jit(solution)/shard_map/ppermute | solution.py:468
  32.2 9.1 %collective-permute-start.2 = (bf16[512,256]{1,0:T(8,128)(2,1)S(1)}, bf16[512,256]{1,0:T(8,128)(2,1)S(1)}, u32[]{:S(2)}, u32[]{:S(2)}) collective-permute-start(bf16[512,256]{1,0:T(8,128)(2,1)S(1)} %collective-permute-done.1.refs_2_), channel_id=1, source_target_pairs={{0,2},{1,3},{2,0},{3,1},{4,6},{5,7},{6,4},{7,5},{8,10},{9,11},{10,... | collective-permute-start | bytes 786440 | tf_op jit(solution)/shard_map/ppermute | solution.py:462
  38.1 7.4 %collective-permute-start.17 = (bf16[512,256]{1,0:T(8,128)(2,1)}, bf16[512,256]{1,0:T(8,128)(2,1)}, u32[]{:S(2)}, u32[]{:S(2)}) collective-permute-start(bf16[512,256]{1,0:T(8,128)(2,1)} %collective-permute-done.9.refs_10_), channel_id=1, source_target_pairs={{0,8},{8,16},{16,24},{24,28},{28,20},{20,12},{12,4},{4,0},{1,9},{9... | collective-permute-start | bytes 786440 | tf_op jit(solution)/shard_map/ppermute | solution.py:468
  41.3 9.1 %collective-permute-start.10 = (bf16[512,256]{1,0:T(8,128)(2,1)}, bf16[512,256]{1,0:T(8,128)(2,1)}, u32[]{:S(2)}, u32[]{:S(2)}) collective-permute-start(bf16[512,256]{1,0:T(8,128)(2,1)} %collective-permute-done.9.refs_10_), channel_id=1, source_target_pairs={{0,2},{1,3},{2,0},{3,1},{4,6},{5,7},{6,4},{7,5},{8,10},{9,11},{10,... | collective-permute-start | bytes 786440 | tf_op jit(solution)/shard_map/ppermute | solution.py:462
  44.9 11.2 %collective-permute-start.14 = (bf16[512,256]{1,0:T(8,128)(2,1)}, bf16[512,256]{1,0:T(8,128)(2,1)}, u32[]{:S(2)}, u32[]{:S(2)}) collective-permute-start(bf16[512,256]{1,0:T(8,128)(2,1)} %collective-permute-done.13.refs_14_), channel_id=1, source_target_pairs={{0,2},{1,3},{2,0},{3,1},{4,6},{5,7},{6,4},{7,5},{8,10},{9,11},{10,... | collective-permute-start | bytes 786440 | tf_op jit(solution)/shard_map/ppermute | solution.py:462
  45.4 11.8 %collective-permute-start.29 = (bf16[512,256]{1,0:T(8,128)(2,1)}, bf16[512,256]{1,0:T(8,128)(2,1)}, u32[]{:S(2)}, u32[]{:S(2)}) collective-permute-start(bf16[512,256]{1,0:T(8,128)(2,1)} %collective-permute-done.16.refs_17_), channel_id=1, source_target_pairs={{0,4},{8,0},{16,8},{24,16},{28,24},{20,28},{12,20},{4,12},{1,5},{9... | collective-permute-start | bytes 786440 | tf_op jit(solution)/shard_map/ppermute | solution.py:468
  46.3 11.1 %collective-permute-start.26 = (bf16[512,256]{1,0:T(8,128)(2,1)}, bf16[512,256]{1,0:T(8,128)(2,1)S(1)}, u32[]{:S(2)}, u32[]{:S(2)}) collective-permute-start(bf16[512,256]{1,0:T(8,128)(2,1)} %collective-permute-done.11.refs_12_), channel_id=1, source_target_pairs={{0,8},{8,16},{16,24},{24,28},{28,20},{20,12},{12,4},{4,0},{1,9},{9... | collective-permute-start | bytes 786440 | tf_op jit(solution)/shard_map/ppermute | solution.py:468
  50.5 9.5 %collective-permute-start.21 = (bf16[256,256]{1,0:T(8,128)(2,1)S(1)}, bf16[256,256]{1,0:T(8,128)(2,1)S(1)}, u32[]{:S(2)}, u32[]{:S(2)}) collective-permute-start(bf16[256,256]{1,0:T(8,128)(2,1)S(1)} %slice.42), channel_id=1, source_target_pairs={{0,8},{8,16},{16,24},{24,28},{28,20},{20,12},{12,4},{4,0},{1,9},{9... | collective-permute-start | bytes 393224 | tf_op jit(solution)/shard_map/ppermute | solution.py:468
  57.2 18.5 %collective-permute-start.18 = (bf16[512,256]{1,0:T(8,128)(2,1)}, bf16[512,256]{1,0:T(8,128)(2,1)}, u32[]{:S(2)}, u32[]{:S(2)}) collective-permute-start(bf16[512,256]{1,0:T(8,128)(2,1)} %collective-permute-done.17.refs_18_), channel_id=1, source_target_pairs={{0,2},{1,3},{2,0},{3,1},{4,6},{5,7},{6,4},{7,5},{8,10},{9,11},{10,... | collective-permute-start | bytes 786440 | tf_op jit(solution)/shard_map/ppermute | solution.py:462
  57.5 19.5 %collective-permute-start.20 = (bf16[512,256]{1,0:T(8,128)(2,1)}, bf16[512,256]{1,0:T(8,128)(2,1)}, u32[]{:S(2)}, u32[]{:S(2)}) collective-permute-start(bf16[512,256]{1,0:T(8,128)(2,1)} %collective-permute-done.19.refs_20_), channel_id=1, source_target_pairs={{0,2},{1,3},{2,0},{3,1},{4,6},{5,7},{6,4},{7,5},{8,10},{9,11},{10,... | collective-permute-start | bytes 786440 | tf_op jit(solution)/shard_map/ppermute | solution.py:462
  59.9 11.7 %collective-permute-start.22 = (bf16[256,256]{1,0:T(8,128)(2,1)S(1)}, bf16[256,256]{1,0:T(8,128)(2,1)S(1)}, u32[]{:S(2)}, u32[]{:S(2)}) collective-permute-start(bf16[256,256]{1,0:T(8,128)(2,1)S(1)} %collective-permute-done.21.refs_22_), channel_id=1, source_target_pairs={{0,2},{1,3},{2,0},{3,1},{4,6},{5,7},{6,4},{7,5},{8,10},{9,11},{10,... | collective-permute-start | bytes 393224 | tf_op jit(solution)/shard_map/ppermute | solution.py:462
  60.2 14.2 %collective-permute-start.24 = (bf16[256,256]{1,0:T(8,128)(2,1)}, bf16[256,256]{1,0:T(8,128)(2,1)S(1)}, u32[]{:S(2)}, u32[]{:S(2)}) collective-permute-start(bf16[256,256]{1,0:T(8,128)(2,1)} %collective-permute-done.23.refs_24_), channel_id=1, source_target_pairs={{0,2},{1,3},{2,0},{3,1},{4,6},{5,7},{6,4},{7,5},{8,10},{9,11},{10,... | collective-permute-start | bytes 393224 | tf_op jit(solution)/shard_map/ppermute | solution.py:462
  71.7 17.2 %collective-permute-start.27 = (bf16[512,256]{1,0:T(8,128)(2,1)}, bf16[512,256]{1,0:T(8,128)(2,1)S(1)}, u32[]{:S(2)}, u32[]{:S(2)}) collective-permute-start(bf16[512,256]{1,0:T(8,128)(2,1)} %copy-done.10), channel_id=1, source_target_pairs={{0,8},{8,16},{16,24},{24,28},{28,20},{20,12},{12,4},{4,0},{1,9},{9... | collective-permute-start | bytes 786440 | tf_op jit(solution)/shard_map/ppermute | solution.py:468
  74.4 16.1 %collective-permute-start.28 = (bf16[512,256]{1,0:T(8,128)(2,1)}, bf16[512,256]{1,0:T(8,128)(2,1)}, u32[]{:S(2)}, u32[]{:S(2)}) collective-permute-start(bf16[512,256]{1,0:T(8,128)(2,1)} %copy-done.9), channel_id=1, source_target_pairs={{0,4},{8,0},{16,8},{24,16},{28,24},{20,28},{12,20},{4,12},{1,5},{9... | collective-permute-start | bytes 786440 | tf_op jit(solution)/shard_map/ppermute | solution.py:468
  75.7 16.1 %collective-permute-start.31 = (bf16[512,256]{1,0:T(8,128)(2,1)}, bf16[512,256]{1,0:T(8,128)(2,1)S(1)}, u32[]{:S(2)}, u32[]{:S(2)}) collective-permute-start(bf16[512,256]{1,0:T(8,128)(2,1)} %collective-permute-done.29), channel_id=1, source_target_pairs={{0,4},{8,0},{16,8},{24,16},{28,24},{20,28},{12,20},{4,12},{1,5},{9... | collective-permute-start | bytes 786440 | tf_op jit(solution)/shard_map/ppermute | solution.py:468
  77.0 15.1 %collective-permute-start.30 = (bf16[512,256]{1,0:T(8,128)(2,1)}, bf16[512,256]{1,0:T(8,128)(2,1)S(1)}, u32[]{:S(2)}, u32[]{:S(2)}) collective-permute-start(bf16[512,256]{1,0:T(8,128)(2,1)} %copy-done.25), channel_id=1, source_target_pairs={{0,8},{8,16},{16,24},{24,28},{28,20},{20,12},{12,4},{4,0},{1,9},{9... | collective-permute-start | bytes 786440 | tf_op jit(solution)/shard_map/ppermute | solution.py:468
  93.8 12.1 %collective-permute-start.25 = (bf16[512,256]{1,0:T(8,128)(2,1)S(1)}, bf16[512,256]{1,0:T(8,128)(2,1)S(1)}, u32[]{:S(2)}, u32[]{:S(2)}) collective-permute-start(bf16[512,256]{1,0:T(8,128)(2,1)S(1)} %copy-done.26), channel_id=1, source_target_pairs={{0,2},{1,3},{4,6},{5,7},{8,10},{9,11},{12,14},{13,15},{16,18},{17,... | collective-permute-start | bytes 786440 | tf_op jit(solution)/shard_map/ppermute | solution.py:465
  95.3 24.4 %collective-permute-start.35 = (bf16[512,256]{1,0:T(8,128)(2,1)S(1)}, bf16[512,256]{1,0:T(8,128)(2,1)S(1)}, u32[]{:S(2)}, u32[]{:S(2)}) collective-permute-start(bf16[512,256]{1,0:T(8,128)(2,1)S(1)} %fusion.1.refs_0_), channel_id=1, source_target_pairs={{0,1},{1,0},{2,3},{3,2},{4,5},{5,4},{6,7},{7,6},{8,9},{9,8},{10,11... | collective-permute-start | bytes 786440 | tf_op jit(solution)/shard_map/ppermute | solution.py:459
  99.2 20.5 %collective-permute-start.33 = (bf16[512,256]{1,0:T(8,128)(2,1)S(1)}, bf16[512,256]{1,0:T(8,128)(2,1)S(1)}, u32[]{:S(2)}, u32[]{:S(2)}) collective-permute-start(bf16[512,256]{1,0:T(8,128)(2,1)S(1)} %copy-done.26), channel_id=1, source_target_pairs={{0,1},{1,0},{2,3},{3,2},{4,5},{5,4},{6,7},{7,6},{8,9},{9,8},{10,11... | collective-permute-start | bytes 786440 | tf_op jit(solution)/shard_map/ppermute | solution.py:459
  99.6 20.1 %collective-permute-start.36 = (bf16[512,256]{1,0:T(8,128)(2,1)S(1)}, bf16[512,256]{1,0:T(8,128)(2,1)S(1)}, u32[]{:S(2)}, u32[]{:S(2)}) collective-permute-start(bf16[512,256]{1,0:T(8,128)(2,1)S(1)} %collective-permute-done.32.refs_1_), channel_id=1, source_target_pairs={{0,1},{1,0},{2,3},{3,2},{4,5},{5,4},{6,7},{7,6},{8,9},{9,8},{10,11... | collective-permute-start | bytes 786440 | tf_op jit(solution)/shard_map/ppermute | solution.py:459
  105.9 13.8 %collective-permute-start.34 = (bf16[512,256]{1,0:T(8,128)(2,1)S(1)}, bf16[512,256]{1,0:T(8,128)(2,1)S(1)}, u32[]{:S(2)}, u32[]{:S(2)}) collective-permute-start(bf16[512,256]{1,0:T(8,128)(2,1)S(1)} %collective-permute-done.25.refs_1_), channel_id=1, source_target_pairs={{0,1},{1,0},{2,3},{3,2},{4,5},{5,4},{6,7},{7,6},{8,9},{9,8},{10,11... | collective-permute-start | bytes 786440 | tf_op jit(solution)/shard_map/ppermute | solution.py:459
  (33 other events, 536.8 us)

commit v8 on v7

--- a/solution.py
+++ b/solution.py
@@ -370,7 +370,7 @@
         self.inverse = jax.ShapeDtypeStruct((count, self.stacked, BLK), jnp.float32)
         self.pairs = count * self.stacked * self.chunks * CHUNK // 2
 
-    def call(self, kernel, heads, out_shape, in_specs, out_specs, scratch, operands):
+    def call(self, kernel, heads, left, out_shape, in_specs, out_specs, scratch, operands):
         return pl.pallas_call(
             kernel,
             out_shape=out_shape,
@@ -381,7 +381,7 @@
                 out_specs=out_specs,
                 scratch_shapes=scratch,
             ),
-            compiler_params=pltpu.CompilerParams(vmem_limit_bytes=MOST_VMEM - LEFT_VMEM),
+            compiler_params=pltpu.CompilerParams(vmem_limit_bytes=MOST_VMEM - left),
             cost_estimate=pl.CostEstimate(
                 flops=4 * self.pairs * HEAD_SIZE,
                 bytes_accessed=2 * self.queries.size,
@@ -394,6 +394,7 @@
         return self.call(
             functools.partial(score_kernel, self.hops, rows, self.group),
             heads,
+            LEFT_VMEM,
             (self.probs, self.inverse),
             [self.kv_spec] * self.hops,
             (
@@ -409,6 +410,7 @@
         return self.call(
             functools.partial(attend_kernel, self.hops, self.row_blocks, self.group, heads),
             KEY_VALUE_HEADS,
+            21 << 18,
             jax.ShapeDtypeStruct(self.queries.shape, self.queries.dtype),
             [
                 pl.BlockSpec(memory_space=pltpu.MemorySpace.HBM),
@@ -575,7 +577,9 @@
     for hop in range(1, chips):
         keys.append(to_next_chip(keys[-1]))
         values.append(to_next_chip(values[-1]))
-    sibling_keys = [to_sibling(x) for x in keys]
+    sibling_keys = []
+    for hop, rows in enumerate(keys):
+        sibling_keys.append(to_sibling(rows))
     sibling_values = [to_sibling(x) for x in values]
 
     facts = jnp.concatenate([jnp.stack([core, my_index]), block_segments[0]])

time: 139 us -> 139 us (level)
  no operation moved by 1% of the time
where the time goes in v8:
time: 139 us; the launch traced here: 138 us
  starting transfers between devices  43.9 us (32%)
  waiting for transfers between devices  39.3 us (28%)
  Pallas kernels  36.6 us (26%)
  local copies, waits for them, and re-layouts  9.89 us (7%)
  matrix products  4.72 us (3%)
  other arithmetic  3.24 us (2%)
    pallas_call x2, Pallas kernels, call(): pl.pallas_call(kernel, out_shape=out_shape, grid_spec=pltpu.PrefetchScala...  27.7 us
    ppermute x22, starting transfers between devices, along_ring(): lax.ppermute(x, 'dp', [(ring[i], ring[(i + step) % dp_size]) for i in ran...  22.3 us
    ppermute x22, waiting for transfers between devices, along_ring(): lax.ppermute(x, 'dp', [(ring[i], ring[(i + step) % dp_size]) for i in ran...  21.4 us
    ppermute x8, waiting for transfers between devices, to_plane(): return lax.ppermute(x, 'ctx', [(i, i ^ CORES) for i in range(ctx_size)])  17.6 us
    ppermute x5, starting transfers between devices, to_sibling(): return lax.ppermute(x, 'ctx', [(i, i ^ 1) for i in range(ctx_size)])  13.8 us
    pallas_call x1, Pallas kernels, project_main(): pl.pallas_call(functools.partial(main_kernel, tuple(copies), early, shard...  8.92 us
    ppermute x8, starting transfers between devices, to_plane(): return lax.ppermute(x, 'ctx', [(i, i ^ CORES) for i in range(ctx_size)])  5.05 us
    dot_general x6, matrix products, late_product(): jnp.dot(columns[:, side * strip:(side + 1) * strip], piece, preferred_ele...  4.72 us
  transfers between devices with their start and end apart: 37, of which 12 were waited for; matrix products, arithmetic and copies ran while one was open for 12% of the time, Pallas kernels for 14%

profile of v8, /device:TPU:5, one launch (start us, length us, event | category | flops | bytes accessed | tf_op | source)
XLA Modules:
  0.0 138.2 jit_solution(6723084904393518150)
XLA Ops:
  1.8 1.3 collective-permute-start.1
  4.4 1.3 collective-permute-start.3
  5.8 1.3 collective-permute-start.4
  7.1 2.5 %collective-permute-done.1.refs_2_ = bf16[512,256]{1,0:T(8,128)(2,1)S(1)} collective-permute-done((bf16[512,256]{1,0:T(8,128)(2,1)S(1)}, bf16[512,256]{1,0:T(8,128)(2,1)S(1)}, u32[]{:S(2)}, u32[]{:S(2)}) %collective-permute-start.1) | collective-permute-done | bytes 262176 | tf_op jit(solution)/shard_map/ppermute | solution.py:470
  10.8 1.3 collective-permute-start.8
  12.1 3.1 %collective-permute-done.3.refs_4_ = bf16[512,256]{1,0:T(8,128)(2,1)S(1)} collective-permute-done((bf16[512,256]{1,0:T(8,128)(2,1)S(1)}, bf16[512,256]{1,0:T(8,128)(2,1)S(1)}, u32[]{:S(2)}, u32[]{:S(2)}) %collective-permute-start.3) | collective-permute-done | bytes 262176 | tf_op jit(solution)/shard_map/ppermute | solution.py:470
  15.2 1.3 collective-permute-start.9
  16.5 4.3 %collective-permute-done.4.refs_5_ = bf16[512,256]{1,0:T(8,128)(2,1)S(1)} collective-permute-done((bf16[512,256]{1,0:T(8,128)(2,1)S(1)}, bf16[512,256]{1,0:T(8,128)(2,1)S(1)}, u32[]{:S(2)}, u32[]{:S(2)}) %collective-permute-start.4) | collective-permute-done | bytes 262176 | tf_op jit(solution)/shard_map/ppermute | solution.py:470
  22.3 1.3 collective-permute-start.12
  23.6 2.9 %collective-permute-done.9.refs_10_ = bf16[512,256]{1,0:T(8,128)(2,1)} collective-permute-done((bf16[512,256]{1,0:T(8,128)(2,1)S(1)}, bf16[512,256]{1,0:T(8,128)(2,1)}, u32[]{:S(2)}, u32[]{:S(2)}) %collective-permute-start.9) | collective-permute-done | bytes 262176 | tf_op jit(solution)/shard_map/ppermute | solution.py:470
  27.8 1.3 collective-permute-start.16
  29.1 3.1 %collective-permute-done.11.refs_12_ = bf16[512,256]{1,0:T(8,128)(2,1)} collective-permute-done((bf16[512,256]{1,0:T(8,128)(2,1)S(1)}, bf16[512,256]{1,0:T(8,128)(2,1)}, u32[]{:S(2)}, u32[]{:S(2)}) %collective-permute-start.11) | collective-permute-done | bytes 262176 | tf_op jit(solution)/shard_map/ppermute | solution.py:470
  32.4 5.4 %collective-permute-done.12.refs_13_ = bf16[512,256]{1,0:T(8,128)(2,1)S(1)} collective-permute-done((bf16[512,256]{1,0:T(8,128)(2,1)S(1)}, bf16[512,256]{1,0:T(8,128)(2,1)S(1)}, u32[]{:S(2)}, u32[]{:S(2)}) %collective-permute-start.12) | collective-permute-done | bytes 262176 | tf_op jit(solution)/shard_map/ppermute | solution.py:470
  39.8 1.5 %dynamic-slice_bitcast_fusion.2 = (bf16[256,1024]{1,0:T(8,128)(2,1)S(1)}, bf16[256,1024]{1,0:T(8,128)(2,1)S(1)}, bf16[256,1024]{1,0:T(8,128)(2,1)S(1)}) fusion(bf16[1,256,8192]{2,1,0:T(8,128)(2,1)} %param.7, s32[]{:T(128)S(6)} %select_n.145, s32[]{:T(128)S(6)} %select_n.147, s32[]{:T(128)S(6)} %select_n.146), kind=kLoop, calls=%fused_computation.26 | loop fusion | bytes 3145740 | tf_op jit(solution)/shard_map/dynamic_slice | solution.py:554
  42.4 2.5 %collective-permute-done.6.refs_7_ = bf16[512,256]{1,0:T(8,128)(2,1)S(1)} collective-permute-done((bf16[512,256]{1,0:T(8,128)(2,1)S(1)}, bf16[512,256]{1,0:T(8,128)(2,1)S(1)}, u32[]{:S(2)}, u32[]{:S(2)}) %collective-permute-start.6) | collective-permute-done | bytes 262176 | tf_op jit(solution)/shard_map/ppermute | solution.py:464
  50.5 1.3 collective-permute-start.21
  51.8 4.3 %collective-permute-done.14.refs_15_ = bf16[512,256]{1,0:T(8,128)(2,1)} collective-permute-done((bf16[512,256]{1,0:T(8,128)(2,1)}, bf16[512,256]{1,0:T(8,128)(2,1)}, u32[]{:S(2)}, u32[]{:S(2)}) %collective-permute-start.14) | collective-permute-done | bytes 262176 | tf_op jit(solution)/shard_map/ppermute | solution.py:464
  63.7 8.0 %collective-permute-done.22.refs_23_ = bf16[256,256]{1,0:T(8,128)(2,1)S(1)} collective-permute-done((bf16[256,256]{1,0:T(8,128)(2,1)S(1)}, bf16[256,256]{1,0:T(8,128)(2,1)S(1)}, u32[]{:S(2)}, u32[]{:S(2)}) %collective-permute-start.22) | collective-permute-done | bytes 131104 | tf_op jit(solution)/shard_map/ppermute | solution.py:464
  72.1 2.3 %collective-permute-done.24.refs_25_ = bf16[256,256]{1,0:T(8,128)(2,1)S(1)} collective-permute-done((bf16[256,256]{1,0:T(8,128)(2,1)}, bf16[256,256]{1,0:T(8,128)(2,1)S(1)}, u32[]{:S(2)}, u32[]{:S(2)}) %collective-permute-start.24) | collective-permute-done | bytes 131104 | tf_op jit(solution)/shard_map/ppermute | solution.py:464
  74.4 1.3 collective-permute-start.28
  75.7 1.3 collective-permute-start.31
  77.2 8.9 %project_main.1 = (bf16[512,256]{1,0:T(8,128)(2,1)}, f32[512,256]{1,0:T(8,128)}) custom-call(s32[9]{0:T(128)} %stack.47.facts, bf16[256,8192]{1,0:T(8,128)(2,1)} %bitcast.29, bf16[256,8192]{1,0:T(8,128)(2,1)} %collective-permute-done.sibling_ref, f32[1,512]{1,0:T(1,128)} %bitcast.32, f32[512,256]{1,0:T(8,128)} %pad_maximum_fusion.6.table_hbm, ...), custom_call_target="tpu_custom_call" | custom-call | flops 3489660928 | bytes 12582912 | tf_op jit(solution)/shard_map/project_main/pallas_call | solution.py:114
  86.1 1.5 %constant_dynamic-slice_fusion.3 = (bf16[256,1024]{1,0:T(8,128)(2,1)S(1)}, bf16[256,1024]{1,0:T(8,128)(2,1)S(1)}, bf16[256,1024]{1,0:T(8,128)(2,1)S(1)}) fusion(bf16[256,8192]{1,0:T(8,128)(2,1)} %collective-permute-done.sibling_ref, s32[]{:T(128)S(6)} %select_n.145, s32[]{:T(128)S(6)} %select_n.147, s32[]{:T(128)S(6)} %select_n.146), kind=kLoop, calls=%fused_computation.33 | loop fusion | bytes 3145740 | tf_op jit(solution)/shard_map/dynamic_slice | solution.py:554
  87.6 1.3 fusion.8
  90.5 1.3 fusion.5
  92.5 1.3 collective-permute-start.32
  93.8 1.5 %collective-permute-start.25 = (bf16[512,256]{1,0:T(8,128)(2,1)S(1)}, bf16[512,256]{1,0:T(8,128)(2,1)S(1)}, u32[]{:S(2)}, u32[]{:S(2)}) collective-permute-start(bf16[512,256]{1,0:T(8,128)(2,1)S(1)} %copy-done.26), channel_id=1, source_target_pairs={{0,2},{1,3},{4,6},{5,7},{8,10},{9,11},{12,14},{13,15},{16,18},{17,... | collective-permute-start | bytes 786440 | tf_op jit(solution)/shard_map/ppermute | solution.py:467
  95.3 3.9 %collective-permute-start.35 = (bf16[512,256]{1,0:T(8,128)(2,1)S(1)}, bf16[512,256]{1,0:T(8,128)(2,1)S(1)}, u32[]{:S(2)}, u32[]{:S(2)}) collective-permute-start(bf16[512,256]{1,0:T(8,128)(2,1)S(1)} %fusion.1.refs_0_), channel_id=1, source_target_pairs={{0,1},{1,0},{2,3},{3,2},{4,5},{5,4},{6,7},{7,6},{8,9},{9,8},{10,11... | collective-permute-start | bytes 786440 | tf_op jit(solution)/shard_map/ppermute | solution.py:461
  99.6 6.3 %collective-permute-start.36 = (bf16[512,256]{1,0:T(8,128)(2,1)S(1)}, bf16[512,256]{1,0:T(8,128)(2,1)S(1)}, u32[]{:S(2)}, u32[]{:S(2)}) collective-permute-start(bf16[512,256]{1,0:T(8,128)(2,1)S(1)} %collective-permute-done.32.refs_1_), channel_id=1, source_target_pairs={{0,1},{1,0},{2,3},{3,2},{4,5},{5,4},{6,7},{7,6},{8,9},{9,8},{10,11... | collective-permute-start | bytes 786440 | tf_op jit(solution)/shard_map/ppermute | solution.py:461
  105.9 2.8 %collective-permute-start.34 = (bf16[512,256]{1,0:T(8,128)(2,1)S(1)}, bf16[512,256]{1,0:T(8,128)(2,1)S(1)}, u32[]{:S(2)}, u32[]{:S(2)}) collective-permute-start(bf16[512,256]{1,0:T(8,128)(2,1)S(1)} %collective-permute-done.25.refs_1_), channel_id=1, source_target_pairs={{0,1},{1,0},{2,3},{3,2},{4,5},{5,4},{6,7},{7,6},{8,9},{9,8},{10,11... | collective-permute-start | bytes 786440 | tf_op jit(solution)/shard_map/ppermute | solution.py:461
  109.3 10.3 %shard_map.73 = (bf16[4,4,1024,256]{3,2,1,0:T(8,128)(2,1)}, f32[4,1024,128]{2,1,0:T(8,128)}) custom-call(s32[10]{0:T(128)} %pad_add_fusion.facts, bf16[256,4096]{1,0:T(8,128)(2,1)} %bitcast.30, bf16[512,256]{1,0:T(8,128)(2,1)} %get-tuple-element.9.refs_0_, bf16[512,256]{1,0:T(8,128)(2,1)} %copy-done.27), custom_call_target="tpu_custom_call" | custom-call | flops 1073741824 | bytes 2097152 | tf_op jit(solution)/shard_map/pallas_call | solution.py:374
  120.6 17.4 %shard_map.74 = bf16[256,4096]{1,0:T(8,128)(2,1)} custom-call(s32[10]{0:T(128)} %pad_add_fusion.facts, bf16[256,4096]{1,0:T(8,128)(2,1)} %bitcast.31, bf16[4,4,1024,256]{3,2,1,0:T(8,128)(2,1)} %get-tuple-element.10.probs_hbm, f32[4,1024,128]{2,1,0:T(8,128)} %get-tuple-element.11.inverse_ref, bf16[512,256]{1,0:T(8,128)(2,1)} %copy-done, ...), custom_call_target="tpu_custom_call" | custom-call | flops 1073741824 | bytes 2097152 | tf_op jit(solution)/shard_map/pallas_call | solution.py:374
  (124 shorter events, 28.2 us)
Async XLA Ops:
  0.0 77.2 %collective-permute-start = (bf16[256,8192]{1,0:T(8,128)(2,1)}, bf16[256,8192]{1,0:T(8,128)(2,1)}, u32[]{:S(2)}, u32[]{:S(2)}) collective-permute-start(bf16[256,8192]{1,0:T(8,128)(2,1)} %bitcast.28), channel_id=1, source_target_pairs={{0,1},{1,0},{2,3},{3,2},{4,5},{5,4},{6,7},{7,6},{8,9},{9,8},{10,11... | collective-permute-start | bytes 12582920 | tf_op jit(solution)/shard_map/ppermute | solution.py:461
  1.8 7.8 %collective-permute-start.1 = (bf16[512,256]{1,0:T(8,128)(2,1)S(1)}, bf16[512,256]{1,0:T(8,128)(2,1)S(1)}, u32[]{:S(2)}, u32[]{:S(2)}) collective-permute-start(bf16[512,256]{1,0:T(8,128)(2,1)S(1)} %dynamic_slice.43), channel_id=1, source_target_pairs={{0,8},{8,16},{16,24},{24,28},{28,20},{20,12},{12,4},{4,0},{1,9},{9... | collective-permute-start | bytes 786440 | tf_op jit(solution)/shard_map/ppermute | solution.py:470
  3.2 7.6 %collective-permute-start.5 = (bf16[512,256]{1,0:T(8,128)(2,1)S(1)}, bf16[512,256]{1,0:T(8,128)(2,1)S(1)}, u32[]{:S(2)}, u32[]{:S(2)}) collective-permute-start(bf16[512,256]{1,0:T(8,128)(2,1)S(1)} %dynamic_slice.43), channel_id=1, source_target_pairs={{0,4},{8,0},{16,8},{24,16},{28,24},{20,28},{12,20},{4,12},{1,5},{9... | collective-permute-start | bytes 786440 | tf_op jit(solution)/shard_map/ppermute | solution.py:470
  4.4 10.8 %collective-permute-start.3 = (bf16[512,256]{1,0:T(8,128)(2,1)S(1)}, bf16[512,256]{1,0:T(8,128)(2,1)S(1)}, u32[]{:S(2)}, u32[]{:S(2)}) collective-permute-start(bf16[512,256]{1,0:T(8,128)(2,1)S(1)} %get-tuple-element.20), channel_id=1, source_target_pairs={{0,8},{8,16},{16,24},{24,28},{28,20},{20,12},{12,4},{4,0},{1,9},{9... | collective-permute-start | bytes 786440 | tf_op jit(solution)/shard_map/ppermute | solution.py:470
  5.8 15.1 %collective-permute-start.4 = (bf16[512,256]{1,0:T(8,128)(2,1)S(1)}, bf16[512,256]{1,0:T(8,128)(2,1)S(1)}, u32[]{:S(2)}, u32[]{:S(2)}) collective-permute-start(bf16[512,256]{1,0:T(8,128)(2,1)S(1)} %get-tuple-element.19), channel_id=1, source_target_pairs={{0,8},{8,16},{16,24},{24,28},{28,20},{20,12},{12,4},{4,0},{1,9},{9... | collective-permute-start | bytes 786440 | tf_op jit(solution)/shard_map/ppermute | solution.py:470
  9.6 12.4 %collective-permute-start.7 = (bf16[512,256]{1,0:T(8,128)(2,1)S(1)}, bf16[512,256]{1,0:T(8,128)(2,1)S(1)}, u32[]{:S(2)}, u32[]{:S(2)}) collective-permute-start(bf16[512,256]{1,0:T(8,128)(2,1)S(1)} %get-tuple-element.20), channel_id=1, source_target_pairs={{0,4},{8,0},{16,8},{24,16},{28,24},{20,28},{12,20},{4,12},{1,5},{9... | collective-permute-start | bytes 786440 | tf_op jit(solution)/shard_map/ppermute | solution.py:470
  10.8 11.5 %collective-permute-start.8 = (bf16[512,256]{1,0:T(8,128)(2,1)S(1)}, bf16[512,256]{1,0:T(8,128)(2,1)S(1)}, u32[]{:S(2)}, u32[]{:S(2)}) collective-permute-start(bf16[512,256]{1,0:T(8,128)(2,1)S(1)} %get-tuple-element.19), channel_id=1, source_target_pairs={{0,4},{8,0},{16,8},{24,16},{28,24},{20,28},{12,20},{4,12},{1,5},{9... | collective-permute-start | bytes 786440 | tf_op jit(solution)/shard_map/ppermute | solution.py:470
  15.2 11.3 %collective-permute-start.9 = (bf16[512,256]{1,0:T(8,128)(2,1)S(1)}, bf16[512,256]{1,0:T(8,128)(2,1)}, u32[]{:S(2)}, u32[]{:S(2)}) collective-permute-start(bf16[512,256]{1,0:T(8,128)(2,1)S(1)} %collective-permute-done.1.refs_2_), channel_id=1, source_target_pairs={{0,8},{8,16},{16,24},{24,28},{28,20},{20,12},{12,4},{4,0},{1,9},{9... | collective-permute-start | bytes 786440 | tf_op jit(solution)/shard_map/ppermute | solution.py:470
  22.1 10.1 %collective-permute-start.11 = (bf16[512,256]{1,0:T(8,128)(2,1)S(1)}, bf16[512,256]{1,0:T(8,128)(2,1)}, u32[]{:S(2)}, u32[]{:S(2)}) collective-permute-start(bf16[512,256]{1,0:T(8,128)(2,1)S(1)} %collective-permute-done.3.refs_4_), channel_id=1, source_target_pairs={{0,8},{8,16},{16,24},{24,28},{28,20},{20,12},{12,4},{4,0},{1,9},{9... | collective-permute-start | bytes 786440 | tf_op jit(solution)/shard_map/ppermute | solution.py:470
  22.3 15.5 %collective-permute-start.12 = (bf16[512,256]{1,0:T(8,128)(2,1)S(1)}, bf16[512,256]{1,0:T(8,128)(2,1)S(1)}, u32[]{:S(2)}, u32[]{:S(2)}) collective-permute-start(bf16[512,256]{1,0:T(8,128)(2,1)S(1)} %collective-permute-done.4.refs_5_), channel_id=1, source_target_pairs={{0,8},{8,16},{16,24},{24,28},{28,20},{20,12},{12,4},{4,0},{1,9},{9... | collective-permute-start | bytes 786440 | tf_op jit(solution)/shard_map/ppermute | solution.py:470
  26.6 11.5 %collective-permute-start.15 = (bf16[512,256]{1,0:T(8,128)(2,1)S(1)}, bf16[512,256]{1,0:T(8,128)(2,1)S(1)}, u32[]{:S(2)}, u32[]{:S(2)}) collective-permute-start(bf16[512,256]{1,0:T(8,128)(2,1)S(1)} %collective-permute-done.7.refs_8_), channel_id=1, source_target_pairs={{0,4},{8,0},{16,8},{24,16},{28,24},{20,28},{12,20},{4,12},{1,5},{9... | collective-permute-start | bytes 786440 | tf_op jit(solution)/shard_map/ppermute | solution.py:470
  27.8 11.6 %collective-permute-start.16 = (bf16[512,256]{1,0:T(8,128)(2,1)S(1)}, bf16[512,256]{1,0:T(8,128)(2,1)}, u32[]{:S(2)}, u32[]{:S(2)}) collective-permute-start(bf16[512,256]{1,0:T(8,128)(2,1)S(1)} %collective-permute-done.8.refs_9_), channel_id=1, source_target_pairs={{0,4},{8,0},{16,8},{24,16},{28,24},{20,28},{12,20},{4,12},{1,5},{9... | collective-permute-start | bytes 786440 | tf_op jit(solution)/shard_map/ppermute | solution.py:470
  32.2 9.1 %collective-permute-start.2 = (bf16[512,256]{1,0:T(8,128)(2,1)S(1)}, bf16[512,256]{1,0:T(8,128)(2,1)S(1)}, u32[]{:S(2)}, u32[]{:S(2)}) collective-permute-start(bf16[512,256]{1,0:T(8,128)(2,1)S(1)} %collective-permute-done.1.refs_2_), channel_id=1, source_target_pairs={{0,2},{1,3},{2,0},{3,1},{4,6},{5,7},{6,4},{7,5},{8,10},{9,11},{10,... | collective-permute-start | bytes 786440 | tf_op jit(solution)/shard_map/ppermute | solution.py:464
  38.1 7.4 %collective-permute-start.17 = (bf16[512,256]{1,0:T(8,128)(2,1)}, bf16[512,256]{1,0:T(8,128)(2,1)}, u32[]{:S(2)}, u32[]{:S(2)}) collective-permute-start(bf16[512,256]{1,0:T(8,128)(2,1)} %collective-permute-done.9.refs_10_), channel_id=1, source_target_pairs={{0,8},{8,16},{16,24},{24,28},{28,20},{20,12},{12,4},{4,0},{1,9},{9... | collective-permute-start | bytes 786440 | tf_op jit(solution)/shard_map/ppermute | solution.py:470
  41.3 9.1 %collective-permute-start.10 = (bf16[512,256]{1,0:T(8,128)(2,1)}, bf16[512,256]{1,0:T(8,128)(2,1)}, u32[]{:S(2)}, u32[]{:S(2)}) collective-permute-start(bf16[512,256]{1,0:T(8,128)(2,1)} %collective-permute-done.9.refs_10_), channel_id=1, source_target_pairs={{0,2},{1,3},{2,0},{3,1},{4,6},{5,7},{6,4},{7,5},{8,10},{9,11},{10,... | collective-permute-start | bytes 786440 | tf_op jit(solution)/shard_map/ppermute | solution.py:464
  44.9 11.2 %collective-permute-start.14 = (bf16[512,256]{1,0:T(8,128)(2,1)}, bf16[512,256]{1,0:T(8,128)(2,1)}, u32[]{:S(2)}, u32[]{:S(2)}) collective-permute-start(bf16[512,256]{1,0:T(8,128)(2,1)} %collective-permute-done.13.refs_14_), channel_id=1, source_target_pairs={{0,2},{1,3},{2,0},{3,1},{4,6},{5,7},{6,4},{7,5},{8,10},{9,11},{10,... | collective-permute-start | bytes 786440 | tf_op jit(solution)/shard_map/ppermute | solution.py:464
  45.4 11.8 %collective-permute-start.29 = (bf16[512,256]{1,0:T(8,128)(2,1)}, bf16[512,256]{1,0:T(8,128)(2,1)}, u32[]{:S(2)}, u32[]{:S(2)}) collective-permute-start(bf16[512,256]{1,0:T(8,128)(2,1)} %collective-permute-done.16.refs_17_), channel_id=1, source_target_pairs={{0,4},{8,0},{16,8},{24,16},{28,24},{20,28},{12,20},{4,12},{1,5},{9... | collective-permute-start | bytes 786440 | tf_op jit(solution)/shard_map/ppermute | solution.py:470
  46.3 11.1 %collective-permute-start.26 = (bf16[512,256]{1,0:T(8,128)(2,1)}, bf16[512,256]{1,0:T(8,128)(2,1)S(1)}, u32[]{:S(2)}, u32[]{:S(2)}) collective-permute-start(bf16[512,256]{1,0:T(8,128)(2,1)} %collective-permute-done.11.refs_12_), channel_id=1, source_target_pairs={{0,8},{8,16},{16,24},{24,28},{28,20},{20,12},{12,4},{4,0},{1,9},{9... | collective-permute-start | bytes 786440 | tf_op jit(solution)/shard_map/ppermute | solution.py:470
  50.5 9.5 %collective-permute-start.21 = (bf16[256,256]{1,0:T(8,128)(2,1)S(1)}, bf16[256,256]{1,0:T(8,128)(2,1)S(1)}, u32[]{:S(2)}, u32[]{:S(2)}) collective-permute-start(bf16[256,256]{1,0:T(8,128)(2,1)S(1)} %slice.42), channel_id=1, source_target_pairs={{0,8},{8,16},{16,24},{24,28},{28,20},{20,12},{12,4},{4,0},{1,9},{9... | collective-permute-start | bytes 393224 | tf_op jit(solution)/shard_map/ppermute | solution.py:470
  57.2 18.5 %collective-permute-start.18 = (bf16[512,256]{1,0:T(8,128)(2,1)}, bf16[512,256]{1,0:T(8,128)(2,1)}, u32[]{:S(2)}, u32[]{:S(2)}) collective-permute-start(bf16[512,256]{1,0:T(8,128)(2,1)} %collective-permute-done.17.refs_18_), channel_id=1, source_target_pairs={{0,2},{1,3},{2,0},{3,1},{4,6},{5,7},{6,4},{7,5},{8,10},{9,11},{10,... | collective-permute-start | bytes 786440 | tf_op jit(solution)/shard_map/ppermute | solution.py:464
  57.5 19.5 %collective-permute-start.20 = (bf16[512,256]{1,0:T(8,128)(2,1)}, bf16[512,256]{1,0:T(8,128)(2,1)}, u32[]{:S(2)}, u32[]{:S(2)}) collective-permute-start(bf16[512,256]{1,0:T(8,128)(2,1)} %collective-permute-done.19.refs_20_), channel_id=1, source_target_pairs={{0,2},{1,3},{2,0},{3,1},{4,6},{5,7},{6,4},{7,5},{8,10},{9,11},{10,... | collective-permute-start | bytes 786440 | tf_op jit(solution)/shard_map/ppermute | solution.py:464
  59.9 11.7 %collective-permute-start.22 = (bf16[256,256]{1,0:T(8,128)(2,1)S(1)}, bf16[256,256]{1,0:T(8,128)(2,1)S(1)}, u32[]{:S(2)}, u32[]{:S(2)}) collective-permute-start(bf16[256,256]{1,0:T(8,128)(2,1)S(1)} %collective-permute-done.21.refs_22_), channel_id=1, source_target_pairs={{0,2},{1,3},{2,0},{3,1},{4,6},{5,7},{6,4},{7,5},{8,10},{9,11},{10,... | collective-permute-start | bytes 393224 | tf_op jit(solution)/shard_map/ppermute | solution.py:464
  60.2 14.2 %collective-permute-start.24 = (bf16[256,256]{1,0:T(8,128)(2,1)}, bf16[256,256]{1,0:T(8,128)(2,1)S(1)}, u32[]{:S(2)}, u32[]{:S(2)}) collective-permute-start(bf16[256,256]{1,0:T(8,128)(2,1)} %collective-permute-done.23.refs_24_), channel_id=1, source_target_pairs={{0,2},{1,3},{2,0},{3,1},{4,6},{5,7},{6,4},{7,5},{8,10},{9,11},{10,... | collective-permute-start | bytes 393224 | tf_op jit(solution)/shard_map/ppermute | solution.py:464
  71.7 17.2 %collective-permute-start.27 = (bf16[512,256]{1,0:T(8,128)(2,1)}, bf16[512,256]{1,0:T(8,128)(2,1)S(1)}, u32[]{:S(2)}, u32[]{:S(2)}) collective-permute-start(bf16[512,256]{1,0:T(8,128)(2,1)} %copy-done.10), channel_id=1, source_target_pairs={{0,8},{8,16},{16,24},{24,28},{28,20},{20,12},{12,4},{4,0},{1,9},{9... | collective-permute-start | bytes 786440 | tf_op jit(solution)/shard_map/ppermute | solution.py:470
  74.4 16.1 %collective-permute-start.28 = (bf16[512,256]{1,0:T(8,128)(2,1)}, bf16[512,256]{1,0:T(8,128)(2,1)}, u32[]{:S(2)}, u32[]{:S(2)}) collective-permute-start(bf16[512,256]{1,0:T(8,128)(2,1)} %copy-done.9), channel_id=1, source_target_pairs={{0,4},{8,0},{16,8},{24,16},{28,24},{20,28},{12,20},{4,12},{1,5},{9... | collective-permute-start | bytes 786440 | tf_op jit(solution)/shard_map/ppermute | solution.py:470
  75.7 16.1 %collective-permute-start.31 = (bf16[512,256]{1,0:T(8,128)(2,1)}, bf16[512,256]{1,0:T(8,128)(2,1)S(1)}, u32[]{:S(2)}, u32[]{:S(2)}) collective-permute-start(bf16[512,256]{1,0:T(8,128)(2,1)} %collective-permute-done.29), channel_id=1, source_target_pairs={{0,4},{8,0},{16,8},{24,16},{28,24},{20,28},{12,20},{4,12},{1,5},{9... | collective-permute-start | bytes 786440 | tf_op jit(solution)/shard_map/ppermute | solution.py:470
  77.0 15.1 %collective-permute-start.30 = (bf16[512,256]{1,0:T(8,128)(2,1)}, bf16[512,256]{1,0:T(8,128)(2,1)S(1)}, u32[]{:S(2)}, u32[]{:S(2)}) collective-permute-start(bf16[512,256]{1,0:T(8,128)(2,1)} %copy-done.25), channel_id=1, source_target_pairs={{0,8},{8,16},{16,24},{24,28},{28,20},{20,12},{12,4},{4,0},{1,9},{9... | collective-permute-start | bytes 786440 | tf_op jit(solution)/shard_map/ppermute | solution.py:470
  93.8 12.1 %collective-permute-start.25 = (bf16[512,256]{1,0:T(8,128)(2,1)S(1)}, bf16[512,256]{1,0:T(8,128)(2,1)S(1)}, u32[]{:S(2)}, u32[]{:S(2)}) collective-permute-start(bf16[512,256]{1,0:T(8,128)(2,1)S(1)} %copy-done.26), channel_id=1, source_target_pairs={{0,2},{1,3},{4,6},{5,7},{8,10},{9,11},{12,14},{13,15},{16,18},{17,... | collective-permute-start | bytes 786440 | tf_op jit(solution)/shard_map/ppermute | solution.py:467
  95.3 24.4 %collective-permute-start.35 = (bf16[512,256]{1,0:T(8,128)(2,1)S(1)}, bf16[512,256]{1,0:T(8,128)(2,1)S(1)}, u32[]{:S(2)}, u32[]{:S(2)}) collective-permute-start(bf16[512,256]{1,0:T(8,128)(2,1)S(1)} %fusion.1.refs_0_), channel_id=1, source_target_pairs={{0,1},{1,0},{2,3},{3,2},{4,5},{5,4},{6,7},{7,6},{8,9},{9,8},{10,11... | collective-permute-start | bytes 786440 | tf_op jit(solution)/shard_map/ppermute | solution.py:461
  99.2 20.5 %collective-permute-start.33 = (bf16[512,256]{1,0:T(8,128)(2,1)S(1)}, bf16[512,256]{1,0:T(8,128)(2,1)S(1)}, u32[]{:S(2)}, u32[]{:S(2)}) collective-permute-start(bf16[512,256]{1,0:T(8,128)(2,1)S(1)} %copy-done.26), channel_id=1, source_target_pairs={{0,1},{1,0},{2,3},{3,2},{4,5},{5,4},{6,7},{7,6},{8,9},{9,8},{10,11... | collective-permute-start | bytes 786440 | tf_op jit(solution)/shard_map/ppermute | solution.py:461
  99.6 20.1 %collective-permute-start.36 = (bf16[512,256]{1,0:T(8,128)(2,1)S(1)}, bf16[512,256]{1,0:T(8,128)(2,1)S(1)}, u32[]{:S(2)}, u32[]{:S(2)}) collective-permute-start(bf16[512,256]{1,0:T(8,128)(2,1)S(1)} %collective-permute-done.32.refs_1_), channel_id=1, source_target_pairs={{0,1},{1,0},{2,3},{3,2},{4,5},{5,4},{6,7},{7,6},{8,9},{9,8},{10,11... | collective-permute-start | bytes 786440 | tf_op jit(solution)/shard_map/ppermute | solution.py:461
  105.9 13.8 %collective-permute-start.34 = (bf16[512,256]{1,0:T(8,128)(2,1)S(1)}, bf16[512,256]{1,0:T(8,128)(2,1)S(1)}, u32[]{:S(2)}, u32[]{:S(2)}) collective-permute-start(bf16[512,256]{1,0:T(8,128)(2,1)S(1)} %collective-permute-done.25.refs_1_), channel_id=1, source_target_pairs={{0,1},{1,0},{2,3},{3,2},{4,5},{5,4},{6,7},{7,6},{8,9},{9,8},{10,11... | collective-permute-start | bytes 786440 | tf_op jit(solution)/shard_map/ppermute | solution.py:461
  (33 other events, 536.8 us)
